TPU v7x, 32 devices: a whole 2x2x4 slice. The times are simulated.
32 devices in a mesh: corr: 8 (over z, x), tm: 4 (over y, core).
Axes of the slice: x: 2, y: 2, z: 4, core: 2. Of those that a mesh axis runs over, the one named last changes fastest.
Arguments:
- flows: bfloat16 [2, 96, 8192], P(None, 'tm', 'corr'), may hold values from 0.049804688 to 2
- counts: float32 [2, 96, 8192], P(None, 'tm', 'corr'), may hold values from 0.5 to 4
- local_blocks: bfloat16 [512, 128, 128], P('corr'), may hold values from 0 to 0.00390625
- local_path: int32 [512], P('corr'), may hold values from 0 to 7
- local_link: int32 [512], P('corr'), may hold values from 0 to 7
- local_lag: int32 [512], P('corr'), may hold values from 0 to 15
- remote_blocks: bfloat16 [512, 128, 128], P('corr'), may hold values from 0 to 0.00390625
- remote_path: int32 [512], P('corr'), may hold values from 0 to 7
- remote_link: int32 [512], P('corr'), may hold values from 0 to 7
- remote_lag: int32 [512], P('corr'), may hold values from 0 to 15
- remote_slot: int32 [512], P('corr'), may hold values from 0 to 79, as said below
Outputs:
- link_residual: float32 [2, 96, 8192], P(None, 'tm', 'corr')
- gradient: float32 [2, 96, 8192], P(None, 'tm', 'corr')
- new_flows: float32 [2, 96, 8192], P(None, 'tm', 'corr')
Inputs may be any that keep to these rules, and one draw needn't show every extreme that they name: remote_slot // 10 is the corridor that owns the block's links and never the block's own corridor; the slots of one corridor's remote blocks are distinct.
All inputs are finite; a program needn't handle non-finite values.
Results may differ from a plain program's by a relative error of at most 0.0003.
Values may be sent and summed in bfloat16 or wider, within the bound.
No kernel may reach another device: no remote copies, remote signals or barrier semaphores. Data moves between devices by JAX's collectives and lax.ppermute only.
A program may use at most 64 MiB of HBM per device.

v0:
```python
import jax
import jax.numpy as jnp
from jax import lax
from jax.sharding import PartitionSpec as P

LAGS = 16


HIGH = lax.Precision.HIGHEST
RATE = 0.5


def passed_along(block, axis, distance):
    devices = range(lax.axis_size(axis))
    route = [(i - distance, i) for i in devices if i - distance in devices]
    return lax.ppermute(block, axis, route)


def one_hot(labels, classes, dtype):
    return (labels[:, None] == jnp.arange(classes, dtype=jnp.int32)[None, :]).astype(dtype)


def shift_table(deltas, out_len, in_len, dtype):
    out_pos = jnp.arange(out_len, dtype=jnp.int32)[:, None]
    in_pos = jnp.arange(in_len, dtype=jnp.int32)[None, :]
    return ((in_pos - out_pos)[None, :, :] == deltas[:, None, None]).astype(dtype)


def pick_blocks(cube, hot):
    return jnp.einsum("dsqp,bq->dsbp", cube, hot, preferred_element_type=jnp.float32).astype(
        jnp.bfloat16
    )


def shift_narrow(picked, table):
    return jnp.einsum("dsbp,bts->dtbp", picked, table, preferred_element_type=jnp.float32).astype(
        jnp.bfloat16
    )


def route_partials(local_part, remote_part, local_route, remote_link, slot_hot, link_blocks):
    own = jnp.einsum("dtbl,bk->dtkl", local_part, local_route, precision=HIGH)
    outgoing = jnp.einsum("bdtl,bs->sdtl", remote_part, slot_hot, precision=HIGH)
    slot_int = slot_hot.astype(jnp.int32)
    labels = link_blocks + jnp.sum(slot_int * (remote_link[:, None] - link_blocks), axis=0)
    return (own, outgoing, labels)


def absorb(own, received, got_labels, link_blocks):
    landing = one_hot(got_labels, link_blocks, jnp.float32)
    return own + jnp.einsum("sdtl,sk->dtkl", received, landing, precision=HIGH)


def collect_paths(local_grad, remote_grad, local_paths, remote_paths):
    first_sum = jnp.einsum("dtbp,bq->dtqp", local_grad, local_paths, precision=HIGH)
    return first_sum + jnp.einsum("bdtp,bq->dtqp", remote_grad, remote_paths, precision=HIGH)


def per_device(
    flows,
    counts,
    local_blocks,
    local_path,
    local_link,
    local_lag,
    remote_blocks,
    remote_path,
    remote_link,
    remote_lag,
    remote_slot,
):
    day_count, minutes, path_width = flows.shape
    block_width = local_blocks.shape[1]
    path_blocks = path_width // block_width
    link_blocks = counts.shape[2] // block_width
    lag_span = LAGS - 1
    corridors = lax.axis_size("corr")
    remote_count = remote_lag.shape[0]
    slot_count = corridors * ((remote_count + corridors - 2) // (corridors - 1))
    flow_cube = flows.reshape(day_count, minutes, path_blocks, block_width)
    local_route = one_hot(local_link, link_blocks, jnp.float32)
    slot_hot = one_hot(remote_slot, slot_count, jnp.float32)
    slot_pick = slot_hot.astype(jnp.bfloat16)
    local_path_hot = one_hot(local_path, path_blocks, jnp.bfloat16)
    remote_path_hot = one_hot(remote_path, path_blocks, jnp.bfloat16)
    local_link_hot = one_hot(local_link, link_blocks, jnp.bfloat16)
    local_in = pick_blocks(flow_cube, local_path_hot)
    remote_in = pick_blocks(flow_cube, remote_path_hot)
    local_plain = jnp.einsum(
        "dtbp,blp->dtbl", local_in, local_blocks, preferred_element_type=jnp.float32
    )
    remote_plain = jnp.einsum(
        "dtbp,blp->bdtl", remote_in, remote_blocks, preferred_element_type=jnp.float32
    )
    local_part = jnp.einsum(
        "dsbl,bts->dtbl",
        local_plain,
        shift_table(-local_lag, minutes + lag_span, minutes, jnp.float32),
        precision=HIGH,
    )
    remote_part = jnp.einsum(
        "bdsl,bts->bdtl",
        remote_plain,
        shift_table(-remote_lag, minutes + lag_span, minutes, jnp.float32),
        precision=HIGH,
    )
    own, outgoing, labels = route_partials(
        local_part, remote_part, local_route, remote_link, slot_hot, link_blocks
    )
    received, got_labels = (
        lax.all_to_all(outgoing, "corr", split_axis=0, concat_axis=0, tiled=True),
        lax.all_to_all(labels, "corr", split_axis=0, concat_axis=0, tiled=True),
    )
    extended = absorb(own, received, got_labels, link_blocks)
    spill = passed_along(extended[:, minutes:], "tm", 1)
    totals = extended[:, :minutes] + jnp.pad(
        spill, ((0, 0), (0, minutes - lag_span), (0, 0), (0, 0))
    )
    link_flow = totals.reshape(day_count, minutes, link_blocks * block_width)
    link_residual = (link_flow - counts) / (counts + 1.0)
    signal = (link_residual / (counts + 1.0)).astype(jnp.bfloat16)
    slot_route = one_hot(got_labels, link_blocks, jnp.bfloat16)
    local_paths = one_hot(local_path, path_blocks, jnp.float32)
    remote_paths = one_hot(remote_path, path_blocks, jnp.float32)
    ahead = passed_along(signal[:, :lag_span, :], "tm", -1)
    extended_signal = jnp.concatenate([signal, ahead], axis=1).reshape(
        day_count, minutes + lag_span, link_blocks, block_width
    )
    slot_signal = jnp.einsum(
        "dtkl,sk->sdtl", extended_signal, slot_route, preferred_element_type=jnp.float32
    ).astype(jnp.bfloat16)
    returned = lax.all_to_all(slot_signal, "corr", split_axis=0, concat_axis=0, tiled=True)
    remote_pick = jnp.einsum(
        "sdtl,bs->bdtl", returned, slot_pick, preferred_element_type=jnp.float32
    ).astype(jnp.bfloat16)
    remote_sig = jnp.einsum(
        "bdsl,bts->bdtl",
        remote_pick,
        shift_table(remote_lag, minutes, minutes + lag_span, jnp.bfloat16),
        preferred_element_type=jnp.float32,
    ).astype(jnp.bfloat16)
    local_sig = shift_narrow(
        pick_blocks(extended_signal, local_link_hot),
        shift_table(local_lag, minutes, minutes + lag_span, jnp.bfloat16),
    )
    local_grad = jnp.einsum(
        "dtbl,blp->dtbp", local_sig, local_blocks, preferred_element_type=jnp.float32
    )
    remote_grad = jnp.einsum(
        "bdtl,blp->bdtp", remote_sig, remote_blocks, preferred_element_type=jnp.float32
    )
    grad_cube = collect_paths(local_grad, remote_grad, local_paths, remote_paths)
    gradient = grad_cube.reshape(day_count, minutes, path_width)
    new_flows = jnp.maximum(flows.astype(jnp.float32) - RATE * gradient, 0.0)
    return (link_residual, gradient, new_flows)


def solution(mesh):
    placed = (
        P(None, "tm", "corr"),
        P(None, "tm", "corr"),
        P("corr", None, None),
        P("corr"),
        P("corr"),
        P("corr"),
        P("corr", None, None),
        P("corr"),
        P("corr"),
        P("corr"),
        P("corr"),
    )
    return jax.shard_map(
        per_device,
        mesh=mesh,
        in_specs=placed,
        out_specs=(P(None, "tm", "corr"), P(None, "tm", "corr"), P(None, "tm", "corr")),
        check_vma=False,
    )
```

profile of v0, /device:TPU:1, one launch (start us, length us, event | category | flops | bytes accessed | tf_op | source)
XLA Modules:
  0.0 169.5 jit_solution(16809793898177648229)
XLA Ops:
  0.6 0.0 copy-start
  0.6 0.8 broadcast_add_fusion.1
  1.5 0.8 fusion.83
  2.2 0.7 add.41
  2.9 6.4 %all-to-all-start = ((s32[8,10,1]{1,2,0:T(1,128)}), s32[8,10,1]{1,2,0:T(1,128)S(1)}, u32[]{:S(2)}, u32[]{:S(2)}) async-start(s32[8,10,1]{1,2,0:T(1,128)} %bitcast.11), calls=%async_computation | async-start | bytes 8192 | tf_op jit(solution)/shard_map/all_to_all | solution.py:112
  9.3 0.9 copy.41
  10.2 0.7 neg.7
  10.8 1.1 fusion.31
  11.9 3.1 %fusion.8 = f32[64,2,24,128]{3,2,1,0:T(8,128)S(1)} fusion(bf16[64,128,128]{2,1,0:T(8,128)(2,1)} %param.17, bf16[2,24,64,128]{3,2,1,0:T(8,128)(2,1)S(1)} %fusion.31), kind=kOutput, calls=%fused_computation.8 | convolution fusion | flops 100663296 | bytes 4456448 | tf_op jit(solution)/shard_map/dtbp,blp->bdtl/dot_general | solution.py:92
  15.0 0.0 copy-start.6
  15.0 1.6 convolution_bitcast_fusion
  16.6 0.0 copy-done.6
  16.6 2.4 %fusion.2 = f32[80,2,39,128]{3,0,2,1:T(8,128)S(1)} fusion(f32[64,2,39,128]{3,2,1,0:T(8,128)S(1)} %convolution_bitcast_fusion, s32[64]{0:T(128)S(1)} %copy-done.6), kind=kOutput, calls=%fused_computation.2 | convolution fusion | flops 613422080 | bytes 5751040 | tf_op jit(solution)/shard_map/bdtl,bs->sdtl/dot_general | solution.py:43
  19.0 3.3 %copy.21 = f32[80,2,39,128]{3,1,2,0:T(2,128)} copy(f32[80,2,39,128]{3,0,2,1:T(8,128)S(1)} %fusion.2) | data formatting | bytes 6389760 | tf_op jit(solution)/shard_map/bdtl,bs->sdtl/dot_general | solution.py:43
  22.3 0.0 copy-start.10
  22.3 0.0 copy-start.7
  22.3 0.0 all-to-all-done
  22.3 5.6 %all-to-all-start.1 = ((f32[80,2,39,128]{3,1,2,0:T(2,128)}), f32[80,2,39,128]{3,1,2,0:T(2,128)}, u32[]{:S(2)}, u32[]{:S(2)}) async-start(f32[80,2,39,128]{3,1,2,0:T(2,128)} %copy.21), calls=%async_computation.1 | async-start | bytes 6389760 | tf_op jit(solution)/shard_map/all_to_all | solution.py:111
  27.9 0.0 copy-done.10
  27.9 0.0 copy-done.7
  27.9 0.4 fusion.30
  28.4 0.0 copy-done
  28.4 1.6 fusion.12
  29.9 0.0 copy-start.5
  30.0 1.6 convolution_bitcast_fusion.1
  31.5 0.0 copy-done.5
  31.5 1.6 fusion.4
  33.1 0.5 broadcast.45
  33.6 0.7 reduce.3
  34.3 0.1 eq.68
  34.4 0.0 copy-start.4
  34.4 64.0 %all-to-all-done.1 = f32[80,2,39,128]{3,1,2,0:T(2,128)} async-done(((f32[80,2,39,128]{3,1,2,0:T(2,128)}), f32[80,2,39,128]{3,1,2,0:T(2,128)}, u32[]{:S(2)}, u32[]{:S(2)}) %all-to-all-start.1) | async-done | bytes 3194912 | tf_op jit(solution)/shard_map/all_to_all | solution.py:111
  98.3 3.0 %fusion.45 = f32[2,39,8,128]{3,2,1,0:T(8,128)S(1)} fusion(f32[8,2,39,128]{3,0,2,1:T(8,128)S(1)} %fusion.4, f32[80,2,39,128]{3,1,2,0:T(2,128)} %all-to-all-done.1, s32[80]{0:T(128)S(1)} %eq.68), kind=kOutput, calls=%fused_computation.39 | convolution fusion | flops 76757632 | bytes 3834176 | tf_op jit(solution)/shard_map/sdtl,sk->dtkl/dot_general | solution.py:51
  101.4 5.4 %collective-permute-start = (f32[2,15,8,128]{3,2,1,0:T(8,128)S(1)}, f32[2,15,8,128]{3,2,1,0:T(8,128)S(1)}, u32[]{:S(2)}, u32[]{:S(2)}) collective-permute-start(f32[2,15,8,128]{3,2,1,0:T(8,128)S(1)} %slice.13), channel_id=1, source_target_pairs={{0,1},{1,2},{2,3},{4,5},{5,6},{6,7},{8,9},{9,10},{10,11},{12,13},{... | collective-permute-start | bytes 368648 | tf_op jit(solution)/shard_map/ppermute | solution.py:16
  106.8 1.8 %collective-permute-done = f32[2,15,8,128]{3,2,1,0:T(8,128)S(1)} collective-permute-done((f32[2,15,8,128]{3,2,1,0:T(8,128)S(1)}, f32[2,15,8,128]{3,2,1,0:T(8,128)S(1)}, u32[]{:S(2)}, u32[]{:S(2)}) %collective-permute-start) | collective-permute-done | bytes 122912 | tf_op jit(solution)/shard_map/ppermute | solution.py:16
  108.7 0.0 copy-done.4
  108.7 0.7 divide_convert_fusion
  109.5 1.9 %collective-permute-start.1 = (bf16[2,15,1024]{2,1,0:T(8,128)(2,1)S(1)}, bf16[2,15,1024]{2,1,0:T(8,128)(2,1)S(1)}, u32[]{:S(2)}, u32[]{:S(2)}) collective-permute-start(bf16[2,15,1024]{2,1,0:T(8,128)(2,1)S(1)} %slice.14), channel_id=1, source_target_pairs={{1,0},{2,1},{3,2},{5,4},{6,5},{7,6},{9,8},{10,9},{11,10},{13,12},{... | collective-permute-start | bytes 184328 | tf_op jit(solution)/shard_map/ppermute | solution.py:16
  111.4 4.4 %collective-permute-done.1 = bf16[2,15,1024]{2,1,0:T(8,128)(2,1)S(1)} collective-permute-done((bf16[2,15,1024]{2,1,0:T(8,128)(2,1)S(1)}, bf16[2,15,1024]{2,1,0:T(8,128)(2,1)S(1)}, u32[]{:S(2)}, u32[]{:S(2)}) %collective-permute-start.1) | collective-permute-done | bytes 61472 | tf_op jit(solution)/shard_map/ppermute | solution.py:16
  115.8 0.1 reshape.70
  115.9 0.6 convolution_convert_fusion
  116.5 2.4 %copy.25 = bf16[80,2,39,128]{3,1,2,0:T(2,128)(2,1)} copy(bf16[80,2,39,128]{3,0,2,1:T(8,128)(2,1)S(1)} %convolution_convert_fusion) | data formatting | bytes 3194880 | tf_op jit(solution)/shard_map/convert_element_type | solution.py:131
  118.9 4.5 %all-to-all-start.2 = ((bf16[80,2,39,128]{3,1,2,0:T(2,128)(2,1)}), bf16[80,2,39,128]{3,1,2,0:T(2,128)(2,1)}, u32[]{:S(2)}, u32[]{:S(2)}) async-start(bf16[80,2,39,128]{3,1,2,0:T(2,128)(2,1)} %copy.25), calls=%async_computation.2 | async-start | bytes 3194880 | tf_op jit(solution)/shard_map/all_to_all | solution.py:132
  123.4 0.5 fusion.27
  124.0 3.6 %fusion.24 = f32[2,24,64,128]{3,1,0,2:T(8,128)} fusion(bf16[64,128,128]{2,1,0:T(8,128)(2,1)S(1)} %copy-done, bf16[2,39,64,128]{3,2,1,0:T(8,128)(2,1)S(1)} %fusion.27, s32[24,39]{1,0:T(8,128)S(1)} %iota_subtract_fusion, s32[64]{0:T(128)} %param.16), kind=kOutput, calls=%fused_computation.26 | convolution fusion | flops 131787264 | bytes 4951968 | tf_op jit(solution)/shard_map/dtbl,blp->dtbp/dot_general | solution.py:146
  127.6 0.0 copy-start.11
  127.6 31.0 %all-to-all-done.2 = bf16[80,2,39,128]{3,1,2,0:T(2,128)(2,1)} async-done(((bf16[80,2,39,128]{3,1,2,0:T(2,128)(2,1)}), bf16[80,2,39,128]{3,1,2,0:T(2,128)(2,1)}, u32[]{:S(2)}, u32[]{:S(2)}) %all-to-all-start.2) | async-done | bytes 1597472 | tf_op jit(solution)/shard_map/all_to_all | solution.py:132
  158.6 2.0 %fusion.16 = bf16[64,2,39,128]{3,0,2,1:T(8,128)(2,1)S(1)} fusion(bf16[80,2,39,128]{3,1,2,0:T(2,128)(2,1)} %all-to-all-done.2, s32[64]{0:T(128)S(1)} %copy-done.6), kind=kOutput, calls=%fused_computation.19 | convolution fusion | flops 102890496 | bytes 2875648 | tf_op jit(solution)/shard_map/sdtl,bs->bdtl/dot_general | solution.py:133
  160.6 0.0 copy-done.11
  160.6 0.0 copy-start.9
  160.6 4.6 %fusion.6 = f32[64,2,24,128]{3,2,1,0:T(8,128)} fusion(bf16[64,128,128]{2,1,0:T(8,128)(2,1)} %param.17, bf16[64,2,39,128]{3,0,2,1:T(8,128)(2,1)S(1)} %fusion.16, s32[24,39]{1,0:T(8,128)S(1)} %iota_subtract_fusion, s32[64]{0:T(128)S(1)} %copy-done.11), kind=kOutput, calls=%fused_computation.6 | convolution fusion | flops 131787264 | bytes 4951968 | tf_op jit(solution)/shard_map/bdtl,blp->bdtp/dot_general | solution.py:149
  165.2 0.0 copy-done.9
  165.2 0.0 copy-start.1
  165.2 0.0 copy-start.8
  165.2 2.5 %fusion.20 = f32[8,2,24,128]{3,0,2,1:T(8,128)S(1)} fusion(f32[64,2,24,128]{3,2,1,0:T(8,128)} %fusion.6, s32[64]{0:T(128)S(1)} %copy-done.9), kind=kOutput, calls=%fused_computation.22 | convolution fusion | flops 37749248 | bytes 1769728 | tf_op jit(solution)/shard_map/bdtp,bq->dtqp/dot_general | solution.py:56
  167.7 0.0 copy-done.1
  167.7 0.0 copy-done.8
  167.7 0.0 copy-start.3
  167.7 1.0 fusion.51
  168.8 0.0 copy-done.3
  168.8 0.0 copy-start.2
  168.8 0.7 subtract_maximum_fusion
  169.5 0.0 copy-done.2
  (10 shorter events, 0.1 us)
Async XLA Ops:
  0.6 27.7 %copy-start = (bf16[64,128,128]{2,1,0:T(8,128)(2,1)S(1)}, bf16[64,128,128]{2,1,0:T(8,128)(2,1)}, u32[]{:S(2)}) copy-start(bf16[64,128,128]{2,1,0:T(8,128)(2,1)} %param.13) | copy-start | bytes 6291460
  2.9 19.4 %all-to-all-start = ((s32[8,10,1]{1,2,0:T(1,128)}), s32[8,10,1]{1,2,0:T(1,128)S(1)}, u32[]{:S(2)}, u32[]{:S(2)}) async-start(s32[8,10,1]{1,2,0:T(1,128)} %bitcast.11), calls=%async_computation | async-start | bytes 8192 | tf_op jit(solution)/shard_map/all_to_all | solution.py:112
  15.0 1.6 copy-start.6
  22.3 5.6 %copy-start.10 = (s32[64]{0:T(128)S(1)}, s32[64]{0:T(128)}, u32[]{:S(2)}) copy-start(s32[64]{0:T(128)} %param.16) | copy-start | bytes 772
  22.3 5.6 %copy-start.7 = (s32[64]{0:T(128)S(1)}, s32[64]{0:T(128)}, u32[]{:S(2)}) copy-start(s32[64]{0:T(128)} %param.14) | copy-start | bytes 772
  22.3 76.0 %all-to-all-start.1 = ((f32[80,2,39,128]{3,1,2,0:T(2,128)}), f32[80,2,39,128]{3,1,2,0:T(2,128)}, u32[]{:S(2)}, u32[]{:S(2)}) async-start(f32[80,2,39,128]{3,1,2,0:T(2,128)} %copy.21), calls=%async_computation.1 | async-start | bytes 6389760 | tf_op jit(solution)/shard_map/all_to_all | solution.py:111
  29.9 1.6 copy-start.5
  34.4 74.4 %copy-start.4 = (f32[2,24,1024]{2,1,0:T(8,128)S(1)}, f32[2,24,1024]{2,1,0:T(8,128)}, u32[]{:S(2)}) copy-start(f32[2,24,1024]{2,1,0:T(8,128)} %param.12) | copy-start | bytes 589828
  101.4 7.3 %collective-permute-start = (f32[2,15,8,128]{3,2,1,0:T(8,128)S(1)}, f32[2,15,8,128]{3,2,1,0:T(8,128)S(1)}, u32[]{:S(2)}, u32[]{:S(2)}) collective-permute-start(f32[2,15,8,128]{3,2,1,0:T(8,128)S(1)} %slice.13), channel_id=1, source_target_pairs={{0,1},{1,2},{2,3},{4,5},{5,6},{6,7},{8,9},{9,10},{10,11},{12,13},{... | collective-permute-start | bytes 368648 | tf_op jit(solution)/shard_map/ppermute | solution.py:16
  109.5 6.3 %collective-permute-start.1 = (bf16[2,15,1024]{2,1,0:T(8,128)(2,1)S(1)}, bf16[2,15,1024]{2,1,0:T(8,128)(2,1)S(1)}, u32[]{:S(2)}, u32[]{:S(2)}) collective-permute-start(bf16[2,15,1024]{2,1,0:T(8,128)(2,1)S(1)} %slice.14), channel_id=1, source_target_pairs={{1,0},{2,1},{3,2},{5,4},{6,5},{7,6},{9,8},{10,9},{11,10},{13,12},{... | collective-permute-start | bytes 184328 | tf_op jit(solution)/shard_map/ppermute | solution.py:16
  118.9 39.7 %all-to-all-start.2 = ((bf16[80,2,39,128]{3,1,2,0:T(2,128)(2,1)}), bf16[80,2,39,128]{3,1,2,0:T(2,128)(2,1)}, u32[]{:S(2)}, u32[]{:S(2)}) async-start(bf16[80,2,39,128]{3,1,2,0:T(2,128)(2,1)} %copy.25), calls=%async_computation.2 | async-start | bytes 3194880 | tf_op jit(solution)/shard_map/all_to_all | solution.py:132
  127.6 33.0 %copy-start.11 = (s32[64]{0:T(128)S(1)}, s32[64]{0:T(128)}, u32[]{:S(2)}) copy-start(s32[64]{0:T(128)} %param.20) | copy-start | bytes 772
  160.6 4.6 %copy-start.9 = (s32[64]{0:T(128)S(1)}, s32[64]{0:T(128)}, u32[]{:S(2)}) copy-start(s32[64]{0:T(128)} %param.18) | copy-start | bytes 772
  165.2 2.5 %copy-start.1 = (f32[2,24,64,128]{3,1,0,2:T(8,128)S(1)}, f32[2,24,64,128]{3,1,0,2:T(8,128)}, u32[]{:S(2)}) copy-start(f32[2,24,64,128]{3,1,0,2:T(8,128)} %fusion.24) | copy-start | bytes 4718596
  165.2 2.5 %copy-start.8 = (s32[64]{0:T(128)S(1)}, s32[64]{0:T(128)}, u32[]{:S(2)}) copy-start(s32[64]{0:T(128)} %param.14) | copy-start | bytes 772
  167.7 1.1 copy-start.3
  168.8 0.7 copy-start.2
where the time goes:
time: 170 us
  waiting for transfers between devices  101 us (59%)
  matrix products  31.1 us (18%)
  starting transfers between devices  23.8 us (14%)
  local copies, waits for them, and re-layouts  8.16 us (5%)
  other arithmetic  4.4 us (3%)
    all_to_all x1, waiting for transfers between devices, per_device(): lax.all_to_all(outgoing, 'corr', split_axis=0, concat_axis=0, tiled=True)  64 us
    all_to_all x1, waiting for transfers between devices, per_device(): lax.all_to_all(slot_signal, 'corr', split_axis=0, concat_axis=0, tiled=True)  31 us
    ppermute x2, starting transfers between devices, passed_along(): return lax.ppermute(block, axis, route)  7.34 us
    all_to_all x1, starting transfers between devices, per_device(): lax.all_to_all(labels, 'corr', split_axis=0, concat_axis=0, tiled=True)  6.35 us
    ppermute x2, waiting for transfers between devices, passed_along(): return lax.ppermute(block, axis, route)  6.21 us
    all_to_all x1, starting transfers between devices, per_device(): lax.all_to_all(outgoing, 'corr', split_axis=0, concat_axis=0, tiled=True)  5.57 us
    dot_general x1, matrix products, per_device(): jnp.einsum('bdtl,blp->bdtp', remote_sig, remote_blocks, preferred_element...  4.56 us
    all_to_all x1, starting transfers between devices, per_device(): lax.all_to_all(slot_signal, 'corr', split_axis=0, concat_axis=0, tiled=True)  4.52 us
  transfers between devices with their start and end apart: 5, of which 4 were waited for; matrix products, arithmetic and copies ran while one was open for 14% of the time, Pallas kernels for 0%

commit v1 on v0

--- a/solution.py
+++ b/solution.py
@@ -1,6 +1,9 @@
+import functools
 import jax
 import jax.numpy as jnp
 from jax import lax
+from jax.experimental import pallas as pl
+from jax.experimental.pallas import tpu as pltpu
 from jax.sharding import PartitionSpec as P
 
 LAGS = 16
@@ -56,7 +59,7 @@
     return first_sum + jnp.einsum("bdtp,bq->dtqp", remote_grad, remote_paths, precision=HIGH)
 
 
-def per_device(
+def per_device_slots(
     flows,
     counts,
     local_blocks,
@@ -155,6 +158,260 @@
     return (link_residual, gradient, new_flows)
 
 
+HALO = 16
+WIRE = jnp.float16
+
+
+def window_rows(path, day, lag, days, span):
+    return (path * days + day) * span + HALO - lag
+
+
+def stage_flows(flows_ref, halo_ref, wide, days, minutes, width):
+    span = HALO + minutes
+    for p in range(flows_ref.shape[2] // width):
+        cols = slice(p * width, (p + 1) * width)
+        for d in range(days):
+            row = (p * days + d) * span
+            wide[row : row + HALO, :] = halo_ref[d, :, cols].astype(jnp.float32)
+            wide[row + HALO : row + span, :] = flows_ref[d, :, cols].astype(jnp.float32)
+
+
+def forward_blocks(count, unroll, mats, path, lag, target, wide, acc, days, minutes):
+    span = HALO + minutes
+
+    def group(g, carry):
+        parts = []
+        for u in range(unroll):
+            j = g * unroll + u
+            rows = [
+                wide[pl.ds(window_rows(path[j], d, lag[j], days, span), minutes), :]
+                for d in range(days)
+            ]
+            taken = jnp.concatenate(rows, axis=0).astype(jnp.bfloat16)
+            parts.append(
+                lax.dot_general(
+                    taken,
+                    mats[j],
+                    (((1,), (1,)), ((), ())),
+                    preferred_element_type=jnp.float32,
+                )
+            )
+        for u in range(unroll):
+            t = target(g * unroll + u)
+            acc[t] += parts[u]
+        return carry
+
+    lax.fori_loop(0, count // unroll, group, 0)
+
+
+def backward_blocks(count, unroll, mats, path, lag, source, signals, acc, days, minutes):
+    span = HALO + minutes
+
+    def group(g, carry):
+        parts = []
+        for u in range(unroll):
+            j = g * unroll + u
+            parts.append(
+                jnp.dot(signals(j), mats[j], preferred_element_type=jnp.float32)
+            )
+        for u in range(unroll):
+            j = g * unroll + u
+            for d in range(days):
+                rows = pl.ds(window_rows(path[j], d, lag[j], days, span), minutes)
+                acc[rows, :] += parts[u][d * minutes : (d + 1) * minutes]
+        return carry
+
+    lax.fori_loop(0, count // unroll, group, 0)
+
+
+def forward_remote_kernel(days, cap, blocks, me, path, link, lag, slot, flows, halo, mats, *rest):
+    outs, (wide, acc) = rest[:-2], rest[-2:]
+    minutes = flows.shape[1]
+    stage_flows(flows, halo, wide, days, minutes, mats.shape[2])
+    acc[...] = jnp.zeros_like(acc)
+
+    def target(j):
+        return (lax.div(slot[j], cap) ^ me[0]) * blocks + link[j]
+
+    forward_blocks(mats.shape[0], 8, mats, path, lag, target, wide, acc, days, minutes)
+    for s, out in enumerate(outs):
+        out[...] = acc[(s + 1) * blocks : (s + 2) * blocks].astype(out.dtype)
+
+
+def forward_local_kernel(days, path, link, lag, flows, halo, mats, out, wide):
+    minutes = flows.shape[1]
+    stage_flows(flows, halo, wide, days, minutes, mats.shape[2])
+    out[...] = jnp.zeros_like(out)
+    forward_blocks(
+        mats.shape[0], 8, mats, path, lag, lambda j: link[j], wide, out, days, minutes
+    )
+
+
+def signal_kernel(days, totals, counts, residual, signal):
+    blocks, _, width = totals.shape
+    minutes = counts.shape[1]
+    for b in range(blocks):
+        cols = slice(b * width, (b + 1) * width)
+        total = totals[b]
+        for d in range(days):
+            rows = slice(d * minutes, (d + 1) * minutes)
+            seen = counts[d, :, cols]
+            weight = seen + 1.0
+            res = (total[rows] - seen) / weight
+            residual[d, :, cols] = res
+            signal[b, rows, :] = (res / weight).astype(signal.dtype)
+
+
+def backward_local_kernel(days, path, link, lag, signal, mats, out):
+    minutes = signal.shape[1] // days
+    out[...] = jnp.zeros_like(out)
+    backward_blocks(
+        mats.shape[0],
+        8,
+        mats,
+        path,
+        lag,
+        None,
+        lambda j: signal[link[j]],
+        out,
+        days,
+        minutes,
+    )
+
+
+def backward_remote_kernel(days, cap, blocks, me, path, link, lag, slot, mats, start, *rest):
+    signals, (out, everyone) = rest[:-2], rest[-2:]
+    minutes = signals[0].shape[1] // days
+    for s, part in enumerate(signals):
+        everyone[(s + 1) * blocks : (s + 2) * blocks] = part[...]
+    out[...] = start[...]
+
+    def chosen(j):
+        return everyone[(lax.div(slot[j], cap) ^ me[0]) * blocks + link[j]]
+
+    backward_blocks(mats.shape[0], 8, mats, path, lag, None, chosen, out, days, minutes)
+
+
+def finish_kernel(days, total, spill, flows, gradient, new_flows):
+    minutes = flows.shape[1]
+    width = total.shape[1]
+    span = HALO + minutes
+    for p in range(flows.shape[2] // width):
+        cols = slice(p * width, (p + 1) * width)
+        for d in range(days):
+            row = (p * days + d) * span + HALO
+            own = total[row : row + minutes, :]
+            keep = minutes - HALO
+            late = own[keep:] + spill[p * days + d]
+            for rows, grad in ((slice(0, keep), own[:keep]), (slice(keep, minutes), late)):
+                gradient[d, rows, cols] = grad
+                new_flows[d, rows, cols] = jnp.maximum(
+                    flows[d, rows, cols].astype(jnp.float32) - RATE * grad, 0.0
+                )
+
+
+def kernel_call(body, scalars, arrays, out_shape, scratch=()):
+    smem = pl.BlockSpec(memory_space=pltpu.SMEM)
+    vmem = pl.BlockSpec(memory_space=pltpu.VMEM)
+    single = isinstance(out_shape, jax.ShapeDtypeStruct)
+    return pl.pallas_call(
+        body,
+        out_shape=out_shape,
+        in_specs=[smem] * len(scalars) + [vmem] * len(arrays),
+        out_specs=vmem if single else [vmem] * len(out_shape),
+        scratch_shapes=list(scratch),
+        compiler_params=pltpu.CompilerParams(vmem_limit_bytes=48 * 1024 * 1024),
+    )(*scalars, *arrays)
+
+
+def per_device_dense(
+    flows,
+    counts,
+    local_blocks,
+    local_path,
+    local_link,
+    local_lag,
+    remote_blocks,
+    remote_path,
+    remote_link,
+    remote_lag,
+    remote_slot,
+):
+    days, minutes, path_width = flows.shape
+    width = local_blocks.shape[1]
+    paths = path_width // width
+    links = counts.shape[2] // width
+    corridors = lax.axis_size("corr")
+    cap = (remote_lag.shape[0] + corridors - 2) // (corridors - 1)
+    span = HALO + minutes
+    others = range(1, corridors)
+    me = lax.axis_index("corr").astype(jnp.int32).reshape(1)
+    shape = jax.ShapeDtypeStruct
+    piece = (links, days * minutes, width)
+    wide = pltpu.VMEM((paths * days * span, width), jnp.float32)
+
+    halo = passed_along(flows[:, minutes - HALO :], "tm", 1)
+    outgoing = kernel_call(
+        functools.partial(forward_remote_kernel, days, cap, links),
+        (me, remote_path, remote_link, remote_lag, remote_slot),
+        (flows, halo, remote_blocks),
+        [shape(piece, jnp.float32) for _ in others],
+        [wide, pltpu.VMEM((corridors * links, days * minutes, width), jnp.float32)],
+    )
+
+    def exchanged(part, s):
+        return lax.ppermute(part, "corr", [(i, i ^ s) for i in range(corridors)])
+
+    received = [exchanged(outgoing[s - 1].astype(WIRE), s) for s in others]
+    own = kernel_call(
+        functools.partial(forward_local_kernel, days),
+        (local_path, local_link, local_lag),
+        (flows, halo, local_blocks),
+        shape(piece, jnp.float32),
+        [wide],
+    )
+    link_residual, signal = kernel_call(
+        functools.partial(signal_kernel, days),
+        (),
+        (functools.reduce(jnp.add, [p.astype(jnp.float32) for p in received], own), counts),
+        [shape(counts.shape, jnp.float32), shape(piece, jnp.bfloat16)],
+    )
+    signals = [exchanged(signal, s) for s in others]
+    rows = shape((paths * days * span, width), jnp.float32)
+    local_total = kernel_call(
+        functools.partial(backward_local_kernel, days),
+        (local_path, local_link, local_lag),
+        (signal, local_blocks),
+        rows,
+    )
+    total = kernel_call(
+        functools.partial(backward_remote_kernel, days, cap, links),
+        (me, remote_path, remote_link, remote_lag, remote_slot),
+        (remote_blocks, local_total, *signals),
+        rows,
+        [pltpu.VMEM((corridors * links, days * minutes, width), jnp.bfloat16)],
+    )
+    early = total.reshape(paths * days, span, width)[:, :HALO]
+    spill = passed_along(early, "tm", -1)
+    gradient, new_flows = kernel_call(
+        functools.partial(finish_kernel, days),
+        (),
+        (total, spill, flows),
+        [shape(flows.shape, jnp.float32)] * 2,
+    )
+    return (link_residual, gradient, new_flows)
+
+
+def per_device(*args):
+    counts, blocks, lags = args[1], args[2], args[9]
+    corridors = lax.axis_size("corr")
+    links = counts.shape[2] // blocks.shape[1]
+    cap = (lags.shape[0] + corridors - 2) // (corridors - 1)
+    if cap >= links:
+        return per_device_dense(*args)
+    return per_device_slots(*args)
+
+
 def solution(mesh):
     placed = (
         P(None, "tm", "corr"),

time: 170 us -> 70.2 us (0.41)
  the two profiles are of different devices: /device:TPU:1 before, /device:TPU:17 now
where the time goes in v1:
time: 70.2 us; the launch traced here: 69.9 us
  starting transfers between devices  28.1 us (40%)
  waiting for transfers between devices  22.3 us (32%)
  Pallas kernels  12.4 us (18%)
  local copies, waits for them, and re-layouts  6 us (9%)
  between operations  0.83 us (1%)
    ppermute x14, starting transfers between devices, exchanged(): return lax.ppermute(part, 'corr', [(i, i ^ s) for i in range(corridors)])  21.6 us
    ppermute x14, waiting for transfers between devices, exchanged(): return lax.ppermute(part, 'corr', [(i, i ^ s) for i in range(corridors)])  17.5 us
    pallas_call x6, Pallas kernels, kernel_call(): pl.pallas_call(body, out_shape=out_shape, in_specs=[smem] * len(scalars)...  12.4 us
    ppermute x2, starting transfers between devices, passed_along(): return lax.ppermute(block, axis, route)  6.51 us
    unnamed x26, local copies, waits for them, and re-layouts  5.14 us
    ppermute x2, waiting for transfers between devices, passed_along(): return lax.ppermute(block, axis, route)  4.78 us
  transfers between devices with their start and end apart: 16, of which 9 were waited for; matrix products, arithmetic and copies ran while one was open for 0% of the time, Pallas kernels for 8%

profile of v1, /device:TPU:17, one launch (start us, length us, event | category | flops | bytes accessed | tf_op | source)
XLA Modules:
  0.0 69.9 jit_solution(10095801770621645741)
XLA Ops:
  0.6 0.9 %slice.6 = bf16[2,16,1024]{2,1,0:T(8,128)(2,1)S(1)} slice(bf16[2,24,1024]{2,1,0:T(8,128)(2,1)} %flows.5), slice={[0:2], [8:24], [0:1024]} | slice | bytes 131072 | tf_op jit(solution)/shard_map/slice | solution.py:353
  1.5 3.7 %collective-permute-start = (bf16[2,16,1024]{2,1,0:T(8,128)(2,1)S(1)}, bf16[2,16,1024]{2,1,0:T(8,128)(2,1)S(1)}, u32[]{:S(2)}, u32[]{:S(2)}) collective-permute-start(bf16[2,16,1024]{2,1,0:T(8,128)(2,1)S(1)} %slice.6), channel_id=1, source_target_pairs={{0,1},{1,2},{2,3},{4,5},{5,6},{6,7},{8,9},{9,10},{10,11},{12,13},{... | collective-permute-start | bytes 196616 | tf_op jit(solution)/shard_map/ppermute | solution.py:19
  5.2 1.3 %collective-permute-done.halo = bf16[2,16,1024]{2,1,0:T(8,128)(2,1)S(1)} collective-permute-done((bf16[2,16,1024]{2,1,0:T(8,128)(2,1)S(1)}, bf16[2,16,1024]{2,1,0:T(8,128)(2,1)S(1)}, u32[]{:S(2)}, u32[]{:S(2)}) %collective-permute-start) | collective-permute-done | bytes 65568 | tf_op jit(solution)/shard_map/ppermute | solution.py:19
  6.5 0.0 copy-start.1
  6.5 1.6 %copy-done.1 = bf16[64,128,128]{2,1,0:T(8,128)(2,1)S(1)} copy-done((bf16[64,128,128]{2,1,0:T(8,128)(2,1)S(1)}, bf16[64,128,128]{2,1,0:T(8,128)(2,1)}, u32[]{:S(2)}) %copy-start.1) | copy-done | bytes 2097176
  8.1 0.0 copy-start.3
  8.1 0.9 %copy-done.3 = bf16[2,24,1024]{2,1,0:T(8,128)(2,1)S(1)} copy-done((bf16[2,24,1024]{2,1,0:T(8,128)(2,1)S(1)}, bf16[2,24,1024]{2,1,0:T(8,128)(2,1)}, u32[]{:S(2)}) %copy-start.3) | copy-done | bytes 98328
  9.0 0.0 copy-start.9
  9.0 0.7 copy-done.9
  9.6 0.0 copy-start.10
  9.6 0.7 copy-done.10
  10.3 0.0 copy-start.11
  10.3 0.7 copy-done.11
  10.9 0.0 copy-start.12
  11.0 0.7 copy-done.12
  11.6 0.0 copy-start
  11.6 0.0 copy-start.4
  11.6 0.0 copy-start.8
  11.6 3.1 %shard_map.131 = (f32[8,48,128]{2,1,0:T(8,128)S(1)}, f32[8,48,128]{2,1,0:T(8,128)S(1)}, f32[8,48,128]{2,1,0:T(8,128)S(1)}, f32[8,48,128]{2,1,0:T(8,128)S(1)}, f3...) custom-call(s32[1]{0:T(128)} %bitcast.me, s32[64]{0:T(128)S(1)} %copy-done.9, ...), custom_call_target="tpu_custom_call" | custom-call | tf_op jit(solution)/shard_map/pallas_call | solution.py:317
  14.8 1.3 %collective-permute-start.1 = (f16[8,48,128]{2,1,0:T(8,128)(2,1)S(1)}, f16[8,48,128]{2,1,0:T(8,128)(2,1)S(1)}, u32[]{:S(2)}, u32[]{:S(2)}) collective-permute-start(f16[8,48,128]{2,1,0:T(8,128)(2,1)S(1)} %convert_element_type.42), channel_id=1, source_target_pairs={{0,4},{4,0},{8,12},{12,8},{16,20},{20,16},{24,28},{28,24},{1,5},{5... | collective-permute-start | bytes 294920 | tf_op jit(solution)/shard_map/ppermute | solution.py:363
  16.1 1.4 %collective-permute-start.2 = (f16[8,48,128]{2,1,0:T(8,128)(2,1)S(1)}, f16[8,48,128]{2,1,0:T(8,128)(2,1)S(1)}, u32[]{:S(2)}, u32[]{:S(2)}) collective-permute-start(f16[8,48,128]{2,1,0:T(8,128)(2,1)S(1)} %convert_element_type.44), channel_id=1, source_target_pairs={{0,8},{4,12},{8,0},{12,4},{16,24},{20,28},{24,16},{28,20},{1,9},{5... | collective-permute-start | bytes 294920 | tf_op jit(solution)/shard_map/ppermute | solution.py:363
  17.5 0.2 collective-permute-start.3
  17.7 0.1 collective-permute-start.4
  17.8 0.0 copy-start.5
  17.9 3.3 %collective-permute-start.5 = (f16[8,48,128]{2,1,0:T(8,128)(2,1)S(1)}, f16[8,48,128]{2,1,0:T(8,128)(2,1)S(1)}, u32[]{:S(2)}, u32[]{:S(2)}) collective-permute-start(f16[8,48,128]{2,1,0:T(8,128)(2,1)S(1)} %convert_element_type.50), channel_id=1, source_target_pairs={{0,20},{4,16},{8,28},{12,24},{16,4},{20,0},{24,12},{28,8},{1,21},{... | collective-permute-start | bytes 294920 | tf_op jit(solution)/shard_map/ppermute | solution.py:363
  21.2 0.0 collective-permute-done.1
  21.2 0.2 collective-permute-start.6
  21.4 0.0 collective-permute-done.2
  21.4 1.3 %collective-permute-start.7 = (f16[8,48,128]{2,1,0:T(8,128)(2,1)S(1)}, f16[8,48,128]{2,1,0:T(8,128)(2,1)S(1)}, u32[]{:S(2)}, u32[]{:S(2)}) collective-permute-start(f16[8,48,128]{2,1,0:T(8,128)(2,1)S(1)} %convert_element_type.54), channel_id=1, source_target_pairs={{0,28},{4,24},{8,20},{12,16},{16,12},{20,8},{24,4},{28,0},{1,29},{... | collective-permute-start | bytes 294920 | tf_op jit(solution)/shard_map/ppermute | solution.py:363
  22.7 0.0 copy-done
  22.7 0.0 copy-done.4
  22.7 0.0 copy-done.6
  22.7 0.0 copy-done.7
  22.7 0.0 copy-done.8
  22.7 2.9 %shard_map.130 = f32[8,48,128]{2,1,0:T(8,128)S(1)} custom-call(s32[64]{0:T(128)S(1)} %copy-done.6, s32[64]{0:T(128)S(1)} %copy-done.7, s32[64]{0:T(128)S(1)} %copy-done.8, bf16[2,24,1024]{2,1,0:T(8,128)(2,1)S(1)} %copy-done.4, bf16[2,16,1024]{2,1,0:T(8,128)(2,1)S(1)} %collective-permute-done.halo, bf16[64,128,128]{2,1,0:T(8,128)(2,1)S(1)} %copy-done), custom_call_target="tpu_custom_call" | custom-call | tf_op jit(solution)/shard_map/pallas_call | solution.py:317
  25.7 0.0 copy-start.2
  25.7 0.0 collective-permute-done.3
  25.7 0.0 collective-permute-done.4
  25.7 5.9 %collective-permute-done.5 = f16[8,48,128]{2,1,0:T(8,128)(2,1)S(1)} collective-permute-done((f16[8,48,128]{2,1,0:T(8,128)(2,1)S(1)}, f16[8,48,128]{2,1,0:T(8,128)(2,1)S(1)}, u32[]{:S(2)}, u32[]{:S(2)}) %collective-permute-start.5) | collective-permute-done | bytes 98336 | tf_op jit(solution)/shard_map/ppermute | solution.py:363
  31.7 4.0 %collective-permute-done.6 = f16[8,48,128]{2,1,0:T(8,128)(2,1)S(1)} collective-permute-done((f16[8,48,128]{2,1,0:T(8,128)(2,1)S(1)}, f16[8,48,128]{2,1,0:T(8,128)(2,1)S(1)}, u32[]{:S(2)}, u32[]{:S(2)}) %collective-permute-start.6) | collective-permute-done | bytes 98336 | tf_op jit(solution)/shard_map/ppermute | solution.py:363
  35.7 3.1 %collective-permute-done.7 = f16[8,48,128]{2,1,0:T(8,128)(2,1)S(1)} collective-permute-done((f16[8,48,128]{2,1,0:T(8,128)(2,1)S(1)}, f16[8,48,128]{2,1,0:T(8,128)(2,1)S(1)}, u32[]{:S(2)}, u32[]{:S(2)}) %collective-permute-start.7) | collective-permute-done | bytes 98336 | tf_op jit(solution)/shard_map/ppermute | solution.py:363
  38.8 0.1 convert_add_fusion.totals
  38.9 0.0 copy-done.5
  38.9 0.7 %shard_map.132 = (f32[2,24,1024]{2,1,0:T(8,128)}, bf16[8,48,128]{2,1,0:T(8,128)(2,1)S(1)}) custom-call(f32[8,48,128]{2,1,0:T(8,128)S(1)} %convert_add_fusion.totals, f32[2,24,1024]{2,1,0:T(8,128)S(1)} %copy-done.5), custom_call_target="tpu_custom_call" | custom-call | tf_op jit(solution)/shard_map/pallas_call | solution.py:317
  39.6 0.0 collective-permute-start.10
  39.6 1.2 %collective-permute-start.11 = (bf16[8,48,128]{2,1,0:T(8,128)(2,1)S(1)}, bf16[8,48,128]{2,1,0:T(8,128)(2,1)S(1)}, u32[]{:S(2)}, u32[]{:S(2)}) collective-permute-start(bf16[8,48,128]{2,1,0:T(8,128)(2,1)S(1)} %get-tuple-element.22.signal), channel_id=1, source_target_pairs={{0,16},{4,20},{8,24},{12,28},{16,0},{20,4},{24,8},{28,12},{1,17},{... | collective-permute-start | bytes 294920 | tf_op jit(solution)/shard_map/ppermute | solution.py:363
  40.8 1.0 %collective-permute-start.12 = (bf16[8,48,128]{2,1,0:T(8,128)(2,1)S(1)}, bf16[8,48,128]{2,1,0:T(8,128)(2,1)S(1)}, u32[]{:S(2)}, u32[]{:S(2)}) collective-permute-start(bf16[8,48,128]{2,1,0:T(8,128)(2,1)S(1)} %get-tuple-element.22.signal), channel_id=1, source_target_pairs={{0,20},{4,16},{8,28},{12,24},{16,4},{20,0},{24,12},{28,8},{1,21},{... | collective-permute-start | bytes 294920 | tf_op jit(solution)/shard_map/ppermute | solution.py:363
  41.8 1.4 %collective-permute-start.13 = (bf16[8,48,128]{2,1,0:T(8,128)(2,1)S(1)}, bf16[8,48,128]{2,1,0:T(8,128)(2,1)S(1)}, u32[]{:S(2)}, u32[]{:S(2)}) collective-permute-start(bf16[8,48,128]{2,1,0:T(8,128)(2,1)S(1)} %get-tuple-element.22.signal), channel_id=1, source_target_pairs={{0,24},{4,28},{8,16},{12,20},{16,8},{20,12},{24,0},{28,4},{1,25},{... | collective-permute-start | bytes 294920 | tf_op jit(solution)/shard_map/ppermute | solution.py:363
  43.2 1.2 %collective-permute-start.14 = (bf16[8,48,128]{2,1,0:T(8,128)(2,1)S(1)}, bf16[8,48,128]{2,1,0:T(8,128)(2,1)S(1)}, u32[]{:S(2)}, u32[]{:S(2)}) collective-permute-start(bf16[8,48,128]{2,1,0:T(8,128)(2,1)S(1)} %get-tuple-element.22.signal), channel_id=1, source_target_pairs={{0,28},{4,24},{8,20},{12,16},{16,12},{20,8},{24,4},{28,0},{1,29},{... | collective-permute-start | bytes 294920 | tf_op jit(solution)/shard_map/ppermute | solution.py:363
  44.4 0.1 collective-permute-done.10.rest_2_
  44.5 0.1 collective-permute-start.8
  44.6 0.8 %collective-permute-done.11.rest_3_ = bf16[8,48,128]{2,1,0:T(8,128)(2,1)S(1)} collective-permute-done((bf16[8,48,128]{2,1,0:T(8,128)(2,1)S(1)}, bf16[8,48,128]{2,1,0:T(8,128)(2,1)S(1)}, u32[]{:S(2)}, u32[]{:S(2)}) %collective-permute-start.11) | collective-permute-done | bytes 98336 | tf_op jit(solution)/shard_map/ppermute | solution.py:363
  45.5 9.0 %collective-permute-start.9 = (bf16[8,48,128]{2,1,0:T(8,128)(2,1)S(1)}, bf16[8,48,128]{2,1,0:T(8,128)(2,1)S(1)}, u32[]{:S(2)}, u32[]{:S(2)}) collective-permute-start(bf16[8,48,128]{2,1,0:T(8,128)(2,1)S(1)} %get-tuple-element.22.signal), channel_id=1, source_target_pairs={{0,8},{4,12},{8,0},{12,4},{16,24},{20,28},{24,16},{28,20},{1,9},{5... | collective-permute-start | bytes 294920 | tf_op jit(solution)/shard_map/ppermute | solution.py:363
  54.5 2.4 %shard_map.133.start = f32[640,128]{1,0:T(8,128)S(1)} custom-call(s32[64]{0:T(128)S(1)} %copy-done.6, s32[64]{0:T(128)S(1)} %copy-done.7, s32[64]{0:T(128)S(1)} %copy-done.8, bf16[8,48,128]{2,1,0:T(8,128)(2,1)S(1)} %get-tuple-element.22.signal, bf16[64,128,128]{2,1,0:T(8,128)(2,1)S(1)} %copy-done), custom_call_target="tpu_custom_call" | custom-call | tf_op jit(solution)/shard_map/pallas_call | solution.py:317
  56.9 0.0 collective-permute-done.12.rest_4_
  56.9 0.6 collective-permute-done.13.rest_5_
  57.5 2.8 %collective-permute-done.14.rest_6_ = bf16[8,48,128]{2,1,0:T(8,128)(2,1)S(1)} collective-permute-done((bf16[8,48,128]{2,1,0:T(8,128)(2,1)S(1)}, bf16[8,48,128]{2,1,0:T(8,128)(2,1)S(1)}, u32[]{:S(2)}, u32[]{:S(2)}) %collective-permute-start.14) | collective-permute-done | bytes 98336 | tf_op jit(solution)/shard_map/ppermute | solution.py:363
  60.3 0.0 collective-permute-done.8.rest_0_
  60.3 0.0 collective-permute-done.9.rest_1_
  60.3 0.0 copy-done.2
  60.3 2.4 %shard_map.134.total = f32[640,128]{1,0:T(8,128)S(1)} custom-call(s32[1]{0:T(128)} %bitcast.me, s32[64]{0:T(128)S(1)} %copy-done.9, s32[64]{0:T(128)S(1)} %copy-done.10, s32[64]{0:T(128)S(1)} %copy-done.11, s32[64]{0:T(128)S(1)} %copy-done.12, bf16[64,128,128]{2,1,0:T(8,128)(2,1)S(1)} %copy-done.2, f32[640,128]{1,0:T(8,128)S(1)} %shard_map.133.start, ...), custom_call_target="tpu_custom_call" | custom-call | tf_op jit(solution)/shard_map/pallas_call | solution.py:317
  62.8 2.8 %collective-permute-start.15 = (f32[16,16,128]{2,1,0:T(8,128)S(1)}, f32[16,16,128]{2,1,0:T(8,128)S(1)}, u32[]{:S(2)}, u32[]{:S(2)}) collective-permute-start(f32[16,16,128]{2,1,0:T(8,128)S(1)} %slice.8), channel_id=1, source_target_pairs={{1,0},{2,1},{3,2},{5,4},{6,5},{7,6},{9,8},{10,9},{11,10},{13,12},{... | collective-permute-start | bytes 393224 | tf_op jit(solution)/shard_map/ppermute | solution.py:19
  65.6 3.5 %collective-permute-done.15.spill = f32[16,16,128]{2,1,0:T(8,128)S(1)} collective-permute-done((f32[16,16,128]{2,1,0:T(8,128)S(1)}, f32[16,16,128]{2,1,0:T(8,128)S(1)}, u32[]{:S(2)}, u32[]{:S(2)}) %collective-permute-start.15) | collective-permute-done | bytes 131104 | tf_op jit(solution)/shard_map/ppermute | solution.py:19
  69.1 0.8 %shard_map.135 = (f32[2,24,1024]{2,1,0:T(8,128)}, f32[2,24,1024]{2,1,0:T(8,128)}) custom-call(f32[640,128]{1,0:T(8,128)S(1)} %shard_map.134.total, f32[16,16,128]{2,1,0:T(8,128)S(1)} %collective-permute-done.15.spill, bf16[2,24,1024]{2,1,0:T(8,128)(2,1)S(1)} %copy-done.4), custom_call_target="tpu_custom_call" | custom-call | tf_op jit(solution)/shard_map/pallas_call | solution.py:317
  (10 shorter events, 0.1 us)
Async XLA Ops:
  1.5 5.0 %collective-permute-start = (bf16[2,16,1024]{2,1,0:T(8,128)(2,1)S(1)}, bf16[2,16,1024]{2,1,0:T(8,128)(2,1)S(1)}, u32[]{:S(2)}, u32[]{:S(2)}) collective-permute-start(bf16[2,16,1024]{2,1,0:T(8,128)(2,1)S(1)} %slice.6), channel_id=1, source_target_pairs={{0,1},{1,2},{2,3},{4,5},{5,6},{6,7},{8,9},{9,10},{10,11},{12,13},{... | collective-permute-start | bytes 196616 | tf_op jit(solution)/shard_map/ppermute | solution.py:19
  6.5 1.6 %copy-start.1 = (bf16[64,128,128]{2,1,0:T(8,128)(2,1)S(1)}, bf16[64,128,128]{2,1,0:T(8,128)(2,1)}, u32[]{:S(2)}) copy-start(bf16[64,128,128]{2,1,0:T(8,128)(2,1)} %mats.7) | copy-start | bytes 6291460
  8.1 0.9 %copy-start.3 = (bf16[2,24,1024]{2,1,0:T(8,128)(2,1)S(1)}, bf16[2,24,1024]{2,1,0:T(8,128)(2,1)}, u32[]{:S(2)}) copy-start(bf16[2,24,1024]{2,1,0:T(8,128)(2,1)} %flows.5) | copy-start | bytes 294916
  9.0 0.7 copy-start.9
  9.6 0.7 copy-start.10
  10.3 0.7 copy-start.11
  10.9 0.7 copy-start.12
  11.6 11.1 %copy-start = (bf16[64,128,128]{2,1,0:T(8,128)(2,1)S(1)}, bf16[64,128,128]{2,1,0:T(8,128)(2,1)}, u32[]{:S(2)}) copy-start(bf16[64,128,128]{2,1,0:T(8,128)(2,1)} %mats.6) | copy-start | bytes 6291460
  11.6 11.1 %copy-start.4 = (bf16[2,24,1024]{2,1,0:T(8,128)(2,1)S(1)}, bf16[2,24,1024]{2,1,0:T(8,128)(2,1)}, u32[]{:S(2)}) copy-start(bf16[2,24,1024]{2,1,0:T(8,128)(2,1)} %flows.5) | copy-start | bytes 294916
  11.6 11.1 %copy-start.6 = (s32[64]{0:T(128)S(1)}, s32[64]{0:T(128)}, u32[]{:S(2)}) copy-start(s32[64]{0:T(128)} %path.6) | copy-start | bytes 772
  11.6 11.1 %copy-start.7 = (s32[64]{0:T(128)S(1)}, s32[64]{0:T(128)}, u32[]{:S(2)}) copy-start(s32[64]{0:T(128)} %link.6) | copy-start | bytes 772
  11.6 11.1 %copy-start.8 = (s32[64]{0:T(128)S(1)}, s32[64]{0:T(128)}, u32[]{:S(2)}) copy-start(s32[64]{0:T(128)} %lag.6) | copy-start | bytes 772
  14.8 6.4 %collective-permute-start.1 = (f16[8,48,128]{2,1,0:T(8,128)(2,1)S(1)}, f16[8,48,128]{2,1,0:T(8,128)(2,1)S(1)}, u32[]{:S(2)}, u32[]{:S(2)}) collective-permute-start(f16[8,48,128]{2,1,0:T(8,128)(2,1)S(1)} %convert_element_type.42), channel_id=1, source_target_pairs={{0,4},{4,0},{8,12},{12,8},{16,20},{20,16},{24,28},{28,24},{1,5},{5... | collective-permute-start | bytes 294920 | tf_op jit(solution)/shard_map/ppermute | solution.py:363
  16.1 5.4 %collective-permute-start.2 = (f16[8,48,128]{2,1,0:T(8,128)(2,1)S(1)}, f16[8,48,128]{2,1,0:T(8,128)(2,1)S(1)}, u32[]{:S(2)}, u32[]{:S(2)}) collective-permute-start(f16[8,48,128]{2,1,0:T(8,128)(2,1)S(1)} %convert_element_type.44), channel_id=1, source_target_pairs={{0,8},{4,12},{8,0},{12,4},{16,24},{20,28},{24,16},{28,20},{1,9},{5... | collective-permute-start | bytes 294920 | tf_op jit(solution)/shard_map/ppermute | solution.py:363
  17.5 8.2 %collective-permute-start.3 = (f16[8,48,128]{2,1,0:T(8,128)(2,1)S(1)}, f16[8,48,128]{2,1,0:T(8,128)(2,1)S(1)}, u32[]{:S(2)}, u32[]{:S(2)}) collective-permute-start(f16[8,48,128]{2,1,0:T(8,128)(2,1)S(1)} %convert_element_type.46), channel_id=1, source_target_pairs={{0,12},{4,8},{8,4},{12,0},{16,28},{20,24},{24,20},{28,16},{1,13},{... | collective-permute-start | bytes 294920 | tf_op jit(solution)/shard_map/ppermute | solution.py:363
  17.7 8.0 %collective-permute-start.4 = (f16[8,48,128]{2,1,0:T(8,128)(2,1)S(1)}, f16[8,48,128]{2,1,0:T(8,128)(2,1)S(1)}, u32[]{:S(2)}, u32[]{:S(2)}) collective-permute-start(f16[8,48,128]{2,1,0:T(8,128)(2,1)S(1)} %convert_element_type.48), channel_id=1, source_target_pairs={{0,16},{4,20},{8,24},{12,28},{16,0},{20,4},{24,8},{28,12},{1,17},{... | collective-permute-start | bytes 294920 | tf_op jit(solution)/shard_map/ppermute | solution.py:363
  17.8 21.1 %copy-start.5 = (f32[2,24,1024]{2,1,0:T(8,128)S(1)}, f32[2,24,1024]{2,1,0:T(8,128)}, u32[]{:S(2)}) copy-start(f32[2,24,1024]{2,1,0:T(8,128)} %counts.1) | copy-start | bytes 589828
  17.9 13.8 %collective-permute-start.5 = (f16[8,48,128]{2,1,0:T(8,128)(2,1)S(1)}, f16[8,48,128]{2,1,0:T(8,128)(2,1)S(1)}, u32[]{:S(2)}, u32[]{:S(2)}) collective-permute-start(f16[8,48,128]{2,1,0:T(8,128)(2,1)S(1)} %convert_element_type.50), channel_id=1, source_target_pairs={{0,20},{4,16},{8,28},{12,24},{16,4},{20,0},{24,12},{28,8},{1,21},{... | collective-permute-start | bytes 294920 | tf_op jit(solution)/shard_map/ppermute | solution.py:363
  21.2 14.5 %collective-permute-start.6 = (f16[8,48,128]{2,1,0:T(8,128)(2,1)S(1)}, f16[8,48,128]{2,1,0:T(8,128)(2,1)S(1)}, u32[]{:S(2)}, u32[]{:S(2)}) collective-permute-start(f16[8,48,128]{2,1,0:T(8,128)(2,1)S(1)} %convert_element_type.52), channel_id=1, source_target_pairs={{0,24},{4,28},{8,16},{12,20},{16,8},{20,12},{24,0},{28,4},{1,25},{... | collective-permute-start | bytes 294920 | tf_op jit(solution)/shard_map/ppermute | solution.py:363
  21.4 17.3 %collective-permute-start.7 = (f16[8,48,128]{2,1,0:T(8,128)(2,1)S(1)}, f16[8,48,128]{2,1,0:T(8,128)(2,1)S(1)}, u32[]{:S(2)}, u32[]{:S(2)}) collective-permute-start(f16[8,48,128]{2,1,0:T(8,128)(2,1)S(1)} %convert_element_type.54), channel_id=1, source_target_pairs={{0,28},{4,24},{8,20},{12,16},{16,12},{20,8},{24,4},{28,0},{1,29},{... | collective-permute-start | bytes 294920 | tf_op jit(solution)/shard_map/ppermute | solution.py:363
  25.7 34.6 %copy-start.2 = (bf16[64,128,128]{2,1,0:T(8,128)(2,1)S(1)}, bf16[64,128,128]{2,1,0:T(8,128)(2,1)}, u32[]{:S(2)}) copy-start(bf16[64,128,128]{2,1,0:T(8,128)(2,1)} %mats.7) | copy-start | bytes 6291460
  39.6 4.9 %collective-permute-start.10 = (bf16[8,48,128]{2,1,0:T(8,128)(2,1)S(1)}, bf16[8,48,128]{2,1,0:T(8,128)(2,1)S(1)}, u32[]{:S(2)}, u32[]{:S(2)}) collective-permute-start(bf16[8,48,128]{2,1,0:T(8,128)(2,1)S(1)} %get-tuple-element.22.signal), channel_id=1, source_target_pairs={{0,12},{4,8},{8,4},{12,0},{16,28},{20,24},{24,20},{28,16},{1,13},{... | collective-permute-start | bytes 294920 | tf_op jit(solution)/shard_map/ppermute | solution.py:363
  39.6 5.8 %collective-permute-start.11 = (bf16[8,48,128]{2,1,0:T(8,128)(2,1)S(1)}, bf16[8,48,128]{2,1,0:T(8,128)(2,1)S(1)}, u32[]{:S(2)}, u32[]{:S(2)}) collective-permute-start(bf16[8,48,128]{2,1,0:T(8,128)(2,1)S(1)} %get-tuple-element.22.signal), channel_id=1, source_target_pairs={{0,16},{4,20},{8,24},{12,28},{16,0},{20,4},{24,8},{28,12},{1,17},{... | collective-permute-start | bytes 294920 | tf_op jit(solution)/shard_map/ppermute | solution.py:363
  40.8 16.0 %collective-permute-start.12 = (bf16[8,48,128]{2,1,0:T(8,128)(2,1)S(1)}, bf16[8,48,128]{2,1,0:T(8,128)(2,1)S(1)}, u32[]{:S(2)}, u32[]{:S(2)}) collective-permute-start(bf16[8,48,128]{2,1,0:T(8,128)(2,1)S(1)} %get-tuple-element.22.signal), channel_id=1, source_target_pairs={{0,20},{4,16},{8,28},{12,24},{16,4},{20,0},{24,12},{28,8},{1,21},{... | collective-permute-start | bytes 294920 | tf_op jit(solution)/shard_map/ppermute | solution.py:363
  41.8 15.7 %collective-permute-start.13 = (bf16[8,48,128]{2,1,0:T(8,128)(2,1)S(1)}, bf16[8,48,128]{2,1,0:T(8,128)(2,1)S(1)}, u32[]{:S(2)}, u32[]{:S(2)}) collective-permute-start(bf16[8,48,128]{2,1,0:T(8,128)(2,1)S(1)} %get-tuple-element.22.signal), channel_id=1, source_target_pairs={{0,24},{4,28},{8,16},{12,20},{16,8},{20,12},{24,0},{28,4},{1,25},{... | collective-permute-start | bytes 294920 | tf_op jit(solution)/shard_map/ppermute | solution.py:363
  43.2 17.1 %collective-permute-start.14 = (bf16[8,48,128]{2,1,0:T(8,128)(2,1)S(1)}, bf16[8,48,128]{2,1,0:T(8,128)(2,1)S(1)}, u32[]{:S(2)}, u32[]{:S(2)}) collective-permute-start(bf16[8,48,128]{2,1,0:T(8,128)(2,1)S(1)} %get-tuple-element.22.signal), channel_id=1, source_target_pairs={{0,28},{4,24},{8,20},{12,16},{16,12},{20,8},{24,4},{28,0},{1,29},{... | collective-permute-start | bytes 294920 | tf_op jit(solution)/shard_map/ppermute | solution.py:363
  44.5 15.8 %collective-permute-start.8 = (bf16[8,48,128]{2,1,0:T(8,128)(2,1)S(1)}, bf16[8,48,128]{2,1,0:T(8,128)(2,1)S(1)}, u32[]{:S(2)}, u32[]{:S(2)}) collective-permute-start(bf16[8,48,128]{2,1,0:T(8,128)(2,1)S(1)} %get-tuple-element.22.signal), channel_id=1, source_target_pairs={{0,4},{4,0},{8,12},{12,8},{16,20},{20,16},{24,28},{28,24},{1,5},{5... | collective-permute-start | bytes 294920 | tf_op jit(solution)/shard_map/ppermute | solution.py:363
  45.5 14.9 %collective-permute-start.9 = (bf16[8,48,128]{2,1,0:T(8,128)(2,1)S(1)}, bf16[8,48,128]{2,1,0:T(8,128)(2,1)S(1)}, u32[]{:S(2)}, u32[]{:S(2)}) collective-permute-start(bf16[8,48,128]{2,1,0:T(8,128)(2,1)S(1)} %get-tuple-element.22.signal), channel_id=1, source_target_pairs={{0,8},{4,12},{8,0},{12,4},{16,24},{20,28},{24,16},{28,20},{1,9},{5... | collective-permute-start | bytes 294920 | tf_op jit(solution)/shard_map/ppermute | solution.py:363
  62.8 6.3 %collective-permute-start.15 = (f32[16,16,128]{2,1,0:T(8,128)S(1)}, f32[16,16,128]{2,1,0:T(8,128)S(1)}, u32[]{:S(2)}, u32[]{:S(2)}) collective-permute-start(f32[16,16,128]{2,1,0:T(8,128)S(1)} %slice.8), channel_id=1, source_target_pairs={{1,0},{2,1},{3,2},{5,4},{6,5},{7,6},{9,8},{10,9},{11,10},{13,12},{... | collective-permute-start | bytes 393224 | tf_op jit(solution)/shard_map/ppermute | solution.py:19

commit v2 on v1

--- a/solution.py
+++ b/solution.py
@@ -162,89 +162,184 @@
 WIRE = jnp.float16
 
 
-def window_rows(path, day, lag, days, span):
-    return (path * days + day) * span + HALO - lag
-
-
-def stage_flows(flows_ref, halo_ref, wide, days, minutes, width):
+def stage_flows(flows_ref, before_ref, wide, days, width):
+    minutes = flows_ref.shape[1]
     span = HALO + minutes
     for p in range(flows_ref.shape[2] // width):
         cols = slice(p * width, (p + 1) * width)
         for d in range(days):
             row = (p * days + d) * span
-            wide[row : row + HALO, :] = halo_ref[d, :, cols].astype(jnp.float32)
+            before = before_ref[d, :, cols].astype(jnp.float32)
+            wide[row : row + HALO, :] = before[minutes - HALO :]
             wide[row + HALO : row + span, :] = flows_ref[d, :, cols].astype(jnp.float32)
 
 
-def forward_blocks(count, unroll, mats, path, lag, target, wide, acc, days, minutes):
+def forward_blocks(start, count, unroll, mat, base, target, wide, acc, days, minutes):
     span = HALO + minutes
 
     def group(g, carry):
         parts = []
         for u in range(unroll):
-            j = g * unroll + u
+            j = start + g * unroll + u
             rows = [
-                wide[pl.ds(window_rows(path[j], d, lag[j], days, span), minutes), :]
-                for d in range(days)
+                wide[pl.ds(base(j) + d * span, minutes), :] for d in range(days)
             ]
             taken = jnp.concatenate(rows, axis=0).astype(jnp.bfloat16)
             parts.append(
                 lax.dot_general(
                     taken,
-                    mats[j],
+                    mat(j),
                     (((1,), (1,)), ((), ())),
                     preferred_element_type=jnp.float32,
                 )
             )
         for u in range(unroll):
-            t = target(g * unroll + u)
-            acc[t] += parts[u]
+            acc[target(start + g * unroll + u)] += parts[u]
         return carry
 
     lax.fori_loop(0, count // unroll, group, 0)
 
 
-def backward_blocks(count, unroll, mats, path, lag, source, signals, acc, days, minutes):
+def backward_blocks(start, count, unroll, mat, base, signal, acc, days, minutes):
     span = HALO + minutes
 
     def group(g, carry):
         parts = []
         for u in range(unroll):
-            j = g * unroll + u
-            parts.append(
-                jnp.dot(signals(j), mats[j], preferred_element_type=jnp.float32)
-            )
+            j = start + g * unroll + u
+            parts.append(jnp.dot(signal(j), mat(j), preferred_element_type=jnp.float32))
         for u in range(unroll):
-            j = g * unroll + u
             for d in range(days):
-                rows = pl.ds(window_rows(path[j], d, lag[j], days, span), minutes)
+                rows = pl.ds(base(start + g * unroll + u) + d * span, minutes)
                 acc[rows, :] += parts[u][d * minutes : (d + 1) * minutes]
         return carry
 
     lax.fori_loop(0, count // unroll, group, 0)
 
 
-def forward_remote_kernel(days, cap, blocks, me, path, link, lag, slot, flows, halo, mats, *rest):
+class Table:
+    def __init__(self, slots, blocks):
+        self.mat = 0
+        self.base = slots
+        self.block = 2 * slots
+        self.local_base = 3 * slots
+        self.local_block = 3 * slots + blocks
+        self.size = 3 * slots + 2 * blocks
+
+
+def prepare_kernel(
+    days,
+    span,
+    cap,
+    corridors,
+    links,
+    order,
+    me,
+    local_path,
+    local_link,
+    local_lag,
+    remote_path,
+    remote_link,
+    remote_lag,
+    remote_slot,
+    local_mats,
+    remote_mats,
+    table,
+    local_out,
+    remote_out,
+    lp,
+    ll,
+    lk,
+    rp,
+    rl,
+    rk,
+    rs,
+    sems,
+):
+    slots = (corridors - 1) * cap
+    locals_, remotes = lp.shape[0], rp.shape[0]
+    t = Table(slots, locals_)
+    pairs = (
+        (local_path, lp),
+        (local_link, ll),
+        (local_lag, lk),
+        (remote_path, rp),
+        (remote_link, rl),
+        (remote_lag, rk),
+        (remote_slot, rs),
+        (remote_mats, remote_out),
+        (local_mats, local_out),
+    )
+    copies = [pltpu.make_async_copy(a, b, sems.at[i]) for i, (a, b) in enumerate(pairs)]
+    for copy in copies:
+        copy.start()
+
+    def blank(i, carry):
+        table[t.mat + i] = 0
+        table[t.base + i] = HALO
+        table[t.block + i] = (corridors - 1) * links
+        return carry
+
+    lax.fori_loop(0, slots, blank, 0, unroll=10 if slots % 10 == 0 else 1)
+    for copy in copies[:7]:
+        copy.wait()
+
+    def remote(j, carry):
+        owner = lax.div(rs[j], cap)
+        rel = owner ^ me[0]
+        place = jnp.int32(0)
+        for p, s in enumerate(order):
+            place = jnp.where(rel == s, p, place)
+        i = place * cap + rs[j] - owner * cap
+        table[t.mat + i] = j
+        table[t.base + i] = rp[j] * (days * span) + HALO - rk[j]
+        table[t.block + i] = place * links + rl[j]
+        return carry
+
+    def local(j, carry):
+        table[t.local_base + j] = lp[j] * (days * span) + HALO - lk[j]
+        table[t.local_block + j] = ll[j]
+        return carry
+
+    lax.fori_loop(0, remotes, remote, 0, unroll=8)
+    lax.fori_loop(0, locals_, local, 0, unroll=8)
+    for copy in copies[7:]:
+        copy.wait()
+
+
+def slot_views(table, t, mats):
+    return (
+        lambda i: mats[table[t.mat + i]],
+        lambda i: table[t.base + i],
+        lambda i: table[t.block + i],
+    )
+
+
+def local_views(table, t, mats):
+    return (
+        lambda j: mats[j],
+        lambda j: table[t.local_base + j],
+        lambda j: table[t.local_block + j],
+    )
+
+
+def forward_remote_kernel(days, cap, cuts, links, t, table, flows, before, mats, *rest):
     outs, (wide, acc) = rest[:-2], rest[-2:]
-    minutes = flows.shape[1]
-    stage_flows(flows, halo, wide, days, minutes, mats.shape[2])
+    minutes, width = flows.shape[1], mats.shape[2]
+    stage_flows(flows, before, wide, days, width)
     acc[...] = jnp.zeros_like(acc)
-
-    def target(j):
-        return (lax.div(slot[j], cap) ^ me[0]) * blocks + link[j]
-
-    forward_blocks(mats.shape[0], 8, mats, path, lag, target, wide, acc, days, minutes)
-    for s, out in enumerate(outs):
-        out[...] = acc[(s + 1) * blocks : (s + 2) * blocks].astype(out.dtype)
-
-
-def forward_local_kernel(days, path, link, lag, flows, halo, mats, out, wide):
-    minutes = flows.shape[1]
-    stage_flows(flows, halo, wide, days, minutes, mats.shape[2])
-    out[...] = jnp.zeros_like(out)
-    forward_blocks(
-        mats.shape[0], 8, mats, path, lag, lambda j: link[j], wide, out, days, minutes
-    )
+    mat, base, block = slot_views(table, t, mats)
+    forward_blocks(0, cuts[-1] * cap, cap, mat, base, block, wide, acc, days, minutes)
+    for first, end, out in zip(cuts, cuts[1:], outs):
+        out[...] = acc[first * links : end * links]
+
+
+def forward_local_kernel(days, t, table, flows, before, mats, own, wide):
+    minutes, width = flows.shape[1], mats.shape[2]
+    stage_flows(flows, before, wide, days, width)
+    own[...] = jnp.zeros_like(own)
+    mat, base, block = local_views(table, t, mats)
+    forward_blocks(0, mats.shape[0], 8, mat, base, block, wide, own, days, minutes)
 
 
 def signal_kernel(days, totals, counts, residual, signal):
@@ -262,34 +357,37 @@
             signal[b, rows, :] = (res / weight).astype(signal.dtype)
 
 
-def backward_local_kernel(days, path, link, lag, signal, mats, out):
+def backward_local_kernel(days, t, table, signal, mats, out):
     minutes = signal.shape[1] // days
     out[...] = jnp.zeros_like(out)
+    mat, base, block = local_views(table, t, mats)
     backward_blocks(
-        mats.shape[0],
-        8,
-        mats,
-        path,
-        lag,
-        None,
-        lambda j: signal[link[j]],
+        0, mats.shape[0], 8, mat, base, lambda j: signal[block(j)], out, days, minutes
+    )
+
+
+def backward_remote_kernel(days, cap, first, end, links, t, table, mats, start, *rest):
+    signals, (out, everyone) = rest[:-2], rest[-2:]
+    minutes = signals[0].shape[1] // days
+    place = first * links
+    for part in signals:
+        everyone[place : place + part.shape[0]] = part[...]
+        place += part.shape[0]
+    blank = everyone.shape[0] - 1
+    everyone[blank] = jnp.zeros(everyone.shape[1:], everyone.dtype)
+    out[...] = start[...]
+    mat, base, block = slot_views(table, t, mats)
+    backward_blocks(
+        first * cap,
+        (end - first) * cap,
+        cap,
+        mat,
+        base,
+        lambda i: everyone[block(i)],
         out,
         days,
         minutes,
     )
-
-
-def backward_remote_kernel(days, cap, blocks, me, path, link, lag, slot, mats, start, *rest):
-    signals, (out, everyone) = rest[:-2], rest[-2:]
-    minutes = signals[0].shape[1] // days
-    for s, part in enumerate(signals):
-        everyone[(s + 1) * blocks : (s + 2) * blocks] = part[...]
-    out[...] = start[...]
-
-    def chosen(j):
-        return everyone[(lax.div(slot[j], cap) ^ me[0]) * blocks + link[j]]
-
-    backward_blocks(mats.shape[0], 8, mats, path, lag, None, chosen, out, days, minutes)
 
 
 def finish_kernel(days, total, spill, flows, gradient, new_flows):
@@ -310,17 +408,20 @@
                 )
 
 
-def kernel_call(body, scalars, arrays, out_shape, scratch=()):
-    smem = pl.BlockSpec(memory_space=pltpu.SMEM)
-    vmem = pl.BlockSpec(memory_space=pltpu.VMEM)
-    single = isinstance(out_shape, jax.ShapeDtypeStruct)
+SMEM = pl.BlockSpec(memory_space=pltpu.SMEM)
+VMEM = pl.BlockSpec(memory_space=pltpu.VMEM)
+HBM = pl.BlockSpec(memory_space=pltpu.HBM)
+
+
+def kernel_call(body, scalars, arrays, out_shape, scratch=(), cost=None):
     return pl.pallas_call(
         body,
         out_shape=out_shape,
-        in_specs=[smem] * len(scalars) + [vmem] * len(arrays),
-        out_specs=vmem if single else [vmem] * len(out_shape),
+        in_specs=[SMEM] * len(scalars) + [VMEM] * len(arrays),
+        out_specs=[VMEM] * len(out_shape),
         scratch_shapes=list(scratch),
-        compiler_params=pltpu.CompilerParams(vmem_limit_bytes=48 * 1024 * 1024),
+        compiler_params=pltpu.CompilerParams(vmem_limit_bytes=40 * 1024 * 1024),
+        cost_estimate=cost,
     )(*scalars, *arrays)
 
 
@@ -342,62 +443,112 @@
     paths = path_width // width
     links = counts.shape[2] // width
     corridors = lax.axis_size("corr")
-    cap = (remote_lag.shape[0] + corridors - 2) // (corridors - 1)
+    locals_, remotes = local_lag.shape[0], remote_lag.shape[0]
+    cap = (remotes + corridors - 2) // (corridors - 1)
     span = HALO + minutes
-    others = range(1, corridors)
+    through = sorted({2, corridors - 2}, reverse=True)
+    crossing = [s ^ 1 for s in through]
+    direct = [s for s in range(corridors - 1, 1, -1) if s not in through + crossing]
+    order = crossing + [1] + direct + through
+    many = len(through)
+    cuts = [0, *range(many, len(order) - many + 1), len(order)]
+    t = Table((corridors - 1) * cap, locals_)
     me = lax.axis_index("corr").astype(jnp.int32).reshape(1)
     shape = jax.ShapeDtypeStruct
     piece = (links, days * minutes, width)
     wide = pltpu.VMEM((paths * days * span, width), jnp.float32)
-
-    halo = passed_along(flows[:, minutes - HALO :], "tm", 1)
-    outgoing = kernel_call(
-        functools.partial(forward_remote_kernel, days, cap, links),
-        (me, remote_path, remote_link, remote_lag, remote_slot),
-        (flows, halo, remote_blocks),
-        [shape(piece, jnp.float32) for _ in others],
-        [wide, pltpu.VMEM((corridors * links, days * minutes, width), jnp.float32)],
+    slots_shape = (len(order) * links + 1, days * minutes, width)
+    index = [local_path, local_link, local_lag, remote_path, remote_link, remote_lag, remote_slot]
+
+    before = passed_along(flows, "tm", 1)
+    table, local_mats, remote_mats = pl.pallas_call(
+        functools.partial(prepare_kernel, days, span, cap, corridors, links, order),
+        out_shape=[
+            shape((t.size,), jnp.int32),
+            shape(local_blocks.shape, local_blocks.dtype),
+            shape(remote_blocks.shape, remote_blocks.dtype),
+        ],
+        in_specs=[SMEM] + [HBM] * (len(index) + 2),
+        out_specs=[SMEM, VMEM, VMEM],
+        scratch_shapes=[pltpu.SMEM(i.shape, jnp.int32) for i in index]
+        + [pltpu.SemaphoreType.DMA((len(index) + 2,))],
+        compiler_params=pltpu.CompilerParams(vmem_limit_bytes=40 * 1024 * 1024),
+    )(
+        me,
+        *(
+            pltpu.with_memory_space_constraint(i, pltpu.HBM)
+            for i in (*index, local_blocks, remote_blocks)
+        ),
     )
 
     def exchanged(part, s):
         return lax.ppermute(part, "corr", [(i, i ^ s) for i in range(corridors)])
 
-    received = [exchanged(outgoing[s - 1].astype(WIRE), s) for s in others]
-    own = kernel_call(
-        functools.partial(forward_local_kernel, days),
-        (local_path, local_link, local_lag),
-        (flows, halo, local_blocks),
-        shape(piece, jnp.float32),
+    f32 = jnp.float32
+    crossed, *parts, kept = kernel_call(
+        functools.partial(forward_remote_kernel, days, cap, cuts, links, t),
+        (table,),
+        (flows, before, remote_mats),
+        [shape(((end - first) * links, *piece[1:]), f32) for first, end in zip(cuts, cuts[1:])],
+        [wide, pltpu.VMEM(slots_shape, f32)],
+    )
+    crossed = exchanged(crossed.astype(WIRE), 1)
+    received = [exchanged(p.astype(WIRE), s) for p, s in zip(parts, (1, *direct))]
+    (own,) = kernel_call(
+        functools.partial(forward_local_kernel, days, t),
+        (table,),
+        (flows, before, local_mats),
+        [shape(piece, f32)],
         [wide],
     )
+    kept = (kept + crossed.astype(f32)).astype(WIRE).reshape(many, *piece)
+    received += [exchanged(kept[i], s) for i, s in enumerate(through)]
+    totals = functools.reduce(jnp.add, [p.astype(f32) for p in received], own)
     link_residual, signal = kernel_call(
         functools.partial(signal_kernel, days),
         (),
-        (functools.reduce(jnp.add, [p.astype(jnp.float32) for p in received], own), counts),
-        [shape(counts.shape, jnp.float32), shape(piece, jnp.bfloat16)],
-    )
-    signals = [exchanged(signal, s) for s in others]
-    rows = shape((paths * days * span, width), jnp.float32)
-    local_total = kernel_call(
-        functools.partial(backward_local_kernel, days),
-        (local_path, local_link, local_lag),
-        (signal, local_blocks),
+        (totals, counts),
+        [shape(counts.shape, f32), shape(piece, jnp.bfloat16)],
+    )
+    arrived = [exchanged(signal, s) for s in (*through, 1, *direct)]
+    both = jnp.concatenate(arrived[:many], axis=0)
+    both, signal = lax.optimization_barrier((both, signal))
+    rows = [shape((paths * days * span, width), f32)]
+    (total,) = kernel_call(
+        functools.partial(backward_local_kernel, days, t),
+        (table,),
+        (signal, local_mats),
         rows,
     )
-    total = kernel_call(
-        functools.partial(backward_remote_kernel, days, cap, links),
-        (me, remote_path, remote_link, remote_lag, remote_slot),
-        (remote_blocks, local_total, *signals),
-        rows,
-        [pltpu.VMEM((corridors * links, days * minutes, width), jnp.bfloat16)],
-    )
+    passed = exchanged(both, 1)
+    late = many + 1
+
+    def weigh(first):
+        if first == 0:
+            return None
+        return pl.CostEstimate(
+            flops=2_000_000_000, transcendentals=0, bytes_accessed=6_000_000
+        )
+
+    for first, end, signals in (
+        (late, len(order), [*arrived[late:], *arrived[:many]]),
+        (0, late, [passed, arrived[many]]),
+    ):
+        (total,) = kernel_call(
+            functools.partial(backward_remote_kernel, days, cap, first, end, links, t),
+            (table,),
+            (remote_mats, total, *signals),
+            rows,
+            [pltpu.VMEM(slots_shape, jnp.bfloat16)],
+            weigh(first),
+        )
     early = total.reshape(paths * days, span, width)[:, :HALO]
     spill = passed_along(early, "tm", -1)
     gradient, new_flows = kernel_call(
         functools.partial(finish_kernel, days),
         (),
         (total, spill, flows),
-        [shape(flows.shape, jnp.float32)] * 2,
+        [shape(flows.shape, f32)] * 2,
     )
     return (link_residual, gradient, new_flows)
 
@@ -407,7 +558,7 @@
     corridors = lax.axis_size("corr")
     links = counts.shape[2] // blocks.shape[1]
     cap = (lags.shape[0] + corridors - 2) // (corridors - 1)
-    if cap >= links:
+    if cap >= links and corridors >= 4 and corridors & (corridors - 1) == 0:
         return per_device_dense(*args)
     return per_device_slots(*args)
 

time: 70.2 us -> 56.7 us (0.81)
  the two profiles are of different devices: /device:TPU:17 before, /device:TPU:1 now
where the time goes in v2:
time: 56.7 us; the launch traced here: 56.5 us
  starting transfers between devices  23.6 us (42%)
  Pallas kernels  15.9 us (28%)
  waiting for transfers between devices  15.8 us (28%)
  between operations  0.81 us (1%)
    ppermute x12, starting transfers between devices, exchanged(): return lax.ppermute(part, 'corr', [(i, i ^ s) for i in range(corridors)])  16.2 us
    pallas_call x7, Pallas kernels, kernel_call(): pl.pallas_call(body, out_shape=out_shape, in_specs=[SMEM] * len(scalars)...  13 us
    ppermute x12, waiting for transfers between devices, exchanged(): return lax.ppermute(part, 'corr', [(i, i ^ s) for i in range(corridors)])  12.4 us
    ppermute x2, starting transfers between devices, passed_along(): return lax.ppermute(block, axis, route)  7.41 us
    ppermute x2, waiting for transfers between devices, passed_along(): return lax.ppermute(block, axis, route)  3.41 us
    pallas_call x1, Pallas kernels, per_device_dense(): pl.pallas_call(functools.partial(prepare_kernel, days, span, cap, corrido...  2.95 us
  transfers between devices with their start and end apart: 14, of which 8 were waited for; matrix products, arithmetic and copies ran while one was open for 0% of the time, Pallas kernels for 18%

profile of v2, /device:TPU:1, one launch (start us, length us, event | category | flops | bytes accessed | tf_op | source)
XLA Modules:
  0.0 56.5 jit_solution(17411682363033386159)
XLA Ops:
  0.6 4.5 %collective-permute-start = (bf16[2,24,1024]{2,1,0:T(8,128)(2,1)}, bf16[2,24,1024]{2,1,0:T(8,128)(2,1)S(1)}, u32[]{:S(2)}, u32[]{:S(2)}) collective-permute-start(bf16[2,24,1024]{2,1,0:T(8,128)(2,1)} %flows.5), channel_id=1, source_target_pairs={{0,1},{1,2},{2,3},{4,5},{5,6},{6,7},{8,9},{9,10},{10,11},{12,13},{... | collective-permute-start | bytes 294920 | tf_op jit(solution)/shard_map/ppermute | solution.py:19
  5.2 0.0 copy-start
  5.2 3.0 %shard_map.130 = (s32[338]{0:T(512)S(1)}, bf16[64,128,128]{2,1,0:T(8,128)(2,1)S(1)}, bf16[64,128,128]{2,1,0:T(8,128)(2,1)S(1)}) custom-call(s32[1]{0:T(128)} %bitcast.me, s32[64]{0:T(128)} %local_path.1, s32[64]{0:T(128)} %local_link.1, s32[64]{0:T(128)} %local_lag.1, s32[64]{0:T(128)} %remote_path.1, s32[64]{0:T(128)} %remote_link.1, s32[64]{0:T(128)} %remote_lag.1, ...), custom_call_target="tpu_custom_call" | custom-call | tf_op jit(solution)/shard_map/pallas_call | solution.py:464
  8.2 0.0 collective-permute-done.before
  8.2 0.0 copy-done
  8.2 3.1 %shard_map.132 = (f32[16,48,128]{2,1,0:T(8,128)S(1)}, f32[8,48,128]{2,1,0:T(8,128)S(1)}, f32[8,48,128]{2,1,0:T(8,128)S(1)}, f32[8,48,128]{2,1,0:T(8,128)S(1)}, f32[16,48,128]{2,1,0:T(8,128)S(1)}) custom-call(s32[338]{0:T(512)S(1)} %get-tuple-element.17.table, bf16[2,24,1024]{2,1,0:T(8,128)(2,1)S(1)} %copy-done, ...), custom_call_target="tpu_custom_call" | custom-call | tf_op jit(solution)/shard_map/pallas_call | solution.py:417
  11.4 1.3 %collective-permute-start.4 = (f16[16,48,128]{2,1,0:T(8,128)(2,1)S(1)}, f16[16,48,128]{2,1,0:T(8,128)(2,1)S(1)}, u32[]{:S(2)}, u32[]{:S(2)}) collective-permute-start(f16[16,48,128]{2,1,0:T(8,128)(2,1)S(1)} %convert_element_type.39), channel_id=1, source_target_pairs={{0,4},{4,0},{8,12},{12,8},{16,20},{20,16},{24,28},{28,24},{1,5},{5... | collective-permute-start | bytes 589832 | tf_op jit(solution)/shard_map/ppermute | solution.py:485
  12.7 2.4 %collective-permute-start.3 = (f16[8,48,128]{2,1,0:T(8,128)(2,1)S(1)}, f16[8,48,128]{2,1,0:T(8,128)(2,1)S(1)}, u32[]{:S(2)}, u32[]{:S(2)}) collective-permute-start(f16[8,48,128]{2,1,0:T(8,128)(2,1)S(1)} %convert_element_type.37), channel_id=1, source_target_pairs={{0,16},{4,20},{8,24},{12,28},{16,0},{20,4},{24,8},{28,12},{1,17},{... | collective-permute-start | bytes 294920 | tf_op jit(solution)/shard_map/ppermute | solution.py:485
  15.1 0.1 collective-permute-start.2
  15.1 1.2 %collective-permute-start.1 = (f16[8,48,128]{2,1,0:T(8,128)(2,1)S(1)}, f16[8,48,128]{2,1,0:T(8,128)(2,1)S(1)}, u32[]{:S(2)}, u32[]{:S(2)}) collective-permute-start(f16[8,48,128]{2,1,0:T(8,128)(2,1)S(1)} %convert_element_type.33), channel_id=1, source_target_pairs={{0,4},{4,0},{8,12},{12,8},{16,20},{20,16},{24,28},{28,24},{1,5},{5... | collective-permute-start | bytes 294920 | tf_op jit(solution)/shard_map/ppermute | solution.py:485
  16.3 0.6 %collective-permute-done.4 = f16[16,48,128]{2,1,0:T(8,128)(2,1)S(1)} collective-permute-done((f16[16,48,128]{2,1,0:T(8,128)(2,1)S(1)}, f16[16,48,128]{2,1,0:T(8,128)(2,1)S(1)}, u32[]{:S(2)}, u32[]{:S(2)}) %collective-permute-start.4) | collective-permute-done | bytes 196640 | tf_op jit(solution)/shard_map/ppermute | solution.py:485
  17.0 0.0 copy-start.1
  17.0 0.1 add_convert_fusion
  17.1 3.9 %collective-permute-start.5 = (f16[8,48,128]{2,1,0:T(8,128)(2,1)S(1)}, f16[8,48,128]{2,1,0:T(8,128)(2,1)S(1)}, u32[]{:S(2)}, u32[]{:S(2)}) collective-permute-start(f16[8,48,128]{2,1,0:T(8,128)(2,1)S(1)} %get-tuple-element.31), channel_id=1, source_target_pairs={{0,24},{4,28},{8,16},{12,20},{16,8},{20,12},{24,0},{28,4},{1,25},{... | collective-permute-start | bytes 294920 | tf_op jit(solution)/shard_map/ppermute | solution.py:485
  21.0 0.0 collective-permute-start.6
  21.0 3.0 %shard_map.131 = f32[8,48,128]{2,1,0:T(8,128)S(1)} custom-call(s32[338]{0:T(512)S(1)} %get-tuple-element.17.table, bf16[2,24,1024]{2,1,0:T(8,128)(2,1)S(1)} %copy-done, bf16[2,24,1024]{2,1,0:T(8,128)(2,1)S(1)} %collective-permute-done.before, bf16[64,128,128]{2,1,0:T(8,128)(2,1)S(1)} %get-tuple-element.18.mats), custom_call_target="tpu_custom_call" | custom-call | tf_op jit(solution)/shard_map/pallas_call | solution.py:417
  24.0 0.7 %collective-permute-done.3 = f16[8,48,128]{2,1,0:T(8,128)(2,1)S(1)} collective-permute-done((f16[8,48,128]{2,1,0:T(8,128)(2,1)S(1)}, f16[8,48,128]{2,1,0:T(8,128)(2,1)S(1)}, u32[]{:S(2)}, u32[]{:S(2)}) %collective-permute-start.3) | collective-permute-done | bytes 98336 | tf_op jit(solution)/shard_map/ppermute | solution.py:485
  24.7 1.3 %collective-permute-done.2 = f16[8,48,128]{2,1,0:T(8,128)(2,1)S(1)} collective-permute-done((f16[8,48,128]{2,1,0:T(8,128)(2,1)S(1)}, f16[8,48,128]{2,1,0:T(8,128)(2,1)S(1)}, u32[]{:S(2)}, u32[]{:S(2)}) %collective-permute-start.2) | collective-permute-done | bytes 98336 | tf_op jit(solution)/shard_map/ppermute | solution.py:485
  26.0 0.0 collective-permute-done.1
  26.0 0.0 collective-permute-done.5
  26.0 2.4 %collective-permute-done.6 = f16[8,48,128]{2,1,0:T(8,128)(2,1)S(1)} collective-permute-done((f16[8,48,128]{2,1,0:T(8,128)(2,1)S(1)}, f16[8,48,128]{2,1,0:T(8,128)(2,1)S(1)}, u32[]{:S(2)}, u32[]{:S(2)}) %collective-permute-start.6) | collective-permute-done | bytes 98336 | tf_op jit(solution)/shard_map/ppermute | solution.py:485
  28.4 0.1 convert_add_fusion.totals
  28.5 0.0 copy-done.1
  28.6 0.7 %shard_map.133 = (f32[2,24,1024]{2,1,0:T(8,128)}, bf16[8,48,128]{2,1,0:T(8,128)(2,1)S(1)}) custom-call(f32[8,48,128]{2,1,0:T(8,128)S(1)} %convert_add_fusion.totals, f32[2,24,1024]{2,1,0:T(8,128)S(1)} %copy-done.1), custom_call_target="tpu_custom_call" | custom-call | tf_op jit(solution)/shard_map/pallas_call | solution.py:417
  29.3 0.5 collective-permute-start.8
  29.8 3.0 %collective-permute-start.7 = (bf16[8,48,128]{2,1,0:T(8,128)(2,1)S(1)}, bf16[8,48,128]{2,1,0:T(8,128)(2,1)S(1)}, u32[]{:S(2)}, u32[]{:S(2)}) collective-permute-start(bf16[8,48,128]{2,1,0:T(8,128)(2,1)S(1)} %get-tuple-element.27.signal), channel_id=1, source_target_pairs={{0,24},{4,28},{8,16},{12,20},{16,8},{20,12},{24,0},{28,4},{1,25},{... | collective-permute-start | bytes 294920 | tf_op jit(solution)/shard_map/ppermute | solution.py:485
  32.8 0.0 collective-permute-start.10
  32.8 2.3 %collective-permute-start.9 = (bf16[8,48,128]{2,1,0:T(8,128)(2,1)S(1)}, bf16[8,48,128]{2,1,0:T(8,128)(2,1)S(1)}, u32[]{:S(2)}, u32[]{:S(2)}) collective-permute-start(bf16[8,48,128]{2,1,0:T(8,128)(2,1)S(1)} %get-tuple-element.27.signal), channel_id=1, source_target_pairs={{0,20},{4,16},{8,28},{12,24},{16,4},{20,0},{24,12},{28,8},{1,21},{... | collective-permute-start | bytes 294920 | tf_op jit(solution)/shard_map/ppermute | solution.py:485
  35.1 0.0 collective-permute-done.8.rest_3_
  35.1 2.3 %collective-permute-done.7.rest_2_ = bf16[8,48,128]{2,1,0:T(8,128)(2,1)S(1)} collective-permute-done((bf16[8,48,128]{2,1,0:T(8,128)(2,1)S(1)}, bf16[8,48,128]{2,1,0:T(8,128)(2,1)S(1)}, u32[]{:S(2)}, u32[]{:S(2)}) %collective-permute-start.7) | collective-permute-done | bytes 98336 | tf_op jit(solution)/shard_map/ppermute | solution.py:485
  37.4 0.3 collective-permute-start.11
  37.8 1.2 %collective-permute-start.12 = (bf16[8,48,128]{2,1,0:T(8,128)(2,1)S(1)}, bf16[8,48,128]{2,1,0:T(8,128)(2,1)S(1)}, u32[]{:S(2)}, u32[]{:S(2)}) collective-permute-start(bf16[8,48,128]{2,1,0:T(8,128)(2,1)S(1)} %get-tuple-element.27.signal), channel_id=1, source_target_pairs={{0,4},{4,0},{8,12},{12,8},{16,20},{20,16},{24,28},{28,24},{1,5},{5... | collective-permute-start | bytes 294920 | tf_op jit(solution)/shard_map/ppermute | solution.py:485
  39.0 2.4 %shard_map.134.start = f32[640,128]{1,0:T(8,128)S(1)} custom-call(s32[338]{0:T(512)S(1)} %get-tuple-element.17.table, bf16[8,48,128]{2,1,0:T(8,128)(2,1)S(1)} %get-tuple-element.27.signal, bf16[64,128,128]{2,1,0:T(8,128)(2,1)S(1)} %get-tuple-element.18.mats), custom_call_target="tpu_custom_call" | custom-call | tf_op jit(solution)/shard_map/pallas_call | solution.py:417
  41.4 3.0 %collective-permute-done.10.rest_1_ = bf16[8,48,128]{2,1,0:T(8,128)(2,1)S(1)} collective-permute-done((bf16[8,48,128]{2,1,0:T(8,128)(2,1)S(1)}, bf16[8,48,128]{2,1,0:T(8,128)(2,1)S(1)}, u32[]{:S(2)}, u32[]{:S(2)}) %collective-permute-start.10) | collective-permute-done | bytes 98336 | tf_op jit(solution)/shard_map/ppermute | solution.py:485
  44.3 2.1 %collective-permute-done.9.rest_0_ = bf16[8,48,128]{2,1,0:T(8,128)(2,1)S(1)} collective-permute-done((bf16[8,48,128]{2,1,0:T(8,128)(2,1)S(1)}, bf16[8,48,128]{2,1,0:T(8,128)(2,1)S(1)}, u32[]{:S(2)}, u32[]{:S(2)}) %collective-permute-start.9) | collective-permute-done | bytes 98336 | tf_op jit(solution)/shard_map/ppermute | solution.py:485
  46.4 1.6 %shard_map.135.start = f32[640,128]{1,0:T(8,128)S(1)} custom-call(s32[338]{0:T(512)S(1)} %get-tuple-element.17.table, bf16[64,128,128]{2,1,0:T(8,128)(2,1)S(1)} %get-tuple-element.19.mats, f32[640,128]{1,0:T(8,128)S(1)} %shard_map.134.start, bf16[8,48,128]{2,1,0:T(8,128)(2,1)S(1)} %collective-permute-done.9.rest_0_, ...), custom_call_target="tpu_custom_call" | custom-call | flops 2000000000 | bytes 6000000 | tf_op jit(solution)/shard_map/pallas_call | solution.py:417
  48.1 0.0 collective-permute-done.12.rest_1_
  48.1 0.0 collective-permute-done.11.rest_0_
  48.1 1.4 %shard_map.136.total = f32[640,128]{1,0:T(8,128)S(1)} custom-call(s32[338]{0:T(512)S(1)} %get-tuple-element.17.table, bf16[64,128,128]{2,1,0:T(8,128)(2,1)S(1)} %get-tuple-element.19.mats, f32[640,128]{1,0:T(8,128)S(1)} %shard_map.135.start, bf16[16,48,128]{2,1,0:T(8,128)(2,1)S(1)} %collective-permute-done.11.rest_0_, ...), custom_call_target="tpu_custom_call" | custom-call | tf_op jit(solution)/shard_map/pallas_call | solution.py:417
  49.5 2.9 %collective-permute-start.13 = (f32[16,16,128]{2,1,0:T(8,128)S(1)}, f32[16,16,128]{2,1,0:T(8,128)S(1)}, u32[]{:S(2)}, u32[]{:S(2)}) collective-permute-start(f32[16,16,128]{2,1,0:T(8,128)S(1)} %slice.16), channel_id=1, source_target_pairs={{1,0},{2,1},{3,2},{5,4},{6,5},{7,6},{9,8},{10,9},{11,10},{13,12},{... | collective-permute-start | bytes 393224 | tf_op jit(solution)/shard_map/ppermute | solution.py:19
  52.3 3.4 %collective-permute-done.13.spill = f32[16,16,128]{2,1,0:T(8,128)S(1)} collective-permute-done((f32[16,16,128]{2,1,0:T(8,128)S(1)}, f32[16,16,128]{2,1,0:T(8,128)S(1)}, u32[]{:S(2)}, u32[]{:S(2)}) %collective-permute-start.13) | collective-permute-done | bytes 131104 | tf_op jit(solution)/shard_map/ppermute | solution.py:19
  55.7 0.8 %shard_map.137 = (f32[2,24,1024]{2,1,0:T(8,128)}, f32[2,24,1024]{2,1,0:T(8,128)}) custom-call(f32[640,128]{1,0:T(8,128)S(1)} %shard_map.136.total, f32[16,16,128]{2,1,0:T(8,128)S(1)} %collective-permute-done.13.spill, bf16[2,24,1024]{2,1,0:T(8,128)(2,1)S(1)} %copy-done), custom_call_target="tpu_custom_call" | custom-call | tf_op jit(solution)/shard_map/pallas_call | solution.py:417
  (7 shorter events, 0.2 us)
Async XLA Ops:
  0.6 7.5 %collective-permute-start = (bf16[2,24,1024]{2,1,0:T(8,128)(2,1)}, bf16[2,24,1024]{2,1,0:T(8,128)(2,1)S(1)}, u32[]{:S(2)}, u32[]{:S(2)}) collective-permute-start(bf16[2,24,1024]{2,1,0:T(8,128)(2,1)} %flows.5), channel_id=1, source_target_pairs={{0,1},{1,2},{2,3},{4,5},{5,6},{6,7},{8,9},{9,10},{10,11},{12,13},{... | collective-permute-start | bytes 294920 | tf_op jit(solution)/shard_map/ppermute | solution.py:19
  5.2 3.0 %copy-start = (bf16[2,24,1024]{2,1,0:T(8,128)(2,1)S(1)}, bf16[2,24,1024]{2,1,0:T(8,128)(2,1)}, u32[]{:S(2)}) copy-start(bf16[2,24,1024]{2,1,0:T(8,128)(2,1)} %flows.5) | copy-start | bytes 294916
  11.4 5.6 %collective-permute-start.4 = (f16[16,48,128]{2,1,0:T(8,128)(2,1)S(1)}, f16[16,48,128]{2,1,0:T(8,128)(2,1)S(1)}, u32[]{:S(2)}, u32[]{:S(2)}) collective-permute-start(f16[16,48,128]{2,1,0:T(8,128)(2,1)S(1)} %convert_element_type.39), channel_id=1, source_target_pairs={{0,4},{4,0},{8,12},{12,8},{16,20},{20,16},{24,28},{28,24},{1,5},{5... | collective-permute-start | bytes 589832 | tf_op jit(solution)/shard_map/ppermute | solution.py:485
  12.7 12.0 %collective-permute-start.3 = (f16[8,48,128]{2,1,0:T(8,128)(2,1)S(1)}, f16[8,48,128]{2,1,0:T(8,128)(2,1)S(1)}, u32[]{:S(2)}, u32[]{:S(2)}) collective-permute-start(f16[8,48,128]{2,1,0:T(8,128)(2,1)S(1)} %convert_element_type.37), channel_id=1, source_target_pairs={{0,16},{4,20},{8,24},{12,28},{16,0},{20,4},{24,8},{28,12},{1,17},{... | collective-permute-start | bytes 294920 | tf_op jit(solution)/shard_map/ppermute | solution.py:485
  15.1 10.9 %collective-permute-start.2 = (f16[8,48,128]{2,1,0:T(8,128)(2,1)S(1)}, f16[8,48,128]{2,1,0:T(8,128)(2,1)S(1)}, u32[]{:S(2)}, u32[]{:S(2)}) collective-permute-start(f16[8,48,128]{2,1,0:T(8,128)(2,1)S(1)} %convert_element_type.35), channel_id=1, source_target_pairs={{0,20},{4,16},{8,28},{12,24},{16,4},{20,0},{24,12},{28,8},{1,21},{... | collective-permute-start | bytes 294920 | tf_op jit(solution)/shard_map/ppermute | solution.py:485
  15.1 10.9 %collective-permute-start.1 = (f16[8,48,128]{2,1,0:T(8,128)(2,1)S(1)}, f16[8,48,128]{2,1,0:T(8,128)(2,1)S(1)}, u32[]{:S(2)}, u32[]{:S(2)}) collective-permute-start(f16[8,48,128]{2,1,0:T(8,128)(2,1)S(1)} %convert_element_type.33), channel_id=1, source_target_pairs={{0,4},{4,0},{8,12},{12,8},{16,20},{20,16},{24,28},{28,24},{1,5},{5... | collective-permute-start | bytes 294920 | tf_op jit(solution)/shard_map/ppermute | solution.py:485
  17.0 11.6 %copy-start.1 = (f32[2,24,1024]{2,1,0:T(8,128)S(1)}, f32[2,24,1024]{2,1,0:T(8,128)}, u32[]{:S(2)}) copy-start(f32[2,24,1024]{2,1,0:T(8,128)} %counts.1) | copy-start | bytes 589828
  17.1 8.9 %collective-permute-start.5 = (f16[8,48,128]{2,1,0:T(8,128)(2,1)S(1)}, f16[8,48,128]{2,1,0:T(8,128)(2,1)S(1)}, u32[]{:S(2)}, u32[]{:S(2)}) collective-permute-start(f16[8,48,128]{2,1,0:T(8,128)(2,1)S(1)} %get-tuple-element.31), channel_id=1, source_target_pairs={{0,24},{4,28},{8,16},{12,20},{16,8},{20,12},{24,0},{28,4},{1,25},{... | collective-permute-start | bytes 294920 | tf_op jit(solution)/shard_map/ppermute | solution.py:485
  21.0 7.4 %collective-permute-start.6 = (f16[8,48,128]{2,1,0:T(8,128)(2,1)S(1)}, f16[8,48,128]{2,1,0:T(8,128)(2,1)S(1)}, u32[]{:S(2)}, u32[]{:S(2)}) collective-permute-start(f16[8,48,128]{2,1,0:T(8,128)(2,1)S(1)} %get-tuple-element.32), channel_id=1, source_target_pairs={{0,8},{4,12},{8,0},{12,4},{16,24},{20,28},{24,16},{28,20},{1,9},{5... | collective-permute-start | bytes 294920 | tf_op jit(solution)/shard_map/ppermute | solution.py:485
  29.3 5.9 %collective-permute-start.8 = (bf16[8,48,128]{2,1,0:T(8,128)(2,1)S(1)}, bf16[8,48,128]{2,1,0:T(8,128)(2,1)S(1)}, u32[]{:S(2)}, u32[]{:S(2)}) collective-permute-start(bf16[8,48,128]{2,1,0:T(8,128)(2,1)S(1)} %get-tuple-element.27.signal), channel_id=1, source_target_pairs={{0,8},{4,12},{8,0},{12,4},{16,24},{20,28},{24,16},{28,20},{1,9},{5... | collective-permute-start | bytes 294920 | tf_op jit(solution)/shard_map/ppermute | solution.py:485
  29.8 7.6 %collective-permute-start.7 = (bf16[8,48,128]{2,1,0:T(8,128)(2,1)S(1)}, bf16[8,48,128]{2,1,0:T(8,128)(2,1)S(1)}, u32[]{:S(2)}, u32[]{:S(2)}) collective-permute-start(bf16[8,48,128]{2,1,0:T(8,128)(2,1)S(1)} %get-tuple-element.27.signal), channel_id=1, source_target_pairs={{0,24},{4,28},{8,16},{12,20},{16,8},{20,12},{24,0},{28,4},{1,25},{... | collective-permute-start | bytes 294920 | tf_op jit(solution)/shard_map/ppermute | solution.py:485
  32.8 11.6 %collective-permute-start.10 = (bf16[8,48,128]{2,1,0:T(8,128)(2,1)S(1)}, bf16[8,48,128]{2,1,0:T(8,128)(2,1)S(1)}, u32[]{:S(2)}, u32[]{:S(2)}) collective-permute-start(bf16[8,48,128]{2,1,0:T(8,128)(2,1)S(1)} %get-tuple-element.27.signal), channel_id=1, source_target_pairs={{0,16},{4,20},{8,24},{12,28},{16,0},{20,4},{24,8},{28,12},{1,17},{... | collective-permute-start | bytes 294920 | tf_op jit(solution)/shard_map/ppermute | solution.py:485
  32.8 13.6 %collective-permute-start.9 = (bf16[8,48,128]{2,1,0:T(8,128)(2,1)S(1)}, bf16[8,48,128]{2,1,0:T(8,128)(2,1)S(1)}, u32[]{:S(2)}, u32[]{:S(2)}) collective-permute-start(bf16[8,48,128]{2,1,0:T(8,128)(2,1)S(1)} %get-tuple-element.27.signal), channel_id=1, source_target_pairs={{0,20},{4,16},{8,28},{12,24},{16,4},{20,0},{24,12},{28,8},{1,21},{... | collective-permute-start | bytes 294920 | tf_op jit(solution)/shard_map/ppermute | solution.py:485
  37.4 10.6 %collective-permute-start.11 = (bf16[16,48,128]{2,1,0:T(8,128)(2,1)S(1)}, bf16[16,48,128]{2,1,0:T(8,128)(2,1)S(1)}, u32[]{:S(2)}, u32[]{:S(2)}) collective-permute-start(bf16[16,48,128]{2,1,0:T(8,128)(2,1)S(1)} %pad_maximum_fusion), channel_id=1, source_target_pairs={{0,4},{4,0},{8,12},{12,8},{16,20},{20,16},{24,28},{28,24},{1,5},{5... | collective-permute-start | bytes 589832 | tf_op jit(solution)/shard_map/ppermute | solution.py:485
  37.8 10.3 %collective-permute-start.12 = (bf16[8,48,128]{2,1,0:T(8,128)(2,1)S(1)}, bf16[8,48,128]{2,1,0:T(8,128)(2,1)S(1)}, u32[]{:S(2)}, u32[]{:S(2)}) collective-permute-start(bf16[8,48,128]{2,1,0:T(8,128)(2,1)S(1)} %get-tuple-element.27.signal), channel_id=1, source_target_pairs={{0,4},{4,0},{8,12},{12,8},{16,20},{20,16},{24,28},{28,24},{1,5},{5... | collective-permute-start | bytes 294920 | tf_op jit(solution)/shard_map/ppermute | solution.py:485
  49.5 6.3 %collective-permute-start.13 = (f32[16,16,128]{2,1,0:T(8,128)S(1)}, f32[16,16,128]{2,1,0:T(8,128)S(1)}, u32[]{:S(2)}, u32[]{:S(2)}) collective-permute-start(f32[16,16,128]{2,1,0:T(8,128)S(1)} %slice.16), channel_id=1, source_target_pairs={{1,0},{2,1},{3,2},{5,4},{6,5},{7,6},{9,8},{10,9},{11,10},{13,12},{... | collective-permute-start | bytes 393224 | tf_op jit(solution)/shard_map/ppermute | solution.py:19

commit v3 on v2

--- a/solution.py
+++ b/solution.py
@@ -174,152 +174,102 @@
             wide[row + HALO : row + span, :] = flows_ref[d, :, cols].astype(jnp.float32)
 
 
-def forward_blocks(start, count, unroll, mat, base, target, wide, acc, days, minutes):
+def forward_blocks(groups, unroll, mat, base, target, wide, acc, days, minutes):
     span = HALO + minutes
 
     def group(g, carry):
         parts = []
         for u in range(unroll):
-            j = start + g * unroll + u
-            rows = [
-                wide[pl.ds(base(j) + d * span, minutes), :] for d in range(days)
-            ]
+            rows = [wide[pl.ds(base(g, u) + d * span, minutes), :] for d in range(days)]
             taken = jnp.concatenate(rows, axis=0).astype(jnp.bfloat16)
             parts.append(
                 lax.dot_general(
                     taken,
-                    mat(j),
+                    mat(g, u),
                     (((1,), (1,)), ((), ())),
                     preferred_element_type=jnp.float32,
                 )
             )
         for u in range(unroll):
-            acc[target(start + g * unroll + u)] += parts[u]
+            acc[target(g, u)] += parts[u]
         return carry
 
-    lax.fori_loop(0, count // unroll, group, 0)
-
-
-def backward_blocks(start, count, unroll, mat, base, signal, acc, days, minutes):
+    lax.fori_loop(*groups, group, 0)
+
+
+def backward_blocks(groups, unroll, mat, base, signal, acc, days, minutes):
     span = HALO + minutes
 
     def group(g, carry):
-        parts = []
-        for u in range(unroll):
-            j = start + g * unroll + u
-            parts.append(jnp.dot(signal(j), mat(j), preferred_element_type=jnp.float32))
+        parts = [
+            jnp.dot(signal(g, u), mat(g, u), preferred_element_type=jnp.float32)
+            for u in range(unroll)
+        ]
         for u in range(unroll):
             for d in range(days):
-                rows = pl.ds(base(start + g * unroll + u) + d * span, minutes)
+                rows = pl.ds(base(g, u) + d * span, minutes)
                 acc[rows, :] += parts[u][d * minutes : (d + 1) * minutes]
         return carry
 
-    lax.fori_loop(0, count // unroll, group, 0)
+    lax.fori_loop(*groups, group, 0)
 
 
 class Table:
-    def __init__(self, slots, blocks):
-        self.mat = 0
-        self.base = slots
-        self.block = 2 * slots
-        self.local_base = 3 * slots
-        self.local_block = 3 * slots + blocks
-        self.size = 3 * slots + 2 * blocks
-
-
-def prepare_kernel(
-    days,
-    span,
-    cap,
-    corridors,
-    links,
-    order,
-    me,
-    local_path,
-    local_link,
-    local_lag,
-    remote_path,
-    remote_link,
-    remote_lag,
-    remote_slot,
-    local_mats,
-    remote_mats,
-    table,
-    local_out,
-    remote_out,
-    lp,
-    ll,
-    lk,
-    rp,
-    rl,
-    rk,
-    rs,
-    sems,
-):
-    slots = (corridors - 1) * cap
-    locals_, remotes = lp.shape[0], rp.shape[0]
-    t = Table(slots, locals_)
-    pairs = (
-        (local_path, lp),
-        (local_link, ll),
-        (local_lag, lk),
-        (remote_path, rp),
-        (remote_link, rl),
-        (remote_lag, rk),
-        (remote_slot, rs),
-        (remote_mats, remote_out),
-        (local_mats, local_out),
-    )
+    def __init__(self, places, slots, blocks):
+        self.start = 0
+        self.block = self.start + places
+        self.base = self.block + slots
+        self.link = self.base + blocks
+        self.size = self.link + blocks
+
+
+def prepare_kernel(cap, order, t, row_step, me, *rest):
+    sources, (table, mats_out, path, link, lag, slot, sems) = rest[:5], rest[5:]
+    blocks = slot.shape[0]
+    pairs = zip(sources, (path, link, lag, slot, mats_out))
     copies = [pltpu.make_async_copy(a, b, sems.at[i]) for i, (a, b) in enumerate(pairs)]
     for copy in copies:
         copy.start()
-
-    def blank(i, carry):
-        table[t.mat + i] = 0
-        table[t.base + i] = HALO
-        table[t.block + i] = (corridors - 1) * links
+    for p, s in enumerate(order):
+        table[t.start + p] = t.block + (me[0] ^ s) * cap
+    for i in range((len(order) + 1) * cap):
+        table[t.block + i] = -1
+    for copy in copies[:4]:
+        copy.wait()
+
+    def place(j, carry):
+        table[t.block + slot[j]] = j
+        table[t.base + j] = path[j] * row_step + HALO - lag[j]
+        table[t.link + j] = link[j]
         return carry
 
-    lax.fori_loop(0, slots, blank, 0, unroll=10 if slots % 10 == 0 else 1)
-    for copy in copies[:7]:
-        copy.wait()
-
-    def remote(j, carry):
-        owner = lax.div(rs[j], cap)
-        rel = owner ^ me[0]
-        place = jnp.int32(0)
-        for p, s in enumerate(order):
-            place = jnp.where(rel == s, p, place)
-        i = place * cap + rs[j] - owner * cap
-        table[t.mat + i] = j
-        table[t.base + i] = rp[j] * (days * span) + HALO - rk[j]
-        table[t.block + i] = place * links + rl[j]
-        return carry
-
-    def local(j, carry):
-        table[t.local_base + j] = lp[j] * (days * span) + HALO - lk[j]
-        table[t.local_block + j] = ll[j]
-        return carry
-
-    lax.fori_loop(0, remotes, remote, 0, unroll=8)
-    lax.fori_loop(0, locals_, local, 0, unroll=8)
-    for copy in copies[7:]:
-        copy.wait()
-
-
-def slot_views(table, t, mats):
+    lax.fori_loop(0, blocks, place, 0, unroll=8)
+    copies[4].wait()
+
+
+def slot_views(table, t, mats, links, blank):
+    def index(place, rank):
+        return table[table[t.start + place] + rank]
+
+    def mat(place, rank):
+        return mats[jnp.maximum(index(place, rank), 0)]
+
+    def base(place, rank):
+        return table[t.base + jnp.maximum(index(place, rank), 0)]
+
+    def block(place, rank):
+        j = index(place, rank)
+        spot = place * links + table[t.link + jnp.maximum(j, 0)]
+        return jnp.where(j < 0, blank, spot)
+
+    return mat, base, block
+
+
+def local_views(path, link, lag, mats, unroll, row_step):
     return (
-        lambda i: mats[table[t.mat + i]],
-        lambda i: table[t.base + i],
-        lambda i: table[t.block + i],
-    )
-
-
-def local_views(table, t, mats):
-    return (
-        lambda j: mats[j],
-        lambda j: table[t.local_base + j],
-        lambda j: table[t.local_block + j],
+        lambda g, u: mats[g * unroll + u],
+        lambda g, u: path[g * unroll + u] * row_step + HALO - lag[g * unroll + u],
+        lambda g, u: link[g * unroll + u],
     )
 
 
@@ -328,18 +278,18 @@
     minutes, width = flows.shape[1], mats.shape[2]
     stage_flows(flows, before, wide, days, width)
     acc[...] = jnp.zeros_like(acc)
-    mat, base, block = slot_views(table, t, mats)
-    forward_blocks(0, cuts[-1] * cap, cap, mat, base, block, wide, acc, days, minutes)
+    views = slot_views(table, t, mats, links, acc.shape[0] - 1)
+    forward_blocks((cuts[0], cuts[-1]), cap, *views, wide, acc, days, minutes)
     for first, end, out in zip(cuts, cuts[1:], outs):
         out[...] = acc[first * links : end * links]
 
 
-def forward_local_kernel(days, t, table, flows, before, mats, own, wide):
+def forward_local_kernel(days, path, link, lag, flows, before, mats, own, wide):
     minutes, width = flows.shape[1], mats.shape[2]
     stage_flows(flows, before, wide, days, width)
     own[...] = jnp.zeros_like(own)
-    mat, base, block = local_views(table, t, mats)
-    forward_blocks(0, mats.shape[0], 8, mat, base, block, wide, own, days, minutes)
+    views = local_views(path, link, lag, mats, 8, days * (HALO + minutes))
+    forward_blocks((0, mats.shape[0] // 8), 8, *views, wide, own, days, minutes)
 
 
 def signal_kernel(days, totals, counts, residual, signal):
@@ -357,17 +307,29 @@
             signal[b, rows, :] = (res / weight).astype(signal.dtype)
 
 
-def backward_local_kernel(days, t, table, signal, mats, out):
+def backward_local_kernel(days, path, link, lag, signal, mats, out):
     minutes = signal.shape[1] // days
     out[...] = jnp.zeros_like(out)
-    mat, base, block = local_views(table, t, mats)
+    mat, base, block = local_views(path, link, lag, mats, 8, days * (HALO + minutes))
     backward_blocks(
-        0, mats.shape[0], 8, mat, base, lambda j: signal[block(j)], out, days, minutes
+        (0, mats.shape[0] // 8),
+        8,
+        mat,
+        base,
+        lambda g, u: signal[block(g, u)],
+        out,
+        days,
+        minutes,
     )
 
 
 def backward_remote_kernel(days, cap, first, end, links, t, table, mats, start, *rest):
-    signals, (out, everyone) = rest[:-2], rest[-2:]
+    count = (end - first) * links
+    signals, sources, rest = [], 0, list(rest)
+    while sources < count:
+        signals.append(rest.pop(0))
+        sources += signals[-1].shape[0]
+    out, early, everyone = rest[0], rest[1:-1], rest[-1]
     minutes = signals[0].shape[1] // days
     place = first * links
     for part in signals:
@@ -376,18 +338,14 @@
     blank = everyone.shape[0] - 1
     everyone[blank] = jnp.zeros(everyone.shape[1:], everyone.dtype)
     out[...] = start[...]
-    mat, base, block = slot_views(table, t, mats)
+    span = HALO + minutes
+    mat, base, block = slot_views(table, t, mats, links, blank)
     backward_blocks(
-        first * cap,
-        (end - first) * cap,
-        cap,
-        mat,
-        base,
-        lambda i: everyone[block(i)],
-        out,
-        days,
-        minutes,
-    )
+        (first, end), cap, mat, base, lambda g, u: everyone[block(g, u)], out, days, minutes
+    )
+    if early:
+        for i in range(early[0].shape[0]):
+            early[0][i] = out[i * span : i * span + HALO, :]
 
 
 def finish_kernel(days, total, spill, flows, gradient, new_flows):
@@ -443,43 +401,37 @@
     paths = path_width // width
     links = counts.shape[2] // width
     corridors = lax.axis_size("corr")
-    locals_, remotes = local_lag.shape[0], remote_lag.shape[0]
+    remotes = remote_lag.shape[0]
     cap = (remotes + corridors - 2) // (corridors - 1)
     span = HALO + minutes
-    through = sorted({2, corridors - 2}, reverse=True)
+    through = sorted({2, corridors - 2})
     crossing = [s ^ 1 for s in through]
     direct = [s for s in range(corridors - 1, 1, -1) if s not in through + crossing]
     order = crossing + [1] + direct + through
     many = len(through)
     cuts = [0, *range(many, len(order) - many + 1), len(order)]
-    t = Table((corridors - 1) * cap, locals_)
+    t = Table(len(order), corridors * cap, remotes)
     me = lax.axis_index("corr").astype(jnp.int32).reshape(1)
     shape = jax.ShapeDtypeStruct
     piece = (links, days * minutes, width)
     wide = pltpu.VMEM((paths * days * span, width), jnp.float32)
     slots_shape = (len(order) * links + 1, days * minutes, width)
-    index = [local_path, local_link, local_lag, remote_path, remote_link, remote_lag, remote_slot]
+    local_index = (local_path, local_link, local_lag)
 
     before = passed_along(flows, "tm", 1)
-    table, local_mats, remote_mats = pl.pallas_call(
-        functools.partial(prepare_kernel, days, span, cap, corridors, links, order),
+    fixed = (remote_path, remote_link, remote_lag, remote_slot, remote_blocks)
+    table, remote_mats = pl.pallas_call(
+        functools.partial(prepare_kernel, cap, order, t, days * span),
         out_shape=[
             shape((t.size,), jnp.int32),
-            shape(local_blocks.shape, local_blocks.dtype),
             shape(remote_blocks.shape, remote_blocks.dtype),
         ],
-        in_specs=[SMEM] + [HBM] * (len(index) + 2),
-        out_specs=[SMEM, VMEM, VMEM],
-        scratch_shapes=[pltpu.SMEM(i.shape, jnp.int32) for i in index]
-        + [pltpu.SemaphoreType.DMA((len(index) + 2,))],
+        in_specs=[SMEM] + [HBM] * len(fixed),
+        out_specs=[SMEM, VMEM],
+        scratch_shapes=[pltpu.SMEM(remote_slot.shape, jnp.int32) for _ in fixed[1:]]
+        + [pltpu.SemaphoreType.DMA((len(fixed),))],
         compiler_params=pltpu.CompilerParams(vmem_limit_bytes=40 * 1024 * 1024),
-    )(
-        me,
-        *(
-            pltpu.with_memory_space_constraint(i, pltpu.HBM)
-            for i in (*index, local_blocks, remote_blocks)
-        ),
-    )
+    )(me, *(pltpu.with_memory_space_constraint(i, pltpu.HBM) for i in fixed))
 
     def exchanged(part, s):
         return lax.ppermute(part, "corr", [(i, i ^ s) for i in range(corridors)])
@@ -495,14 +447,14 @@
     crossed = exchanged(crossed.astype(WIRE), 1)
     received = [exchanged(p.astype(WIRE), s) for p, s in zip(parts, (1, *direct))]
     (own,) = kernel_call(
-        functools.partial(forward_local_kernel, days, t),
-        (table,),
-        (flows, before, local_mats),
+        functools.partial(forward_local_kernel, days),
+        local_index,
+        (flows, before, local_blocks),
         [shape(piece, f32)],
         [wide],
     )
     kept = (kept + crossed.astype(f32)).astype(WIRE).reshape(many, *piece)
-    received += [exchanged(kept[i], s) for i, s in enumerate(through)]
+    received += [exchanged(kept[i], through[i]) for i in reversed(range(many))]
     totals = functools.reduce(jnp.add, [p.astype(f32) for p in received], own)
     link_residual, signal = kernel_call(
         functools.partial(signal_kernel, days),
@@ -515,14 +467,12 @@
     both, signal = lax.optimization_barrier((both, signal))
     rows = [shape((paths * days * span, width), f32)]
     (total,) = kernel_call(
-        functools.partial(backward_local_kernel, days, t),
-        (table,),
-        (signal, local_mats),
+        functools.partial(backward_local_kernel, days),
+        local_index,
+        (signal, local_blocks),
         rows,
     )
     passed = exchanged(both, 1)
-    late = many + 1
-
     def weigh(first):
         if first == 0:
             return None
@@ -530,20 +480,20 @@
             flops=2_000_000_000, transcendentals=0, bytes_accessed=6_000_000
         )
 
-    for first, end, signals in (
-        (late, len(order), [*arrived[late:], *arrived[:many]]),
-        (0, late, [passed, arrived[many]]),
+    edge = shape((paths * days, HALO, width), f32)
+    for first, end, signals, made in (
+        (many, len(order), [*arrived[many:], *arrived[:many]], rows),
+        (0, many, [passed], [*rows, edge]),
     ):
-        (total,) = kernel_call(
+        total, *early = kernel_call(
             functools.partial(backward_remote_kernel, days, cap, first, end, links, t),
             (table,),
             (remote_mats, total, *signals),
-            rows,
+            made,
             [pltpu.VMEM(slots_shape, jnp.bfloat16)],
             weigh(first),
         )
-    early = total.reshape(paths * days, span, width)[:, :HALO]
-    spill = passed_along(early, "tm", -1)
+    spill = passed_along(early[0], "tm", -1)
     gradient, new_flows = kernel_call(
         functools.partial(finish_kernel, days),
         (),

time: 56.7 us -> 54.7 us (0.965)
  waiting for transfers between devices: 15.8 us -> 14.3 us
  Pallas kernels: 15.9 us -> 15.2 us
    ppermute x12, waiting for transfers between devices: 12.4 us -> 11 us  [exchanged(): return lax.ppermute(part, 'corr', [(i, i ^ s) for i in range(corridors)])]
    pallas_call x1, Pallas kernels: 2.95 us -> 2.24 us  [per_device_dense(): pl.pallas_call(functools.partial(prepare_kernel, cap, order, t, days * sp...]
  transfers between devices with their start and end apart: 14 -> 14, of which waited for: 8 -> 8; matrix products, arithmetic and copies ran while one was open for 0% -> 0% of each run, Pallas kernels for 18% -> 17%
where the time goes in v3:
time: 54.7 us; the launch traced here: 54.5 us
  starting transfers between devices  23.8 us (44%)
  Pallas kernels  15.2 us (28%)
  waiting for transfers between devices  14.3 us (26%)
  between operations  0.84 us (2%)
    ppermute x12, starting transfers between devices, exchanged(): return lax.ppermute(part, 'corr', [(i, i ^ s) for i in range(corridors)])  16.2 us
    pallas_call x7, Pallas kernels, kernel_call(): pl.pallas_call(body, out_shape=out_shape, in_specs=[SMEM] * len(scalars)...  13 us
    ppermute x12, waiting for transfers between devices, exchanged(): return lax.ppermute(part, 'corr', [(i, i ^ s) for i in range(corridors)])  11 us
    ppermute x2, starting transfers between devices, passed_along(): return lax.ppermute(block, axis, route)  7.6 us
    ppermute x2, waiting for transfers between devices, passed_along(): return lax.ppermute(block, axis, route)  3.35 us
    pallas_call x1, Pallas kernels, per_device_dense(): pl.pallas_call(functools.partial(prepare_kernel, cap, order, t, days * sp...  2.24 us
  transfers between devices with their start and end apart: 14, of which 8 were waited for; matrix products, arithmetic and copies ran while one was open for 0% of the time, Pallas kernels for 17%

profile of v3, /device:TPU:1, one launch (start us, length us, event | category | flops | bytes accessed | tf_op | source)
XLA Modules:
  0.0 54.5 jit_solution(4267321648102387460)
XLA Ops:
  0.6 0.0 copy-start.1
  0.6 4.7 %collective-permute-start = (bf16[2,24,1024]{2,1,0:T(8,128)(2,1)}, bf16[2,24,1024]{2,1,0:T(8,128)(2,1)S(1)}, u32[]{:S(2)}, u32[]{:S(2)}) collective-permute-start(bf16[2,24,1024]{2,1,0:T(8,128)(2,1)} %flows.5), channel_id=1, source_target_pairs={{0,1},{1,2},{2,3},{4,5},{5,6},{6,7},{8,9},{9,10},{10,11},{12,13},{... | collective-permute-start | bytes 294920 | tf_op jit(solution)/shard_map/ppermute | solution.py:19
  5.3 2.2 %shard_map.131 = (s32[215]{0:T(256)S(1)}, bf16[64,128,128]{2,1,0:T(8,128)(2,1)S(1)}) custom-call(s32[1]{0:T(128)} %bitcast.me, s32[64]{0:T(128)} %rest_0_.1, s32[64]{0:T(128)} %rest_1_.1, s32[64]{0:T(128)} %rest_2_.1, s32[64]{0:T(128)} %rest_3_.1, bf16[64,128,128]{2,1,0:T(8,128)(2,1)} %rest_4_.1), custom_call_target="tpu_custom_call" | custom-call | tf_op jit(solution)/shard_map/pallas_call | solution.py:423
  7.6 0.0 collective-permute-done.before
  7.6 0.0 copy-done.1
  7.6 0.0 copy-start
  7.6 0.0 copy-start.3
  7.6 0.0 copy-start.4
  7.6 0.0 copy-start.5
  7.6 3.1 %shard_map.132 = (f32[16,48,128]{2,1,0:T(8,128)S(1)}, f32[8,48,128]{2,1,0:T(8,128)S(1)}, f32[8,48,128]{2,1,0:T(8,128)S(1)}, f32[8,48,128]{2,1,0:T(8,128)S(1)}, f32[16,48,128]{2,1,0:T(8,128)S(1)}) custom-call(s32[215]{0:T(256)S(1)} %get-tuple-element.18.table, bf16[2,24,1024]{2,1,0:T(8,128)(2,1)S(1)} %copy-done.1, ...), custom_call_target="tpu_custom_call" | custom-call | tf_op jit(solution)/shard_map/pallas_call | solution.py:375
  10.8 1.3 %collective-permute-start.4 = (f16[16,48,128]{2,1,0:T(8,128)(2,1)S(1)}, f16[16,48,128]{2,1,0:T(8,128)(2,1)S(1)}, u32[]{:S(2)}, u32[]{:S(2)}) collective-permute-start(f16[16,48,128]{2,1,0:T(8,128)(2,1)S(1)} %convert_element_type.39), channel_id=1, source_target_pairs={{0,4},{4,0},{8,12},{12,8},{16,20},{20,16},{24,28},{28,24},{1,5},{5... | collective-permute-start | bytes 589832 | tf_op jit(solution)/shard_map/ppermute | solution.py:437
  12.2 2.4 %collective-permute-start.3 = (f16[8,48,128]{2,1,0:T(8,128)(2,1)S(1)}, f16[8,48,128]{2,1,0:T(8,128)(2,1)S(1)}, u32[]{:S(2)}, u32[]{:S(2)}) collective-permute-start(f16[8,48,128]{2,1,0:T(8,128)(2,1)S(1)} %convert_element_type.37), channel_id=1, source_target_pairs={{0,16},{4,20},{8,24},{12,28},{16,0},{20,4},{24,8},{28,12},{1,17},{... | collective-permute-start | bytes 294920 | tf_op jit(solution)/shard_map/ppermute | solution.py:437
  14.6 0.1 collective-permute-start.2
  14.6 1.2 %collective-permute-start.1 = (f16[8,48,128]{2,1,0:T(8,128)(2,1)S(1)}, f16[8,48,128]{2,1,0:T(8,128)(2,1)S(1)}, u32[]{:S(2)}, u32[]{:S(2)}) collective-permute-start(f16[8,48,128]{2,1,0:T(8,128)(2,1)S(1)} %convert_element_type.33), channel_id=1, source_target_pairs={{0,4},{4,0},{8,12},{12,8},{16,20},{20,16},{24,28},{28,24},{1,5},{5... | collective-permute-start | bytes 294920 | tf_op jit(solution)/shard_map/ppermute | solution.py:437
  15.8 0.7 %collective-permute-done.4 = f16[16,48,128]{2,1,0:T(8,128)(2,1)S(1)} collective-permute-done((f16[16,48,128]{2,1,0:T(8,128)(2,1)S(1)}, f16[16,48,128]{2,1,0:T(8,128)(2,1)S(1)}, u32[]{:S(2)}, u32[]{:S(2)}) %collective-permute-start.4) | collective-permute-done | bytes 196640 | tf_op jit(solution)/shard_map/ppermute | solution.py:437
  16.5 0.0 copy-start.2
  16.5 0.1 add_convert_fusion
  16.6 3.9 %collective-permute-start.5 = (f16[8,48,128]{2,1,0:T(8,128)(2,1)S(1)}, f16[8,48,128]{2,1,0:T(8,128)(2,1)S(1)}, u32[]{:S(2)}, u32[]{:S(2)}) collective-permute-start(f16[8,48,128]{2,1,0:T(8,128)(2,1)S(1)} %get-tuple-element.33), channel_id=1, source_target_pairs={{0,24},{4,28},{8,16},{12,20},{16,8},{20,12},{24,0},{28,4},{1,25},{... | collective-permute-start | bytes 294920 | tf_op jit(solution)/shard_map/ppermute | solution.py:437
  20.5 0.0 collective-permute-start.6
  20.5 0.0 copy-done
  20.5 0.0 copy-done.3
  20.5 0.0 copy-done.4
  20.5 0.0 copy-done.5
  20.5 2.9 %shard_map.130 = f32[8,48,128]{2,1,0:T(8,128)S(1)} custom-call(s32[64]{0:T(128)S(1)} %copy-done.3, s32[64]{0:T(128)S(1)} %copy-done.4, s32[64]{0:T(128)S(1)} %copy-done.5, bf16[2,24,1024]{2,1,0:T(8,128)(2,1)S(1)} %copy-done.1, bf16[2,24,1024]{2,1,0:T(8,128)(2,1)S(1)} %collective-permute-done.before, bf16[64,128,128]{2,1,0:T(8,128)(2,1)S(1)} %copy-done), custom_call_target="tpu_custom_call" | custom-call | tf_op jit(solution)/shard_map/pallas_call | solution.py:375
  23.5 0.7 %collective-permute-done.3 = f16[8,48,128]{2,1,0:T(8,128)(2,1)S(1)} collective-permute-done((f16[8,48,128]{2,1,0:T(8,128)(2,1)S(1)}, f16[8,48,128]{2,1,0:T(8,128)(2,1)S(1)}, u32[]{:S(2)}, u32[]{:S(2)}) %collective-permute-start.3) | collective-permute-done | bytes 98336 | tf_op jit(solution)/shard_map/ppermute | solution.py:437
  24.2 1.3 %collective-permute-done.2 = f16[8,48,128]{2,1,0:T(8,128)(2,1)S(1)} collective-permute-done((f16[8,48,128]{2,1,0:T(8,128)(2,1)S(1)}, f16[8,48,128]{2,1,0:T(8,128)(2,1)S(1)}, u32[]{:S(2)}, u32[]{:S(2)}) %collective-permute-start.2) | collective-permute-done | bytes 98336 | tf_op jit(solution)/shard_map/ppermute | solution.py:437
  25.5 0.0 collective-permute-done.1
  25.5 0.0 collective-permute-done.5
  25.5 2.4 %collective-permute-done.6 = f16[8,48,128]{2,1,0:T(8,128)(2,1)S(1)} collective-permute-done((f16[8,48,128]{2,1,0:T(8,128)(2,1)S(1)}, f16[8,48,128]{2,1,0:T(8,128)(2,1)S(1)}, u32[]{:S(2)}, u32[]{:S(2)}) %collective-permute-start.6) | collective-permute-done | bytes 98336 | tf_op jit(solution)/shard_map/ppermute | solution.py:437
  27.9 0.1 convert_add_fusion.totals
  28.0 0.0 copy-done.2
  28.0 0.7 %shard_map.133 = (f32[2,24,1024]{2,1,0:T(8,128)}, bf16[8,48,128]{2,1,0:T(8,128)(2,1)S(1)}) custom-call(f32[8,48,128]{2,1,0:T(8,128)S(1)} %convert_add_fusion.totals, f32[2,24,1024]{2,1,0:T(8,128)S(1)} %copy-done.2), custom_call_target="tpu_custom_call" | custom-call | tf_op jit(solution)/shard_map/pallas_call | solution.py:375
  28.7 3.2 %collective-permute-start.8 = (bf16[8,48,128]{2,1,0:T(8,128)(2,1)S(1)}, bf16[8,48,128]{2,1,0:T(8,128)(2,1)S(1)}, u32[]{:S(2)}, u32[]{:S(2)}) collective-permute-start(bf16[8,48,128]{2,1,0:T(8,128)(2,1)S(1)} %get-tuple-element.27.signal), channel_id=1, source_target_pairs={{0,24},{4,28},{8,16},{12,20},{16,8},{20,12},{24,0},{28,4},{1,25},{... | collective-permute-start | bytes 294920 | tf_op jit(solution)/shard_map/ppermute | solution.py:437
  32.0 0.0 collective-permute-start.7
  32.0 0.3 collective-permute-start.11
  32.3 2.0 %collective-permute-start.10 = (bf16[8,48,128]{2,1,0:T(8,128)(2,1)S(1)}, bf16[8,48,128]{2,1,0:T(8,128)(2,1)S(1)}, u32[]{:S(2)}, u32[]{:S(2)}) collective-permute-start(bf16[8,48,128]{2,1,0:T(8,128)(2,1)S(1)} %get-tuple-element.27.signal), channel_id=1, source_target_pairs={{0,20},{4,16},{8,28},{12,24},{16,4},{20,0},{24,12},{28,8},{1,21},{... | collective-permute-start | bytes 294920 | tf_op jit(solution)/shard_map/ppermute | solution.py:437
  34.3 1.2 %collective-permute-start.9 = (bf16[8,48,128]{2,1,0:T(8,128)(2,1)S(1)}, bf16[8,48,128]{2,1,0:T(8,128)(2,1)S(1)}, u32[]{:S(2)}, u32[]{:S(2)}) collective-permute-start(bf16[8,48,128]{2,1,0:T(8,128)(2,1)S(1)} %get-tuple-element.27.signal), channel_id=1, source_target_pairs={{0,4},{4,0},{8,12},{12,8},{16,20},{20,16},{24,28},{28,24},{1,5},{5... | collective-permute-start | bytes 294920 | tf_op jit(solution)/shard_map/ppermute | solution.py:437
  35.5 0.0 collective-permute-done.8.rest_4_
  35.5 2.2 %collective-permute-done.7.rest_3_ = bf16[8,48,128]{2,1,0:T(8,128)(2,1)S(1)} collective-permute-done((bf16[8,48,128]{2,1,0:T(8,128)(2,1)S(1)}, bf16[8,48,128]{2,1,0:T(8,128)(2,1)S(1)}, u32[]{:S(2)}, u32[]{:S(2)}) %collective-permute-start.7) | collective-permute-done | bytes 98336 | tf_op jit(solution)/shard_map/ppermute | solution.py:437
  37.7 0.6 %collective-permute-start.12 = (bf16[16,48,128]{2,1,0:T(8,128)(2,1)S(1)}, bf16[16,48,128]{2,1,0:T(8,128)(2,1)S(1)}, u32[]{:S(2)}, u32[]{:S(2)}) collective-permute-start(bf16[16,48,128]{2,1,0:T(8,128)(2,1)S(1)} %pad_maximum_fusion), channel_id=1, source_target_pairs={{0,4},{4,0},{8,12},{12,8},{16,20},{20,16},{24,28},{28,24},{1,5},{5... | collective-permute-start | bytes 589832 | tf_op jit(solution)/shard_map/ppermute | solution.py:437
  38.3 2.4 %shard_map.134.start = f32[640,128]{1,0:T(8,128)S(1)} custom-call(s32[64]{0:T(128)S(1)} %copy-done.3, s32[64]{0:T(128)S(1)} %copy-done.4, s32[64]{0:T(128)S(1)} %copy-done.5, bf16[8,48,128]{2,1,0:T(8,128)(2,1)S(1)} %get-tuple-element.27.signal, bf16[64,128,128]{2,1,0:T(8,128)(2,1)S(1)} %copy-done), custom_call_target="tpu_custom_call" | custom-call | tf_op jit(solution)/shard_map/pallas_call | solution.py:375
  40.7 1.6 %collective-permute-done.11.rest_2_ = bf16[8,48,128]{2,1,0:T(8,128)(2,1)S(1)} collective-permute-done((bf16[8,48,128]{2,1,0:T(8,128)(2,1)S(1)}, bf16[8,48,128]{2,1,0:T(8,128)(2,1)S(1)}, u32[]{:S(2)}, u32[]{:S(2)}) %collective-permute-start.11) | collective-permute-done | bytes 98336 | tf_op jit(solution)/shard_map/ppermute | solution.py:437
  42.3 2.1 %collective-permute-done.10.rest_1_ = bf16[8,48,128]{2,1,0:T(8,128)(2,1)S(1)} collective-permute-done((bf16[8,48,128]{2,1,0:T(8,128)(2,1)S(1)}, bf16[8,48,128]{2,1,0:T(8,128)(2,1)S(1)}, u32[]{:S(2)}, u32[]{:S(2)}) %collective-permute-start.10) | collective-permute-done | bytes 98336 | tf_op jit(solution)/shard_map/ppermute | solution.py:437
  44.4 0.0 collective-permute-done.9.rest_0_
  44.4 1.9 %shard_map.135.start = f32[640,128]{1,0:T(8,128)S(1)} custom-call(s32[215]{0:T(256)S(1)} %get-tuple-element.18.table, bf16[64,128,128]{2,1,0:T(8,128)(2,1)S(1)} %get-tuple-element.19.mats, f32[640,128]{1,0:T(8,128)S(1)} %shard_map.134.start, bf16[8,48,128]{2,1,0:T(8,128)(2,1)S(1)} %collective-permute-done.9.rest_0_, ...), custom_call_target="tpu_custom_call" | custom-call | flops 2000000000 | bytes 6000000 | tf_op jit(solution)/shard_map/pallas_call | solution.py:375
  46.3 0.0 collective-permute-done.12.rest_0_
  46.3 1.1 %shard_map.136 = (f32[640,128]{1,0:T(8,128)S(1)}, f32[16,16,128]{2,1,0:T(8,128)S(1)}) custom-call(s32[215]{0:T(256)S(1)} %get-tuple-element.18.table, bf16[64,128,128]{2,1,0:T(8,128)(2,1)S(1)} %get-tuple-element.19.mats, f32[640,128]{1,0:T(8,128)S(1)} %shard_map.135.start, bf16[16,48,128]{2,1,0:T(8,128)(2,1)S(1)} %collective-permute-done.12.rest_0_), custom_call_target="tpu_custom_call" | custom-call | tf_op jit(solution)/shard_map/pallas_call | solution.py:375
  47.4 2.9 %collective-permute-start.13 = (f32[16,16,128]{2,1,0:T(8,128)S(1)}, f32[16,16,128]{2,1,0:T(8,128)S(1)}, u32[]{:S(2)}, u32[]{:S(2)}) collective-permute-start(f32[16,16,128]{2,1,0:T(8,128)S(1)} %get-tuple-element.30), channel_id=1, source_target_pairs={{1,0},{2,1},{3,2},{5,4},{6,5},{7,6},{9,8},{10,9},{11,10},{13,12},{... | collective-permute-start | bytes 393224 | tf_op jit(solution)/shard_map/ppermute | solution.py:19
  50.3 3.4 %collective-permute-done.13.spill = f32[16,16,128]{2,1,0:T(8,128)S(1)} collective-permute-done((f32[16,16,128]{2,1,0:T(8,128)S(1)}, f32[16,16,128]{2,1,0:T(8,128)S(1)}, u32[]{:S(2)}, u32[]{:S(2)}) %collective-permute-start.13) | collective-permute-done | bytes 131104 | tf_op jit(solution)/shard_map/ppermute | solution.py:19
  53.7 0.8 %shard_map.137 = (f32[2,24,1024]{2,1,0:T(8,128)}, f32[2,24,1024]{2,1,0:T(8,128)}) custom-call(f32[640,128]{1,0:T(8,128)S(1)} %get-tuple-element.29.total, f32[16,16,128]{2,1,0:T(8,128)S(1)} %collective-permute-done.13.spill, bf16[2,24,1024]{2,1,0:T(8,128)(2,1)S(1)} %copy-done.1), custom_call_target="tpu_custom_call" | custom-call | tf_op jit(solution)/shard_map/pallas_call | solution.py:375
  (6 shorter events, 0.1 us)
Async XLA Ops:
  0.6 7.0 %copy-start.1 = (bf16[2,24,1024]{2,1,0:T(8,128)(2,1)S(1)}, bf16[2,24,1024]{2,1,0:T(8,128)(2,1)}, u32[]{:S(2)}) copy-start(bf16[2,24,1024]{2,1,0:T(8,128)(2,1)} %flows.5) | copy-start | bytes 294916
  0.6 6.9 %collective-permute-start = (bf16[2,24,1024]{2,1,0:T(8,128)(2,1)}, bf16[2,24,1024]{2,1,0:T(8,128)(2,1)S(1)}, u32[]{:S(2)}, u32[]{:S(2)}) collective-permute-start(bf16[2,24,1024]{2,1,0:T(8,128)(2,1)} %flows.5), channel_id=1, source_target_pairs={{0,1},{1,2},{2,3},{4,5},{5,6},{6,7},{8,9},{9,10},{10,11},{12,13},{... | collective-permute-start | bytes 294920 | tf_op jit(solution)/shard_map/ppermute | solution.py:19
  7.6 12.9 %copy-start = (bf16[64,128,128]{2,1,0:T(8,128)(2,1)S(1)}, bf16[64,128,128]{2,1,0:T(8,128)(2,1)}, u32[]{:S(2)}) copy-start(bf16[64,128,128]{2,1,0:T(8,128)(2,1)} %mats.3) | copy-start | bytes 6291460
  7.6 12.9 %copy-start.3 = (s32[64]{0:T(128)S(1)}, s32[64]{0:T(128)}, u32[]{:S(2)}) copy-start(s32[64]{0:T(128)} %path.3) | copy-start | bytes 772
  7.6 12.9 %copy-start.4 = (s32[64]{0:T(128)S(1)}, s32[64]{0:T(128)}, u32[]{:S(2)}) copy-start(s32[64]{0:T(128)} %link.3) | copy-start | bytes 772
  7.6 12.9 %copy-start.5 = (s32[64]{0:T(128)S(1)}, s32[64]{0:T(128)}, u32[]{:S(2)}) copy-start(s32[64]{0:T(128)} %lag.3) | copy-start | bytes 772
  10.8 5.6 %collective-permute-start.4 = (f16[16,48,128]{2,1,0:T(8,128)(2,1)S(1)}, f16[16,48,128]{2,1,0:T(8,128)(2,1)S(1)}, u32[]{:S(2)}, u32[]{:S(2)}) collective-permute-start(f16[16,48,128]{2,1,0:T(8,128)(2,1)S(1)} %convert_element_type.39), channel_id=1, source_target_pairs={{0,4},{4,0},{8,12},{12,8},{16,20},{20,16},{24,28},{28,24},{1,5},{5... | collective-permute-start | bytes 589832 | tf_op jit(solution)/shard_map/ppermute | solution.py:437
  12.2 12.0 %collective-permute-start.3 = (f16[8,48,128]{2,1,0:T(8,128)(2,1)S(1)}, f16[8,48,128]{2,1,0:T(8,128)(2,1)S(1)}, u32[]{:S(2)}, u32[]{:S(2)}) collective-permute-start(f16[8,48,128]{2,1,0:T(8,128)(2,1)S(1)} %convert_element_type.37), channel_id=1, source_target_pairs={{0,16},{4,20},{8,24},{12,28},{16,0},{20,4},{24,8},{28,12},{1,17},{... | collective-permute-start | bytes 294920 | tf_op jit(solution)/shard_map/ppermute | solution.py:437
  14.6 10.9 %collective-permute-start.2 = (f16[8,48,128]{2,1,0:T(8,128)(2,1)S(1)}, f16[8,48,128]{2,1,0:T(8,128)(2,1)S(1)}, u32[]{:S(2)}, u32[]{:S(2)}) collective-permute-start(f16[8,48,128]{2,1,0:T(8,128)(2,1)S(1)} %convert_element_type.35), channel_id=1, source_target_pairs={{0,20},{4,16},{8,28},{12,24},{16,4},{20,0},{24,12},{28,8},{1,21},{... | collective-permute-start | bytes 294920 | tf_op jit(solution)/shard_map/ppermute | solution.py:437
  14.6 10.9 %collective-permute-start.1 = (f16[8,48,128]{2,1,0:T(8,128)(2,1)S(1)}, f16[8,48,128]{2,1,0:T(8,128)(2,1)S(1)}, u32[]{:S(2)}, u32[]{:S(2)}) collective-permute-start(f16[8,48,128]{2,1,0:T(8,128)(2,1)S(1)} %convert_element_type.33), channel_id=1, source_target_pairs={{0,4},{4,0},{8,12},{12,8},{16,20},{20,16},{24,28},{28,24},{1,5},{5... | collective-permute-start | bytes 294920 | tf_op jit(solution)/shard_map/ppermute | solution.py:437
  16.5 11.5 %copy-start.2 = (f32[2,24,1024]{2,1,0:T(8,128)S(1)}, f32[2,24,1024]{2,1,0:T(8,128)}, u32[]{:S(2)}) copy-start(f32[2,24,1024]{2,1,0:T(8,128)} %counts.1) | copy-start | bytes 589828
  16.6 8.9 %collective-permute-start.5 = (f16[8,48,128]{2,1,0:T(8,128)(2,1)S(1)}, f16[8,48,128]{2,1,0:T(8,128)(2,1)S(1)}, u32[]{:S(2)}, u32[]{:S(2)}) collective-permute-start(f16[8,48,128]{2,1,0:T(8,128)(2,1)S(1)} %get-tuple-element.33), channel_id=1, source_target_pairs={{0,24},{4,28},{8,16},{12,20},{16,8},{20,12},{24,0},{28,4},{1,25},{... | collective-permute-start | bytes 294920 | tf_op jit(solution)/shard_map/ppermute | solution.py:437
  20.5 7.4 %collective-permute-start.6 = (f16[8,48,128]{2,1,0:T(8,128)(2,1)S(1)}, f16[8,48,128]{2,1,0:T(8,128)(2,1)S(1)}, u32[]{:S(2)}, u32[]{:S(2)}) collective-permute-start(f16[8,48,128]{2,1,0:T(8,128)(2,1)S(1)} %get-tuple-element.34), channel_id=1, source_target_pairs={{0,8},{4,12},{8,0},{12,4},{16,24},{20,28},{24,16},{28,20},{1,9},{5... | collective-permute-start | bytes 294920 | tf_op jit(solution)/shard_map/ppermute | solution.py:437
  28.7 6.8 %collective-permute-start.8 = (bf16[8,48,128]{2,1,0:T(8,128)(2,1)S(1)}, bf16[8,48,128]{2,1,0:T(8,128)(2,1)S(1)}, u32[]{:S(2)}, u32[]{:S(2)}) collective-permute-start(bf16[8,48,128]{2,1,0:T(8,128)(2,1)S(1)} %get-tuple-element.27.signal), channel_id=1, source_target_pairs={{0,24},{4,28},{8,16},{12,20},{16,8},{20,12},{24,0},{28,4},{1,25},{... | collective-permute-start | bytes 294920 | tf_op jit(solution)/shard_map/ppermute | solution.py:437
  32.0 5.8 %collective-permute-start.7 = (bf16[8,48,128]{2,1,0:T(8,128)(2,1)S(1)}, bf16[8,48,128]{2,1,0:T(8,128)(2,1)S(1)}, u32[]{:S(2)}, u32[]{:S(2)}) collective-permute-start(bf16[8,48,128]{2,1,0:T(8,128)(2,1)S(1)} %get-tuple-element.27.signal), channel_id=1, source_target_pairs={{0,8},{4,12},{8,0},{12,4},{16,24},{20,28},{24,16},{28,20},{1,9},{5... | collective-permute-start | bytes 294920 | tf_op jit(solution)/shard_map/ppermute | solution.py:437
  32.0 10.4 %collective-permute-start.11 = (bf16[8,48,128]{2,1,0:T(8,128)(2,1)S(1)}, bf16[8,48,128]{2,1,0:T(8,128)(2,1)S(1)}, u32[]{:S(2)}, u32[]{:S(2)}) collective-permute-start(bf16[8,48,128]{2,1,0:T(8,128)(2,1)S(1)} %get-tuple-element.27.signal), channel_id=1, source_target_pairs={{0,16},{4,20},{8,24},{12,28},{16,0},{20,4},{24,8},{28,12},{1,17},{... | collective-permute-start | bytes 294920 | tf_op jit(solution)/shard_map/ppermute | solution.py:437
  32.3 12.1 %collective-permute-start.10 = (bf16[8,48,128]{2,1,0:T(8,128)(2,1)S(1)}, bf16[8,48,128]{2,1,0:T(8,128)(2,1)S(1)}, u32[]{:S(2)}, u32[]{:S(2)}) collective-permute-start(bf16[8,48,128]{2,1,0:T(8,128)(2,1)S(1)} %get-tuple-element.27.signal), channel_id=1, source_target_pairs={{0,20},{4,16},{8,28},{12,24},{16,4},{20,0},{24,12},{28,8},{1,21},{... | collective-permute-start | bytes 294920 | tf_op jit(solution)/shard_map/ppermute | solution.py:437
  34.3 10.1 %collective-permute-start.9 = (bf16[8,48,128]{2,1,0:T(8,128)(2,1)S(1)}, bf16[8,48,128]{2,1,0:T(8,128)(2,1)S(1)}, u32[]{:S(2)}, u32[]{:S(2)}) collective-permute-start(bf16[8,48,128]{2,1,0:T(8,128)(2,1)S(1)} %get-tuple-element.27.signal), channel_id=1, source_target_pairs={{0,4},{4,0},{8,12},{12,8},{16,20},{20,16},{24,28},{28,24},{1,5},{5... | collective-permute-start | bytes 294920 | tf_op jit(solution)/shard_map/ppermute | solution.py:437
  37.7 8.5 %collective-permute-start.12 = (bf16[16,48,128]{2,1,0:T(8,128)(2,1)S(1)}, bf16[16,48,128]{2,1,0:T(8,128)(2,1)S(1)}, u32[]{:S(2)}, u32[]{:S(2)}) collective-permute-start(bf16[16,48,128]{2,1,0:T(8,128)(2,1)S(1)} %pad_maximum_fusion), channel_id=1, source_target_pairs={{0,4},{4,0},{8,12},{12,8},{16,20},{20,16},{24,28},{28,24},{1,5},{5... | collective-permute-start | bytes 589832 | tf_op jit(solution)/shard_map/ppermute | solution.py:437
  47.4 6.3 %collective-permute-start.13 = (f32[16,16,128]{2,1,0:T(8,128)S(1)}, f32[16,16,128]{2,1,0:T(8,128)S(1)}, u32[]{:S(2)}, u32[]{:S(2)}) collective-permute-start(f32[16,16,128]{2,1,0:T(8,128)S(1)} %get-tuple-element.30), channel_id=1, source_target_pairs={{1,0},{2,1},{3,2},{5,4},{6,5},{7,6},{9,8},{10,9},{11,10},{13,12},{... | collective-permute-start | bytes 393224 | tf_op jit(solution)/shard_map/ppermute | solution.py:19

commit v4 on v3

--- a/solution.py
+++ b/solution.py
@@ -454,7 +454,7 @@
         [wide],
     )
     kept = (kept + crossed.astype(f32)).astype(WIRE).reshape(many, *piece)
-    received += [exchanged(kept[i], through[i]) for i in reversed(range(many))]
+    received += [exchanged(kept[i], s) for i, s in enumerate(through)]
     totals = functools.reduce(jnp.add, [p.astype(f32) for p in received], own)
     link_residual, signal = kernel_call(
         functools.partial(signal_kernel, days),

time: 54.7 us -> 54.7 us (level)
  starting transfers between devices: 23.8 us -> 25.8 us
  waiting for transfers between devices: 14.3 us -> 12.3 us
    ppermute x12, waiting for transfers between devices: 11 us -> 9.28 us  [exchanged(): return lax.ppermute(part, 'corr', [(i, i ^ s) for i in range(corridors)])]
    ppermute x12, starting transfers between devices: 16.2 us -> 17.8 us  [exchanged(): return lax.ppermute(part, 'corr', [(i, i ^ s) for i in range(corridors)])]
  transfers between devices with their start and end apart: 14 -> 14, of which waited for: 8 -> 6; matrix products, arithmetic and copies ran while one was open for 0% -> 0% of each run, Pallas kernels for 17% -> 17%
where the time goes in v4:
time: 54.7 us; the launch traced here: 54.5 us
  starting transfers between devices  25.8 us (47%)
  Pallas kernels  15.2 us (28%)
  waiting for transfers between devices  12.3 us (22%)
  between operations  0.85 us (2%)
    ppermute x12, starting transfers between devices, exchanged(): return lax.ppermute(part, 'corr', [(i, i ^ s) for i in range(corridors)])  17.8 us
    pallas_call x7, Pallas kernels, kernel_call(): pl.pallas_call(body, out_shape=out_shape, in_specs=[SMEM] * len(scalars)...  13 us
    ppermute x12, waiting for transfers between devices, exchanged(): return lax.ppermute(part, 'corr', [(i, i ^ s) for i in range(corridors)])  9.28 us
    ppermute x2, starting transfers between devices, passed_along(): return lax.ppermute(block, axis, route)  7.92 us
    ppermute x2, waiting for transfers between devices, passed_along(): return lax.ppermute(block, axis, route)  3.03 us
    pallas_call x1, Pallas kernels, per_device_dense(): pl.pallas_call(functools.partial(prepare_kernel, cap, order, t, days * sp...  2.24 us
  transfers between devices with their start and end apart: 14, of which 6 were waited for; matrix products, arithmetic and copies ran while one was open for 0% of the time, Pallas kernels for 17%

profile of v4, /device:TPU:1, one launch (start us, length us, event | category | flops | bytes accessed | tf_op | source)
XLA Modules:
  0.0 54.5 jit_solution(12096750400555116335)
XLA Ops:
  0.6 0.0 copy-start.1
  0.6 4.7 %collective-permute-start = (bf16[2,24,1024]{2,1,0:T(8,128)(2,1)}, bf16[2,24,1024]{2,1,0:T(8,128)(2,1)S(1)}, u32[]{:S(2)}, u32[]{:S(2)}) collective-permute-start(bf16[2,24,1024]{2,1,0:T(8,128)(2,1)} %flows.5), channel_id=1, source_target_pairs={{0,1},{1,2},{2,3},{4,5},{5,6},{6,7},{8,9},{9,10},{10,11},{12,13},{... | collective-permute-start | bytes 294920 | tf_op jit(solution)/shard_map/ppermute | solution.py:19
  5.3 2.2 %shard_map.131 = (s32[215]{0:T(256)S(1)}, bf16[64,128,128]{2,1,0:T(8,128)(2,1)S(1)}) custom-call(s32[1]{0:T(128)} %bitcast.me, s32[64]{0:T(128)} %rest_0_.1, s32[64]{0:T(128)} %rest_1_.1, s32[64]{0:T(128)} %rest_2_.1, s32[64]{0:T(128)} %rest_3_.1, bf16[64,128,128]{2,1,0:T(8,128)(2,1)} %rest_4_.1), custom_call_target="tpu_custom_call" | custom-call | tf_op jit(solution)/shard_map/pallas_call | solution.py:423
  7.6 0.0 collective-permute-done.before
  7.6 0.0 copy-done.1
  7.6 0.0 copy-start
  7.6 0.0 copy-start.3
  7.6 0.0 copy-start.4
  7.6 0.0 copy-start.5
  7.6 3.2 %shard_map.132 = (f32[16,48,128]{2,1,0:T(8,128)S(1)}, f32[8,48,128]{2,1,0:T(8,128)S(1)}, f32[8,48,128]{2,1,0:T(8,128)S(1)}, f32[8,48,128]{2,1,0:T(8,128)S(1)}, f32[16,48,128]{2,1,0:T(8,128)S(1)}) custom-call(s32[215]{0:T(256)S(1)} %get-tuple-element.18.table, bf16[2,24,1024]{2,1,0:T(8,128)(2,1)S(1)} %copy-done.1, ...), custom_call_target="tpu_custom_call" | custom-call | tf_op jit(solution)/shard_map/pallas_call | solution.py:375
  10.8 1.3 %collective-permute-start.4 = (f16[16,48,128]{2,1,0:T(8,128)(2,1)S(1)}, f16[16,48,128]{2,1,0:T(8,128)(2,1)S(1)}, u32[]{:S(2)}, u32[]{:S(2)}) collective-permute-start(f16[16,48,128]{2,1,0:T(8,128)(2,1)S(1)} %convert_element_type.39), channel_id=1, source_target_pairs={{0,4},{4,0},{8,12},{12,8},{16,20},{20,16},{24,28},{28,24},{1,5},{5... | collective-permute-start | bytes 589832 | tf_op jit(solution)/shard_map/ppermute | solution.py:437
  12.2 2.4 %collective-permute-start.3 = (f16[8,48,128]{2,1,0:T(8,128)(2,1)S(1)}, f16[8,48,128]{2,1,0:T(8,128)(2,1)S(1)}, u32[]{:S(2)}, u32[]{:S(2)}) collective-permute-start(f16[8,48,128]{2,1,0:T(8,128)(2,1)S(1)} %convert_element_type.37), channel_id=1, source_target_pairs={{0,16},{4,20},{8,24},{12,28},{16,0},{20,4},{24,8},{28,12},{1,17},{... | collective-permute-start | bytes 294920 | tf_op jit(solution)/shard_map/ppermute | solution.py:437
  14.6 0.0 collective-permute-start.2
  14.6 1.2 %collective-permute-start.1 = (f16[8,48,128]{2,1,0:T(8,128)(2,1)S(1)}, f16[8,48,128]{2,1,0:T(8,128)(2,1)S(1)}, u32[]{:S(2)}, u32[]{:S(2)}) collective-permute-start(f16[8,48,128]{2,1,0:T(8,128)(2,1)S(1)} %convert_element_type.33), channel_id=1, source_target_pairs={{0,4},{4,0},{8,12},{12,8},{16,20},{20,16},{24,28},{28,24},{1,5},{5... | collective-permute-start | bytes 294920 | tf_op jit(solution)/shard_map/ppermute | solution.py:437
  15.8 0.6 %collective-permute-done.4 = f16[16,48,128]{2,1,0:T(8,128)(2,1)S(1)} collective-permute-done((f16[16,48,128]{2,1,0:T(8,128)(2,1)S(1)}, f16[16,48,128]{2,1,0:T(8,128)(2,1)S(1)}, u32[]{:S(2)}, u32[]{:S(2)}) %collective-permute-start.4) | collective-permute-done | bytes 196640 | tf_op jit(solution)/shard_map/ppermute | solution.py:437
  16.5 0.0 copy-start.2
  16.5 0.1 add_convert_fusion
  16.6 1.9 %collective-permute-start.5 = (f16[8,48,128]{2,1,0:T(8,128)(2,1)S(1)}, f16[8,48,128]{2,1,0:T(8,128)(2,1)S(1)}, u32[]{:S(2)}, u32[]{:S(2)}) collective-permute-start(f16[8,48,128]{2,1,0:T(8,128)(2,1)S(1)} %get-tuple-element.33), channel_id=1, source_target_pairs={{0,8},{4,12},{8,0},{12,4},{16,24},{20,28},{24,16},{28,20},{1,9},{5... | collective-permute-start | bytes 294920 | tf_op jit(solution)/shard_map/ppermute | solution.py:437
  18.5 2.2 %collective-permute-start.6 = (f16[8,48,128]{2,1,0:T(8,128)(2,1)S(1)}, f16[8,48,128]{2,1,0:T(8,128)(2,1)S(1)}, u32[]{:S(2)}, u32[]{:S(2)}) collective-permute-start(f16[8,48,128]{2,1,0:T(8,128)(2,1)S(1)} %get-tuple-element.34), channel_id=1, source_target_pairs={{0,24},{4,28},{8,16},{12,20},{16,8},{20,12},{24,0},{28,4},{1,25},{... | collective-permute-start | bytes 294920 | tf_op jit(solution)/shard_map/ppermute | solution.py:437
  20.7 0.0 copy-done
  20.7 0.0 copy-done.3
  20.7 0.0 copy-done.4
  20.7 0.0 copy-done.5
  20.7 2.9 %shard_map.130 = f32[8,48,128]{2,1,0:T(8,128)S(1)} custom-call(s32[64]{0:T(128)S(1)} %copy-done.3, s32[64]{0:T(128)S(1)} %copy-done.4, s32[64]{0:T(128)S(1)} %copy-done.5, bf16[2,24,1024]{2,1,0:T(8,128)(2,1)S(1)} %copy-done.1, bf16[2,24,1024]{2,1,0:T(8,128)(2,1)S(1)} %collective-permute-done.before, bf16[64,128,128]{2,1,0:T(8,128)(2,1)S(1)} %copy-done), custom_call_target="tpu_custom_call" | custom-call | tf_op jit(solution)/shard_map/pallas_call | solution.py:375
  23.6 0.0 collective-permute-done.3
  23.6 0.0 collective-permute-done.2
  23.6 0.0 collective-permute-done.1
  23.7 2.5 %collective-permute-done.5 = f16[8,48,128]{2,1,0:T(8,128)(2,1)S(1)} collective-permute-done((f16[8,48,128]{2,1,0:T(8,128)(2,1)S(1)}, f16[8,48,128]{2,1,0:T(8,128)(2,1)S(1)}, u32[]{:S(2)}, u32[]{:S(2)}) %collective-permute-start.5) | collective-permute-done | bytes 98336 | tf_op jit(solution)/shard_map/ppermute | solution.py:437
  26.2 0.0 collective-permute-done.6
  26.2 0.1 convert_add_fusion.totals
  26.2 0.0 copy-done.2
  26.3 0.7 %shard_map.133 = (f32[2,24,1024]{2,1,0:T(8,128)}, bf16[8,48,128]{2,1,0:T(8,128)(2,1)S(1)}) custom-call(f32[8,48,128]{2,1,0:T(8,128)S(1)} %convert_add_fusion.totals, f32[2,24,1024]{2,1,0:T(8,128)S(1)} %copy-done.2), custom_call_target="tpu_custom_call" | custom-call | tf_op jit(solution)/shard_map/pallas_call | solution.py:375
  27.0 5.0 %collective-permute-start.8 = (bf16[8,48,128]{2,1,0:T(8,128)(2,1)S(1)}, bf16[8,48,128]{2,1,0:T(8,128)(2,1)S(1)}, u32[]{:S(2)}, u32[]{:S(2)}) collective-permute-start(bf16[8,48,128]{2,1,0:T(8,128)(2,1)S(1)} %get-tuple-element.27.signal), channel_id=1, source_target_pairs={{0,24},{4,28},{8,16},{12,20},{16,8},{20,12},{24,0},{28,4},{1,25},{... | collective-permute-start | bytes 294920 | tf_op jit(solution)/shard_map/ppermute | solution.py:437
  32.0 0.0 collective-permute-start.7
  32.0 0.3 collective-permute-start.11
  32.2 2.1 %collective-permute-start.10 = (bf16[8,48,128]{2,1,0:T(8,128)(2,1)S(1)}, bf16[8,48,128]{2,1,0:T(8,128)(2,1)S(1)}, u32[]{:S(2)}, u32[]{:S(2)}) collective-permute-start(bf16[8,48,128]{2,1,0:T(8,128)(2,1)S(1)} %get-tuple-element.27.signal), channel_id=1, source_target_pairs={{0,20},{4,16},{8,28},{12,24},{16,4},{20,0},{24,12},{28,8},{1,21},{... | collective-permute-start | bytes 294920 | tf_op jit(solution)/shard_map/ppermute | solution.py:437
  34.3 1.2 %collective-permute-start.9 = (bf16[8,48,128]{2,1,0:T(8,128)(2,1)S(1)}, bf16[8,48,128]{2,1,0:T(8,128)(2,1)S(1)}, u32[]{:S(2)}, u32[]{:S(2)}) collective-permute-start(bf16[8,48,128]{2,1,0:T(8,128)(2,1)S(1)} %get-tuple-element.27.signal), channel_id=1, source_target_pairs={{0,4},{4,0},{8,12},{12,8},{16,20},{20,16},{24,28},{28,24},{1,5},{5... | collective-permute-start | bytes 294920 | tf_op jit(solution)/shard_map/ppermute | solution.py:437
  35.5 0.0 collective-permute-done.8.rest_4_
  35.5 2.6 %collective-permute-done.7.rest_3_ = bf16[8,48,128]{2,1,0:T(8,128)(2,1)S(1)} collective-permute-done((bf16[8,48,128]{2,1,0:T(8,128)(2,1)S(1)}, bf16[8,48,128]{2,1,0:T(8,128)(2,1)S(1)}, u32[]{:S(2)}, u32[]{:S(2)}) %collective-permute-start.7) | collective-permute-done | bytes 98336 | tf_op jit(solution)/shard_map/ppermute | solution.py:437
  38.1 0.3 collective-permute-start.12
  38.5 2.4 %shard_map.134.start = f32[640,128]{1,0:T(8,128)S(1)} custom-call(s32[64]{0:T(128)S(1)} %copy-done.3, s32[64]{0:T(128)S(1)} %copy-done.4, s32[64]{0:T(128)S(1)} %copy-done.5, bf16[8,48,128]{2,1,0:T(8,128)(2,1)S(1)} %get-tuple-element.27.signal, bf16[64,128,128]{2,1,0:T(8,128)(2,1)S(1)} %copy-done), custom_call_target="tpu_custom_call" | custom-call | tf_op jit(solution)/shard_map/pallas_call | solution.py:375
  40.9 1.4 %collective-permute-done.11.rest_2_ = bf16[8,48,128]{2,1,0:T(8,128)(2,1)S(1)} collective-permute-done((bf16[8,48,128]{2,1,0:T(8,128)(2,1)S(1)}, bf16[8,48,128]{2,1,0:T(8,128)(2,1)S(1)}, u32[]{:S(2)}, u32[]{:S(2)}) %collective-permute-start.11) | collective-permute-done | bytes 98336 | tf_op jit(solution)/shard_map/ppermute | solution.py:437
  42.3 2.1 %collective-permute-done.10.rest_1_ = bf16[8,48,128]{2,1,0:T(8,128)(2,1)S(1)} collective-permute-done((bf16[8,48,128]{2,1,0:T(8,128)(2,1)S(1)}, bf16[8,48,128]{2,1,0:T(8,128)(2,1)S(1)}, u32[]{:S(2)}, u32[]{:S(2)}) %collective-permute-start.10) | collective-permute-done | bytes 98336 | tf_op jit(solution)/shard_map/ppermute | solution.py:437
  44.4 0.0 collective-permute-done.9.rest_0_
  44.4 1.9 %shard_map.135.start = f32[640,128]{1,0:T(8,128)S(1)} custom-call(s32[215]{0:T(256)S(1)} %get-tuple-element.18.table, bf16[64,128,128]{2,1,0:T(8,128)(2,1)S(1)} %get-tuple-element.19.mats, f32[640,128]{1,0:T(8,128)S(1)} %shard_map.134.start, bf16[8,48,128]{2,1,0:T(8,128)(2,1)S(1)} %collective-permute-done.9.rest_0_, ...), custom_call_target="tpu_custom_call" | custom-call | flops 2000000000 | bytes 6000000 | tf_op jit(solution)/shard_map/pallas_call | solution.py:375
  46.3 0.0 collective-permute-done.12.rest_0_
  46.3 1.1 %shard_map.136 = (f32[640,128]{1,0:T(8,128)S(1)}, f32[16,16,128]{2,1,0:T(8,128)S(1)}) custom-call(s32[215]{0:T(256)S(1)} %get-tuple-element.18.table, bf16[64,128,128]{2,1,0:T(8,128)(2,1)S(1)} %get-tuple-element.19.mats, f32[640,128]{1,0:T(8,128)S(1)} %shard_map.135.start, bf16[16,48,128]{2,1,0:T(8,128)(2,1)S(1)} %collective-permute-done.12.rest_0_), custom_call_target="tpu_custom_call" | custom-call | tf_op jit(solution)/shard_map/pallas_call | solution.py:375
  47.4 3.3 %collective-permute-start.13 = (f32[16,16,128]{2,1,0:T(8,128)S(1)}, f32[16,16,128]{2,1,0:T(8,128)S(1)}, u32[]{:S(2)}, u32[]{:S(2)}) collective-permute-start(f32[16,16,128]{2,1,0:T(8,128)S(1)} %get-tuple-element.30), channel_id=1, source_target_pairs={{1,0},{2,1},{3,2},{5,4},{6,5},{7,6},{9,8},{10,9},{11,10},{13,12},{... | collective-permute-start | bytes 393224 | tf_op jit(solution)/shard_map/ppermute | solution.py:19
  50.7 3.0 %collective-permute-done.13.spill = f32[16,16,128]{2,1,0:T(8,128)S(1)} collective-permute-done((f32[16,16,128]{2,1,0:T(8,128)S(1)}, f32[16,16,128]{2,1,0:T(8,128)S(1)}, u32[]{:S(2)}, u32[]{:S(2)}) %collective-permute-start.13) | collective-permute-done | bytes 131104 | tf_op jit(solution)/shard_map/ppermute | solution.py:19
  53.7 0.8 %shard_map.137 = (f32[2,24,1024]{2,1,0:T(8,128)}, f32[2,24,1024]{2,1,0:T(8,128)}) custom-call(f32[640,128]{1,0:T(8,128)S(1)} %get-tuple-element.29.total, f32[16,16,128]{2,1,0:T(8,128)S(1)} %collective-permute-done.13.spill, bf16[2,24,1024]{2,1,0:T(8,128)(2,1)S(1)} %copy-done.1), custom_call_target="tpu_custom_call" | custom-call | tf_op jit(solution)/shard_map/pallas_call | solution.py:375
  (6 shorter events, 0.1 us)
Async XLA Ops:
  0.6 7.0 %copy-start.1 = (bf16[2,24,1024]{2,1,0:T(8,128)(2,1)S(1)}, bf16[2,24,1024]{2,1,0:T(8,128)(2,1)}, u32[]{:S(2)}) copy-start(bf16[2,24,1024]{2,1,0:T(8,128)(2,1)} %flows.5) | copy-start | bytes 294916
  0.6 6.9 %collective-permute-start = (bf16[2,24,1024]{2,1,0:T(8,128)(2,1)}, bf16[2,24,1024]{2,1,0:T(8,128)(2,1)S(1)}, u32[]{:S(2)}, u32[]{:S(2)}) collective-permute-start(bf16[2,24,1024]{2,1,0:T(8,128)(2,1)} %flows.5), channel_id=1, source_target_pairs={{0,1},{1,2},{2,3},{4,5},{5,6},{6,7},{8,9},{9,10},{10,11},{12,13},{... | collective-permute-start | bytes 294920 | tf_op jit(solution)/shard_map/ppermute | solution.py:19
  7.6 13.1 %copy-start = (bf16[64,128,128]{2,1,0:T(8,128)(2,1)S(1)}, bf16[64,128,128]{2,1,0:T(8,128)(2,1)}, u32[]{:S(2)}) copy-start(bf16[64,128,128]{2,1,0:T(8,128)(2,1)} %mats.3) | copy-start | bytes 6291460
  7.6 13.1 %copy-start.3 = (s32[64]{0:T(128)S(1)}, s32[64]{0:T(128)}, u32[]{:S(2)}) copy-start(s32[64]{0:T(128)} %path.3) | copy-start | bytes 772
  7.6 13.1 %copy-start.4 = (s32[64]{0:T(128)S(1)}, s32[64]{0:T(128)}, u32[]{:S(2)}) copy-start(s32[64]{0:T(128)} %link.3) | copy-start | bytes 772
  7.6 13.1 %copy-start.5 = (s32[64]{0:T(128)S(1)}, s32[64]{0:T(128)}, u32[]{:S(2)}) copy-start(s32[64]{0:T(128)} %lag.3) | copy-start | bytes 772
  10.8 5.6 %collective-permute-start.4 = (f16[16,48,128]{2,1,0:T(8,128)(2,1)S(1)}, f16[16,48,128]{2,1,0:T(8,128)(2,1)S(1)}, u32[]{:S(2)}, u32[]{:S(2)}) collective-permute-start(f16[16,48,128]{2,1,0:T(8,128)(2,1)S(1)} %convert_element_type.39), channel_id=1, source_target_pairs={{0,4},{4,0},{8,12},{12,8},{16,20},{20,16},{24,28},{28,24},{1,5},{5... | collective-permute-start | bytes 589832 | tf_op jit(solution)/shard_map/ppermute | solution.py:437
  12.2 11.5 %collective-permute-start.3 = (f16[8,48,128]{2,1,0:T(8,128)(2,1)S(1)}, f16[8,48,128]{2,1,0:T(8,128)(2,1)S(1)}, u32[]{:S(2)}, u32[]{:S(2)}) collective-permute-start(f16[8,48,128]{2,1,0:T(8,128)(2,1)S(1)} %convert_element_type.37), channel_id=1, source_target_pairs={{0,16},{4,20},{8,24},{12,28},{16,0},{20,4},{24,8},{28,12},{1,17},{... | collective-permute-start | bytes 294920 | tf_op jit(solution)/shard_map/ppermute | solution.py:437
  14.6 9.1 %collective-permute-start.2 = (f16[8,48,128]{2,1,0:T(8,128)(2,1)S(1)}, f16[8,48,128]{2,1,0:T(8,128)(2,1)S(1)}, u32[]{:S(2)}, u32[]{:S(2)}) collective-permute-start(f16[8,48,128]{2,1,0:T(8,128)(2,1)S(1)} %convert_element_type.35), channel_id=1, source_target_pairs={{0,20},{4,16},{8,28},{12,24},{16,4},{20,0},{24,12},{28,8},{1,21},{... | collective-permute-start | bytes 294920 | tf_op jit(solution)/shard_map/ppermute | solution.py:437
  14.6 9.0 %collective-permute-start.1 = (f16[8,48,128]{2,1,0:T(8,128)(2,1)S(1)}, f16[8,48,128]{2,1,0:T(8,128)(2,1)S(1)}, u32[]{:S(2)}, u32[]{:S(2)}) collective-permute-start(f16[8,48,128]{2,1,0:T(8,128)(2,1)S(1)} %convert_element_type.33), channel_id=1, source_target_pairs={{0,4},{4,0},{8,12},{12,8},{16,20},{20,16},{24,28},{28,24},{1,5},{5... | collective-permute-start | bytes 294920 | tf_op jit(solution)/shard_map/ppermute | solution.py:437
  16.5 9.8 %copy-start.2 = (f32[2,24,1024]{2,1,0:T(8,128)S(1)}, f32[2,24,1024]{2,1,0:T(8,128)}, u32[]{:S(2)}) copy-start(f32[2,24,1024]{2,1,0:T(8,128)} %counts.1) | copy-start | bytes 589828
  16.6 9.6 %collective-permute-start.5 = (f16[8,48,128]{2,1,0:T(8,128)(2,1)S(1)}, f16[8,48,128]{2,1,0:T(8,128)(2,1)S(1)}, u32[]{:S(2)}, u32[]{:S(2)}) collective-permute-start(f16[8,48,128]{2,1,0:T(8,128)(2,1)S(1)} %get-tuple-element.33), channel_id=1, source_target_pairs={{0,8},{4,12},{8,0},{12,4},{16,24},{20,28},{24,16},{28,20},{1,9},{5... | collective-permute-start | bytes 294920 | tf_op jit(solution)/shard_map/ppermute | solution.py:437
  18.5 7.7 %collective-permute-start.6 = (f16[8,48,128]{2,1,0:T(8,128)(2,1)S(1)}, f16[8,48,128]{2,1,0:T(8,128)(2,1)S(1)}, u32[]{:S(2)}, u32[]{:S(2)}) collective-permute-start(f16[8,48,128]{2,1,0:T(8,128)(2,1)S(1)} %get-tuple-element.34), channel_id=1, source_target_pairs={{0,24},{4,28},{8,16},{12,20},{16,8},{20,12},{24,0},{28,4},{1,25},{... | collective-permute-start | bytes 294920 | tf_op jit(solution)/shard_map/ppermute | solution.py:437
  27.0 8.5 %collective-permute-start.8 = (bf16[8,48,128]{2,1,0:T(8,128)(2,1)S(1)}, bf16[8,48,128]{2,1,0:T(8,128)(2,1)S(1)}, u32[]{:S(2)}, u32[]{:S(2)}) collective-permute-start(bf16[8,48,128]{2,1,0:T(8,128)(2,1)S(1)} %get-tuple-element.27.signal), channel_id=1, source_target_pairs={{0,24},{4,28},{8,16},{12,20},{16,8},{20,12},{24,0},{28,4},{1,25},{... | collective-permute-start | bytes 294920 | tf_op jit(solution)/shard_map/ppermute | solution.py:437
  32.0 6.2 %collective-permute-start.7 = (bf16[8,48,128]{2,1,0:T(8,128)(2,1)S(1)}, bf16[8,48,128]{2,1,0:T(8,128)(2,1)S(1)}, u32[]{:S(2)}, u32[]{:S(2)}) collective-permute-start(bf16[8,48,128]{2,1,0:T(8,128)(2,1)S(1)} %get-tuple-element.27.signal), channel_id=1, source_target_pairs={{0,8},{4,12},{8,0},{12,4},{16,24},{20,28},{24,16},{28,20},{1,9},{5... | collective-permute-start | bytes 294920 | tf_op jit(solution)/shard_map/ppermute | solution.py:437
  32.0 10.4 %collective-permute-start.11 = (bf16[8,48,128]{2,1,0:T(8,128)(2,1)S(1)}, bf16[8,48,128]{2,1,0:T(8,128)(2,1)S(1)}, u32[]{:S(2)}, u32[]{:S(2)}) collective-permute-start(bf16[8,48,128]{2,1,0:T(8,128)(2,1)S(1)} %get-tuple-element.27.signal), channel_id=1, source_target_pairs={{0,16},{4,20},{8,24},{12,28},{16,0},{20,4},{24,8},{28,12},{1,17},{... | collective-permute-start | bytes 294920 | tf_op jit(solution)/shard_map/ppermute | solution.py:437
  32.2 12.1 %collective-permute-start.10 = (bf16[8,48,128]{2,1,0:T(8,128)(2,1)S(1)}, bf16[8,48,128]{2,1,0:T(8,128)(2,1)S(1)}, u32[]{:S(2)}, u32[]{:S(2)}) collective-permute-start(bf16[8,48,128]{2,1,0:T(8,128)(2,1)S(1)} %get-tuple-element.27.signal), channel_id=1, source_target_pairs={{0,20},{4,16},{8,28},{12,24},{16,4},{20,0},{24,12},{28,8},{1,21},{... | collective-permute-start | bytes 294920 | tf_op jit(solution)/shard_map/ppermute | solution.py:437
  34.3 10.1 %collective-permute-start.9 = (bf16[8,48,128]{2,1,0:T(8,128)(2,1)S(1)}, bf16[8,48,128]{2,1,0:T(8,128)(2,1)S(1)}, u32[]{:S(2)}, u32[]{:S(2)}) collective-permute-start(bf16[8,48,128]{2,1,0:T(8,128)(2,1)S(1)} %get-tuple-element.27.signal), channel_id=1, source_target_pairs={{0,4},{4,0},{8,12},{12,8},{16,20},{20,16},{24,28},{28,24},{1,5},{5... | collective-permute-start | bytes 294920 | tf_op jit(solution)/shard_map/ppermute | solution.py:437
  38.1 8.1 %collective-permute-start.12 = (bf16[16,48,128]{2,1,0:T(8,128)(2,1)S(1)}, bf16[16,48,128]{2,1,0:T(8,128)(2,1)S(1)}, u32[]{:S(2)}, u32[]{:S(2)}) collective-permute-start(bf16[16,48,128]{2,1,0:T(8,128)(2,1)S(1)} %pad_maximum_fusion), channel_id=1, source_target_pairs={{0,4},{4,0},{8,12},{12,8},{16,20},{20,16},{24,28},{28,24},{1,5},{5... | collective-permute-start | bytes 589832 | tf_op jit(solution)/shard_map/ppermute | solution.py:437
  47.4 6.3 %collective-permute-start.13 = (f32[16,16,128]{2,1,0:T(8,128)S(1)}, f32[16,16,128]{2,1,0:T(8,128)S(1)}, u32[]{:S(2)}, u32[]{:S(2)}) collective-permute-start(f32[16,16,128]{2,1,0:T(8,128)S(1)} %get-tuple-element.30), channel_id=1, source_target_pairs={{1,0},{2,1},{3,2},{5,4},{6,5},{7,6},{9,8},{10,9},{11,10},{13,12},{... | collective-permute-start | bytes 393224 | tf_op jit(solution)/shard_map/ppermute | solution.py:19

commit v5 on v4

--- a/solution.py
+++ b/solution.py
@@ -160,6 +160,12 @@
 
 HALO = 16
 WIRE = jnp.float16
+UNROLL = 32
+CHUNKS = 8
+
+
+def step_of(count):
+    return next(u for u in range(min(count, UNROLL), 0, -1) if count % u == 0)
 
 
 def stage_flows(flows_ref, before_ref, wide, days, width):
@@ -194,7 +200,7 @@
             acc[target(g, u)] += parts[u]
         return carry
 
-    lax.fori_loop(*groups, group, 0)
+    lax.fori_loop(0, groups, group, 0)
 
 
 def backward_blocks(groups, unroll, mat, base, signal, acc, days, minutes):
@@ -211,7 +217,7 @@
                 acc[rows, :] += parts[u][d * minutes : (d + 1) * minutes]
         return carry
 
-    lax.fori_loop(*groups, group, 0)
+    lax.fori_loop(0, groups, group, 0)
 
 
 class Table:
@@ -223,46 +229,88 @@
         self.size = self.link + blocks
 
 
-def prepare_kernel(cap, order, t, row_step, me, *rest):
-    sources, (table, mats_out, path, link, lag, slot, sems) = rest[:5], rest[5:]
+def prepare_kernel(cap, order, links, chunks, row_step, me, *rest):
+    sources, (ahead, mats_out, path, link, lag, slot, place, sems) = rest[:5], rest[5:]
     blocks = slot.shape[0]
-    pairs = zip(sources, (path, link, lag, slot, mats_out))
+    pairs = list(zip(sources[:4], (path, link, lag, slot)))
+    step = blocks // chunks
+    for c in range(chunks):
+        rows = slice(c * step, blocks if c == chunks - 1 else (c + 1) * step)
+        pairs.append((sources[4].at[rows], mats_out.at[rows]))
     copies = [pltpu.make_async_copy(a, b, sems.at[i]) for i, (a, b) in enumerate(pairs)]
     for copy in copies:
         copy.start()
+    place[0] = 0
+    for p, s in enumerate(order):
+        place[s] = p * links
+    for copy in copies[:4]:
+        copy.wait()
+
+    def entry(j, carry):
+        ahead[j] = path[j] * row_step + HALO - lag[j]
+        ahead[blocks + j] = place[lax.div(slot[j], cap) ^ me[0]] + link[j]
+        return carry
+
+    lax.fori_loop(0, blocks, entry, 0, unroll=16)
+    for copy in copies[4:]:
+        copy.wait()
+
+
+def fill_table(cap, order, links, t, me, ahead, slot, table):
+    blocks = slot.shape[0]
     for p, s in enumerate(order):
         table[t.start + p] = t.block + (me[0] ^ s) * cap
     for i in range((len(order) + 1) * cap):
         table[t.block + i] = -1
-    for copy in copies[:4]:
-        copy.wait()
-
-    def place(j, carry):
+
+    def entry(j, carry):
         table[t.block + slot[j]] = j
-        table[t.base + j] = path[j] * row_step + HALO - lag[j]
-        table[t.link + j] = link[j]
+        table[t.base + j] = ahead[j]
+        table[t.link + j] = ahead[blocks + j]
         return carry
 
-    lax.fori_loop(0, blocks, place, 0, unroll=8)
-    copies[4].wait()
-
-
-def slot_views(table, t, mats, links, blank):
-    def index(place, rank):
-        return table[table[t.start + place] + rank]
-
-    def mat(place, rank):
-        return mats[jnp.maximum(index(place, rank), 0)]
-
-    def base(place, rank):
-        return table[t.base + jnp.maximum(index(place, rank), 0)]
-
-    def block(place, rank):
-        j = index(place, rank)
-        spot = place * links + table[t.link + jnp.maximum(j, 0)]
-        return jnp.where(j < 0, blank, spot)
+    lax.fori_loop(0, blocks, entry, 0, unroll=16)
+
+
+def slot_views(table, t, mats, cap, first, unroll, blank):
+    def index(g, u):
+        at = first * cap + g * unroll + u
+        place = lax.div(at, cap)
+        return table[table[t.start + place] + at - place * cap]
+
+    def mat(g, u):
+        return mats[jnp.maximum(index(g, u), 0)]
+
+    def base(g, u):
+        return table[t.base + jnp.maximum(index(g, u), 0)]
+
+    def block(g, u):
+        j = index(g, u)
+        return jnp.where(j < 0, blank, table[t.link + jnp.maximum(j, 0)])
 
     return mat, base, block
+
+
+def forward_remote_kernel(days, cuts, links, ahead, flows, before, mats, *rest):
+    outs, (wide, acc) = rest[:-2], rest[-2:]
+    minutes, width = flows.shape[1], mats.shape[2]
+    blocks = mats.shape[0]
+    stage_flows(flows, before, wide, days, width)
+    acc[...] = jnp.zeros_like(acc)
+    unroll = step_of(blocks)
+    forward_blocks(
+        blocks // unroll,
+        unroll,
+        lambda g, u: mats[g * unroll + u],
+        lambda g, u: ahead[g * unroll + u],
+        lambda g, u: ahead[blocks + g * unroll + u],
+        wide,
+        acc,
+        days,
+        minutes,
+    )
+    for first, end, out in zip(cuts, cuts[1:], outs):
+        out[...] = acc[first * links : end * links]
 
 
 def local_views(path, link, lag, mats, unroll, row_step):
@@ -273,23 +321,16 @@
     )
 
 
-def forward_remote_kernel(days, cap, cuts, links, t, table, flows, before, mats, *rest):
-    outs, (wide, acc) = rest[:-2], rest[-2:]
-    minutes, width = flows.shape[1], mats.shape[2]
-    stage_flows(flows, before, wide, days, width)
-    acc[...] = jnp.zeros_like(acc)
-    views = slot_views(table, t, mats, links, acc.shape[0] - 1)
-    forward_blocks((cuts[0], cuts[-1]), cap, *views, wide, acc, days, minutes)
-    for first, end, out in zip(cuts, cuts[1:], outs):
-        out[...] = acc[first * links : end * links]
-
-
-def forward_local_kernel(days, path, link, lag, flows, before, mats, own, wide):
+def forward_local_kernel(
+    days, cap, order, t, links, me, ahead, slot, path, link, lag, flows, before, mats, own, table, wide
+):
     minutes, width = flows.shape[1], mats.shape[2]
     stage_flows(flows, before, wide, days, width)
     own[...] = jnp.zeros_like(own)
-    views = local_views(path, link, lag, mats, 8, days * (HALO + minutes))
-    forward_blocks((0, mats.shape[0] // 8), 8, *views, wide, own, days, minutes)
+    unroll = step_of(mats.shape[0])
+    views = local_views(path, link, lag, mats, unroll, days * (HALO + minutes))
+    forward_blocks(mats.shape[0] // unroll, unroll, *views, wide, own, days, minutes)
+    fill_table(cap, order, links, t, me, ahead, slot, table)
 
 
 def signal_kernel(days, totals, counts, residual, signal):
@@ -310,10 +351,11 @@
 def backward_local_kernel(days, path, link, lag, signal, mats, out):
     minutes = signal.shape[1] // days
     out[...] = jnp.zeros_like(out)
-    mat, base, block = local_views(path, link, lag, mats, 8, days * (HALO + minutes))
+    unroll = step_of(mats.shape[0])
+    mat, base, block = local_views(path, link, lag, mats, unroll, days * (HALO + minutes))
     backward_blocks(
-        (0, mats.shape[0] // 8),
-        8,
+        mats.shape[0] // unroll,
+        unroll,
         mat,
         base,
         lambda g, u: signal[block(g, u)],
@@ -339,9 +381,18 @@
     everyone[blank] = jnp.zeros(everyone.shape[1:], everyone.dtype)
     out[...] = start[...]
     span = HALO + minutes
-    mat, base, block = slot_views(table, t, mats, links, blank)
+    slots = (end - first) * cap
+    unroll = step_of(slots)
+    mat, base, block = slot_views(table, t, mats, cap, first, unroll, blank)
     backward_blocks(
-        (first, end), cap, mat, base, lambda g, u: everyone[block(g, u)], out, days, minutes
+        slots // unroll,
+        unroll,
+        mat,
+        base,
+        lambda g, u: everyone[block(g, u)],
+        out,
+        days,
+        minutes,
     )
     if early:
         for i in range(early[0].shape[0]):
@@ -371,12 +422,12 @@
 HBM = pl.BlockSpec(memory_space=pltpu.HBM)
 
 
-def kernel_call(body, scalars, arrays, out_shape, scratch=(), cost=None):
+def kernel_call(body, scalars, arrays, out_shape, scratch=(), cost=None, outs=None):
     return pl.pallas_call(
         body,
         out_shape=out_shape,
         in_specs=[SMEM] * len(scalars) + [VMEM] * len(arrays),
-        out_specs=[VMEM] * len(out_shape),
+        out_specs=outs or [VMEM] * len(out_shape),
         scratch_shapes=list(scratch),
         compiler_params=pltpu.CompilerParams(vmem_limit_bytes=40 * 1024 * 1024),
         cost_estimate=cost,
@@ -420,16 +471,16 @@
 
     before = passed_along(flows, "tm", 1)
     fixed = (remote_path, remote_link, remote_lag, remote_slot, remote_blocks)
-    table, remote_mats = pl.pallas_call(
-        functools.partial(prepare_kernel, cap, order, t, days * span),
+    ahead, remote_mats = pl.pallas_call(
+        functools.partial(prepare_kernel, cap, order, links, CHUNKS, days * span),
         out_shape=[
-            shape((t.size,), jnp.int32),
+            shape((2 * remotes,), jnp.int32),
             shape(remote_blocks.shape, remote_blocks.dtype),
         ],
         in_specs=[SMEM] + [HBM] * len(fixed),
         out_specs=[SMEM, VMEM],
         scratch_shapes=[pltpu.SMEM(remote_slot.shape, jnp.int32) for _ in fixed[1:]]
-        + [pltpu.SemaphoreType.DMA((len(fixed),))],
+        + [pltpu.SMEM((corridors,), jnp.int32), pltpu.SemaphoreType.DMA((len(fixed) - 1 + CHUNKS,))],
         compiler_params=pltpu.CompilerParams(vmem_limit_bytes=40 * 1024 * 1024),
     )(me, *(pltpu.with_memory_space_constraint(i, pltpu.HBM) for i in fixed))
 
@@ -438,20 +489,23 @@
 
     f32 = jnp.float32
     crossed, *parts, kept = kernel_call(
-        functools.partial(forward_remote_kernel, days, cap, cuts, links, t),
-        (table,),
+        functools.partial(forward_remote_kernel, days, cuts, links),
+        (ahead,),
         (flows, before, remote_mats),
         [shape(((end - first) * links, *piece[1:]), f32) for first, end in zip(cuts, cuts[1:])],
-        [wide, pltpu.VMEM(slots_shape, f32)],
+        [wide, pltpu.VMEM((len(order) * links, *piece[1:]), f32)],
     )
     crossed = exchanged(crossed.astype(WIRE), 1)
-    received = [exchanged(p.astype(WIRE), s) for p, s in zip(parts, (1, *direct))]
-    (own,) = kernel_call(
-        functools.partial(forward_local_kernel, days),
-        local_index,
+    near, crossed = lax.optimization_barrier((parts[0].astype(WIRE), crossed))
+    received = [exchanged(p.astype(WIRE), s) for p, s in zip(parts[1:], direct)]
+    received.append(exchanged(near, 1))
+    own, table = kernel_call(
+        functools.partial(forward_local_kernel, days, cap, order, t, links),
+        (me, ahead, remote_slot, *local_index),
         (flows, before, local_blocks),
-        [shape(piece, f32)],
+        [shape(piece, f32), shape((t.size,), jnp.int32)],
         [wide],
+        outs=[VMEM, SMEM],
     )
     kept = (kept + crossed.astype(f32)).astype(WIRE).reshape(many, *piece)
     received += [exchanged(kept[i], s) for i, s in enumerate(through)]
@@ -462,8 +516,8 @@
         (totals, counts),
         [shape(counts.shape, f32), shape(piece, jnp.bfloat16)],
     )
-    arrived = [exchanged(signal, s) for s in (*through, 1, *direct)]
-    both = jnp.concatenate(arrived[:many], axis=0)
+    arrived = [exchanged(signal, s) for s in (*through, *direct)]
+    both = jnp.concatenate([*arrived[:many], signal], axis=0)
     both, signal = lax.optimization_barrier((both, signal))
     rows = [shape((paths * days * span, width), f32)]
     (total,) = kernel_call(
@@ -482,8 +536,8 @@
 
     edge = shape((paths * days, HALO, width), f32)
     for first, end, signals, made in (
-        (many, len(order), [*arrived[many:], *arrived[:many]], rows),
-        (0, many, [passed], [*rows, edge]),
+        (many + 1, len(order), [*arrived[many:], *arrived[:many]], rows),
+        (0, many + 1, [passed], [*rows, edge]),
     ):
         total, *early = kernel_call(
             functools.partial(backward_remote_kernel, days, cap, first, end, links, t),

time: 54.7 us -> 58.3 us (1.066)
  waiting for transfers between devices: 12.3 us -> 20 us
  starting transfers between devices: 25.8 us -> 23.7 us
  Pallas kernels: 15.2 us -> 13.3 us
    ppermute x12 -> x11, waiting for transfers between devices: 9.28 us -> 17 us  [exchanged(): return lax.ppermute(part, 'corr', [(i, i ^ s) for i in range(corridors)])]
    ppermute x12 -> x11, starting transfers between devices: 17.8 us -> 15.7 us  [exchanged(): return lax.ppermute(part, 'corr', [(i, i ^ s) for i in range(corridors)])]
    pallas_call x7, Pallas kernels: 13 us -> 11.1 us  [kernel_call(): pl.pallas_call(body, out_shape=out_shape, in_specs=[SMEM] * len(scalars)...]
  transfers between devices with their start and end apart: 14 -> 13, of which waited for: 6 -> 8; matrix products, arithmetic and copies ran while one was open for 0% -> 0% of each run, Pallas kernels for 17% -> 14%
where the time goes in v5:
time: 58.3 us; the launch traced here: 58.1 us
  starting transfers between devices  23.7 us (41%)
  waiting for transfers between devices  20 us (34%)
  Pallas kernels  13.3 us (23%)
  between operations  0.85 us (1%)
    ppermute x11, waiting for transfers between devices, exchanged(): return lax.ppermute(part, 'corr', [(i, i ^ s) for i in range(corridors)])  17 us
    ppermute x11, starting transfers between devices, exchanged(): return lax.ppermute(part, 'corr', [(i, i ^ s) for i in range(corridors)])  15.7 us
    pallas_call x7, Pallas kernels, kernel_call(): pl.pallas_call(body, out_shape=out_shape, in_specs=[SMEM] * len(scalars)...  11.1 us
    ppermute x2, starting transfers between devices, passed_along(): return lax.ppermute(block, axis, route)  7.97 us
    ppermute x2, waiting for transfers between devices, passed_along(): return lax.ppermute(block, axis, route)  2.98 us
    pallas_call x1, Pallas kernels, per_device_dense(): pl.pallas_call(functools.partial(prepare_kernel, cap, order, links, CHUNK...  2.21 us
  transfers between devices with their start and end apart: 13, of which 8 were waited for; matrix products, arithmetic and copies ran while one was open for 0% of the time, Pallas kernels for 14%

profile of v5, /device:TPU:1, one launch (start us, length us, event | category | flops | bytes accessed | tf_op | source)
XLA Modules:
  0.0 58.1 jit_solution(5538847632676669227)
XLA Ops:
  0.6 0.0 copy-start.1
  0.6 4.7 %collective-permute-start = (bf16[2,24,1024]{2,1,0:T(8,128)(2,1)}, bf16[2,24,1024]{2,1,0:T(8,128)(2,1)S(1)}, u32[]{:S(2)}, u32[]{:S(2)}) collective-permute-start(bf16[2,24,1024]{2,1,0:T(8,128)(2,1)} %flows.5), channel_id=1, source_target_pairs={{0,1},{1,2},{2,3},{4,5},{5,6},{6,7},{8,9},{9,10},{10,11},{12,13},{... | collective-permute-start | bytes 294920 | tf_op jit(solution)/shard_map/ppermute | solution.py:19
  5.3 2.2 %shard_map.130 = (s32[128]{0:T(128)S(1)}, bf16[64,128,128]{2,1,0:T(8,128)(2,1)S(1)}) custom-call(s32[1]{0:T(128)} %bitcast.me, s32[64]{0:T(128)} %rest_0_.1, s32[64]{0:T(128)} %rest_1_.1, s32[64]{0:T(128)} %rest_2_.1, s32[64]{0:T(128)} %slot.1, bf16[64,128,128]{2,1,0:T(8,128)(2,1)} %rest_4_.1), custom_call_target="tpu_custom_call" | custom-call | tf_op jit(solution)/shard_map/pallas_call | solution.py:474
  7.5 0.0 collective-permute-done.before
  7.5 0.0 copy-done.1
  7.6 0.0 copy-start
  7.6 0.0 copy-start.3
  7.6 0.0 copy-start.4
  7.6 0.0 copy-start.5
  7.6 0.0 copy-start.6
  7.6 2.4 %shard_map.132 = (f32[16,48,128]{2,1,0:T(8,128)S(1)}, f32[8,48,128]{2,1,0:T(8,128)S(1)}, f32[8,48,128]{2,1,0:T(8,128)S(1)}, f32[8,48,128]{2,1,0:T(8,128)S(1)}, f32[16,48,128]{2,1,0:T(8,128)S(1)}) custom-call(s32[128]{0:T(128)S(1)} %get-tuple-element.22.ahead, bf16[2,24,1024]{2,1,0:T(8,128)(2,1)S(1)} %copy-done.1, ...), custom_call_target="tpu_custom_call" | custom-call | tf_op jit(solution)/shard_map/pallas_call | solution.py:426
  10.1 1.3 %collective-permute-start.3 = (f16[16,48,128]{2,1,0:T(8,128)(2,1)S(1)}, f16[16,48,128]{2,1,0:T(8,128)(2,1)S(1)}, u32[]{:S(2)}, u32[]{:S(2)}) collective-permute-start(f16[16,48,128]{2,1,0:T(8,128)(2,1)S(1)} %convert_element_type.38), channel_id=1, source_target_pairs={{0,4},{4,0},{8,12},{12,8},{16,20},{20,16},{24,28},{28,24},{1,5},{5... | collective-permute-start | bytes 589832 | tf_op jit(solution)/shard_map/ppermute | solution.py:488
  11.4 2.4 %collective-permute-start.2 = (f16[8,48,128]{2,1,0:T(8,128)(2,1)S(1)}, f16[8,48,128]{2,1,0:T(8,128)(2,1)S(1)}, u32[]{:S(2)}, u32[]{:S(2)}) collective-permute-start(f16[8,48,128]{2,1,0:T(8,128)(2,1)S(1)} %convert_element_type.35), channel_id=1, source_target_pairs={{0,16},{4,20},{8,24},{12,28},{16,0},{20,4},{24,8},{28,12},{1,17},{... | collective-permute-start | bytes 294920 | tf_op jit(solution)/shard_map/ppermute | solution.py:488
  13.8 0.1 collective-permute-start.1
  13.9 1.8 %collective-permute-done.3 = f16[16,48,128]{2,1,0:T(8,128)(2,1)S(1)} collective-permute-done((f16[16,48,128]{2,1,0:T(8,128)(2,1)S(1)}, f16[16,48,128]{2,1,0:T(8,128)(2,1)S(1)}, u32[]{:S(2)}, u32[]{:S(2)}) %collective-permute-start.3) | collective-permute-done | bytes 196640 | tf_op jit(solution)/shard_map/ppermute | solution.py:488
  15.7 0.0 copy-start.2
  15.7 0.1 add_convert_fusion
  15.8 3.9 %collective-permute-start.6 = (f16[8,48,128]{2,1,0:T(8,128)(2,1)S(1)}, f16[8,48,128]{2,1,0:T(8,128)(2,1)S(1)}, u32[]{:S(2)}, u32[]{:S(2)}) collective-permute-start(f16[8,48,128]{2,1,0:T(8,128)(2,1)S(1)} %get-tuple-element.42), channel_id=1, source_target_pairs={{0,24},{4,28},{8,16},{12,20},{16,8},{20,12},{24,0},{28,4},{1,25},{... | collective-permute-start | bytes 294920 | tf_op jit(solution)/shard_map/ppermute | solution.py:488
  19.8 0.0 collective-permute-start.5
  19.8 1.2 %collective-permute-start.4 = (f16[8,48,128]{2,1,0:T(8,128)(2,1)S(1)}, f16[8,48,128]{2,1,0:T(8,128)(2,1)S(1)}, u32[]{:S(2)}, u32[]{:S(2)}) collective-permute-start(f16[8,48,128]{2,1,0:T(8,128)(2,1)S(1)} %convert_element_type.37), channel_id=1, source_target_pairs={{0,4},{4,0},{8,12},{12,8},{16,20},{20,16},{24,28},{28,24},{1,5},{5... | collective-permute-start | bytes 294920 | tf_op jit(solution)/shard_map/ppermute | solution.py:488
  21.0 0.0 copy-done
  21.0 0.0 copy-done.3
  21.0 0.0 copy-done.4
  21.0 0.0 copy-done.5
  21.0 0.0 copy-done.6
  21.0 3.1 %shard_map.131 = (f32[8,48,128]{2,1,0:T(8,128)S(1)}, s32[215]{0:T(256)S(1)}) custom-call(s32[1]{0:T(128)} %bitcast.me, s32[128]{0:T(128)S(1)} %get-tuple-element.22.ahead, s32[64]{0:T(128)S(1)} %copy-done.6, s32[64]{0:T(128)S(1)} %copy-done.3, s32[64]{0:T(128)S(1)} %copy-done.4, s32[64]{0:T(128)S(1)} %copy-done.5, bf16[2,24,1024]{2,1,0:T(8,128)(2,1)S(1)} %copy-done.1, ...), custom_call_target="tpu_custom_call" | custom-call | tf_op jit(solution)/shard_map/pallas_call | solution.py:426
  24.1 0.0 collective-permute-done.2
  24.1 0.5 collective-permute-done.1
  24.6 0.0 collective-permute-done.6
  24.7 2.5 %collective-permute-done.5 = f16[8,48,128]{2,1,0:T(8,128)(2,1)S(1)} collective-permute-done((f16[8,48,128]{2,1,0:T(8,128)(2,1)S(1)}, f16[8,48,128]{2,1,0:T(8,128)(2,1)S(1)}, u32[]{:S(2)}, u32[]{:S(2)}) %collective-permute-start.5) | collective-permute-done | bytes 98336 | tf_op jit(solution)/shard_map/ppermute | solution.py:488
  27.2 0.0 collective-permute-done.4
  27.2 0.1 convert_add_fusion.totals
  27.3 0.0 copy-done.2
  27.3 0.7 %shard_map.133 = (f32[2,24,1024]{2,1,0:T(8,128)}, bf16[8,48,128]{2,1,0:T(8,128)(2,1)S(1)}) custom-call(f32[8,48,128]{2,1,0:T(8,128)S(1)} %convert_add_fusion.totals, f32[2,24,1024]{2,1,0:T(8,128)S(1)} %copy-done.2), custom_call_target="tpu_custom_call" | custom-call | tf_op jit(solution)/shard_map/pallas_call | solution.py:426
  28.0 3.2 %collective-permute-start.8 = (bf16[8,48,128]{2,1,0:T(8,128)(2,1)S(1)}, bf16[8,48,128]{2,1,0:T(8,128)(2,1)S(1)}, u32[]{:S(2)}, u32[]{:S(2)}) collective-permute-start(bf16[8,48,128]{2,1,0:T(8,128)(2,1)S(1)} %get-tuple-element.35.signal), channel_id=1, source_target_pairs={{0,24},{4,28},{8,16},{12,20},{16,8},{20,12},{24,0},{28,4},{1,25},{... | collective-permute-start | bytes 294920 | tf_op jit(solution)/shard_map/ppermute | solution.py:488
  31.2 0.0 collective-permute-start.7
  31.2 2.6 %collective-permute-done.8.rest_3_ = bf16[8,48,128]{2,1,0:T(8,128)(2,1)S(1)} collective-permute-done((bf16[8,48,128]{2,1,0:T(8,128)(2,1)S(1)}, bf16[8,48,128]{2,1,0:T(8,128)(2,1)S(1)}, u32[]{:S(2)}, u32[]{:S(2)}) %collective-permute-start.8) | collective-permute-done | bytes 98336 | tf_op jit(solution)/shard_map/ppermute | solution.py:488
  33.8 2.5 %collective-permute-done.7.rest_2_ = bf16[8,48,128]{2,1,0:T(8,128)(2,1)S(1)} collective-permute-done((bf16[8,48,128]{2,1,0:T(8,128)(2,1)S(1)}, bf16[8,48,128]{2,1,0:T(8,128)(2,1)S(1)}, u32[]{:S(2)}, u32[]{:S(2)}) %collective-permute-start.7) | collective-permute-done | bytes 98336 | tf_op jit(solution)/shard_map/ppermute | solution.py:488
  36.3 0.4 collective-permute-start.11
  36.7 0.8 %collective-permute-start.9 = (bf16[8,48,128]{2,1,0:T(8,128)(2,1)S(1)}, bf16[8,48,128]{2,1,0:T(8,128)(2,1)S(1)}, u32[]{:S(2)}, u32[]{:S(2)}) collective-permute-start(bf16[8,48,128]{2,1,0:T(8,128)(2,1)S(1)} %get-tuple-element.35.signal), channel_id=1, source_target_pairs={{0,20},{4,16},{8,28},{12,24},{16,4},{20,0},{24,12},{28,8},{1,21},{... | collective-permute-start | bytes 294920 | tf_op jit(solution)/shard_map/ppermute | solution.py:488
  37.5 2.4 %collective-permute-start.10 = (bf16[8,48,128]{2,1,0:T(8,128)(2,1)S(1)}, bf16[8,48,128]{2,1,0:T(8,128)(2,1)S(1)}, u32[]{:S(2)}, u32[]{:S(2)}) collective-permute-start(bf16[8,48,128]{2,1,0:T(8,128)(2,1)S(1)} %get-tuple-element.35.signal), channel_id=1, source_target_pairs={{0,16},{4,20},{8,24},{12,28},{16,0},{20,4},{24,8},{28,12},{1,17},{... | collective-permute-start | bytes 294920 | tf_op jit(solution)/shard_map/ppermute | solution.py:488
  39.9 1.5 %shard_map.134.start = f32[640,128]{1,0:T(8,128)S(1)} custom-call(s32[64]{0:T(128)S(1)} %copy-done.3, s32[64]{0:T(128)S(1)} %copy-done.4, s32[64]{0:T(128)S(1)} %copy-done.5, bf16[8,48,128]{2,1,0:T(8,128)(2,1)S(1)} %get-tuple-element.35.signal, bf16[64,128,128]{2,1,0:T(8,128)(2,1)S(1)} %copy-done), custom_call_target="tpu_custom_call" | custom-call | tf_op jit(solution)/shard_map/pallas_call | solution.py:426
  41.5 5.2 %collective-permute-done.9.rest_0_ = bf16[8,48,128]{2,1,0:T(8,128)(2,1)S(1)} collective-permute-done((bf16[8,48,128]{2,1,0:T(8,128)(2,1)S(1)}, bf16[8,48,128]{2,1,0:T(8,128)(2,1)S(1)}, u32[]{:S(2)}, u32[]{:S(2)}) %collective-permute-start.9) | collective-permute-done | bytes 98336 | tf_op jit(solution)/shard_map/ppermute | solution.py:488
  46.6 1.9 %collective-permute-done.10.rest_1_ = bf16[8,48,128]{2,1,0:T(8,128)(2,1)S(1)} collective-permute-done((bf16[8,48,128]{2,1,0:T(8,128)(2,1)S(1)}, bf16[8,48,128]{2,1,0:T(8,128)(2,1)S(1)}, u32[]{:S(2)}, u32[]{:S(2)}) %collective-permute-start.10) | collective-permute-done | bytes 98336 | tf_op jit(solution)/shard_map/ppermute | solution.py:488
  48.6 1.4 %shard_map.135.start = f32[640,128]{1,0:T(8,128)S(1)} custom-call(s32[215]{0:T(256)S(1)} %get-tuple-element.33.table, bf16[64,128,128]{2,1,0:T(8,128)(2,1)S(1)} %get-tuple-element.24.mats, f32[640,128]{1,0:T(8,128)S(1)} %shard_map.134.start, bf16[8,48,128]{2,1,0:T(8,128)(2,1)S(1)} %collective-permute-done.9.rest_0_, ...), custom_call_target="tpu_custom_call" | custom-call | flops 2000000000 | bytes 6000000 | tf_op jit(solution)/shard_map/pallas_call | solution.py:426
  50.0 0.0 collective-permute-done.11.rest_0_
  50.0 1.1 %shard_map.136 = (f32[640,128]{1,0:T(8,128)S(1)}, f32[16,16,128]{2,1,0:T(8,128)S(1)}) custom-call(s32[215]{0:T(256)S(1)} %get-tuple-element.33.table, bf16[64,128,128]{2,1,0:T(8,128)(2,1)S(1)} %get-tuple-element.24.mats, f32[640,128]{1,0:T(8,128)S(1)} %shard_map.135.start, bf16[24,48,128]{2,1,0:T(8,128)(2,1)S(1)} %collective-permute-done.11.rest_0_), custom_call_target="tpu_custom_call" | custom-call | tf_op jit(solution)/shard_map/pallas_call | solution.py:426
  51.1 3.3 %collective-permute-start.12 = (f32[16,16,128]{2,1,0:T(8,128)S(1)}, f32[16,16,128]{2,1,0:T(8,128)S(1)}, u32[]{:S(2)}, u32[]{:S(2)}) collective-permute-start(f32[16,16,128]{2,1,0:T(8,128)S(1)} %get-tuple-element.38), channel_id=1, source_target_pairs={{1,0},{2,1},{3,2},{5,4},{6,5},{7,6},{9,8},{10,9},{11,10},{13,12},{... | collective-permute-start | bytes 393224 | tf_op jit(solution)/shard_map/ppermute | solution.py:19
  54.4 3.0 %collective-permute-done.12.spill = f32[16,16,128]{2,1,0:T(8,128)S(1)} collective-permute-done((f32[16,16,128]{2,1,0:T(8,128)S(1)}, f32[16,16,128]{2,1,0:T(8,128)S(1)}, u32[]{:S(2)}, u32[]{:S(2)}) %collective-permute-start.12) | collective-permute-done | bytes 131104 | tf_op jit(solution)/shard_map/ppermute | solution.py:19
  57.3 0.8 %shard_map.137 = (f32[2,24,1024]{2,1,0:T(8,128)}, f32[2,24,1024]{2,1,0:T(8,128)}) custom-call(f32[640,128]{1,0:T(8,128)S(1)} %get-tuple-element.37.total, f32[16,16,128]{2,1,0:T(8,128)S(1)} %collective-permute-done.12.spill, bf16[2,24,1024]{2,1,0:T(8,128)(2,1)S(1)} %copy-done.1), custom_call_target="tpu_custom_call" | custom-call | tf_op jit(solution)/shard_map/pallas_call | solution.py:426
  (6 shorter events, 0.2 us)
Async XLA Ops:
  0.6 6.9 %copy-start.1 = (bf16[2,24,1024]{2,1,0:T(8,128)(2,1)S(1)}, bf16[2,24,1024]{2,1,0:T(8,128)(2,1)}, u32[]{:S(2)}) copy-start(bf16[2,24,1024]{2,1,0:T(8,128)(2,1)} %flows.5) | copy-start | bytes 294916
  0.6 6.9 %collective-permute-start = (bf16[2,24,1024]{2,1,0:T(8,128)(2,1)}, bf16[2,24,1024]{2,1,0:T(8,128)(2,1)S(1)}, u32[]{:S(2)}, u32[]{:S(2)}) collective-permute-start(bf16[2,24,1024]{2,1,0:T(8,128)(2,1)} %flows.5), channel_id=1, source_target_pairs={{0,1},{1,2},{2,3},{4,5},{5,6},{6,7},{8,9},{9,10},{10,11},{12,13},{... | collective-permute-start | bytes 294920 | tf_op jit(solution)/shard_map/ppermute | solution.py:19
  7.6 13.4 %copy-start = (bf16[64,128,128]{2,1,0:T(8,128)(2,1)S(1)}, bf16[64,128,128]{2,1,0:T(8,128)(2,1)}, u32[]{:S(2)}) copy-start(bf16[64,128,128]{2,1,0:T(8,128)(2,1)} %mats.3) | copy-start | bytes 6291460
  7.6 13.4 %copy-start.3 = (s32[64]{0:T(128)S(1)}, s32[64]{0:T(128)}, u32[]{:S(2)}) copy-start(s32[64]{0:T(128)} %path.3) | copy-start | bytes 772
  7.6 13.4 %copy-start.4 = (s32[64]{0:T(128)S(1)}, s32[64]{0:T(128)}, u32[]{:S(2)}) copy-start(s32[64]{0:T(128)} %link.3) | copy-start | bytes 772
  7.6 13.4 %copy-start.5 = (s32[64]{0:T(128)S(1)}, s32[64]{0:T(128)}, u32[]{:S(2)}) copy-start(s32[64]{0:T(128)} %lag.3) | copy-start | bytes 772
  7.6 13.4 %copy-start.6 = (s32[64]{0:T(128)S(1)}, s32[64]{0:T(128)}, u32[]{:S(2)}) copy-start(s32[64]{0:T(128)} %slot.1) | copy-start | bytes 772
  10.1 5.6 %collective-permute-start.3 = (f16[16,48,128]{2,1,0:T(8,128)(2,1)S(1)}, f16[16,48,128]{2,1,0:T(8,128)(2,1)S(1)}, u32[]{:S(2)}, u32[]{:S(2)}) collective-permute-start(f16[16,48,128]{2,1,0:T(8,128)(2,1)S(1)} %convert_element_type.38), channel_id=1, source_target_pairs={{0,4},{4,0},{8,12},{12,8},{16,20},{20,16},{24,28},{28,24},{1,5},{5... | collective-permute-start | bytes 589832 | tf_op jit(solution)/shard_map/ppermute | solution.py:488
  11.4 12.7 %collective-permute-start.2 = (f16[8,48,128]{2,1,0:T(8,128)(2,1)S(1)}, f16[8,48,128]{2,1,0:T(8,128)(2,1)S(1)}, u32[]{:S(2)}, u32[]{:S(2)}) collective-permute-start(f16[8,48,128]{2,1,0:T(8,128)(2,1)S(1)} %convert_element_type.35), channel_id=1, source_target_pairs={{0,16},{4,20},{8,24},{12,28},{16,0},{20,4},{24,8},{28,12},{1,17},{... | collective-permute-start | bytes 294920 | tf_op jit(solution)/shard_map/ppermute | solution.py:488
  13.8 10.8 %collective-permute-start.1 = (f16[8,48,128]{2,1,0:T(8,128)(2,1)S(1)}, f16[8,48,128]{2,1,0:T(8,128)(2,1)S(1)}, u32[]{:S(2)}, u32[]{:S(2)}) collective-permute-start(f16[8,48,128]{2,1,0:T(8,128)(2,1)S(1)} %convert_element_type.33), channel_id=1, source_target_pairs={{0,20},{4,16},{8,28},{12,24},{16,4},{20,0},{24,12},{28,8},{1,21},{... | collective-permute-start | bytes 294920 | tf_op jit(solution)/shard_map/ppermute | solution.py:488
  15.7 11.5 %copy-start.2 = (f32[2,24,1024]{2,1,0:T(8,128)S(1)}, f32[2,24,1024]{2,1,0:T(8,128)}, u32[]{:S(2)}) copy-start(f32[2,24,1024]{2,1,0:T(8,128)} %counts.1) | copy-start | bytes 589828
  15.8 8.8 %collective-permute-start.6 = (f16[8,48,128]{2,1,0:T(8,128)(2,1)S(1)}, f16[8,48,128]{2,1,0:T(8,128)(2,1)S(1)}, u32[]{:S(2)}, u32[]{:S(2)}) collective-permute-start(f16[8,48,128]{2,1,0:T(8,128)(2,1)S(1)} %get-tuple-element.42), channel_id=1, source_target_pairs={{0,24},{4,28},{8,16},{12,20},{16,8},{20,12},{24,0},{28,4},{1,25},{... | collective-permute-start | bytes 294920 | tf_op jit(solution)/shard_map/ppermute | solution.py:488
  19.8 7.4 %collective-permute-start.5 = (f16[8,48,128]{2,1,0:T(8,128)(2,1)S(1)}, f16[8,48,128]{2,1,0:T(8,128)(2,1)S(1)}, u32[]{:S(2)}, u32[]{:S(2)}) collective-permute-start(f16[8,48,128]{2,1,0:T(8,128)(2,1)S(1)} %get-tuple-element.41), channel_id=1, source_target_pairs={{0,8},{4,12},{8,0},{12,4},{16,24},{20,28},{24,16},{28,20},{1,9},{5... | collective-permute-start | bytes 294920 | tf_op jit(solution)/shard_map/ppermute | solution.py:488
  19.8 7.4 %collective-permute-start.4 = (f16[8,48,128]{2,1,0:T(8,128)(2,1)S(1)}, f16[8,48,128]{2,1,0:T(8,128)(2,1)S(1)}, u32[]{:S(2)}, u32[]{:S(2)}) collective-permute-start(f16[8,48,128]{2,1,0:T(8,128)(2,1)S(1)} %convert_element_type.37), channel_id=1, source_target_pairs={{0,4},{4,0},{8,12},{12,8},{16,20},{20,16},{24,28},{28,24},{1,5},{5... | collective-permute-start | bytes 294920 | tf_op jit(solution)/shard_map/ppermute | solution.py:488
  28.0 5.8 %collective-permute-start.8 = (bf16[8,48,128]{2,1,0:T(8,128)(2,1)S(1)}, bf16[8,48,128]{2,1,0:T(8,128)(2,1)S(1)}, u32[]{:S(2)}, u32[]{:S(2)}) collective-permute-start(bf16[8,48,128]{2,1,0:T(8,128)(2,1)S(1)} %get-tuple-element.35.signal), channel_id=1, source_target_pairs={{0,24},{4,28},{8,16},{12,20},{16,8},{20,12},{24,0},{28,4},{1,25},{... | collective-permute-start | bytes 294920 | tf_op jit(solution)/shard_map/ppermute | solution.py:488
  31.2 5.0 %collective-permute-start.7 = (bf16[8,48,128]{2,1,0:T(8,128)(2,1)S(1)}, bf16[8,48,128]{2,1,0:T(8,128)(2,1)S(1)}, u32[]{:S(2)}, u32[]{:S(2)}) collective-permute-start(bf16[8,48,128]{2,1,0:T(8,128)(2,1)S(1)} %get-tuple-element.35.signal), channel_id=1, source_target_pairs={{0,8},{4,12},{8,0},{12,4},{16,24},{20,28},{24,16},{28,20},{1,9},{5... | collective-permute-start | bytes 294920 | tf_op jit(solution)/shard_map/ppermute | solution.py:488
  36.3 13.7 %collective-permute-start.11 = (bf16[24,48,128]{2,1,0:T(8,128)(2,1)S(1)}, bf16[24,48,128]{2,1,0:T(8,128)(2,1)S(1)}, u32[]{:S(2)}, u32[]{:S(2)}) collective-permute-start(bf16[24,48,128]{2,1,0:T(8,128)(2,1)S(1)} %pad_maximum_fusion), channel_id=1, source_target_pairs={{0,4},{4,0},{8,12},{12,8},{16,20},{20,16},{24,28},{28,24},{1,5},{5... | collective-permute-start | bytes 884744 | tf_op jit(solution)/shard_map/ppermute | solution.py:488
  36.7 9.9 %collective-permute-start.9 = (bf16[8,48,128]{2,1,0:T(8,128)(2,1)S(1)}, bf16[8,48,128]{2,1,0:T(8,128)(2,1)S(1)}, u32[]{:S(2)}, u32[]{:S(2)}) collective-permute-start(bf16[8,48,128]{2,1,0:T(8,128)(2,1)S(1)} %get-tuple-element.35.signal), channel_id=1, source_target_pairs={{0,20},{4,16},{8,28},{12,24},{16,4},{20,0},{24,12},{28,8},{1,21},{... | collective-permute-start | bytes 294920 | tf_op jit(solution)/shard_map/ppermute | solution.py:488
  37.5 11.1 %collective-permute-start.10 = (bf16[8,48,128]{2,1,0:T(8,128)(2,1)S(1)}, bf16[8,48,128]{2,1,0:T(8,128)(2,1)S(1)}, u32[]{:S(2)}, u32[]{:S(2)}) collective-permute-start(bf16[8,48,128]{2,1,0:T(8,128)(2,1)S(1)} %get-tuple-element.35.signal), channel_id=1, source_target_pairs={{0,16},{4,20},{8,24},{12,28},{16,0},{20,4},{24,8},{28,12},{1,17},{... | collective-permute-start | bytes 294920 | tf_op jit(solution)/shard_map/ppermute | solution.py:488
  51.1 6.3 %collective-permute-start.12 = (f32[16,16,128]{2,1,0:T(8,128)S(1)}, f32[16,16,128]{2,1,0:T(8,128)S(1)}, u32[]{:S(2)}, u32[]{:S(2)}) collective-permute-start(f32[16,16,128]{2,1,0:T(8,128)S(1)} %get-tuple-element.38), channel_id=1, source_target_pairs={{1,0},{2,1},{3,2},{5,4},{6,5},{7,6},{9,8},{10,9},{11,10},{13,12},{... | collective-permute-start | bytes 393224 | tf_op jit(solution)/shard_map/ppermute | solution.py:19

commit v6 on v5

--- a/solution.py
+++ b/solution.py
@@ -168,7 +168,8 @@
     return next(u for u in range(min(count, UNROLL), 0, -1) if count % u == 0)
 
 
-def stage_flows(flows_ref, before_ref, wide, days, width):
+def stage_flows(group, flows_ref, before_ref, wide, days, width):
+    real = jnp.where(group[0] > 0, 1.0, 0.0)
     minutes = flows_ref.shape[1]
     span = HALO + minutes
     for p in range(flows_ref.shape[2] // width):
@@ -176,7 +177,7 @@
         for d in range(days):
             row = (p * days + d) * span
             before = before_ref[d, :, cols].astype(jnp.float32)
-            wide[row : row + HALO, :] = before[minutes - HALO :]
+            wide[row : row + HALO, :] = before[minutes - HALO :] * real
             wide[row + HALO : row + span, :] = flows_ref[d, :, cols].astype(jnp.float32)
 
 
@@ -291,11 +292,11 @@
     return mat, base, block
 
 
-def forward_remote_kernel(days, cuts, links, ahead, flows, before, mats, *rest):
+def forward_remote_kernel(days, cuts, links, group, ahead, flows, before, mats, *rest):
     outs, (wide, acc) = rest[:-2], rest[-2:]
     minutes, width = flows.shape[1], mats.shape[2]
     blocks = mats.shape[0]
-    stage_flows(flows, before, wide, days, width)
+    stage_flows(group, flows, before, wide, days, width)
     acc[...] = jnp.zeros_like(acc)
     unroll = step_of(blocks)
     forward_blocks(
@@ -322,10 +323,10 @@
 
 
 def forward_local_kernel(
-    days, cap, order, t, links, me, ahead, slot, path, link, lag, flows, before, mats, own, table, wide
+    days, cap, order, t, links, group, me, ahead, slot, path, link, lag, flows, before, mats, own, table, wide
 ):
     minutes, width = flows.shape[1], mats.shape[2]
-    stage_flows(flows, before, wide, days, width)
+    stage_flows(group, flows, before, wide, days, width)
     own[...] = jnp.zeros_like(own)
     unroll = step_of(mats.shape[0])
     views = local_views(path, link, lag, mats, unroll, days * (HALO + minutes))
@@ -399,17 +400,18 @@
             early[0][i] = out[i * span : i * span + HALO, :]
 
 
-def finish_kernel(days, total, spill, flows, gradient, new_flows):
+def finish_kernel(days, groups, group, total, spill, flows, gradient, new_flows):
     minutes = flows.shape[1]
     width = total.shape[1]
     span = HALO + minutes
+    real = jnp.where(group[0] < groups - 1, 1.0, 0.0)
     for p in range(flows.shape[2] // width):
         cols = slice(p * width, (p + 1) * width)
         for d in range(days):
             row = (p * days + d) * span + HALO
             own = total[row : row + minutes, :]
             keep = minutes - HALO
-            late = own[keep:] + spill[p * days + d]
+            late = own[keep:] + spill[p * days + d] * real
             for rows, grad in ((slice(0, keep), own[:keep]), (slice(keep, minutes), late)):
                 gradient[d, rows, cols] = grad
                 new_flows[d, rows, cols] = jnp.maximum(
@@ -463,13 +465,15 @@
     cuts = [0, *range(many, len(order) - many + 1), len(order)]
     t = Table(len(order), corridors * cap, remotes)
     me = lax.axis_index("corr").astype(jnp.int32).reshape(1)
+    group = lax.axis_index("tm").astype(jnp.int32).reshape(1)
+    groups = lax.axis_size("tm")
     shape = jax.ShapeDtypeStruct
     piece = (links, days * minutes, width)
     wide = pltpu.VMEM((paths * days * span, width), jnp.float32)
     slots_shape = (len(order) * links + 1, days * minutes, width)
     local_index = (local_path, local_link, local_lag)
 
-    before = passed_along(flows, "tm", 1)
+    before = lax.ppermute(flows, "tm", [(i, (i + 1) % groups) for i in range(groups)])
     fixed = (remote_path, remote_link, remote_lag, remote_slot, remote_blocks)
     ahead, remote_mats = pl.pallas_call(
         functools.partial(prepare_kernel, cap, order, links, CHUNKS, days * span),
@@ -490,7 +494,7 @@
     f32 = jnp.float32
     crossed, *parts, kept = kernel_call(
         functools.partial(forward_remote_kernel, days, cuts, links),
-        (ahead,),
+        (group, ahead),
         (flows, before, remote_mats),
         [shape(((end - first) * links, *piece[1:]), f32) for first, end in zip(cuts, cuts[1:])],
         [wide, pltpu.VMEM((len(order) * links, *piece[1:]), f32)],
@@ -501,14 +505,14 @@
     received.append(exchanged(near, 1))
     own, table = kernel_call(
         functools.partial(forward_local_kernel, days, cap, order, t, links),
-        (me, ahead, remote_slot, *local_index),
+        (group, me, ahead, remote_slot, *local_index),
         (flows, before, local_blocks),
         [shape(piece, f32), shape((t.size,), jnp.int32)],
         [wide],
         outs=[VMEM, SMEM],
     )
     kept = (kept + crossed.astype(f32)).astype(WIRE).reshape(many, *piece)
-    received += [exchanged(kept[i], s) for i, s in enumerate(through)]
+    received += [exchanged(kept[i], through[i]) for i in reversed(range(many))]
     totals = functools.reduce(jnp.add, [p.astype(f32) for p in received], own)
     link_residual, signal = kernel_call(
         functools.partial(signal_kernel, days),
@@ -531,7 +535,7 @@
         if first == 0:
             return None
         return pl.CostEstimate(
-            flops=2_000_000_000, transcendentals=0, bytes_accessed=6_000_000
+            flops=2_700_000_000, transcendentals=0, bytes_accessed=8_100_000
         )
 
     edge = shape((paths * days, HALO, width), f32)
@@ -547,10 +551,10 @@
             [pltpu.VMEM(slots_shape, jnp.bfloat16)],
             weigh(first),
         )
-    spill = passed_along(early[0], "tm", -1)
+    spill = lax.ppermute(early[0], "tm", [(i, (i - 1) % groups) for i in range(groups)])
     gradient, new_flows = kernel_call(
-        functools.partial(finish_kernel, days),
-        (),
+        functools.partial(finish_kernel, days, groups),
+        (group,),
         (total, spill, flows),
         [shape(flows.shape, f32)] * 2,
     )

time: 58.3 us -> 49.2 us (0.84)
  waiting for transfers between devices: 20 us -> 9.39 us
  starting transfers between devices: 23.7 us -> 25 us
    ppermute x11, waiting for transfers between devices: 17 us -> 7.1 us  [exchanged(): return lax.ppermute(part, 'corr', [(i, i ^ s) for i in range(corridors)])]
    ppermute x11, starting transfers between devices: 15.7 us -> 20.1 us  [exchanged(): return lax.ppermute(part, 'corr', [(i, i ^ s) for i in range(corridors)])]
    ppermute x2, starting transfers between devices: 7.97 us -> 4.84 us  [the longest x1 2.68 us: per_device_dense(): lax.ppermute(flows, 'tm', [(i, (i + 1) % groups) for i in range(groups)])]
    ppermute x2, waiting for transfers between devices: 2.98 us -> 2.29 us  [the longest x1 2.29 us: per_device_dense(): lax.ppermute(early[0], 'tm', [(i, (i - 1) % groups) for i in range(groups)])]
  transfers between devices with their start and end apart: 13 -> 13, of which waited for: 8 -> 5; matrix products, arithmetic and copies ran while one was open for 0% -> 0% of each run, Pallas kernels for 14% -> 17%
where the time goes in v6:
time: 49.2 us; the launch traced here: 48.8 us
  starting transfers between devices  25 us (51%)
  Pallas kernels  13.3 us (27%)
  waiting for transfers between devices  9.39 us (19%)
  between operations  0.86 us (2%)
    ppermute x11, starting transfers between devices, exchanged(): return lax.ppermute(part, 'corr', [(i, i ^ s) for i in range(corridors)])  20.1 us
    pallas_call x7, Pallas kernels, kernel_call(): pl.pallas_call(body, out_shape=out_shape, in_specs=[SMEM] * len(scalars)...  11.1 us
    ppermute x11, waiting for transfers between devices, exchanged(): return lax.ppermute(part, 'corr', [(i, i ^ s) for i in range(corridors)])  7.1 us
    ppermute x1, starting transfers between devices, per_device_dense(): lax.ppermute(flows, 'tm', [(i, (i + 1) % groups) for i in range(groups)])  2.68 us
    ppermute x1, waiting for transfers between devices, per_device_dense(): lax.ppermute(early[0], 'tm', [(i, (i - 1) % groups) for i in range(groups)])  2.29 us
    pallas_call x1, Pallas kernels, per_device_dense(): pl.pallas_call(functools.partial(prepare_kernel, cap, order, links, CHUNK...  2.2 us
    ppermute x1, starting transfers between devices, per_device_dense(): lax.ppermute(early[0], 'tm', [(i, (i - 1) % groups) for i in range(groups)])  2.16 us
  transfers between devices with their start and end apart: 13, of which 5 were waited for; matrix products, arithmetic and copies ran while one was open for 0% of the time, Pallas kernels for 17%

profile of v6, /device:TPU:1, one launch (start us, length us, event | category | flops | bytes accessed | tf_op | source)
XLA Modules:
  0.0 48.8 jit_solution(17947607818093195262)
XLA Ops:
  0.6 0.0 copy-start.1
  0.6 2.7 %collective-permute-start = (bf16[2,24,1024]{2,1,0:T(8,128)(2,1)}, bf16[2,24,1024]{2,1,0:T(8,128)(2,1)S(1)}, u32[]{:S(2)}, u32[]{:S(2)}) collective-permute-start(bf16[2,24,1024]{2,1,0:T(8,128)(2,1)} %flows.5), channel_id=1, source_target_pairs={{0,1},{1,2},{2,3},{3,0},{4,5},{5,6},{6,7},{7,4},{8,9},{9,10},{10,1... | collective-permute-start | bytes 294920 | tf_op jit(solution)/shard_map/ppermute | solution.py:476
  3.3 2.2 %shard_map.130 = (s32[128]{0:T(128)S(1)}, bf16[64,128,128]{2,1,0:T(8,128)(2,1)S(1)}) custom-call(s32[1]{0:T(128)} %bitcast.1.me, s32[64]{0:T(128)} %rest_0_.1, s32[64]{0:T(128)} %rest_1_.1, s32[64]{0:T(128)} %rest_2_.1, s32[64]{0:T(128)} %slot.1, bf16[64,128,128]{2,1,0:T(8,128)(2,1)} %rest_4_.1), custom_call_target="tpu_custom_call" | custom-call | tf_op jit(solution)/shard_map/pallas_call | solution.py:478
  5.5 0.0 collective-permute-done.before
  5.5 0.0 copy-done.1
  5.6 0.0 copy-start
  5.6 0.0 copy-start.3
  5.6 0.0 copy-start.4
  5.6 0.0 copy-start.5
  5.6 0.0 copy-start.6
  5.6 2.4 %shard_map.132 = (f32[16,48,128]{2,1,0:T(8,128)S(1)}, f32[8,48,128]{2,1,0:T(8,128)S(1)}, f32[8,48,128]{2,1,0:T(8,128)S(1)}, f32[8,48,128]{2,1,0:T(8,128)S(1)}, f32[16,48,128]{2,1,0:T(8,128)S(1)}) custom-call(s32[1]{0:T(128)} %bitcast.group, s32[128]{0:T(128)S(1)} %get-tuple-element.22.ahead, bf16[2,24,1024]{2,1,0:T(8,128)(2,1)S(1)} %copy-done.1, ...), custom_call_target="tpu_custom_call" | custom-call | tf_op jit(solution)/shard_map/pallas_call | solution.py:428
  8.1 1.3 %collective-permute-start.3 = (f16[16,48,128]{2,1,0:T(8,128)(2,1)S(1)}, f16[16,48,128]{2,1,0:T(8,128)(2,1)S(1)}, u32[]{:S(2)}, u32[]{:S(2)}) collective-permute-start(f16[16,48,128]{2,1,0:T(8,128)(2,1)S(1)} %convert_element_type.38), channel_id=1, source_target_pairs={{0,4},{4,0},{8,12},{12,8},{16,20},{20,16},{24,28},{28,24},{1,5},{5... | collective-permute-start | bytes 589832 | tf_op jit(solution)/shard_map/ppermute | solution.py:492
  9.4 2.4 %collective-permute-start.2 = (f16[8,48,128]{2,1,0:T(8,128)(2,1)S(1)}, f16[8,48,128]{2,1,0:T(8,128)(2,1)S(1)}, u32[]{:S(2)}, u32[]{:S(2)}) collective-permute-start(f16[8,48,128]{2,1,0:T(8,128)(2,1)S(1)} %convert_element_type.35), channel_id=1, source_target_pairs={{0,16},{4,20},{8,24},{12,28},{16,0},{20,4},{24,8},{28,12},{1,17},{... | collective-permute-start | bytes 294920 | tf_op jit(solution)/shard_map/ppermute | solution.py:492
  11.8 0.1 collective-permute-start.1
  11.9 2.4 %collective-permute-done.3 = f16[16,48,128]{2,1,0:T(8,128)(2,1)S(1)} collective-permute-done((f16[16,48,128]{2,1,0:T(8,128)(2,1)S(1)}, f16[16,48,128]{2,1,0:T(8,128)(2,1)S(1)}, u32[]{:S(2)}, u32[]{:S(2)}) %collective-permute-start.3) | collective-permute-done | bytes 196640 | tf_op jit(solution)/shard_map/ppermute | solution.py:492
  14.4 0.0 copy-start.2
  14.4 0.1 add_convert_fusion
  14.5 0.7 %collective-permute-start.6 = (f16[8,48,128]{2,1,0:T(8,128)(2,1)S(1)}, f16[8,48,128]{2,1,0:T(8,128)(2,1)S(1)}, u32[]{:S(2)}, u32[]{:S(2)}) collective-permute-start(f16[8,48,128]{2,1,0:T(8,128)(2,1)S(1)} %get-tuple-element.42), channel_id=1, source_target_pairs={{0,8},{4,12},{8,0},{12,4},{16,24},{20,28},{24,16},{28,20},{1,9},{5... | collective-permute-start | bytes 294920 | tf_op jit(solution)/shard_map/ppermute | solution.py:492
  15.2 2.2 %collective-permute-start.5 = (f16[8,48,128]{2,1,0:T(8,128)(2,1)S(1)}, f16[8,48,128]{2,1,0:T(8,128)(2,1)S(1)}, u32[]{:S(2)}, u32[]{:S(2)}) collective-permute-start(f16[8,48,128]{2,1,0:T(8,128)(2,1)S(1)} %get-tuple-element.41), channel_id=1, source_target_pairs={{0,24},{4,28},{8,16},{12,20},{16,8},{20,12},{24,0},{28,4},{1,25},{... | collective-permute-start | bytes 294920 | tf_op jit(solution)/shard_map/ppermute | solution.py:492
  17.4 1.2 %collective-permute-start.4 = (f16[8,48,128]{2,1,0:T(8,128)(2,1)S(1)}, f16[8,48,128]{2,1,0:T(8,128)(2,1)S(1)}, u32[]{:S(2)}, u32[]{:S(2)}) collective-permute-start(f16[8,48,128]{2,1,0:T(8,128)(2,1)S(1)} %convert_element_type.37), channel_id=1, source_target_pairs={{0,4},{4,0},{8,12},{12,8},{16,20},{20,16},{24,28},{28,24},{1,5},{5... | collective-permute-start | bytes 294920 | tf_op jit(solution)/shard_map/ppermute | solution.py:492
  18.6 0.0 copy-done
  18.6 0.0 copy-done.3
  18.6 0.0 copy-done.4
  18.6 0.0 copy-done.5
  18.6 0.0 copy-done.6
  18.6 3.1 %shard_map.131 = (f32[8,48,128]{2,1,0:T(8,128)S(1)}, s32[215]{0:T(256)S(1)}) custom-call(s32[1]{0:T(128)} %bitcast.group, s32[1]{0:T(128)} %bitcast.1.me, s32[128]{0:T(128)S(1)} %get-tuple-element.22.ahead, s32[64]{0:T(128)S(1)} %copy-done.6, s32[64]{0:T(128)S(1)} %copy-done.3, s32[64]{0:T(128)S(1)} %copy-done.4, s32[64]{0:T(128)S(1)} %copy-done.5, ...), custom_call_target="tpu_custom_call" | custom-call | tf_op jit(solution)/shard_map/pallas_call | solution.py:428
  21.7 0.0 collective-permute-done.2
  21.8 0.0 collective-permute-done.1
  21.8 0.0 collective-permute-done.6
  21.8 0.0 collective-permute-done.5
  21.8 0.0 collective-permute-done.4
  21.8 0.1 convert_add_fusion.totals
  21.9 0.0 copy-done.2
  21.9 0.7 %shard_map.133 = (f32[2,24,1024]{2,1,0:T(8,128)}, bf16[8,48,128]{2,1,0:T(8,128)(2,1)S(1)}) custom-call(f32[8,48,128]{2,1,0:T(8,128)S(1)} %convert_add_fusion.totals, f32[2,24,1024]{2,1,0:T(8,128)S(1)} %copy-done.2), custom_call_target="tpu_custom_call" | custom-call | tf_op jit(solution)/shard_map/pallas_call | solution.py:428
  22.6 5.5 %collective-permute-start.8 = (bf16[8,48,128]{2,1,0:T(8,128)(2,1)S(1)}, bf16[8,48,128]{2,1,0:T(8,128)(2,1)S(1)}, u32[]{:S(2)}, u32[]{:S(2)}) collective-permute-start(bf16[8,48,128]{2,1,0:T(8,128)(2,1)S(1)} %get-tuple-element.35.signal), channel_id=1, source_target_pairs={{0,24},{4,28},{8,16},{12,20},{16,8},{20,12},{24,0},{28,4},{1,25},{... | collective-permute-start | bytes 294920 | tf_op jit(solution)/shard_map/ppermute | solution.py:492
  28.2 1.0 %collective-permute-start.7 = (bf16[8,48,128]{2,1,0:T(8,128)(2,1)S(1)}, bf16[8,48,128]{2,1,0:T(8,128)(2,1)S(1)}, u32[]{:S(2)}, u32[]{:S(2)}) collective-permute-start(bf16[8,48,128]{2,1,0:T(8,128)(2,1)S(1)} %get-tuple-element.35.signal), channel_id=1, source_target_pairs={{0,8},{4,12},{8,0},{12,4},{16,24},{20,28},{24,16},{28,20},{1,9},{5... | collective-permute-start | bytes 294920 | tf_op jit(solution)/shard_map/ppermute | solution.py:492
  29.2 0.8 %collective-permute-start.9 = (bf16[8,48,128]{2,1,0:T(8,128)(2,1)S(1)}, bf16[8,48,128]{2,1,0:T(8,128)(2,1)S(1)}, u32[]{:S(2)}, u32[]{:S(2)}) collective-permute-start(bf16[8,48,128]{2,1,0:T(8,128)(2,1)S(1)} %get-tuple-element.35.signal), channel_id=1, source_target_pairs={{0,20},{4,16},{8,28},{12,24},{16,4},{20,0},{24,12},{28,8},{1,21},{... | collective-permute-start | bytes 294920 | tf_op jit(solution)/shard_map/ppermute | solution.py:492
  29.9 2.1 %collective-permute-start.10 = (bf16[8,48,128]{2,1,0:T(8,128)(2,1)S(1)}, bf16[8,48,128]{2,1,0:T(8,128)(2,1)S(1)}, u32[]{:S(2)}, u32[]{:S(2)}) collective-permute-start(bf16[8,48,128]{2,1,0:T(8,128)(2,1)S(1)} %get-tuple-element.35.signal), channel_id=1, source_target_pairs={{0,16},{4,20},{8,24},{12,28},{16,0},{20,4},{24,8},{28,12},{1,17},{... | collective-permute-start | bytes 294920 | tf_op jit(solution)/shard_map/ppermute | solution.py:492
  32.0 0.0 collective-permute-done.8.rest_3_
  32.0 0.6 %collective-permute-done.7.rest_2_ = bf16[8,48,128]{2,1,0:T(8,128)(2,1)S(1)} collective-permute-done((bf16[8,48,128]{2,1,0:T(8,128)(2,1)S(1)}, bf16[8,48,128]{2,1,0:T(8,128)(2,1)S(1)}, u32[]{:S(2)}, u32[]{:S(2)}) %collective-permute-start.7) | collective-permute-done | bytes 98336 | tf_op jit(solution)/shard_map/ppermute | solution.py:492
  32.6 2.8 %collective-permute-start.11 = (bf16[24,48,128]{2,1,0:T(8,128)(2,1)S(1)}, bf16[24,48,128]{2,1,0:T(8,128)(2,1)S(1)}, u32[]{:S(2)}, u32[]{:S(2)}) collective-permute-start(bf16[24,48,128]{2,1,0:T(8,128)(2,1)S(1)} %pad_maximum_fusion), channel_id=1, source_target_pairs={{0,4},{4,0},{8,12},{12,8},{16,20},{20,16},{24,28},{28,24},{1,5},{5... | collective-permute-start | bytes 884744 | tf_op jit(solution)/shard_map/ppermute | solution.py:492
  35.5 1.5 %shard_map.134.start = f32[640,128]{1,0:T(8,128)S(1)} custom-call(s32[64]{0:T(128)S(1)} %copy-done.3, s32[64]{0:T(128)S(1)} %copy-done.4, s32[64]{0:T(128)S(1)} %copy-done.5, bf16[8,48,128]{2,1,0:T(8,128)(2,1)S(1)} %get-tuple-element.35.signal, bf16[64,128,128]{2,1,0:T(8,128)(2,1)S(1)} %copy-done), custom_call_target="tpu_custom_call" | custom-call | tf_op jit(solution)/shard_map/pallas_call | solution.py:428
  37.0 3.3 %collective-permute-done.9.rest_0_ = bf16[8,48,128]{2,1,0:T(8,128)(2,1)S(1)} collective-permute-done((bf16[8,48,128]{2,1,0:T(8,128)(2,1)S(1)}, bf16[8,48,128]{2,1,0:T(8,128)(2,1)S(1)}, u32[]{:S(2)}, u32[]{:S(2)}) %collective-permute-start.9) | collective-permute-done | bytes 98336 | tf_op jit(solution)/shard_map/ppermute | solution.py:492
  40.3 0.8 %collective-permute-done.10.rest_1_ = bf16[8,48,128]{2,1,0:T(8,128)(2,1)S(1)} collective-permute-done((bf16[8,48,128]{2,1,0:T(8,128)(2,1)S(1)}, bf16[8,48,128]{2,1,0:T(8,128)(2,1)S(1)}, u32[]{:S(2)}, u32[]{:S(2)}) %collective-permute-start.10) | collective-permute-done | bytes 98336 | tf_op jit(solution)/shard_map/ppermute | solution.py:492
  41.1 1.4 %shard_map.135.start = f32[640,128]{1,0:T(8,128)S(1)} custom-call(s32[215]{0:T(256)S(1)} %get-tuple-element.33.table, bf16[64,128,128]{2,1,0:T(8,128)(2,1)S(1)} %get-tuple-element.24.mats, f32[640,128]{1,0:T(8,128)S(1)} %shard_map.134.start, bf16[8,48,128]{2,1,0:T(8,128)(2,1)S(1)} %collective-permute-done.9.rest_0_, ...), custom_call_target="tpu_custom_call" | custom-call | flops 2700000000 | bytes 8100000 | tf_op jit(solution)/shard_map/pallas_call | solution.py:428
  42.5 0.0 collective-permute-done.11.rest_0_
  42.5 1.1 %shard_map.136 = (f32[640,128]{1,0:T(8,128)S(1)}, f32[16,16,128]{2,1,0:T(8,128)S(1)}) custom-call(s32[215]{0:T(256)S(1)} %get-tuple-element.33.table, bf16[64,128,128]{2,1,0:T(8,128)(2,1)S(1)} %get-tuple-element.24.mats, f32[640,128]{1,0:T(8,128)S(1)} %shard_map.135.start, bf16[24,48,128]{2,1,0:T(8,128)(2,1)S(1)} %collective-permute-done.11.rest_0_), custom_call_target="tpu_custom_call" | custom-call | tf_op jit(solution)/shard_map/pallas_call | solution.py:428
  43.6 2.2 %collective-permute-start.12 = (f32[16,16,128]{2,1,0:T(8,128)S(1)}, f32[16,16,128]{2,1,0:T(8,128)S(1)}, u32[]{:S(2)}, u32[]{:S(2)}) collective-permute-start(f32[16,16,128]{2,1,0:T(8,128)S(1)} %get-tuple-element.38), channel_id=1, source_target_pairs={{0,3},{1,0},{2,1},{3,2},{4,7},{5,4},{6,5},{7,6},{8,11},{9,8},{10,9... | collective-permute-start | bytes 393224 | tf_op jit(solution)/shard_map/ppermute | solution.py:554
  45.8 2.3 %collective-permute-done.12.spill = f32[16,16,128]{2,1,0:T(8,128)S(1)} collective-permute-done((f32[16,16,128]{2,1,0:T(8,128)S(1)}, f32[16,16,128]{2,1,0:T(8,128)S(1)}, u32[]{:S(2)}, u32[]{:S(2)}) %collective-permute-start.12) | collective-permute-done | bytes 131104 | tf_op jit(solution)/shard_map/ppermute | solution.py:554
  48.0 0.8 %shard_map.137 = (f32[2,24,1024]{2,1,0:T(8,128)}, f32[2,24,1024]{2,1,0:T(8,128)}) custom-call(s32[1]{0:T(128)} %bitcast.group, f32[640,128]{1,0:T(8,128)S(1)} %get-tuple-element.37.total, f32[16,16,128]{2,1,0:T(8,128)S(1)} %collective-permute-done.12.spill, bf16[2,24,1024]{2,1,0:T(8,128)(2,1)S(1)} %copy-done.1), custom_call_target="tpu_custom_call" | custom-call | tf_op jit(solution)/shard_map/pallas_call | solution.py:428
  (6 shorter events, 0.2 us)
Async XLA Ops:
  0.6 4.9 %copy-start.1 = (bf16[2,24,1024]{2,1,0:T(8,128)(2,1)S(1)}, bf16[2,24,1024]{2,1,0:T(8,128)(2,1)}, u32[]{:S(2)}) copy-start(bf16[2,24,1024]{2,1,0:T(8,128)(2,1)} %flows.5) | copy-start | bytes 294916
  0.6 4.9 %collective-permute-start = (bf16[2,24,1024]{2,1,0:T(8,128)(2,1)}, bf16[2,24,1024]{2,1,0:T(8,128)(2,1)S(1)}, u32[]{:S(2)}, u32[]{:S(2)}) collective-permute-start(bf16[2,24,1024]{2,1,0:T(8,128)(2,1)} %flows.5), channel_id=1, source_target_pairs={{0,1},{1,2},{2,3},{3,0},{4,5},{5,6},{6,7},{7,4},{8,9},{9,10},{10,1... | collective-permute-start | bytes 294920 | tf_op jit(solution)/shard_map/ppermute | solution.py:476
  5.6 13.0 %copy-start = (bf16[64,128,128]{2,1,0:T(8,128)(2,1)S(1)}, bf16[64,128,128]{2,1,0:T(8,128)(2,1)}, u32[]{:S(2)}) copy-start(bf16[64,128,128]{2,1,0:T(8,128)(2,1)} %mats.3) | copy-start | bytes 6291460
  5.6 13.0 %copy-start.3 = (s32[64]{0:T(128)S(1)}, s32[64]{0:T(128)}, u32[]{:S(2)}) copy-start(s32[64]{0:T(128)} %path.3) | copy-start | bytes 772
  5.6 13.0 %copy-start.4 = (s32[64]{0:T(128)S(1)}, s32[64]{0:T(128)}, u32[]{:S(2)}) copy-start(s32[64]{0:T(128)} %link.3) | copy-start | bytes 772
  5.6 13.0 %copy-start.5 = (s32[64]{0:T(128)S(1)}, s32[64]{0:T(128)}, u32[]{:S(2)}) copy-start(s32[64]{0:T(128)} %lag.3) | copy-start | bytes 772
  5.6 13.0 %copy-start.6 = (s32[64]{0:T(128)S(1)}, s32[64]{0:T(128)}, u32[]{:S(2)}) copy-start(s32[64]{0:T(128)} %slot.1) | copy-start | bytes 772
  8.1 6.3 %collective-permute-start.3 = (f16[16,48,128]{2,1,0:T(8,128)(2,1)S(1)}, f16[16,48,128]{2,1,0:T(8,128)(2,1)S(1)}, u32[]{:S(2)}, u32[]{:S(2)}) collective-permute-start(f16[16,48,128]{2,1,0:T(8,128)(2,1)S(1)} %convert_element_type.38), channel_id=1, source_target_pairs={{0,4},{4,0},{8,12},{12,8},{16,20},{20,16},{24,28},{28,24},{1,5},{5... | collective-permute-start | bytes 589832 | tf_op jit(solution)/shard_map/ppermute | solution.py:492
  9.4 12.3 %collective-permute-start.2 = (f16[8,48,128]{2,1,0:T(8,128)(2,1)S(1)}, f16[8,48,128]{2,1,0:T(8,128)(2,1)S(1)}, u32[]{:S(2)}, u32[]{:S(2)}) collective-permute-start(f16[8,48,128]{2,1,0:T(8,128)(2,1)S(1)} %convert_element_type.35), channel_id=1, source_target_pairs={{0,16},{4,20},{8,24},{12,28},{16,0},{20,4},{24,8},{28,12},{1,17},{... | collective-permute-start | bytes 294920 | tf_op jit(solution)/shard_map/ppermute | solution.py:492
  11.8 9.9 %collective-permute-start.1 = (f16[8,48,128]{2,1,0:T(8,128)(2,1)S(1)}, f16[8,48,128]{2,1,0:T(8,128)(2,1)S(1)}, u32[]{:S(2)}, u32[]{:S(2)}) collective-permute-start(f16[8,48,128]{2,1,0:T(8,128)(2,1)S(1)} %convert_element_type.33), channel_id=1, source_target_pairs={{0,20},{4,16},{8,28},{12,24},{16,4},{20,0},{24,12},{28,8},{1,21},{... | collective-permute-start | bytes 294920 | tf_op jit(solution)/shard_map/ppermute | solution.py:492
  14.4 7.5 %copy-start.2 = (f32[2,24,1024]{2,1,0:T(8,128)S(1)}, f32[2,24,1024]{2,1,0:T(8,128)}, u32[]{:S(2)}) copy-start(f32[2,24,1024]{2,1,0:T(8,128)} %counts.1) | copy-start | bytes 589828
  14.5 7.3 %collective-permute-start.6 = (f16[8,48,128]{2,1,0:T(8,128)(2,1)S(1)}, f16[8,48,128]{2,1,0:T(8,128)(2,1)S(1)}, u32[]{:S(2)}, u32[]{:S(2)}) collective-permute-start(f16[8,48,128]{2,1,0:T(8,128)(2,1)S(1)} %get-tuple-element.42), channel_id=1, source_target_pairs={{0,8},{4,12},{8,0},{12,4},{16,24},{20,28},{24,16},{28,20},{1,9},{5... | collective-permute-start | bytes 294920 | tf_op jit(solution)/shard_map/ppermute | solution.py:492
  15.2 6.6 %collective-permute-start.5 = (f16[8,48,128]{2,1,0:T(8,128)(2,1)S(1)}, f16[8,48,128]{2,1,0:T(8,128)(2,1)S(1)}, u32[]{:S(2)}, u32[]{:S(2)}) collective-permute-start(f16[8,48,128]{2,1,0:T(8,128)(2,1)S(1)} %get-tuple-element.41), channel_id=1, source_target_pairs={{0,24},{4,28},{8,16},{12,20},{16,8},{20,12},{24,0},{28,4},{1,25},{... | collective-permute-start | bytes 294920 | tf_op jit(solution)/shard_map/ppermute | solution.py:492
  17.4 4.4 %collective-permute-start.4 = (f16[8,48,128]{2,1,0:T(8,128)(2,1)S(1)}, f16[8,48,128]{2,1,0:T(8,128)(2,1)S(1)}, u32[]{:S(2)}, u32[]{:S(2)}) collective-permute-start(f16[8,48,128]{2,1,0:T(8,128)(2,1)S(1)} %convert_element_type.37), channel_id=1, source_target_pairs={{0,4},{4,0},{8,12},{12,8},{16,20},{20,16},{24,28},{28,24},{1,5},{5... | collective-permute-start | bytes 294920 | tf_op jit(solution)/shard_map/ppermute | solution.py:492
  22.6 9.4 %collective-permute-start.8 = (bf16[8,48,128]{2,1,0:T(8,128)(2,1)S(1)}, bf16[8,48,128]{2,1,0:T(8,128)(2,1)S(1)}, u32[]{:S(2)}, u32[]{:S(2)}) collective-permute-start(bf16[8,48,128]{2,1,0:T(8,128)(2,1)S(1)} %get-tuple-element.35.signal), channel_id=1, source_target_pairs={{0,24},{4,28},{8,16},{12,20},{16,8},{20,12},{24,0},{28,4},{1,25},{... | collective-permute-start | bytes 294920 | tf_op jit(solution)/shard_map/ppermute | solution.py:492
  28.2 4.4 %collective-permute-start.7 = (bf16[8,48,128]{2,1,0:T(8,128)(2,1)S(1)}, bf16[8,48,128]{2,1,0:T(8,128)(2,1)S(1)}, u32[]{:S(2)}, u32[]{:S(2)}) collective-permute-start(bf16[8,48,128]{2,1,0:T(8,128)(2,1)S(1)} %get-tuple-element.35.signal), channel_id=1, source_target_pairs={{0,8},{4,12},{8,0},{12,4},{16,24},{20,28},{24,16},{28,20},{1,9},{5... | collective-permute-start | bytes 294920 | tf_op jit(solution)/shard_map/ppermute | solution.py:492
  29.2 11.1 %collective-permute-start.9 = (bf16[8,48,128]{2,1,0:T(8,128)(2,1)S(1)}, bf16[8,48,128]{2,1,0:T(8,128)(2,1)S(1)}, u32[]{:S(2)}, u32[]{:S(2)}) collective-permute-start(bf16[8,48,128]{2,1,0:T(8,128)(2,1)S(1)} %get-tuple-element.35.signal), channel_id=1, source_target_pairs={{0,20},{4,16},{8,28},{12,24},{16,4},{20,0},{24,12},{28,8},{1,21},{... | collective-permute-start | bytes 294920 | tf_op jit(solution)/shard_map/ppermute | solution.py:492
  29.9 11.2 %collective-permute-start.10 = (bf16[8,48,128]{2,1,0:T(8,128)(2,1)S(1)}, bf16[8,48,128]{2,1,0:T(8,128)(2,1)S(1)}, u32[]{:S(2)}, u32[]{:S(2)}) collective-permute-start(bf16[8,48,128]{2,1,0:T(8,128)(2,1)S(1)} %get-tuple-element.35.signal), channel_id=1, source_target_pairs={{0,16},{4,20},{8,24},{12,28},{16,0},{20,4},{24,8},{28,12},{1,17},{... | collective-permute-start | bytes 294920 | tf_op jit(solution)/shard_map/ppermute | solution.py:492
  32.6 9.9 %collective-permute-start.11 = (bf16[24,48,128]{2,1,0:T(8,128)(2,1)S(1)}, bf16[24,48,128]{2,1,0:T(8,128)(2,1)S(1)}, u32[]{:S(2)}, u32[]{:S(2)}) collective-permute-start(bf16[24,48,128]{2,1,0:T(8,128)(2,1)S(1)} %pad_maximum_fusion), channel_id=1, source_target_pairs={{0,4},{4,0},{8,12},{12,8},{16,20},{20,16},{24,28},{28,24},{1,5},{5... | collective-permute-start | bytes 884744 | tf_op jit(solution)/shard_map/ppermute | solution.py:492
  43.6 4.4 %collective-permute-start.12 = (f32[16,16,128]{2,1,0:T(8,128)S(1)}, f32[16,16,128]{2,1,0:T(8,128)S(1)}, u32[]{:S(2)}, u32[]{:S(2)}) collective-permute-start(f32[16,16,128]{2,1,0:T(8,128)S(1)} %get-tuple-element.38), channel_id=1, source_target_pairs={{0,3},{1,0},{2,1},{3,2},{4,7},{5,4},{6,5},{7,6},{8,11},{9,8},{10,9... | collective-permute-start | bytes 393224 | tf_op jit(solution)/shard_map/ppermute | solution.py:554

commit v7 on v6

--- a/solution.py
+++ b/solution.py
@@ -460,7 +460,7 @@
     through = sorted({2, corridors - 2})
     crossing = [s ^ 1 for s in through]
     direct = [s for s in range(corridors - 1, 1, -1) if s not in through + crossing]
-    order = crossing + [1] + direct + through
+    order = crossing + direct + [1] + through
     many = len(through)
     cuts = [0, *range(many, len(order) - many + 1), len(order)]
     t = Table(len(order), corridors * cap, remotes)
@@ -500,8 +500,8 @@
         [wide, pltpu.VMEM((len(order) * links, *piece[1:]), f32)],
     )
     crossed = exchanged(crossed.astype(WIRE), 1)
-    near, crossed = lax.optimization_barrier((parts[0].astype(WIRE), crossed))
-    received = [exchanged(p.astype(WIRE), s) for p, s in zip(parts[1:], direct)]
+    near, crossed = lax.optimization_barrier((parts[-1].astype(WIRE), crossed))
+    received = [exchanged(p.astype(WIRE), s) for p, s in zip(parts[:-1], direct)]
     received.append(exchanged(near, 1))
     own, table = kernel_call(
         functools.partial(forward_local_kernel, days, cap, order, t, links),
@@ -521,8 +521,9 @@
         [shape(counts.shape, f32), shape(piece, jnp.bfloat16)],
     )
     arrived = [exchanged(signal, s) for s in (*through, *direct)]
-    both = jnp.concatenate([*arrived[:many], signal], axis=0)
-    both, signal = lax.optimization_barrier((both, signal))
+    near = exchanged(signal, 1)
+    passed = [exchanged(a, 1) for a in arrived[:many]]
+    *held, signal = lax.optimization_barrier((*arrived[:many], signal))
     rows = [shape((paths * days * span, width), f32)]
     (total,) = kernel_call(
         functools.partial(backward_local_kernel, days),
@@ -530,18 +531,17 @@
         (signal, local_blocks),
         rows,
     )
-    passed = exchanged(both, 1)
     def weigh(first):
         if first == 0:
             return None
         return pl.CostEstimate(
-            flops=2_700_000_000, transcendentals=0, bytes_accessed=8_100_000
+            flops=500_000_000, transcendentals=0, bytes_accessed=1_500_000
         )
 
     edge = shape((paths * days, HALO, width), f32)
     for first, end, signals, made in (
-        (many + 1, len(order), [*arrived[many:], *arrived[:many]], rows),
-        (0, many + 1, [passed], [*rows, edge]),
+        (many, len(order), [*arrived[many:], near, *held], rows),
+        (0, many, passed, [*rows, edge]),
     ):
         total, *early = kernel_call(
             functools.partial(backward_remote_kernel, days, cap, first, end, links, t),

time: 49.2 us -> 50.9 us (1.035)
  waiting for transfers between devices: 9.39 us -> 13 us
  starting transfers between devices: 25 us -> 23.3 us
    ppermute x11 -> x13, waiting for transfers between devices: 7.1 us -> 9.58 us  [exchanged(): return lax.ppermute(part, 'corr', [(i, i ^ s) for i in range(corridors)])]
    ppermute x1, starting transfers between devices: 2.16 us -> 1.04 us  [per_device_dense(): lax.ppermute(early[0], 'tm', [(i, (i - 1) % groups) for i in range(groups)])]
    ppermute x1, waiting for transfers between devices: 2.29 us -> 3.4 us  [per_device_dense(): lax.ppermute(early[0], 'tm', [(i, (i - 1) % groups) for i in range(groups)])]
    ppermute x11 -> x13, starting transfers between devices: 20.1 us -> 19.6 us  [exchanged(): return lax.ppermute(part, 'corr', [(i, i ^ s) for i in range(corridors)])]
  transfers between devices with their start and end apart: 13 -> 15, of which waited for: 5 -> 5; matrix products, arithmetic and copies ran while one was open for 0% -> 0% of each run, Pallas kernels for 17% -> 17%
where the time goes in v7:
time: 50.9 us; the launch traced here: 50.7 us
  starting transfers between devices  23.3 us (46%)
  Pallas kernels  13.3 us (26%)
  waiting for transfers between devices  13 us (26%)
  between operations  0.86 us (2%)
    ppermute x13, starting transfers between devices, exchanged(): return lax.ppermute(part, 'corr', [(i, i ^ s) for i in range(corridors)])  19.6 us
    pallas_call x7, Pallas kernels, kernel_call(): pl.pallas_call(body, out_shape=out_shape, in_specs=[SMEM] * len(scalars)...  11.1 us
    ppermute x13, waiting for transfers between devices, exchanged(): return lax.ppermute(part, 'corr', [(i, i ^ s) for i in range(corridors)])  9.58 us
    ppermute x1, waiting for transfers between devices, per_device_dense(): lax.ppermute(early[0], 'tm', [(i, (i - 1) % groups) for i in range(groups)])  3.4 us
    ppermute x1, starting transfers between devices, per_device_dense(): lax.ppermute(flows, 'tm', [(i, (i + 1) % groups) for i in range(groups)])  2.68 us
    pallas_call x1, Pallas kernels, per_device_dense(): pl.pallas_call(functools.partial(prepare_kernel, cap, order, links, CHUNK...  2.2 us
    ppermute x1, starting transfers between devices, per_device_dense(): lax.ppermute(early[0], 'tm', [(i, (i - 1) % groups) for i in range(groups)])  1.04 us
  transfers between devices with their start and end apart: 15, of which 5 were waited for; matrix products, arithmetic and copies ran while one was open for 0% of the time, Pallas kernels for 17%

profile of v7, /device:TPU:1, one launch (start us, length us, event | category | flops | bytes accessed | tf_op | source)
XLA Modules:
  0.0 50.7 jit_solution(5461688811737557614)
XLA Ops:
  0.6 0.0 copy-start.1
  0.6 2.7 %collective-permute-start = (bf16[2,24,1024]{2,1,0:T(8,128)(2,1)}, bf16[2,24,1024]{2,1,0:T(8,128)(2,1)S(1)}, u32[]{:S(2)}, u32[]{:S(2)}) collective-permute-start(bf16[2,24,1024]{2,1,0:T(8,128)(2,1)} %flows.5), channel_id=1, source_target_pairs={{0,1},{1,2},{2,3},{3,0},{4,5},{5,6},{6,7},{7,4},{8,9},{9,10},{10,1... | collective-permute-start | bytes 294920 | tf_op jit(solution)/shard_map/ppermute | solution.py:476
  3.3 2.2 %shard_map.130 = (s32[128]{0:T(128)S(1)}, bf16[64,128,128]{2,1,0:T(8,128)(2,1)S(1)}) custom-call(s32[1]{0:T(128)} %bitcast.1.me, s32[64]{0:T(128)} %rest_0_.1, s32[64]{0:T(128)} %rest_1_.1, s32[64]{0:T(128)} %rest_2_.1, s32[64]{0:T(128)} %slot.1, bf16[64,128,128]{2,1,0:T(8,128)(2,1)} %rest_4_.1), custom_call_target="tpu_custom_call" | custom-call | tf_op jit(solution)/shard_map/pallas_call | solution.py:478
  5.5 0.0 collective-permute-done.before
  5.5 0.0 copy-done.1
  5.6 0.0 copy-start
  5.6 0.0 copy-start.3
  5.6 0.0 copy-start.4
  5.6 0.0 copy-start.5
  5.6 0.0 copy-start.6
  5.6 2.4 %shard_map.132 = (f32[16,48,128]{2,1,0:T(8,128)S(1)}, f32[8,48,128]{2,1,0:T(8,128)S(1)}, f32[8,48,128]{2,1,0:T(8,128)S(1)}, f32[8,48,128]{2,1,0:T(8,128)S(1)}, f32[16,48,128]{2,1,0:T(8,128)S(1)}) custom-call(s32[1]{0:T(128)} %bitcast.group, s32[128]{0:T(128)S(1)} %get-tuple-element.23.ahead, bf16[2,24,1024]{2,1,0:T(8,128)(2,1)S(1)} %copy-done.1, ...), custom_call_target="tpu_custom_call" | custom-call | tf_op jit(solution)/shard_map/pallas_call | solution.py:428
  8.1 1.3 %collective-permute-start.3 = (f16[16,48,128]{2,1,0:T(8,128)(2,1)S(1)}, f16[16,48,128]{2,1,0:T(8,128)(2,1)S(1)}, u32[]{:S(2)}, u32[]{:S(2)}) collective-permute-start(f16[16,48,128]{2,1,0:T(8,128)(2,1)S(1)} %convert_element_type.38), channel_id=1, source_target_pairs={{0,4},{4,0},{8,12},{12,8},{16,20},{20,16},{24,28},{28,24},{1,5},{5... | collective-permute-start | bytes 589832 | tf_op jit(solution)/shard_map/ppermute | solution.py:492
  9.4 2.4 %collective-permute-start.2 = (f16[8,48,128]{2,1,0:T(8,128)(2,1)S(1)}, f16[8,48,128]{2,1,0:T(8,128)(2,1)S(1)}, u32[]{:S(2)}, u32[]{:S(2)}) collective-permute-start(f16[8,48,128]{2,1,0:T(8,128)(2,1)S(1)} %convert_element_type.35), channel_id=1, source_target_pairs={{0,16},{4,20},{8,24},{12,28},{16,0},{20,4},{24,8},{28,12},{1,17},{... | collective-permute-start | bytes 294920 | tf_op jit(solution)/shard_map/ppermute | solution.py:492
  11.8 0.1 collective-permute-start.1
  11.9 2.4 %collective-permute-done.3 = f16[16,48,128]{2,1,0:T(8,128)(2,1)S(1)} collective-permute-done((f16[16,48,128]{2,1,0:T(8,128)(2,1)S(1)}, f16[16,48,128]{2,1,0:T(8,128)(2,1)S(1)}, u32[]{:S(2)}, u32[]{:S(2)}) %collective-permute-start.3) | collective-permute-done | bytes 196640 | tf_op jit(solution)/shard_map/ppermute | solution.py:492
  14.3 0.0 copy-start.2
  14.3 0.1 add_convert_fusion
  14.5 0.7 %collective-permute-start.6 = (f16[8,48,128]{2,1,0:T(8,128)(2,1)S(1)}, f16[8,48,128]{2,1,0:T(8,128)(2,1)S(1)}, u32[]{:S(2)}, u32[]{:S(2)}) collective-permute-start(f16[8,48,128]{2,1,0:T(8,128)(2,1)S(1)} %get-tuple-element.44), channel_id=1, source_target_pairs={{0,8},{4,12},{8,0},{12,4},{16,24},{20,28},{24,16},{28,20},{1,9},{5... | collective-permute-start | bytes 294920 | tf_op jit(solution)/shard_map/ppermute | solution.py:492
  15.2 2.2 %collective-permute-start.5 = (f16[8,48,128]{2,1,0:T(8,128)(2,1)S(1)}, f16[8,48,128]{2,1,0:T(8,128)(2,1)S(1)}, u32[]{:S(2)}, u32[]{:S(2)}) collective-permute-start(f16[8,48,128]{2,1,0:T(8,128)(2,1)S(1)} %get-tuple-element.43), channel_id=1, source_target_pairs={{0,24},{4,28},{8,16},{12,20},{16,8},{20,12},{24,0},{28,4},{1,25},{... | collective-permute-start | bytes 294920 | tf_op jit(solution)/shard_map/ppermute | solution.py:492
  17.4 1.2 %collective-permute-start.4 = (f16[8,48,128]{2,1,0:T(8,128)(2,1)S(1)}, f16[8,48,128]{2,1,0:T(8,128)(2,1)S(1)}, u32[]{:S(2)}, u32[]{:S(2)}) collective-permute-start(f16[8,48,128]{2,1,0:T(8,128)(2,1)S(1)} %convert_element_type.37), channel_id=1, source_target_pairs={{0,4},{4,0},{8,12},{12,8},{16,20},{20,16},{24,28},{28,24},{1,5},{5... | collective-permute-start | bytes 294920 | tf_op jit(solution)/shard_map/ppermute | solution.py:492
  18.6 0.0 copy-done
  18.6 0.0 copy-done.3
  18.6 0.0 copy-done.4
  18.6 0.0 copy-done.5
  18.6 0.0 copy-done.6
  18.6 3.1 %shard_map.131 = (f32[8,48,128]{2,1,0:T(8,128)S(1)}, s32[215]{0:T(256)S(1)}) custom-call(s32[1]{0:T(128)} %bitcast.group, s32[1]{0:T(128)} %bitcast.1.me, s32[128]{0:T(128)S(1)} %get-tuple-element.23.ahead, s32[64]{0:T(128)S(1)} %copy-done.6, s32[64]{0:T(128)S(1)} %copy-done.3, s32[64]{0:T(128)S(1)} %copy-done.4, s32[64]{0:T(128)S(1)} %copy-done.5, ...), custom_call_target="tpu_custom_call" | custom-call | tf_op jit(solution)/shard_map/pallas_call | solution.py:428
  21.7 0.0 collective-permute-done.2
  21.8 0.0 collective-permute-done.1
  21.8 0.0 collective-permute-done.6
  21.8 0.0 collective-permute-done.5
  21.8 0.0 collective-permute-done.4
  21.8 0.1 convert_add_fusion.totals
  21.9 0.0 copy-done.2
  21.9 0.7 %shard_map.133 = (f32[2,24,1024]{2,1,0:T(8,128)}, bf16[8,48,128]{2,1,0:T(8,128)(2,1)S(1)}) custom-call(f32[8,48,128]{2,1,0:T(8,128)S(1)} %convert_add_fusion.totals, f32[2,24,1024]{2,1,0:T(8,128)S(1)} %copy-done.2), custom_call_target="tpu_custom_call" | custom-call | tf_op jit(solution)/shard_map/pallas_call | solution.py:428
  22.6 4.3 %collective-permute-start.7 = (bf16[8,48,128]{2,1,0:T(8,128)(2,1)S(1)}, bf16[8,48,128]{2,1,0:T(8,128)(2,1)S(1)}, u32[]{:S(2)}, u32[]{:S(2)}) collective-permute-start(bf16[8,48,128]{2,1,0:T(8,128)(2,1)S(1)} %get-tuple-element.36.signal), channel_id=1, source_target_pairs={{0,8},{4,12},{8,0},{12,4},{16,24},{20,28},{24,16},{28,20},{1,9},{5... | collective-permute-start | bytes 294920 | tf_op jit(solution)/shard_map/ppermute | solution.py:492
  27.0 3.1 %collective-permute-start.8 = (bf16[8,48,128]{2,1,0:T(8,128)(2,1)S(1)}, bf16[8,48,128]{2,1,0:T(8,128)(2,1)S(1)}, u32[]{:S(2)}, u32[]{:S(2)}) collective-permute-start(bf16[8,48,128]{2,1,0:T(8,128)(2,1)S(1)} %get-tuple-element.36.signal), channel_id=1, source_target_pairs={{0,24},{4,28},{8,16},{12,20},{16,8},{20,12},{24,0},{28,4},{1,25},{... | collective-permute-start | bytes 294920 | tf_op jit(solution)/shard_map/ppermute | solution.py:492
  30.1 0.0 collective-permute-start.9
  30.1 2.3 %collective-permute-start.10 = (bf16[8,48,128]{2,1,0:T(8,128)(2,1)S(1)}, bf16[8,48,128]{2,1,0:T(8,128)(2,1)S(1)}, u32[]{:S(2)}, u32[]{:S(2)}) collective-permute-start(bf16[8,48,128]{2,1,0:T(8,128)(2,1)S(1)} %get-tuple-element.36.signal), channel_id=1, source_target_pairs={{0,16},{4,20},{8,24},{12,28},{16,0},{20,4},{24,8},{28,12},{1,17},{... | collective-permute-start | bytes 294920 | tf_op jit(solution)/shard_map/ppermute | solution.py:492
  32.3 1.3 %collective-permute-start.11 = (bf16[8,48,128]{2,1,0:T(8,128)(2,1)S(1)}, bf16[8,48,128]{2,1,0:T(8,128)(2,1)S(1)}, u32[]{:S(2)}, u32[]{:S(2)}) collective-permute-start(bf16[8,48,128]{2,1,0:T(8,128)(2,1)S(1)} %get-tuple-element.36.signal), channel_id=1, source_target_pairs={{0,4},{4,0},{8,12},{12,8},{16,20},{20,16},{24,28},{28,24},{1,5},{5... | collective-permute-start | bytes 294920 | tf_op jit(solution)/shard_map/ppermute | solution.py:492
  33.6 0.0 collective-permute-done.7.rest_3_
  33.6 0.2 collective-permute-start.12
  33.8 0.8 %collective-permute-done.8.rest_4_ = bf16[8,48,128]{2,1,0:T(8,128)(2,1)S(1)} collective-permute-done((bf16[8,48,128]{2,1,0:T(8,128)(2,1)S(1)}, bf16[8,48,128]{2,1,0:T(8,128)(2,1)S(1)}, u32[]{:S(2)}, u32[]{:S(2)}) %collective-permute-start.8) | collective-permute-done | bytes 98336 | tf_op jit(solution)/shard_map/ppermute | solution.py:492
  34.6 0.5 %collective-permute-start.13 = (bf16[8,48,128]{2,1,0:T(8,128)(2,1)S(1)}, bf16[8,48,128]{2,1,0:T(8,128)(2,1)S(1)}, u32[]{:S(2)}, u32[]{:S(2)}) collective-permute-start(bf16[8,48,128]{2,1,0:T(8,128)(2,1)S(1)} %collective-permute-done.8.rest_4_), channel_id=1, source_target_pairs={{0,4},{4,0},{8,12},{12,8},{16,20},{20,16},{24,28},{28,24},{1,5},{5... | collective-permute-start | bytes 294920 | tf_op jit(solution)/shard_map/ppermute | solution.py:492
  35.1 1.5 %shard_map.134.start = f32[640,128]{1,0:T(8,128)S(1)} custom-call(s32[64]{0:T(128)S(1)} %copy-done.3, s32[64]{0:T(128)S(1)} %copy-done.4, s32[64]{0:T(128)S(1)} %copy-done.5, bf16[8,48,128]{2,1,0:T(8,128)(2,1)S(1)} %get-tuple-element.36.signal, bf16[64,128,128]{2,1,0:T(8,128)(2,1)S(1)} %copy-done), custom_call_target="tpu_custom_call" | custom-call | tf_op jit(solution)/shard_map/pallas_call | solution.py:428
  36.6 5.0 %collective-permute-done.9.rest_0_ = bf16[8,48,128]{2,1,0:T(8,128)(2,1)S(1)} collective-permute-done((bf16[8,48,128]{2,1,0:T(8,128)(2,1)S(1)}, bf16[8,48,128]{2,1,0:T(8,128)(2,1)S(1)}, u32[]{:S(2)}, u32[]{:S(2)}) %collective-permute-start.9) | collective-permute-done | bytes 98336 | tf_op jit(solution)/shard_map/ppermute | solution.py:492
  41.7 1.4 %collective-permute-done.10.rest_1_ = bf16[8,48,128]{2,1,0:T(8,128)(2,1)S(1)} collective-permute-done((bf16[8,48,128]{2,1,0:T(8,128)(2,1)S(1)}, bf16[8,48,128]{2,1,0:T(8,128)(2,1)S(1)}, u32[]{:S(2)}, u32[]{:S(2)}) %collective-permute-start.10) | collective-permute-done | bytes 98336 | tf_op jit(solution)/shard_map/ppermute | solution.py:492
  43.0 0.0 collective-permute-done.11.rest_2_
  43.0 1.5 %shard_map.135.start = f32[640,128]{1,0:T(8,128)S(1)} custom-call(s32[215]{0:T(256)S(1)} %get-tuple-element.34.table, bf16[64,128,128]{2,1,0:T(8,128)(2,1)S(1)} %get-tuple-element.25.mats, f32[640,128]{1,0:T(8,128)S(1)} %shard_map.134.start, bf16[8,48,128]{2,1,0:T(8,128)(2,1)S(1)} %collective-permute-done.9.rest_0_, ...), custom_call_target="tpu_custom_call" | custom-call | flops 500000000 | bytes 1500000 | tf_op jit(solution)/shard_map/pallas_call | solution.py:428
  44.6 0.0 collective-permute-done.12.rest_0_
  44.6 0.0 collective-permute-done.13.rest_1_
  44.6 0.9 %shard_map.136 = (f32[640,128]{1,0:T(8,128)S(1)}, f32[16,16,128]{2,1,0:T(8,128)S(1)}) custom-call(s32[215]{0:T(256)S(1)} %get-tuple-element.34.table, bf16[64,128,128]{2,1,0:T(8,128)(2,1)S(1)} %get-tuple-element.25.mats, f32[640,128]{1,0:T(8,128)S(1)} %shard_map.135.start, bf16[8,48,128]{2,1,0:T(8,128)(2,1)S(1)} %collective-permute-done.12.rest_0_, ...), custom_call_target="tpu_custom_call" | custom-call | tf_op jit(solution)/shard_map/pallas_call | solution.py:428
  45.5 1.0 %collective-permute-start.14 = (f32[16,16,128]{2,1,0:T(8,128)S(1)}, f32[16,16,128]{2,1,0:T(8,128)S(1)}, u32[]{:S(2)}, u32[]{:S(2)}) collective-permute-start(f32[16,16,128]{2,1,0:T(8,128)S(1)} %get-tuple-element.40), channel_id=1, source_target_pairs={{0,3},{1,0},{2,1},{3,2},{4,7},{5,4},{6,5},{7,6},{8,11},{9,8},{10,9... | collective-permute-start | bytes 393224 | tf_op jit(solution)/shard_map/ppermute | solution.py:554
  46.6 3.4 %collective-permute-done.14.spill = f32[16,16,128]{2,1,0:T(8,128)S(1)} collective-permute-done((f32[16,16,128]{2,1,0:T(8,128)S(1)}, f32[16,16,128]{2,1,0:T(8,128)S(1)}, u32[]{:S(2)}, u32[]{:S(2)}) %collective-permute-start.14) | collective-permute-done | bytes 131104 | tf_op jit(solution)/shard_map/ppermute | solution.py:554
  50.0 0.8 %shard_map.137 = (f32[2,24,1024]{2,1,0:T(8,128)}, f32[2,24,1024]{2,1,0:T(8,128)}) custom-call(s32[1]{0:T(128)} %bitcast.group, f32[640,128]{1,0:T(8,128)S(1)} %get-tuple-element.39.total, f32[16,16,128]{2,1,0:T(8,128)S(1)} %collective-permute-done.14.spill, bf16[2,24,1024]{2,1,0:T(8,128)(2,1)S(1)} %copy-done.1), custom_call_target="tpu_custom_call" | custom-call | tf_op jit(solution)/shard_map/pallas_call | solution.py:428
  (5 shorter events, 0.1 us)
Async XLA Ops:
  0.6 4.9 %copy-start.1 = (bf16[2,24,1024]{2,1,0:T(8,128)(2,1)S(1)}, bf16[2,24,1024]{2,1,0:T(8,128)(2,1)}, u32[]{:S(2)}) copy-start(bf16[2,24,1024]{2,1,0:T(8,128)(2,1)} %flows.5) | copy-start | bytes 294916
  0.6 4.9 %collective-permute-start = (bf16[2,24,1024]{2,1,0:T(8,128)(2,1)}, bf16[2,24,1024]{2,1,0:T(8,128)(2,1)S(1)}, u32[]{:S(2)}, u32[]{:S(2)}) collective-permute-start(bf16[2,24,1024]{2,1,0:T(8,128)(2,1)} %flows.5), channel_id=1, source_target_pairs={{0,1},{1,2},{2,3},{3,0},{4,5},{5,6},{6,7},{7,4},{8,9},{9,10},{10,1... | collective-permute-start | bytes 294920 | tf_op jit(solution)/shard_map/ppermute | solution.py:476
  5.6 13.0 %copy-start = (bf16[64,128,128]{2,1,0:T(8,128)(2,1)S(1)}, bf16[64,128,128]{2,1,0:T(8,128)(2,1)}, u32[]{:S(2)}) copy-start(bf16[64,128,128]{2,1,0:T(8,128)(2,1)} %mats.3) | copy-start | bytes 6291460
  5.6 13.0 %copy-start.3 = (s32[64]{0:T(128)S(1)}, s32[64]{0:T(128)}, u32[]{:S(2)}) copy-start(s32[64]{0:T(128)} %path.3) | copy-start | bytes 772
  5.6 13.0 %copy-start.4 = (s32[64]{0:T(128)S(1)}, s32[64]{0:T(128)}, u32[]{:S(2)}) copy-start(s32[64]{0:T(128)} %link.3) | copy-start | bytes 772
  5.6 13.0 %copy-start.5 = (s32[64]{0:T(128)S(1)}, s32[64]{0:T(128)}, u32[]{:S(2)}) copy-start(s32[64]{0:T(128)} %lag.3) | copy-start | bytes 772
  5.6 13.0 %copy-start.6 = (s32[64]{0:T(128)S(1)}, s32[64]{0:T(128)}, u32[]{:S(2)}) copy-start(s32[64]{0:T(128)} %slot.1) | copy-start | bytes 772
  8.1 6.3 %collective-permute-start.3 = (f16[16,48,128]{2,1,0:T(8,128)(2,1)S(1)}, f16[16,48,128]{2,1,0:T(8,128)(2,1)S(1)}, u32[]{:S(2)}, u32[]{:S(2)}) collective-permute-start(f16[16,48,128]{2,1,0:T(8,128)(2,1)S(1)} %convert_element_type.38), channel_id=1, source_target_pairs={{0,4},{4,0},{8,12},{12,8},{16,20},{20,16},{24,28},{28,24},{1,5},{5... | collective-permute-start | bytes 589832 | tf_op jit(solution)/shard_map/ppermute | solution.py:492
  9.4 12.3 %collective-permute-start.2 = (f16[8,48,128]{2,1,0:T(8,128)(2,1)S(1)}, f16[8,48,128]{2,1,0:T(8,128)(2,1)S(1)}, u32[]{:S(2)}, u32[]{:S(2)}) collective-permute-start(f16[8,48,128]{2,1,0:T(8,128)(2,1)S(1)} %convert_element_type.35), channel_id=1, source_target_pairs={{0,16},{4,20},{8,24},{12,28},{16,0},{20,4},{24,8},{28,12},{1,17},{... | collective-permute-start | bytes 294920 | tf_op jit(solution)/shard_map/ppermute | solution.py:492
  11.8 9.9 %collective-permute-start.1 = (f16[8,48,128]{2,1,0:T(8,128)(2,1)S(1)}, f16[8,48,128]{2,1,0:T(8,128)(2,1)S(1)}, u32[]{:S(2)}, u32[]{:S(2)}) collective-permute-start(f16[8,48,128]{2,1,0:T(8,128)(2,1)S(1)} %convert_element_type.33), channel_id=1, source_target_pairs={{0,20},{4,16},{8,28},{12,24},{16,4},{20,0},{24,12},{28,8},{1,21},{... | collective-permute-start | bytes 294920 | tf_op jit(solution)/shard_map/ppermute | solution.py:492
  14.3 7.6 %copy-start.2 = (f32[2,24,1024]{2,1,0:T(8,128)S(1)}, f32[2,24,1024]{2,1,0:T(8,128)}, u32[]{:S(2)}) copy-start(f32[2,24,1024]{2,1,0:T(8,128)} %counts.1) | copy-start | bytes 589828
  14.5 7.3 %collective-permute-start.6 = (f16[8,48,128]{2,1,0:T(8,128)(2,1)S(1)}, f16[8,48,128]{2,1,0:T(8,128)(2,1)S(1)}, u32[]{:S(2)}, u32[]{:S(2)}) collective-permute-start(f16[8,48,128]{2,1,0:T(8,128)(2,1)S(1)} %get-tuple-element.44), channel_id=1, source_target_pairs={{0,8},{4,12},{8,0},{12,4},{16,24},{20,28},{24,16},{28,20},{1,9},{5... | collective-permute-start | bytes 294920 | tf_op jit(solution)/shard_map/ppermute | solution.py:492
  15.2 6.6 %collective-permute-start.5 = (f16[8,48,128]{2,1,0:T(8,128)(2,1)S(1)}, f16[8,48,128]{2,1,0:T(8,128)(2,1)S(1)}, u32[]{:S(2)}, u32[]{:S(2)}) collective-permute-start(f16[8,48,128]{2,1,0:T(8,128)(2,1)S(1)} %get-tuple-element.43), channel_id=1, source_target_pairs={{0,24},{4,28},{8,16},{12,20},{16,8},{20,12},{24,0},{28,4},{1,25},{... | collective-permute-start | bytes 294920 | tf_op jit(solution)/shard_map/ppermute | solution.py:492
  17.4 4.4 %collective-permute-start.4 = (f16[8,48,128]{2,1,0:T(8,128)(2,1)S(1)}, f16[8,48,128]{2,1,0:T(8,128)(2,1)S(1)}, u32[]{:S(2)}, u32[]{:S(2)}) collective-permute-start(f16[8,48,128]{2,1,0:T(8,128)(2,1)S(1)} %convert_element_type.37), channel_id=1, source_target_pairs={{0,4},{4,0},{8,12},{12,8},{16,20},{20,16},{24,28},{28,24},{1,5},{5... | collective-permute-start | bytes 294920 | tf_op jit(solution)/shard_map/ppermute | solution.py:492
  22.6 11.0 %collective-permute-start.7 = (bf16[8,48,128]{2,1,0:T(8,128)(2,1)S(1)}, bf16[8,48,128]{2,1,0:T(8,128)(2,1)S(1)}, u32[]{:S(2)}, u32[]{:S(2)}) collective-permute-start(bf16[8,48,128]{2,1,0:T(8,128)(2,1)S(1)} %get-tuple-element.36.signal), channel_id=1, source_target_pairs={{0,8},{4,12},{8,0},{12,4},{16,24},{20,28},{24,16},{28,20},{1,9},{5... | collective-permute-start | bytes 294920 | tf_op jit(solution)/shard_map/ppermute | solution.py:492
  27.0 7.6 %collective-permute-start.8 = (bf16[8,48,128]{2,1,0:T(8,128)(2,1)S(1)}, bf16[8,48,128]{2,1,0:T(8,128)(2,1)S(1)}, u32[]{:S(2)}, u32[]{:S(2)}) collective-permute-start(bf16[8,48,128]{2,1,0:T(8,128)(2,1)S(1)} %get-tuple-element.36.signal), channel_id=1, source_target_pairs={{0,24},{4,28},{8,16},{12,20},{16,8},{20,12},{24,0},{28,4},{1,25},{... | collective-permute-start | bytes 294920 | tf_op jit(solution)/shard_map/ppermute | solution.py:492
  30.1 11.6 %collective-permute-start.9 = (bf16[8,48,128]{2,1,0:T(8,128)(2,1)S(1)}, bf16[8,48,128]{2,1,0:T(8,128)(2,1)S(1)}, u32[]{:S(2)}, u32[]{:S(2)}) collective-permute-start(bf16[8,48,128]{2,1,0:T(8,128)(2,1)S(1)} %get-tuple-element.36.signal), channel_id=1, source_target_pairs={{0,20},{4,16},{8,28},{12,24},{16,4},{20,0},{24,12},{28,8},{1,21},{... | collective-permute-start | bytes 294920 | tf_op jit(solution)/shard_map/ppermute | solution.py:492
  30.1 12.9 %collective-permute-start.10 = (bf16[8,48,128]{2,1,0:T(8,128)(2,1)S(1)}, bf16[8,48,128]{2,1,0:T(8,128)(2,1)S(1)}, u32[]{:S(2)}, u32[]{:S(2)}) collective-permute-start(bf16[8,48,128]{2,1,0:T(8,128)(2,1)S(1)} %get-tuple-element.36.signal), channel_id=1, source_target_pairs={{0,16},{4,20},{8,24},{12,28},{16,0},{20,4},{24,8},{28,12},{1,17},{... | collective-permute-start | bytes 294920 | tf_op jit(solution)/shard_map/ppermute | solution.py:492
  32.3 10.7 %collective-permute-start.11 = (bf16[8,48,128]{2,1,0:T(8,128)(2,1)S(1)}, bf16[8,48,128]{2,1,0:T(8,128)(2,1)S(1)}, u32[]{:S(2)}, u32[]{:S(2)}) collective-permute-start(bf16[8,48,128]{2,1,0:T(8,128)(2,1)S(1)} %get-tuple-element.36.signal), channel_id=1, source_target_pairs={{0,4},{4,0},{8,12},{12,8},{16,20},{20,16},{24,28},{28,24},{1,5},{5... | collective-permute-start | bytes 294920 | tf_op jit(solution)/shard_map/ppermute | solution.py:492
  33.6 10.9 %collective-permute-start.12 = (bf16[8,48,128]{2,1,0:T(8,128)(2,1)S(1)}, bf16[8,48,128]{2,1,0:T(8,128)(2,1)S(1)}, u32[]{:S(2)}, u32[]{:S(2)}) collective-permute-start(bf16[8,48,128]{2,1,0:T(8,128)(2,1)S(1)} %collective-permute-done.7.rest_3_), channel_id=1, source_target_pairs={{0,4},{4,0},{8,12},{12,8},{16,20},{20,16},{24,28},{28,24},{1,5},{5... | collective-permute-start | bytes 294920 | tf_op jit(solution)/shard_map/ppermute | solution.py:492
  34.6 10.0 %collective-permute-start.13 = (bf16[8,48,128]{2,1,0:T(8,128)(2,1)S(1)}, bf16[8,48,128]{2,1,0:T(8,128)(2,1)S(1)}, u32[]{:S(2)}, u32[]{:S(2)}) collective-permute-start(bf16[8,48,128]{2,1,0:T(8,128)(2,1)S(1)} %collective-permute-done.8.rest_4_), channel_id=1, source_target_pairs={{0,4},{4,0},{8,12},{12,8},{16,20},{20,16},{24,28},{28,24},{1,5},{5... | collective-permute-start | bytes 294920 | tf_op jit(solution)/shard_map/ppermute | solution.py:492
  45.5 4.4 %collective-permute-start.14 = (f32[16,16,128]{2,1,0:T(8,128)S(1)}, f32[16,16,128]{2,1,0:T(8,128)S(1)}, u32[]{:S(2)}, u32[]{:S(2)}) collective-permute-start(f32[16,16,128]{2,1,0:T(8,128)S(1)} %get-tuple-element.40), channel_id=1, source_target_pairs={{0,3},{1,0},{2,1},{3,2},{4,7},{5,4},{6,5},{7,6},{8,11},{9,8},{10,9... | collective-permute-start | bytes 393224 | tf_op jit(solution)/shard_map/ppermute | solution.py:554

commit v8 on v7

--- a/solution.py
+++ b/solution.py
@@ -419,6 +419,15 @@
                 )
 
 
+BACKWARD_COST = 500
+
+
+def weight(nanoseconds):
+    return pl.CostEstimate(
+        flops=1_000_000 * nanoseconds, transcendentals=0, bytes_accessed=3_000 * nanoseconds
+    )
+
+
 SMEM = pl.BlockSpec(memory_space=pltpu.SMEM)
 VMEM = pl.BlockSpec(memory_space=pltpu.VMEM)
 HBM = pl.BlockSpec(memory_space=pltpu.HBM)
@@ -457,12 +466,12 @@
     remotes = remote_lag.shape[0]
     cap = (remotes + corridors - 2) // (corridors - 1)
     span = HALO + minutes
-    through = sorted({2, corridors - 2})
-    crossing = [s ^ 1 for s in through]
-    direct = [s for s in range(corridors - 1, 1, -1) if s not in through + crossing]
-    order = crossing + direct + [1] + through
-    many = len(through)
-    cuts = [0, *range(many, len(order) - many + 1), len(order)]
+    through = list(range(corridors - 2, 0, -2))
+    final = through[len(through) // 2]
+    rest = [s for s in through if s != final]
+    order = [final ^ 1] + [s ^ 1 for s in rest] + [1] + through
+    through = through[::-1]
+    order[-len(through):] = through
     t = Table(len(order), corridors * cap, remotes)
     me = lax.axis_index("corr").astype(jnp.int32).reshape(1)
     group = lax.axis_index("tm").astype(jnp.int32).reshape(1)
@@ -492,17 +501,21 @@
         return lax.ppermute(part, "corr", [(i, i ^ s) for i in range(corridors)])
 
     f32 = jnp.float32
-    crossed, *parts, kept = kernel_call(
+    cuts = [*range(len(rest) + 1), *range(len(rest) + 2, len(order) + 1)]
+    outgoing = kernel_call(
         functools.partial(forward_remote_kernel, days, cuts, links),
         (group, ahead),
         (flows, before, remote_mats),
         [shape(((end - first) * links, *piece[1:]), f32) for first, end in zip(cuts, cuts[1:])],
         [wide, pltpu.VMEM((len(order) * links, *piece[1:]), f32)],
     )
-    crossed = exchanged(crossed.astype(WIRE), 1)
-    near, crossed = lax.optimization_barrier((parts[-1].astype(WIRE), crossed))
-    received = [exchanged(p.astype(WIRE), s) for p, s in zip(parts[:-1], direct)]
-    received.append(exchanged(near, 1))
+    count = len(through)
+    crossed = [exchanged(part.astype(WIRE), 1) for part in outgoing[:count]]
+    received = []
+    for s, kept in zip(through, outgoing[count:]):
+        met = crossed[order.index(s ^ 1)][:links].astype(f32)
+        received.append(exchanged((kept + met).astype(WIRE), s))
+    received.append(crossed[-1][links:])
     own, table = kernel_call(
         functools.partial(forward_local_kernel, days, cap, order, t, links),
         (group, me, ahead, remote_slot, *local_index),
@@ -511,8 +524,6 @@
         [wide],
         outs=[VMEM, SMEM],
     )
-    kept = (kept + crossed.astype(f32)).astype(WIRE).reshape(many, *piece)
-    received += [exchanged(kept[i], through[i]) for i in reversed(range(many))]
     totals = functools.reduce(jnp.add, [p.astype(f32) for p in received], own)
     link_residual, signal = kernel_call(
         functools.partial(signal_kernel, days),
@@ -520,10 +531,9 @@
         (totals, counts),
         [shape(counts.shape, f32), shape(piece, jnp.bfloat16)],
     )
-    arrived = [exchanged(signal, s) for s in (*through, *direct)]
-    near = exchanged(signal, 1)
-    passed = [exchanged(a, 1) for a in arrived[:many]]
-    *held, signal = lax.optimization_barrier((*arrived[:many], signal))
+    arrived = {s: exchanged(signal, s) for s in (*through, 1)}
+    for s in through:
+        arrived[s ^ 1] = exchanged(arrived[s], 1)
     rows = [shape((paths * days * span, width), f32)]
     (total,) = kernel_call(
         functools.partial(backward_local_kernel, days),
@@ -531,25 +541,15 @@
         (signal, local_blocks),
         rows,
     )
-    def weigh(first):
-        if first == 0:
-            return None
-        return pl.CostEstimate(
-            flops=500_000_000, transcendentals=0, bytes_accessed=1_500_000
-        )
-
     edge = shape((paths * days, HALO, width), f32)
-    for first, end, signals, made in (
-        (many, len(order), [*arrived[many:], near, *held], rows),
-        (0, many, passed, [*rows, edge]),
-    ):
+    for first, end, made in ((1, len(order), rows), (0, 1, [*rows, edge])):
         total, *early = kernel_call(
             functools.partial(backward_remote_kernel, days, cap, first, end, links, t),
             (table,),
-            (remote_mats, total, *signals),
+            (remote_mats, total, *(arrived[s] for s in order[first:end])),
             made,
             [pltpu.VMEM(slots_shape, jnp.bfloat16)],
-            weigh(first),
+            cost=weight(BACKWARD_COST) if first else None,
         )
     spill = lax.ppermute(early[0], "tm", [(i, (i - 1) % groups) for i in range(groups)])
     gradient, new_flows = kernel_call(

time: 50.9 us -> 47.2 us (0.927)
  waiting for transfers between devices: 13 us -> 9.38 us
    ppermute x13, waiting for transfers between devices: 9.58 us -> 6.53 us  [exchanged(): return lax.ppermute(part, 'corr', [(i, i ^ s) for i in range(corridors)])]
    ppermute x13, starting transfers between devices: 19.6 us -> 16.6 us  [exchanged(): return lax.ppermute(part, 'corr', [(i, i ^ s) for i in range(corridors)])]
    ppermute x1, starting transfers between devices: 1.04 us -> 3.93 us  [per_device_dense(): lax.ppermute(early[0], 'tm', [(i, (i - 1) % groups) for i in range(groups)])]
    ppermute x1, waiting for transfers between devices: 3.4 us -> 2.85 us  [per_device_dense(): lax.ppermute(early[0], 'tm', [(i, (i - 1) % groups) for i in range(groups)])]
  transfers between devices with their start and end apart: 15 -> 15, of which waited for: 5 -> 7; matrix products, arithmetic and copies ran while one was open for 0% -> 0% of each run, Pallas kernels for 17% -> 18%
where the time goes in v8:
time: 47.2 us; the launch traced here: 47 us
  starting transfers between devices  23.3 us (49%)
  Pallas kernels  13.3 us (28%)
  waiting for transfers between devices  9.38 us (20%)
  between operations  0.84 us (2%)
    ppermute x13, starting transfers between devices, exchanged(): return lax.ppermute(part, 'corr', [(i, i ^ s) for i in range(corridors)])  16.6 us
    pallas_call x7, Pallas kernels, kernel_call(): pl.pallas_call(body, out_shape=out_shape, in_specs=[SMEM] * len(scalars)...  11.1 us
    ppermute x13, waiting for transfers between devices, exchanged(): return lax.ppermute(part, 'corr', [(i, i ^ s) for i in range(corridors)])  6.53 us
    ppermute x1, starting transfers between devices, per_device_dense(): lax.ppermute(early[0], 'tm', [(i, (i - 1) % groups) for i in range(groups)])  3.93 us
    ppermute x1, waiting for transfers between devices, per_device_dense(): lax.ppermute(early[0], 'tm', [(i, (i - 1) % groups) for i in range(groups)])  2.85 us
    ppermute x1, starting transfers between devices, per_device_dense(): lax.ppermute(flows, 'tm', [(i, (i + 1) % groups) for i in range(groups)])  2.68 us
    pallas_call x1, Pallas kernels, per_device_dense(): pl.pallas_call(functools.partial(prepare_kernel, cap, order, links, CHUNK...  2.2 us
  transfers between devices with their start and end apart: 15, of which 7 were waited for; matrix products, arithmetic and copies ran while one was open for 0% of the time, Pallas kernels for 18%

profile of v8, /device:TPU:1, one launch (start us, length us, event | category | flops | bytes accessed | tf_op | source)
XLA Modules:
  0.0 47.0 jit_solution(13630471183516221456)
XLA Ops:
  0.6 0.0 copy-start.1
  0.6 2.7 %collective-permute-start = (bf16[2,24,1024]{2,1,0:T(8,128)(2,1)}, bf16[2,24,1024]{2,1,0:T(8,128)(2,1)S(1)}, u32[]{:S(2)}, u32[]{:S(2)}) collective-permute-start(bf16[2,24,1024]{2,1,0:T(8,128)(2,1)} %flows.5), channel_id=1, source_target_pairs={{0,1},{1,2},{2,3},{3,0},{4,5},{5,6},{6,7},{7,4},{8,9},{9,10},{10,1... | collective-permute-start | bytes 294920 | tf_op jit(solution)/shard_map/ppermute | solution.py:485
  3.3 2.2 %shard_map.130 = (s32[128]{0:T(128)S(1)}, bf16[64,128,128]{2,1,0:T(8,128)(2,1)S(1)}) custom-call(s32[1]{0:T(128)} %bitcast.1.me, s32[64]{0:T(128)} %rest_0_.1, s32[64]{0:T(128)} %rest_1_.1, s32[64]{0:T(128)} %rest_2_.1, s32[64]{0:T(128)} %slot.1, bf16[64,128,128]{2,1,0:T(8,128)(2,1)} %rest_4_.1), custom_call_target="tpu_custom_call" | custom-call | tf_op jit(solution)/shard_map/pallas_call | solution.py:487
  5.5 0.0 collective-permute-done.before
  5.5 0.0 copy-done.1
  5.6 0.0 copy-start
  5.6 0.0 copy-start.3
  5.6 0.0 copy-start.4
  5.6 0.0 copy-start.5
  5.6 0.0 copy-start.6
  5.6 2.4 %shard_map.132 = (f32[8,48,128]{2,1,0:T(8,128)S(1)}, f32[8,48,128]{2,1,0:T(8,128)S(1)}, f32[16,48,128]{2,1,0:T(8,128)S(1)}, f32[8,48,128]{2,1,0:T(8,128)S(1)}, f...) custom-call(s32[1]{0:T(128)} %bitcast.group, s32[128]{0:T(128)S(1)} %get-tuple-element.19.ahead, ...), custom_call_target="tpu_custom_call" | custom-call | tf_op jit(solution)/shard_map/pallas_call | solution.py:437
  8.1 1.3 %collective-permute-start.5 = (f16[8,48,128]{2,1,0:T(8,128)(2,1)S(1)}, f16[8,48,128]{2,1,0:T(8,128)(2,1)S(1)}, u32[]{:S(2)}, u32[]{:S(2)}) collective-permute-start(f16[8,48,128]{2,1,0:T(8,128)(2,1)S(1)} %convert_element_type.47), channel_id=1, source_target_pairs={{0,4},{4,0},{8,12},{12,8},{16,20},{20,16},{24,28},{28,24},{1,5},{5... | collective-permute-start | bytes 294920 | tf_op jit(solution)/shard_map/ppermute | solution.py:501
  9.4 0.3 collective-permute-start.3
  9.8 1.2 %collective-permute-start.1 = (f16[16,48,128]{2,1,0:T(8,128)(2,1)S(1)}, f16[16,48,128]{2,1,0:T(8,128)(2,1)S(1)}, u32[]{:S(2)}, u32[]{:S(2)}) collective-permute-start(f16[16,48,128]{2,1,0:T(8,128)(2,1)S(1)} %convert_element_type.39), channel_id=1, source_target_pairs={{0,4},{4,0},{8,12},{12,8},{16,20},{20,16},{24,28},{28,24},{1,5},{5... | collective-permute-start | bytes 589832 | tf_op jit(solution)/shard_map/ppermute | solution.py:501
  11.0 1.2 %collective-permute-done.5 = f16[8,48,128]{2,1,0:T(8,128)(2,1)S(1)} collective-permute-done((f16[8,48,128]{2,1,0:T(8,128)(2,1)S(1)}, f16[8,48,128]{2,1,0:T(8,128)(2,1)S(1)}, u32[]{:S(2)}, u32[]{:S(2)}) %collective-permute-start.5) | collective-permute-done | bytes 98336 | tf_op jit(solution)/shard_map/ppermute | solution.py:501
  12.3 0.0 copy-start.2
  12.3 2.8 %collective-permute-start.6 = (f16[8,48,128]{2,1,0:T(8,128)(2,1)S(1)}, f16[8,48,128]{2,1,0:T(8,128)(2,1)S(1)}, u32[]{:S(2)}, u32[]{:S(2)}) collective-permute-start(f16[8,48,128]{2,1,0:T(8,128)(2,1)S(1)} %add_convert_fusion), channel_id=1, source_target_pairs={{0,24},{4,28},{8,16},{12,20},{16,8},{20,12},{24,0},{28,4},{1,25},{... | collective-permute-start | bytes 294920 | tf_op jit(solution)/shard_map/ppermute | solution.py:501
  15.1 0.0 collective-permute-done.3
  15.1 1.5 %collective-permute-start.4 = (f16[8,48,128]{2,1,0:T(8,128)(2,1)S(1)}, f16[8,48,128]{2,1,0:T(8,128)(2,1)S(1)}, u32[]{:S(2)}, u32[]{:S(2)}) collective-permute-start(f16[8,48,128]{2,1,0:T(8,128)(2,1)S(1)} %add_convert_fusion.1), channel_id=1, source_target_pairs={{0,16},{4,20},{8,24},{12,28},{16,0},{20,4},{24,8},{28,12},{1,17},{... | collective-permute-start | bytes 294920 | tf_op jit(solution)/shard_map/ppermute | solution.py:501
  16.6 1.8 %collective-permute-done.1 = f16[16,48,128]{2,1,0:T(8,128)(2,1)S(1)} collective-permute-done((f16[16,48,128]{2,1,0:T(8,128)(2,1)S(1)}, f16[16,48,128]{2,1,0:T(8,128)(2,1)S(1)}, u32[]{:S(2)}, u32[]{:S(2)}) %collective-permute-start.1) | collective-permute-done | bytes 196640 | tf_op jit(solution)/shard_map/ppermute | solution.py:501
  18.5 1.3 %collective-permute-start.2 = (f16[8,48,128]{2,1,0:T(8,128)(2,1)S(1)}, f16[8,48,128]{2,1,0:T(8,128)(2,1)S(1)}, u32[]{:S(2)}, u32[]{:S(2)}) collective-permute-start(f16[8,48,128]{2,1,0:T(8,128)(2,1)S(1)} %add_convert_fusion.2), channel_id=1, source_target_pairs={{0,8},{4,12},{8,0},{12,4},{16,24},{20,28},{24,16},{28,20},{1,9},{5... | collective-permute-start | bytes 294920 | tf_op jit(solution)/shard_map/ppermute | solution.py:501
  19.8 0.0 copy-done
  19.8 0.0 copy-done.3
  19.8 0.0 copy-done.4
  19.8 0.0 copy-done.5
  19.8 0.0 copy-done.6
  19.9 3.1 %shard_map.131 = (f32[8,48,128]{2,1,0:T(8,128)S(1)}, s32[215]{0:T(256)S(1)}) custom-call(s32[1]{0:T(128)} %bitcast.group, s32[1]{0:T(128)} %bitcast.1.me, s32[128]{0:T(128)S(1)} %get-tuple-element.19.ahead, s32[64]{0:T(128)S(1)} %copy-done.6, s32[64]{0:T(128)S(1)} %copy-done.3, s32[64]{0:T(128)S(1)} %copy-done.4, s32[64]{0:T(128)S(1)} %copy-done.5, ...), custom_call_target="tpu_custom_call" | custom-call | tf_op jit(solution)/shard_map/pallas_call | solution.py:437
  23.0 0.0 collective-permute-done.6
  23.0 0.5 %collective-permute-done.4 = f16[8,48,128]{2,1,0:T(8,128)(2,1)S(1)} collective-permute-done((f16[8,48,128]{2,1,0:T(8,128)(2,1)S(1)}, f16[8,48,128]{2,1,0:T(8,128)(2,1)S(1)}, u32[]{:S(2)}, u32[]{:S(2)}) %collective-permute-start.4) | collective-permute-done | bytes 98336 | tf_op jit(solution)/shard_map/ppermute | solution.py:501
  23.5 0.0 collective-permute-done.2
  23.5 0.1 convert_add_fusion.totals
  23.6 0.0 copy-done.2
  23.6 0.7 %shard_map.133 = (f32[2,24,1024]{2,1,0:T(8,128)}, bf16[8,48,128]{2,1,0:T(8,128)(2,1)S(1)}) custom-call(f32[8,48,128]{2,1,0:T(8,128)S(1)} %convert_add_fusion.totals, f32[2,24,1024]{2,1,0:T(8,128)S(1)} %copy-done.2), custom_call_target="tpu_custom_call" | custom-call | tf_op jit(solution)/shard_map/pallas_call | solution.py:437
  24.3 2.6 %collective-permute-start.7 = (bf16[8,48,128]{2,1,0:T(8,128)(2,1)S(1)}, bf16[8,48,128]{2,1,0:T(8,128)(2,1)S(1)}, u32[]{:S(2)}, u32[]{:S(2)}) collective-permute-start(bf16[8,48,128]{2,1,0:T(8,128)(2,1)S(1)} %get-tuple-element.30.signal), channel_id=1, source_target_pairs={{0,24},{4,28},{8,16},{12,20},{16,8},{20,12},{24,0},{28,4},{1,25},{... | collective-permute-start | bytes 294920 | tf_op jit(solution)/shard_map/ppermute | solution.py:501
  26.9 0.0 collective-permute-start.9
  26.9 1.0 %collective-permute-start.12 = (bf16[8,48,128]{2,1,0:T(8,128)(2,1)S(1)}, bf16[8,48,128]{2,1,0:T(8,128)(2,1)S(1)}, u32[]{:S(2)}, u32[]{:S(2)}) collective-permute-start(bf16[8,48,128]{2,1,0:T(8,128)(2,1)S(1)} %get-tuple-element.30.signal), channel_id=1, source_target_pairs={{0,16},{4,20},{8,24},{12,28},{16,0},{20,4},{24,8},{28,12},{1,17},{... | collective-permute-start | bytes 294920 | tf_op jit(solution)/shard_map/ppermute | solution.py:501
  27.9 1.0 %collective-permute-start.11 = (bf16[8,48,128]{2,1,0:T(8,128)(2,1)S(1)}, bf16[8,48,128]{2,1,0:T(8,128)(2,1)S(1)}, u32[]{:S(2)}, u32[]{:S(2)}) collective-permute-start(bf16[8,48,128]{2,1,0:T(8,128)(2,1)S(1)} %get-tuple-element.30.signal), channel_id=1, source_target_pairs={{0,4},{4,0},{8,12},{12,8},{16,20},{20,16},{24,28},{28,24},{1,5},{5... | collective-permute-start | bytes 294920 | tf_op jit(solution)/shard_map/ppermute | solution.py:501
  28.9 0.7 %collective-permute-done.7.rest_5_ = bf16[8,48,128]{2,1,0:T(8,128)(2,1)S(1)} collective-permute-done((bf16[8,48,128]{2,1,0:T(8,128)(2,1)S(1)}, bf16[8,48,128]{2,1,0:T(8,128)(2,1)S(1)}, u32[]{:S(2)}, u32[]{:S(2)}) %collective-permute-start.7) | collective-permute-done | bytes 98336 | tf_op jit(solution)/shard_map/ppermute | solution.py:501
  29.6 1.0 %collective-permute-start.8 = (bf16[8,48,128]{2,1,0:T(8,128)(2,1)S(1)}, bf16[8,48,128]{2,1,0:T(8,128)(2,1)S(1)}, u32[]{:S(2)}, u32[]{:S(2)}) collective-permute-start(bf16[8,48,128]{2,1,0:T(8,128)(2,1)S(1)} %collective-permute-done.7.rest_5_), channel_id=1, source_target_pairs={{0,4},{4,0},{8,12},{12,8},{16,20},{20,16},{24,28},{28,24},{1,5},{5... | collective-permute-start | bytes 294920 | tf_op jit(solution)/shard_map/ppermute | solution.py:501
  30.7 0.4 collective-permute-done.9.rest_3_
  31.1 1.0 %collective-permute-start.10 = (bf16[8,48,128]{2,1,0:T(8,128)(2,1)S(1)}, bf16[8,48,128]{2,1,0:T(8,128)(2,1)S(1)}, u32[]{:S(2)}, u32[]{:S(2)}) collective-permute-start(bf16[8,48,128]{2,1,0:T(8,128)(2,1)S(1)} %collective-permute-done.9.rest_3_), channel_id=1, source_target_pairs={{0,4},{4,0},{8,12},{12,8},{16,20},{20,16},{24,28},{28,24},{1,5},{5... | collective-permute-start | bytes 294920 | tf_op jit(solution)/shard_map/ppermute | solution.py:501
  32.1 1.8 %collective-permute-done.12.rest_4_ = bf16[8,48,128]{2,1,0:T(8,128)(2,1)S(1)} collective-permute-done((bf16[8,48,128]{2,1,0:T(8,128)(2,1)S(1)}, bf16[8,48,128]{2,1,0:T(8,128)(2,1)S(1)}, u32[]{:S(2)}, u32[]{:S(2)}) %collective-permute-start.12) | collective-permute-done | bytes 98336 | tf_op jit(solution)/shard_map/ppermute | solution.py:501
  33.9 1.5 %collective-permute-start.13 = (bf16[8,48,128]{2,1,0:T(8,128)(2,1)S(1)}, bf16[8,48,128]{2,1,0:T(8,128)(2,1)S(1)}, u32[]{:S(2)}, u32[]{:S(2)}) collective-permute-start(bf16[8,48,128]{2,1,0:T(8,128)(2,1)S(1)} %collective-permute-done.12.rest_4_), channel_id=1, source_target_pairs={{0,4},{4,0},{8,12},{12,8},{16,20},{20,16},{24,28},{28,24},{1,5},{5... | collective-permute-start | bytes 294920 | tf_op jit(solution)/shard_map/ppermute | solution.py:501
  35.4 1.5 %shard_map.134.start = f32[640,128]{1,0:T(8,128)S(1)} custom-call(s32[64]{0:T(128)S(1)} %copy-done.3, s32[64]{0:T(128)S(1)} %copy-done.4, s32[64]{0:T(128)S(1)} %copy-done.5, bf16[8,48,128]{2,1,0:T(8,128)(2,1)S(1)} %get-tuple-element.30.signal, bf16[64,128,128]{2,1,0:T(8,128)(2,1)S(1)} %copy-done), custom_call_target="tpu_custom_call" | custom-call | tf_op jit(solution)/shard_map/pallas_call | solution.py:437
  36.9 0.0 collective-permute-done.11.rest_2_
  37.0 0.0 collective-permute-done.8.rest_0_
  37.0 0.0 collective-permute-done.10.rest_1_
  37.0 1.7 %shard_map.135.start = f32[640,128]{1,0:T(8,128)S(1)} custom-call(s32[215]{0:T(256)S(1)} %get-tuple-element.29.table, bf16[64,128,128]{2,1,0:T(8,128)(2,1)S(1)} %get-tuple-element.21.mats, f32[640,128]{1,0:T(8,128)S(1)} %shard_map.134.start, bf16[8,48,128]{2,1,0:T(8,128)(2,1)S(1)} %collective-permute-done.8.rest_0_, ...), custom_call_target="tpu_custom_call" | custom-call | flops 500000000 | bytes 1500000 | tf_op jit(solution)/shard_map/pallas_call | solution.py:437
  38.6 0.0 collective-permute-done.13.rest_0_
  38.7 0.8 %shard_map.136 = (f32[640,128]{1,0:T(8,128)S(1)}, f32[16,16,128]{2,1,0:T(8,128)S(1)}) custom-call(s32[215]{0:T(256)S(1)} %get-tuple-element.29.table, bf16[64,128,128]{2,1,0:T(8,128)(2,1)S(1)} %get-tuple-element.21.mats, f32[640,128]{1,0:T(8,128)S(1)} %shard_map.135.start, bf16[8,48,128]{2,1,0:T(8,128)(2,1)S(1)} %collective-permute-done.13.rest_0_), custom_call_target="tpu_custom_call" | custom-call | tf_op jit(solution)/shard_map/pallas_call | solution.py:437
  39.5 3.9 %collective-permute-start.14 = (f32[16,16,128]{2,1,0:T(8,128)S(1)}, f32[16,16,128]{2,1,0:T(8,128)S(1)}, u32[]{:S(2)}, u32[]{:S(2)}) collective-permute-start(f32[16,16,128]{2,1,0:T(8,128)S(1)} %get-tuple-element.32), channel_id=1, source_target_pairs={{0,3},{1,0},{2,1},{3,2},{4,7},{5,4},{6,5},{7,6},{8,11},{9,8},{10,9... | collective-permute-start | bytes 393224 | tf_op jit(solution)/shard_map/ppermute | solution.py:554
  43.4 2.8 %collective-permute-done.14.spill = f32[16,16,128]{2,1,0:T(8,128)S(1)} collective-permute-done((f32[16,16,128]{2,1,0:T(8,128)S(1)}, f32[16,16,128]{2,1,0:T(8,128)S(1)}, u32[]{:S(2)}, u32[]{:S(2)}) %collective-permute-start.14) | collective-permute-done | bytes 131104 | tf_op jit(solution)/shard_map/ppermute | solution.py:554
  46.3 0.8 %shard_map.137 = (f32[2,24,1024]{2,1,0:T(8,128)}, f32[2,24,1024]{2,1,0:T(8,128)}) custom-call(s32[1]{0:T(128)} %bitcast.group, f32[640,128]{1,0:T(8,128)S(1)} %get-tuple-element.31.total, f32[16,16,128]{2,1,0:T(8,128)S(1)} %collective-permute-done.14.spill, bf16[2,24,1024]{2,1,0:T(8,128)(2,1)S(1)} %copy-done.1), custom_call_target="tpu_custom_call" | custom-call | tf_op jit(solution)/shard_map/pallas_call | solution.py:437
  (6 shorter events, 0.2 us)
Async XLA Ops:
  0.6 4.9 %copy-start.1 = (bf16[2,24,1024]{2,1,0:T(8,128)(2,1)S(1)}, bf16[2,24,1024]{2,1,0:T(8,128)(2,1)}, u32[]{:S(2)}) copy-start(bf16[2,24,1024]{2,1,0:T(8,128)(2,1)} %flows.5) | copy-start | bytes 294916
  0.6 4.9 %collective-permute-start = (bf16[2,24,1024]{2,1,0:T(8,128)(2,1)}, bf16[2,24,1024]{2,1,0:T(8,128)(2,1)S(1)}, u32[]{:S(2)}, u32[]{:S(2)}) collective-permute-start(bf16[2,24,1024]{2,1,0:T(8,128)(2,1)} %flows.5), channel_id=1, source_target_pairs={{0,1},{1,2},{2,3},{3,0},{4,5},{5,6},{6,7},{7,4},{8,9},{9,10},{10,1... | collective-permute-start | bytes 294920 | tf_op jit(solution)/shard_map/ppermute | solution.py:485
  5.6 14.3 %copy-start = (bf16[64,128,128]{2,1,0:T(8,128)(2,1)S(1)}, bf16[64,128,128]{2,1,0:T(8,128)(2,1)}, u32[]{:S(2)}) copy-start(bf16[64,128,128]{2,1,0:T(8,128)(2,1)} %mats.3) | copy-start | bytes 6291460
  5.6 14.3 %copy-start.3 = (s32[64]{0:T(128)S(1)}, s32[64]{0:T(128)}, u32[]{:S(2)}) copy-start(s32[64]{0:T(128)} %path.3) | copy-start | bytes 772
  5.6 14.3 %copy-start.4 = (s32[64]{0:T(128)S(1)}, s32[64]{0:T(128)}, u32[]{:S(2)}) copy-start(s32[64]{0:T(128)} %link.3) | copy-start | bytes 772
  5.6 14.3 %copy-start.5 = (s32[64]{0:T(128)S(1)}, s32[64]{0:T(128)}, u32[]{:S(2)}) copy-start(s32[64]{0:T(128)} %lag.3) | copy-start | bytes 772
  5.6 14.2 %copy-start.6 = (s32[64]{0:T(128)S(1)}, s32[64]{0:T(128)}, u32[]{:S(2)}) copy-start(s32[64]{0:T(128)} %slot.1) | copy-start | bytes 772
  8.1 4.2 %collective-permute-start.5 = (f16[8,48,128]{2,1,0:T(8,128)(2,1)S(1)}, f16[8,48,128]{2,1,0:T(8,128)(2,1)S(1)}, u32[]{:S(2)}, u32[]{:S(2)}) collective-permute-start(f16[8,48,128]{2,1,0:T(8,128)(2,1)S(1)} %convert_element_type.47), channel_id=1, source_target_pairs={{0,4},{4,0},{8,12},{12,8},{16,20},{20,16},{24,28},{28,24},{1,5},{5... | collective-permute-start | bytes 294920 | tf_op jit(solution)/shard_map/ppermute | solution.py:501
  9.4 5.7 %collective-permute-start.3 = (f16[8,48,128]{2,1,0:T(8,128)(2,1)S(1)}, f16[8,48,128]{2,1,0:T(8,128)(2,1)S(1)}, u32[]{:S(2)}, u32[]{:S(2)}) collective-permute-start(f16[8,48,128]{2,1,0:T(8,128)(2,1)S(1)} %convert_element_type.43), channel_id=1, source_target_pairs={{0,4},{4,0},{8,12},{12,8},{16,20},{20,16},{24,28},{28,24},{1,5},{5... | collective-permute-start | bytes 294920 | tf_op jit(solution)/shard_map/ppermute | solution.py:501
  9.8 8.7 %collective-permute-start.1 = (f16[16,48,128]{2,1,0:T(8,128)(2,1)S(1)}, f16[16,48,128]{2,1,0:T(8,128)(2,1)S(1)}, u32[]{:S(2)}, u32[]{:S(2)}) collective-permute-start(f16[16,48,128]{2,1,0:T(8,128)(2,1)S(1)} %convert_element_type.39), channel_id=1, source_target_pairs={{0,4},{4,0},{8,12},{12,8},{16,20},{20,16},{24,28},{28,24},{1,5},{5... | collective-permute-start | bytes 589832 | tf_op jit(solution)/shard_map/ppermute | solution.py:501
  12.3 11.4 %copy-start.2 = (f32[2,24,1024]{2,1,0:T(8,128)S(1)}, f32[2,24,1024]{2,1,0:T(8,128)}, u32[]{:S(2)}) copy-start(f32[2,24,1024]{2,1,0:T(8,128)} %counts.1) | copy-start | bytes 589828
  12.3 10.7 %collective-permute-start.6 = (f16[8,48,128]{2,1,0:T(8,128)(2,1)S(1)}, f16[8,48,128]{2,1,0:T(8,128)(2,1)S(1)}, u32[]{:S(2)}, u32[]{:S(2)}) collective-permute-start(f16[8,48,128]{2,1,0:T(8,128)(2,1)S(1)} %add_convert_fusion), channel_id=1, source_target_pairs={{0,24},{4,28},{8,16},{12,20},{16,8},{20,12},{24,0},{28,4},{1,25},{... | collective-permute-start | bytes 294920 | tf_op jit(solution)/shard_map/ppermute | solution.py:501
  15.1 8.4 %collective-permute-start.4 = (f16[8,48,128]{2,1,0:T(8,128)(2,1)S(1)}, f16[8,48,128]{2,1,0:T(8,128)(2,1)S(1)}, u32[]{:S(2)}, u32[]{:S(2)}) collective-permute-start(f16[8,48,128]{2,1,0:T(8,128)(2,1)S(1)} %add_convert_fusion.1), channel_id=1, source_target_pairs={{0,16},{4,20},{8,24},{12,28},{16,0},{20,4},{24,8},{28,12},{1,17},{... | collective-permute-start | bytes 294920 | tf_op jit(solution)/shard_map/ppermute | solution.py:501
  18.5 5.0 %collective-permute-start.2 = (f16[8,48,128]{2,1,0:T(8,128)(2,1)S(1)}, f16[8,48,128]{2,1,0:T(8,128)(2,1)S(1)}, u32[]{:S(2)}, u32[]{:S(2)}) collective-permute-start(f16[8,48,128]{2,1,0:T(8,128)(2,1)S(1)} %add_convert_fusion.2), channel_id=1, source_target_pairs={{0,8},{4,12},{8,0},{12,4},{16,24},{20,28},{24,16},{28,20},{1,9},{5... | collective-permute-start | bytes 294920 | tf_op jit(solution)/shard_map/ppermute | solution.py:501
  24.3 5.3 %collective-permute-start.7 = (bf16[8,48,128]{2,1,0:T(8,128)(2,1)S(1)}, bf16[8,48,128]{2,1,0:T(8,128)(2,1)S(1)}, u32[]{:S(2)}, u32[]{:S(2)}) collective-permute-start(bf16[8,48,128]{2,1,0:T(8,128)(2,1)S(1)} %get-tuple-element.30.signal), channel_id=1, source_target_pairs={{0,24},{4,28},{8,16},{12,20},{16,8},{20,12},{24,0},{28,4},{1,25},{... | collective-permute-start | bytes 294920 | tf_op jit(solution)/shard_map/ppermute | solution.py:501
  26.9 4.2 %collective-permute-start.9 = (bf16[8,48,128]{2,1,0:T(8,128)(2,1)S(1)}, bf16[8,48,128]{2,1,0:T(8,128)(2,1)S(1)}, u32[]{:S(2)}, u32[]{:S(2)}) collective-permute-start(bf16[8,48,128]{2,1,0:T(8,128)(2,1)S(1)} %get-tuple-element.30.signal), channel_id=1, source_target_pairs={{0,8},{4,12},{8,0},{12,4},{16,24},{20,28},{24,16},{28,20},{1,9},{5... | collective-permute-start | bytes 294920 | tf_op jit(solution)/shard_map/ppermute | solution.py:501
  26.9 6.9 %collective-permute-start.12 = (bf16[8,48,128]{2,1,0:T(8,128)(2,1)S(1)}, bf16[8,48,128]{2,1,0:T(8,128)(2,1)S(1)}, u32[]{:S(2)}, u32[]{:S(2)}) collective-permute-start(bf16[8,48,128]{2,1,0:T(8,128)(2,1)S(1)} %get-tuple-element.30.signal), channel_id=1, source_target_pairs={{0,16},{4,20},{8,24},{12,28},{16,0},{20,4},{24,8},{28,12},{1,17},{... | collective-permute-start | bytes 294920 | tf_op jit(solution)/shard_map/ppermute | solution.py:501
  27.9 9.1 %collective-permute-start.11 = (bf16[8,48,128]{2,1,0:T(8,128)(2,1)S(1)}, bf16[8,48,128]{2,1,0:T(8,128)(2,1)S(1)}, u32[]{:S(2)}, u32[]{:S(2)}) collective-permute-start(bf16[8,48,128]{2,1,0:T(8,128)(2,1)S(1)} %get-tuple-element.30.signal), channel_id=1, source_target_pairs={{0,4},{4,0},{8,12},{12,8},{16,20},{20,16},{24,28},{28,24},{1,5},{5... | collective-permute-start | bytes 294920 | tf_op jit(solution)/shard_map/ppermute | solution.py:501
  29.6 7.3 %collective-permute-start.8 = (bf16[8,48,128]{2,1,0:T(8,128)(2,1)S(1)}, bf16[8,48,128]{2,1,0:T(8,128)(2,1)S(1)}, u32[]{:S(2)}, u32[]{:S(2)}) collective-permute-start(bf16[8,48,128]{2,1,0:T(8,128)(2,1)S(1)} %collective-permute-done.7.rest_5_), channel_id=1, source_target_pairs={{0,4},{4,0},{8,12},{12,8},{16,20},{20,16},{24,28},{28,24},{1,5},{5... | collective-permute-start | bytes 294920 | tf_op jit(solution)/shard_map/ppermute | solution.py:501
  31.1 5.9 %collective-permute-start.10 = (bf16[8,48,128]{2,1,0:T(8,128)(2,1)S(1)}, bf16[8,48,128]{2,1,0:T(8,128)(2,1)S(1)}, u32[]{:S(2)}, u32[]{:S(2)}) collective-permute-start(bf16[8,48,128]{2,1,0:T(8,128)(2,1)S(1)} %collective-permute-done.9.rest_3_), channel_id=1, source_target_pairs={{0,4},{4,0},{8,12},{12,8},{16,20},{20,16},{24,28},{28,24},{1,5},{5... | collective-permute-start | bytes 294920 | tf_op jit(solution)/shard_map/ppermute | solution.py:501
  33.9 4.8 %collective-permute-start.13 = (bf16[8,48,128]{2,1,0:T(8,128)(2,1)S(1)}, bf16[8,48,128]{2,1,0:T(8,128)(2,1)S(1)}, u32[]{:S(2)}, u32[]{:S(2)}) collective-permute-start(bf16[8,48,128]{2,1,0:T(8,128)(2,1)S(1)} %collective-permute-done.12.rest_4_), channel_id=1, source_target_pairs={{0,4},{4,0},{8,12},{12,8},{16,20},{20,16},{24,28},{28,24},{1,5},{5... | collective-permute-start | bytes 294920 | tf_op jit(solution)/shard_map/ppermute | solution.py:501
  39.5 6.8 %collective-permute-start.14 = (f32[16,16,128]{2,1,0:T(8,128)S(1)}, f32[16,16,128]{2,1,0:T(8,128)S(1)}, u32[]{:S(2)}, u32[]{:S(2)}) collective-permute-start(f32[16,16,128]{2,1,0:T(8,128)S(1)} %get-tuple-element.32), channel_id=1, source_target_pairs={{0,3},{1,0},{2,1},{3,2},{4,7},{5,4},{6,5},{7,6},{8,11},{9,8},{10,9... | collective-permute-start | bytes 393224 | tf_op jit(solution)/shard_map/ppermute | solution.py:554

commit v9 on v8

--- a/solution.py
+++ b/solution.py
@@ -511,11 +511,7 @@
     )
     count = len(through)
     crossed = [exchanged(part.astype(WIRE), 1) for part in outgoing[:count]]
-    received = []
-    for s, kept in zip(through, outgoing[count:]):
-        met = crossed[order.index(s ^ 1)][:links].astype(f32)
-        received.append(exchanged((kept + met).astype(WIRE), s))
-    received.append(crossed[-1][links:])
+    crossed[0], before = lax.optimization_barrier((crossed[0], before))
     own, table = kernel_call(
         functools.partial(forward_local_kernel, days, cap, order, t, links),
         (group, me, ahead, remote_slot, *local_index),
@@ -524,6 +520,12 @@
         [wide],
         outs=[VMEM, SMEM],
     )
+    crossed[-1], own = lax.optimization_barrier((crossed[-1], own))
+    received = []
+    for s, kept in zip(through, outgoing[count:]):
+        met = crossed[order.index(s ^ 1)][:links].astype(f32)
+        received.append(exchanged((kept + met).astype(WIRE), s))
+    received.append(crossed[-1][links:])
     totals = functools.reduce(jnp.add, [p.astype(f32) for p in received], own)
     link_residual, signal = kernel_call(
         functools.partial(signal_kernel, days),
@@ -532,8 +534,6 @@
         [shape(counts.shape, f32), shape(piece, jnp.bfloat16)],
     )
     arrived = {s: exchanged(signal, s) for s in (*through, 1)}
-    for s in through:
-        arrived[s ^ 1] = exchanged(arrived[s], 1)
     rows = [shape((paths * days * span, width), f32)]
     (total,) = kernel_call(
         functools.partial(backward_local_kernel, days),
@@ -541,6 +541,9 @@
         (signal, local_blocks),
         rows,
     )
+    arrived[final], total = lax.optimization_barrier((arrived[final], total))
+    for s in through:
+        arrived[s ^ 1] = exchanged(arrived[s], 1)
     edge = shape((paths * days, HALO, width), f32)
     for first, end, made in ((1, len(order), rows), (0, 1, [*rows, edge])):
         total, *early = kernel_call(

time: 47.2 us -> 48.9 us (1.036)
  waiting for transfers between devices: 9.38 us -> 11 us
    ppermute x1, starting transfers between devices: 3.93 us -> 5.28 us  [per_device_dense(): lax.ppermute(early[0], 'tm', [(i, (i - 1) % groups) for i in range(groups)])]
    ppermute x13, starting transfers between devices: 16.6 us -> 15.4 us  [exchanged(): return lax.ppermute(part, 'corr', [(i, i ^ s) for i in range(corridors)])]
    ppermute x13, waiting for transfers between devices: 6.53 us -> 7.58 us  [exchanged(): return lax.ppermute(part, 'corr', [(i, i ^ s) for i in range(corridors)])]
    ppermute x1, waiting for transfers between devices: 2.85 us -> 3.43 us  [per_device_dense(): lax.ppermute(early[0], 'tm', [(i, (i - 1) % groups) for i in range(groups)])]
  transfers between devices with their start and end apart: 15 -> 15, of which waited for: 7 -> 8; matrix products, arithmetic and copies ran while one was open for 0% -> 0% of each run, Pallas kernels for 18% -> 17%
where the time goes in v9:
time: 48.9 us; the launch traced here: 48.7 us
  starting transfers between devices  23.4 us (48%)
  Pallas kernels  13.3 us (27%)
  waiting for transfers between devices  11 us (22%)
  between operations  0.82 us (2%)
    ppermute x13, starting transfers between devices, exchanged(): return lax.ppermute(part, 'corr', [(i, i ^ s) for i in range(corridors)])  15.4 us
    pallas_call x7, Pallas kernels, kernel_call(): pl.pallas_call(body, out_shape=out_shape, in_specs=[SMEM] * len(scalars)...  11.1 us
    ppermute x13, waiting for transfers between devices, exchanged(): return lax.ppermute(part, 'corr', [(i, i ^ s) for i in range(corridors)])  7.58 us
    ppermute x1, starting transfers between devices, per_device_dense(): lax.ppermute(early[0], 'tm', [(i, (i - 1) % groups) for i in range(groups)])  5.28 us
    ppermute x1, waiting for transfers between devices, per_device_dense(): lax.ppermute(early[0], 'tm', [(i, (i - 1) % groups) for i in range(groups)])  3.43 us
    ppermute x1, starting transfers between devices, per_device_dense(): lax.ppermute(flows, 'tm', [(i, (i + 1) % groups) for i in range(groups)])  2.68 us
    pallas_call x1, Pallas kernels, per_device_dense(): pl.pallas_call(functools.partial(prepare_kernel, cap, order, links, CHUNK...  2.2 us
  transfers between devices with their start and end apart: 15, of which 8 were waited for; matrix products, arithmetic and copies ran while one was open for 0% of the time, Pallas kernels for 17%

profile of v9, /device:TPU:1, one launch (start us, length us, event | category | flops | bytes accessed | tf_op | source)
XLA Modules:
  0.0 48.7 jit_solution(15649571690738628273)
XLA Ops:
  0.6 0.0 copy-start.1
  0.6 2.7 %collective-permute-start = (bf16[2,24,1024]{2,1,0:T(8,128)(2,1)}, bf16[2,24,1024]{2,1,0:T(8,128)(2,1)S(1)}, u32[]{:S(2)}, u32[]{:S(2)}) collective-permute-start(bf16[2,24,1024]{2,1,0:T(8,128)(2,1)} %flows.5), channel_id=1, source_target_pairs={{0,1},{1,2},{2,3},{3,0},{4,5},{5,6},{6,7},{7,4},{8,9},{9,10},{10,1... | collective-permute-start | bytes 294920 | tf_op jit(solution)/shard_map/ppermute | solution.py:485
  3.3 2.2 %shard_map.130 = (s32[128]{0:T(128)S(1)}, bf16[64,128,128]{2,1,0:T(8,128)(2,1)S(1)}) custom-call(s32[1]{0:T(128)} %bitcast.1.me, s32[64]{0:T(128)} %rest_0_.1, s32[64]{0:T(128)} %rest_1_.1, s32[64]{0:T(128)} %rest_2_.1, s32[64]{0:T(128)} %slot.1, bf16[64,128,128]{2,1,0:T(8,128)(2,1)} %rest_4_.1), custom_call_target="tpu_custom_call" | custom-call | tf_op jit(solution)/shard_map/pallas_call | solution.py:487
  5.5 0.0 collective-permute-done.before
  5.5 0.0 copy-done.1
  5.6 0.0 copy-start
  5.6 0.0 copy-start.3
  5.6 0.0 copy-start.4
  5.6 0.0 copy-start.5
  5.6 0.0 copy-start.6
  5.6 2.4 %shard_map.131 = (f32[8,48,128]{2,1,0:T(8,128)S(1)}, f32[8,48,128]{2,1,0:T(8,128)S(1)}, f32[16,48,128]{2,1,0:T(8,128)S(1)}, f32[8,48,128]{2,1,0:T(8,128)S(1)}, f...) custom-call(s32[1]{0:T(128)} %bitcast.group, s32[128]{0:T(128)S(1)} %get-tuple-element.25.ahead, ...), custom_call_target="tpu_custom_call" | custom-call | tf_op jit(solution)/shard_map/pallas_call | solution.py:437
  8.1 1.3 %collective-permute-start.5 = (f16[8,48,128]{2,1,0:T(8,128)(2,1)S(1)}, f16[8,48,128]{2,1,0:T(8,128)(2,1)S(1)}, u32[]{:S(2)}, u32[]{:S(2)}) collective-permute-start(f16[8,48,128]{2,1,0:T(8,128)(2,1)S(1)} %convert_element_type.47), channel_id=1, source_target_pairs={{0,4},{4,0},{8,12},{12,8},{16,20},{20,16},{24,28},{28,24},{1,5},{5... | collective-permute-start | bytes 294920 | tf_op jit(solution)/shard_map/ppermute | solution.py:501
  9.4 0.3 collective-permute-start.2
  9.8 1.3 %collective-permute-start.1 = (f16[16,48,128]{2,1,0:T(8,128)(2,1)S(1)}, f16[16,48,128]{2,1,0:T(8,128)(2,1)S(1)}, u32[]{:S(2)}, u32[]{:S(2)}) collective-permute-start(f16[16,48,128]{2,1,0:T(8,128)(2,1)S(1)} %convert_element_type.39), channel_id=1, source_target_pairs={{0,4},{4,0},{8,12},{12,8},{16,20},{20,16},{24,28},{28,24},{1,5},{5... | collective-permute-start | bytes 589832 | tf_op jit(solution)/shard_map/ppermute | solution.py:501
  11.0 1.2 %collective-permute-done.5 = f16[8,48,128]{2,1,0:T(8,128)(2,1)S(1)} collective-permute-done((f16[8,48,128]{2,1,0:T(8,128)(2,1)S(1)}, f16[8,48,128]{2,1,0:T(8,128)(2,1)S(1)}, u32[]{:S(2)}, u32[]{:S(2)}) %collective-permute-start.5) | collective-permute-done | bytes 98336 | tf_op jit(solution)/shard_map/ppermute | solution.py:501
  12.2 0.0 copy-start.2
  12.3 2.8 %collective-permute-start.6 = (f16[8,48,128]{2,1,0:T(8,128)(2,1)S(1)}, f16[8,48,128]{2,1,0:T(8,128)(2,1)S(1)}, u32[]{:S(2)}, u32[]{:S(2)}) collective-permute-start(f16[8,48,128]{2,1,0:T(8,128)(2,1)S(1)} %add_convert_fusion), channel_id=1, source_target_pairs={{0,24},{4,28},{8,16},{12,20},{16,8},{20,12},{24,0},{28,4},{1,25},{... | collective-permute-start | bytes 294920 | tf_op jit(solution)/shard_map/ppermute | solution.py:501
  15.0 0.0 collective-permute-done.2
  15.1 1.5 %collective-permute-start.4 = (f16[8,48,128]{2,1,0:T(8,128)(2,1)S(1)}, f16[8,48,128]{2,1,0:T(8,128)(2,1)S(1)}, u32[]{:S(2)}, u32[]{:S(2)}) collective-permute-start(f16[8,48,128]{2,1,0:T(8,128)(2,1)S(1)} %add_convert_fusion.1), channel_id=1, source_target_pairs={{0,16},{4,20},{8,24},{12,28},{16,0},{20,4},{24,8},{28,12},{1,17},{... | collective-permute-start | bytes 294920 | tf_op jit(solution)/shard_map/ppermute | solution.py:501
  16.6 0.0 copy-done
  16.6 0.0 copy-done.3
  16.6 0.0 copy-done.4
  16.6 0.0 copy-done.5
  16.6 0.0 copy-done.6
  16.7 3.1 %shard_map.132 = (f32[8,48,128]{2,1,0:T(8,128)S(1)}, s32[215]{0:T(256)S(1)}) custom-call(s32[1]{0:T(128)} %bitcast.group, s32[1]{0:T(128)} %bitcast.1.me, s32[128]{0:T(128)S(1)} %get-tuple-element.25.ahead, s32[64]{0:T(128)S(1)} %copy-done.6, s32[64]{0:T(128)S(1)} %copy-done.3, s32[64]{0:T(128)S(1)} %copy-done.4, s32[64]{0:T(128)S(1)} %copy-done.5, ...), custom_call_target="tpu_custom_call" | custom-call | tf_op jit(solution)/shard_map/pallas_call | solution.py:437
  19.8 0.0 collective-permute-done.1
  19.8 1.4 %collective-permute-start.3 = (f16[8,48,128]{2,1,0:T(8,128)(2,1)S(1)}, f16[8,48,128]{2,1,0:T(8,128)(2,1)S(1)}, u32[]{:S(2)}, u32[]{:S(2)}) collective-permute-start(f16[8,48,128]{2,1,0:T(8,128)(2,1)S(1)} %add_convert_fusion.2), channel_id=1, source_target_pairs={{0,8},{4,12},{8,0},{12,4},{16,24},{20,28},{24,16},{28,20},{1,9},{5... | collective-permute-start | bytes 294920 | tf_op jit(solution)/shard_map/ppermute | solution.py:501
  21.2 0.0 collective-permute-done.6
  21.2 2.3 %collective-permute-done.4 = f16[8,48,128]{2,1,0:T(8,128)(2,1)S(1)} collective-permute-done((f16[8,48,128]{2,1,0:T(8,128)(2,1)S(1)}, f16[8,48,128]{2,1,0:T(8,128)(2,1)S(1)}, u32[]{:S(2)}, u32[]{:S(2)}) %collective-permute-start.4) | collective-permute-done | bytes 98336 | tf_op jit(solution)/shard_map/ppermute | solution.py:501
  23.5 0.2 collective-permute-done.3
  23.7 0.1 convert_add_fusion.totals
  23.8 0.0 copy-done.2
  23.8 0.7 %shard_map.133 = (f32[2,24,1024]{2,1,0:T(8,128)}, bf16[8,48,128]{2,1,0:T(8,128)(2,1)S(1)}) custom-call(f32[8,48,128]{2,1,0:T(8,128)S(1)} %convert_add_fusion.totals, f32[2,24,1024]{2,1,0:T(8,128)S(1)} %copy-done.2), custom_call_target="tpu_custom_call" | custom-call | tf_op jit(solution)/shard_map/pallas_call | solution.py:437
  24.5 2.4 %collective-permute-start.8 = (bf16[8,48,128]{2,1,0:T(8,128)(2,1)S(1)}, bf16[8,48,128]{2,1,0:T(8,128)(2,1)S(1)}, u32[]{:S(2)}, u32[]{:S(2)}) collective-permute-start(bf16[8,48,128]{2,1,0:T(8,128)(2,1)S(1)} %get-tuple-element.40.signal), channel_id=1, source_target_pairs={{0,24},{4,28},{8,16},{12,20},{16,8},{20,12},{24,0},{28,4},{1,25},{... | collective-permute-start | bytes 294920 | tf_op jit(solution)/shard_map/ppermute | solution.py:501
  26.9 0.0 collective-permute-start.10
  26.9 1.1 %collective-permute-start.7 = (bf16[8,48,128]{2,1,0:T(8,128)(2,1)S(1)}, bf16[8,48,128]{2,1,0:T(8,128)(2,1)S(1)}, u32[]{:S(2)}, u32[]{:S(2)}) collective-permute-start(bf16[8,48,128]{2,1,0:T(8,128)(2,1)S(1)} %get-tuple-element.40.signal), channel_id=1, source_target_pairs={{0,16},{4,20},{8,24},{12,28},{16,0},{20,4},{24,8},{28,12},{1,17},{... | collective-permute-start | bytes 294920 | tf_op jit(solution)/shard_map/ppermute | solution.py:501
  28.1 0.9 %collective-permute-start.12 = (bf16[8,48,128]{2,1,0:T(8,128)(2,1)S(1)}, bf16[8,48,128]{2,1,0:T(8,128)(2,1)S(1)}, u32[]{:S(2)}, u32[]{:S(2)}) collective-permute-start(bf16[8,48,128]{2,1,0:T(8,128)(2,1)S(1)} %get-tuple-element.40.signal), channel_id=1, source_target_pairs={{0,4},{4,0},{8,12},{12,8},{16,20},{20,16},{24,28},{28,24},{1,5},{5... | collective-permute-start | bytes 294920 | tf_op jit(solution)/shard_map/ppermute | solution.py:501
  28.9 0.9 %collective-permute-done.8.rest_5_ = bf16[8,48,128]{2,1,0:T(8,128)(2,1)S(1)} collective-permute-done((bf16[8,48,128]{2,1,0:T(8,128)(2,1)S(1)}, bf16[8,48,128]{2,1,0:T(8,128)(2,1)S(1)}, u32[]{:S(2)}, u32[]{:S(2)}) %collective-permute-start.8) | collective-permute-done | bytes 98336 | tf_op jit(solution)/shard_map/ppermute | solution.py:501
  29.8 0.9 %collective-permute-start.9 = (bf16[8,48,128]{2,1,0:T(8,128)(2,1)S(1)}, bf16[8,48,128]{2,1,0:T(8,128)(2,1)S(1)}, u32[]{:S(2)}, u32[]{:S(2)}) collective-permute-start(bf16[8,48,128]{2,1,0:T(8,128)(2,1)S(1)} %collective-permute-done.8.rest_5_), channel_id=1, source_target_pairs={{0,4},{4,0},{8,12},{12,8},{16,20},{20,16},{24,28},{28,24},{1,5},{5... | collective-permute-start | bytes 294920 | tf_op jit(solution)/shard_map/ppermute | solution.py:501
  30.7 1.2 %collective-permute-done.10.rest_3_ = bf16[8,48,128]{2,1,0:T(8,128)(2,1)S(1)} collective-permute-done((bf16[8,48,128]{2,1,0:T(8,128)(2,1)S(1)}, bf16[8,48,128]{2,1,0:T(8,128)(2,1)S(1)}, u32[]{:S(2)}, u32[]{:S(2)}) %collective-permute-start.10) | collective-permute-done | bytes 98336 | tf_op jit(solution)/shard_map/ppermute | solution.py:501
  31.9 0.9 %collective-permute-start.11 = (bf16[8,48,128]{2,1,0:T(8,128)(2,1)S(1)}, bf16[8,48,128]{2,1,0:T(8,128)(2,1)S(1)}, u32[]{:S(2)}, u32[]{:S(2)}) collective-permute-start(bf16[8,48,128]{2,1,0:T(8,128)(2,1)S(1)} %collective-permute-done.10.rest_3_), channel_id=1, source_target_pairs={{0,4},{4,0},{8,12},{12,8},{16,20},{20,16},{24,28},{28,24},{1,5},{5... | collective-permute-start | bytes 294920 | tf_op jit(solution)/shard_map/ppermute | solution.py:501
  32.8 1.5 %shard_map.134.start = f32[640,128]{1,0:T(8,128)S(1)} custom-call(s32[64]{0:T(128)S(1)} %copy-done.3, s32[64]{0:T(128)S(1)} %copy-done.4, s32[64]{0:T(128)S(1)} %copy-done.5, bf16[8,48,128]{2,1,0:T(8,128)(2,1)S(1)} %get-tuple-element.40.signal, bf16[64,128,128]{2,1,0:T(8,128)(2,1)S(1)} %copy-done), custom_call_target="tpu_custom_call" | custom-call | tf_op jit(solution)/shard_map/pallas_call | solution.py:437
  34.3 0.0 collective-permute-done.7.rest_4_
  34.3 0.7 %collective-permute-start.13 = (bf16[8,48,128]{2,1,0:T(8,128)(2,1)S(1)}, bf16[8,48,128]{2,1,0:T(8,128)(2,1)S(1)}, u32[]{:S(2)}, u32[]{:S(2)}) collective-permute-start(bf16[8,48,128]{2,1,0:T(8,128)(2,1)S(1)} %collective-permute-done.7.rest_4_), channel_id=1, source_target_pairs={{0,4},{4,0},{8,12},{12,8},{16,20},{20,16},{24,28},{28,24},{1,5},{5... | collective-permute-start | bytes 294920 | tf_op jit(solution)/shard_map/ppermute | solution.py:501
  35.0 0.0 collective-permute-done.12.rest_2_
  35.0 0.0 collective-permute-done.9.rest_0_
  35.0 0.7 %collective-permute-done.11.rest_1_ = bf16[8,48,128]{2,1,0:T(8,128)(2,1)S(1)} collective-permute-done((bf16[8,48,128]{2,1,0:T(8,128)(2,1)S(1)}, bf16[8,48,128]{2,1,0:T(8,128)(2,1)S(1)}, u32[]{:S(2)}, u32[]{:S(2)}) %collective-permute-start.11) | collective-permute-done | bytes 98336 | tf_op jit(solution)/shard_map/ppermute | solution.py:501
  35.6 1.7 %shard_map.135.start = f32[640,128]{1,0:T(8,128)S(1)} custom-call(s32[215]{0:T(256)S(1)} %get-tuple-element.39.table, bf16[64,128,128]{2,1,0:T(8,128)(2,1)S(1)} %get-tuple-element.26.mats, f32[640,128]{1,0:T(8,128)S(1)} %shard_map.134.start, bf16[8,48,128]{2,1,0:T(8,128)(2,1)S(1)} %collective-permute-done.9.rest_0_, ...), custom_call_target="tpu_custom_call" | custom-call | flops 500000000 | bytes 1500000 | tf_op jit(solution)/shard_map/pallas_call | solution.py:437
  37.3 1.1 %collective-permute-done.13.rest_0_ = bf16[8,48,128]{2,1,0:T(8,128)(2,1)S(1)} collective-permute-done((bf16[8,48,128]{2,1,0:T(8,128)(2,1)S(1)}, bf16[8,48,128]{2,1,0:T(8,128)(2,1)S(1)}, u32[]{:S(2)}, u32[]{:S(2)}) %collective-permute-start.13) | collective-permute-done | bytes 98336 | tf_op jit(solution)/shard_map/ppermute | solution.py:501
  38.4 0.8 %shard_map.136 = (f32[640,128]{1,0:T(8,128)S(1)}, f32[16,16,128]{2,1,0:T(8,128)S(1)}) custom-call(s32[215]{0:T(256)S(1)} %get-tuple-element.39.table, bf16[64,128,128]{2,1,0:T(8,128)(2,1)S(1)} %get-tuple-element.26.mats, f32[640,128]{1,0:T(8,128)S(1)} %shard_map.135.start, bf16[8,48,128]{2,1,0:T(8,128)(2,1)S(1)} %collective-permute-done.13.rest_0_), custom_call_target="tpu_custom_call" | custom-call | tf_op jit(solution)/shard_map/pallas_call | solution.py:437
  39.3 5.3 %collective-permute-start.14 = (f32[16,16,128]{2,1,0:T(8,128)S(1)}, f32[16,16,128]{2,1,0:T(8,128)S(1)}, u32[]{:S(2)}, u32[]{:S(2)}) collective-permute-start(f32[16,16,128]{2,1,0:T(8,128)S(1)} %get-tuple-element.44), channel_id=1, source_target_pairs={{0,3},{1,0},{2,1},{3,2},{4,7},{5,4},{6,5},{7,6},{8,11},{9,8},{10,9... | collective-permute-start | bytes 393224 | tf_op jit(solution)/shard_map/ppermute | solution.py:557
  44.5 3.4 %collective-permute-done.14.spill = f32[16,16,128]{2,1,0:T(8,128)S(1)} collective-permute-done((f32[16,16,128]{2,1,0:T(8,128)S(1)}, f32[16,16,128]{2,1,0:T(8,128)S(1)}, u32[]{:S(2)}, u32[]{:S(2)}) %collective-permute-start.14) | collective-permute-done | bytes 131104 | tf_op jit(solution)/shard_map/ppermute | solution.py:557
  48.0 0.8 %shard_map.137 = (f32[2,24,1024]{2,1,0:T(8,128)}, f32[2,24,1024]{2,1,0:T(8,128)}) custom-call(s32[1]{0:T(128)} %bitcast.group, f32[640,128]{1,0:T(8,128)S(1)} %get-tuple-element.43.total, f32[16,16,128]{2,1,0:T(8,128)S(1)} %collective-permute-done.14.spill, bf16[2,24,1024]{2,1,0:T(8,128)(2,1)S(1)} %copy-done.1), custom_call_target="tpu_custom_call" | custom-call | tf_op jit(solution)/shard_map/pallas_call | solution.py:437
  (6 shorter events, 0.2 us)
Async XLA Ops:
  0.6 4.9 %copy-start.1 = (bf16[2,24,1024]{2,1,0:T(8,128)(2,1)S(1)}, bf16[2,24,1024]{2,1,0:T(8,128)(2,1)}, u32[]{:S(2)}) copy-start(bf16[2,24,1024]{2,1,0:T(8,128)(2,1)} %flows.5) | copy-start | bytes 294916
  0.6 4.9 %collective-permute-start = (bf16[2,24,1024]{2,1,0:T(8,128)(2,1)}, bf16[2,24,1024]{2,1,0:T(8,128)(2,1)S(1)}, u32[]{:S(2)}, u32[]{:S(2)}) collective-permute-start(bf16[2,24,1024]{2,1,0:T(8,128)(2,1)} %flows.5), channel_id=1, source_target_pairs={{0,1},{1,2},{2,3},{3,0},{4,5},{5,6},{6,7},{7,4},{8,9},{9,10},{10,1... | collective-permute-start | bytes 294920 | tf_op jit(solution)/shard_map/ppermute | solution.py:485
  5.6 11.1 %copy-start = (bf16[64,128,128]{2,1,0:T(8,128)(2,1)S(1)}, bf16[64,128,128]{2,1,0:T(8,128)(2,1)}, u32[]{:S(2)}) copy-start(bf16[64,128,128]{2,1,0:T(8,128)(2,1)} %mats.3) | copy-start | bytes 6291460
  5.6 11.1 %copy-start.3 = (s32[64]{0:T(128)S(1)}, s32[64]{0:T(128)}, u32[]{:S(2)}) copy-start(s32[64]{0:T(128)} %path.3) | copy-start | bytes 772
  5.6 11.1 %copy-start.4 = (s32[64]{0:T(128)S(1)}, s32[64]{0:T(128)}, u32[]{:S(2)}) copy-start(s32[64]{0:T(128)} %link.3) | copy-start | bytes 772
  5.6 11.1 %copy-start.5 = (s32[64]{0:T(128)S(1)}, s32[64]{0:T(128)}, u32[]{:S(2)}) copy-start(s32[64]{0:T(128)} %lag.3) | copy-start | bytes 772
  5.6 11.0 %copy-start.6 = (s32[64]{0:T(128)S(1)}, s32[64]{0:T(128)}, u32[]{:S(2)}) copy-start(s32[64]{0:T(128)} %slot.1) | copy-start | bytes 772
  8.1 4.2 %collective-permute-start.5 = (f16[8,48,128]{2,1,0:T(8,128)(2,1)S(1)}, f16[8,48,128]{2,1,0:T(8,128)(2,1)S(1)}, u32[]{:S(2)}, u32[]{:S(2)}) collective-permute-start(f16[8,48,128]{2,1,0:T(8,128)(2,1)S(1)} %convert_element_type.47), channel_id=1, source_target_pairs={{0,4},{4,0},{8,12},{12,8},{16,20},{20,16},{24,28},{28,24},{1,5},{5... | collective-permute-start | bytes 294920 | tf_op jit(solution)/shard_map/ppermute | solution.py:501
  9.4 5.7 %collective-permute-start.2 = (f16[8,48,128]{2,1,0:T(8,128)(2,1)S(1)}, f16[8,48,128]{2,1,0:T(8,128)(2,1)S(1)}, u32[]{:S(2)}, u32[]{:S(2)}) collective-permute-start(f16[8,48,128]{2,1,0:T(8,128)(2,1)S(1)} %convert_element_type.40), channel_id=1, source_target_pairs={{0,4},{4,0},{8,12},{12,8},{16,20},{20,16},{24,28},{28,24},{1,5},{5... | collective-permute-start | bytes 294920 | tf_op jit(solution)/shard_map/ppermute | solution.py:501
  9.8 10.0 %collective-permute-start.1 = (f16[16,48,128]{2,1,0:T(8,128)(2,1)S(1)}, f16[16,48,128]{2,1,0:T(8,128)(2,1)S(1)}, u32[]{:S(2)}, u32[]{:S(2)}) collective-permute-start(f16[16,48,128]{2,1,0:T(8,128)(2,1)S(1)} %convert_element_type.39), channel_id=1, source_target_pairs={{0,4},{4,0},{8,12},{12,8},{16,20},{20,16},{24,28},{28,24},{1,5},{5... | collective-permute-start | bytes 589832 | tf_op jit(solution)/shard_map/ppermute | solution.py:501
  12.2 11.5 %copy-start.2 = (f32[2,24,1024]{2,1,0:T(8,128)S(1)}, f32[2,24,1024]{2,1,0:T(8,128)}, u32[]{:S(2)}) copy-start(f32[2,24,1024]{2,1,0:T(8,128)} %counts.1) | copy-start | bytes 589828
  12.3 8.9 %collective-permute-start.6 = (f16[8,48,128]{2,1,0:T(8,128)(2,1)S(1)}, f16[8,48,128]{2,1,0:T(8,128)(2,1)S(1)}, u32[]{:S(2)}, u32[]{:S(2)}) collective-permute-start(f16[8,48,128]{2,1,0:T(8,128)(2,1)S(1)} %add_convert_fusion), channel_id=1, source_target_pairs={{0,24},{4,28},{8,16},{12,20},{16,8},{20,12},{24,0},{28,4},{1,25},{... | collective-permute-start | bytes 294920 | tf_op jit(solution)/shard_map/ppermute | solution.py:501
  15.1 8.4 %collective-permute-start.4 = (f16[8,48,128]{2,1,0:T(8,128)(2,1)S(1)}, f16[8,48,128]{2,1,0:T(8,128)(2,1)S(1)}, u32[]{:S(2)}, u32[]{:S(2)}) collective-permute-start(f16[8,48,128]{2,1,0:T(8,128)(2,1)S(1)} %add_convert_fusion.1), channel_id=1, source_target_pairs={{0,16},{4,20},{8,24},{12,28},{16,0},{20,4},{24,8},{28,12},{1,17},{... | collective-permute-start | bytes 294920 | tf_op jit(solution)/shard_map/ppermute | solution.py:501
  19.8 3.9 %collective-permute-start.3 = (f16[8,48,128]{2,1,0:T(8,128)(2,1)S(1)}, f16[8,48,128]{2,1,0:T(8,128)(2,1)S(1)}, u32[]{:S(2)}, u32[]{:S(2)}) collective-permute-start(f16[8,48,128]{2,1,0:T(8,128)(2,1)S(1)} %add_convert_fusion.2), channel_id=1, source_target_pairs={{0,8},{4,12},{8,0},{12,4},{16,24},{20,28},{24,16},{28,20},{1,9},{5... | collective-permute-start | bytes 294920 | tf_op jit(solution)/shard_map/ppermute | solution.py:501
  24.5 5.3 %collective-permute-start.8 = (bf16[8,48,128]{2,1,0:T(8,128)(2,1)S(1)}, bf16[8,48,128]{2,1,0:T(8,128)(2,1)S(1)}, u32[]{:S(2)}, u32[]{:S(2)}) collective-permute-start(bf16[8,48,128]{2,1,0:T(8,128)(2,1)S(1)} %get-tuple-element.40.signal), channel_id=1, source_target_pairs={{0,24},{4,28},{8,16},{12,20},{16,8},{20,12},{24,0},{28,4},{1,25},{... | collective-permute-start | bytes 294920 | tf_op jit(solution)/shard_map/ppermute | solution.py:501
  26.9 5.0 %collective-permute-start.10 = (bf16[8,48,128]{2,1,0:T(8,128)(2,1)S(1)}, bf16[8,48,128]{2,1,0:T(8,128)(2,1)S(1)}, u32[]{:S(2)}, u32[]{:S(2)}) collective-permute-start(bf16[8,48,128]{2,1,0:T(8,128)(2,1)S(1)} %get-tuple-element.40.signal), channel_id=1, source_target_pairs={{0,8},{4,12},{8,0},{12,4},{16,24},{20,28},{24,16},{28,20},{1,9},{5... | collective-permute-start | bytes 294920 | tf_op jit(solution)/shard_map/ppermute | solution.py:501
  26.9 7.4 %collective-permute-start.7 = (bf16[8,48,128]{2,1,0:T(8,128)(2,1)S(1)}, bf16[8,48,128]{2,1,0:T(8,128)(2,1)S(1)}, u32[]{:S(2)}, u32[]{:S(2)}) collective-permute-start(bf16[8,48,128]{2,1,0:T(8,128)(2,1)S(1)} %get-tuple-element.40.signal), channel_id=1, source_target_pairs={{0,16},{4,20},{8,24},{12,28},{16,0},{20,4},{24,8},{28,12},{1,17},{... | collective-permute-start | bytes 294920 | tf_op jit(solution)/shard_map/ppermute | solution.py:501
  28.1 6.9 %collective-permute-start.12 = (bf16[8,48,128]{2,1,0:T(8,128)(2,1)S(1)}, bf16[8,48,128]{2,1,0:T(8,128)(2,1)S(1)}, u32[]{:S(2)}, u32[]{:S(2)}) collective-permute-start(bf16[8,48,128]{2,1,0:T(8,128)(2,1)S(1)} %get-tuple-element.40.signal), channel_id=1, source_target_pairs={{0,4},{4,0},{8,12},{12,8},{16,20},{20,16},{24,28},{28,24},{1,5},{5... | collective-permute-start | bytes 294920 | tf_op jit(solution)/shard_map/ppermute | solution.py:501
  29.8 5.2 %collective-permute-start.9 = (bf16[8,48,128]{2,1,0:T(8,128)(2,1)S(1)}, bf16[8,48,128]{2,1,0:T(8,128)(2,1)S(1)}, u32[]{:S(2)}, u32[]{:S(2)}) collective-permute-start(bf16[8,48,128]{2,1,0:T(8,128)(2,1)S(1)} %collective-permute-done.8.rest_5_), channel_id=1, source_target_pairs={{0,4},{4,0},{8,12},{12,8},{16,20},{20,16},{24,28},{28,24},{1,5},{5... | collective-permute-start | bytes 294920 | tf_op jit(solution)/shard_map/ppermute | solution.py:501
  31.9 3.8 %collective-permute-start.11 = (bf16[8,48,128]{2,1,0:T(8,128)(2,1)S(1)}, bf16[8,48,128]{2,1,0:T(8,128)(2,1)S(1)}, u32[]{:S(2)}, u32[]{:S(2)}) collective-permute-start(bf16[8,48,128]{2,1,0:T(8,128)(2,1)S(1)} %collective-permute-done.10.rest_3_), channel_id=1, source_target_pairs={{0,4},{4,0},{8,12},{12,8},{16,20},{20,16},{24,28},{28,24},{1,5},{5... | collective-permute-start | bytes 294920 | tf_op jit(solution)/shard_map/ppermute | solution.py:501
  34.3 4.1 %collective-permute-start.13 = (bf16[8,48,128]{2,1,0:T(8,128)(2,1)S(1)}, bf16[8,48,128]{2,1,0:T(8,128)(2,1)S(1)}, u32[]{:S(2)}, u32[]{:S(2)}) collective-permute-start(bf16[8,48,128]{2,1,0:T(8,128)(2,1)S(1)} %collective-permute-done.7.rest_4_), channel_id=1, source_target_pairs={{0,4},{4,0},{8,12},{12,8},{16,20},{20,16},{24,28},{28,24},{1,5},{5... | collective-permute-start | bytes 294920 | tf_op jit(solution)/shard_map/ppermute | solution.py:501
  39.3 8.7 %collective-permute-start.14 = (f32[16,16,128]{2,1,0:T(8,128)S(1)}, f32[16,16,128]{2,1,0:T(8,128)S(1)}, u32[]{:S(2)}, u32[]{:S(2)}) collective-permute-start(f32[16,16,128]{2,1,0:T(8,128)S(1)} %get-tuple-element.44), channel_id=1, source_target_pairs={{0,3},{1,0},{2,1},{3,2},{4,7},{5,4},{6,5},{7,6},{8,11},{9,8},{10,9... | collective-permute-start | bytes 393224 | tf_op jit(solution)/shard_map/ppermute | solution.py:557

commit v10 on v8

--- a/solution.py
+++ b/solution.py
@@ -221,15 +221,6 @@
     lax.fori_loop(0, groups, group, 0)
 
 
-class Table:
-    def __init__(self, places, slots, blocks):
-        self.start = 0
-        self.block = self.start + places
-        self.base = self.block + slots
-        self.link = self.base + blocks
-        self.size = self.link + blocks
-
-
 def prepare_kernel(cap, order, links, chunks, row_step, me, *rest):
     sources, (ahead, mats_out, path, link, lag, slot, place, sems) = rest[:5], rest[5:]
     blocks = slot.shape[0]
@@ -257,37 +248,35 @@
         copy.wait()
 
 
-def fill_table(cap, order, links, t, me, ahead, slot, table):
-    blocks = slot.shape[0]
+def fill_table(cap, order, me, slot, table):
+    first = len(order)
     for p, s in enumerate(order):
-        table[t.start + p] = t.block + (me[0] ^ s) * cap
-    for i in range((len(order) + 1) * cap):
-        table[t.block + i] = -1
+        table[p] = first + (me[0] ^ s) * cap
+    for i in range((first + 1) * cap):
+        table[first + i] = -1
 
     def entry(j, carry):
-        table[t.block + slot[j]] = j
-        table[t.base + j] = ahead[j]
-        table[t.link + j] = ahead[blocks + j]
+        table[first + slot[j]] = j
         return carry
 
-    lax.fori_loop(0, blocks, entry, 0, unroll=16)
-
-
-def slot_views(table, t, mats, cap, first, unroll, blank):
+    lax.fori_loop(0, slot.shape[0], entry, 0, unroll=16)
+
+
+def slot_views(table, ahead, mats, cap, first, unroll, blank):
     def index(g, u):
         at = first * cap + g * unroll + u
         place = lax.div(at, cap)
-        return table[table[t.start + place] + at - place * cap]
+        return table[table[place] + at - place * cap]
 
     def mat(g, u):
         return mats[jnp.maximum(index(g, u), 0)]
 
     def base(g, u):
-        return table[t.base + jnp.maximum(index(g, u), 0)]
+        return ahead[jnp.maximum(index(g, u), 0)]
 
     def block(g, u):
         j = index(g, u)
-        return jnp.where(j < 0, blank, table[t.link + jnp.maximum(j, 0)])
+        return jnp.where(j < 0, blank, ahead[mats.shape[0] + jnp.maximum(j, 0)])
 
     return mat, base, block
 
@@ -323,7 +312,7 @@
 
 
 def forward_local_kernel(
-    days, cap, order, t, links, group, me, ahead, slot, path, link, lag, flows, before, mats, own, table, wide
+    days, cap, order, group, me, slot, path, link, lag, flows, before, mats, own, table, wide
 ):
     minutes, width = flows.shape[1], mats.shape[2]
     stage_flows(group, flows, before, wide, days, width)
@@ -331,7 +320,7 @@
     unroll = step_of(mats.shape[0])
     views = local_views(path, link, lag, mats, unroll, days * (HALO + minutes))
     forward_blocks(mats.shape[0] // unroll, unroll, *views, wide, own, days, minutes)
-    fill_table(cap, order, links, t, me, ahead, slot, table)
+    fill_table(cap, order, me, slot, table)
 
 
 def signal_kernel(days, totals, counts, residual, signal):
@@ -366,7 +355,7 @@
     )
 
 
-def backward_remote_kernel(days, cap, first, end, links, t, table, mats, start, *rest):
+def backward_remote_kernel(days, cap, first, end, links, table, ahead, mats, start, *rest):
     count = (end - first) * links
     signals, sources, rest = [], 0, list(rest)
     while sources < count:
@@ -384,7 +373,7 @@
     span = HALO + minutes
     slots = (end - first) * cap
     unroll = step_of(slots)
-    mat, base, block = slot_views(table, t, mats, cap, first, unroll, blank)
+    mat, base, block = slot_views(table, ahead, mats, cap, first, unroll, blank)
     backward_blocks(
         slots // unroll,
         unroll,
@@ -469,10 +458,9 @@
     through = list(range(corridors - 2, 0, -2))
     final = through[len(through) // 2]
     rest = [s for s in through if s != final]
-    order = [final ^ 1] + [s ^ 1 for s in rest] + [1] + through
+    order = [s ^ 1 for s in (*rest, final)] + [1] + through
     through = through[::-1]
     order[-len(through):] = through
-    t = Table(len(order), corridors * cap, remotes)
     me = lax.axis_index("corr").astype(jnp.int32).reshape(1)
     group = lax.axis_index("tm").astype(jnp.int32).reshape(1)
     groups = lax.axis_size("tm")
@@ -501,7 +489,7 @@
         return lax.ppermute(part, "corr", [(i, i ^ s) for i in range(corridors)])
 
     f32 = jnp.float32
-    cuts = [*range(len(rest) + 1), *range(len(rest) + 2, len(order) + 1)]
+    cuts = range(len(order) + 1)
     outgoing = kernel_call(
         functools.partial(forward_remote_kernel, days, cuts, links),
         (group, ahead),
@@ -511,16 +499,17 @@
     )
     count = len(through)
     crossed = [exchanged(part.astype(WIRE), 1) for part in outgoing[:count]]
+    near = exchanged(outgoing[count].astype(WIRE), 1)
     received = []
-    for s, kept in zip(through, outgoing[count:]):
-        met = crossed[order.index(s ^ 1)][:links].astype(f32)
+    for s, kept in reversed(list(zip(through, outgoing[count + 1 :]))):
+        met = crossed[order.index(s ^ 1)].astype(f32)
         received.append(exchanged((kept + met).astype(WIRE), s))
-    received.append(crossed[-1][links:])
+    received.append(near)
     own, table = kernel_call(
-        functools.partial(forward_local_kernel, days, cap, order, t, links),
-        (group, me, ahead, remote_slot, *local_index),
+        functools.partial(forward_local_kernel, days, cap, order),
+        (group, me, remote_slot, *local_index),
         (flows, before, local_blocks),
-        [shape(piece, f32), shape((t.size,), jnp.int32)],
+        [shape(piece, f32), shape((len(order) + corridors * cap,), jnp.int32)],
         [wide],
         outs=[VMEM, SMEM],
     )
@@ -532,8 +521,6 @@
         [shape(counts.shape, f32), shape(piece, jnp.bfloat16)],
     )
     arrived = {s: exchanged(signal, s) for s in (*through, 1)}
-    for s in through:
-        arrived[s ^ 1] = exchanged(arrived[s], 1)
     rows = [shape((paths * days * span, width), f32)]
     (total,) = kernel_call(
         functools.partial(backward_local_kernel, days),
@@ -541,11 +528,14 @@
         (signal, local_blocks),
         rows,
     )
+    arrived[2], total = lax.optimization_barrier((arrived[2], total))
+    for s in through:
+        arrived[s ^ 1] = exchanged(arrived[s], 1)
     edge = shape((paths * days, HALO, width), f32)
-    for first, end, made in ((1, len(order), rows), (0, 1, [*rows, edge])):
+    for first, end, made in ((count, len(order), rows), (0, count, [*rows, edge])):
         total, *early = kernel_call(
-            functools.partial(backward_remote_kernel, days, cap, first, end, links, t),
-            (table,),
+            functools.partial(backward_remote_kernel, days, cap, first, end, links),
+            (table, ahead),
             (remote_mats, total, *(arrived[s] for s in order[first:end])),
             made,
             [pltpu.VMEM(slots_shape, jnp.bfloat16)],

time: 47.2 us -> 46.5 us (0.985)
  starting transfers between devices: 23.3 us -> 20.5 us
  waiting for transfers between devices: 9.38 us -> 11.6 us
    ppermute x13 -> x14, waiting for transfers between devices: 6.53 us -> 9.09 us  [exchanged(): return lax.ppermute(part, 'corr', [(i, i ^ s) for i in range(corridors)])]
    ppermute x13 -> x14, starting transfers between devices: 16.6 us -> 14.9 us  [exchanged(): return lax.ppermute(part, 'corr', [(i, i ^ s) for i in range(corridors)])]
    ppermute x1, starting transfers between devices: 3.93 us -> 2.86 us  [per_device_dense(): lax.ppermute(early[0], 'tm', [(i, (i - 1) % groups) for i in range(groups)])]
  transfers between devices with their start and end apart: 15 -> 16, of which waited for: 7 -> 5; matrix products, arithmetic and copies ran while one was open for 0% -> 0% of each run, Pallas kernels for 18% -> 18%
where the time goes in v10:
time: 46.5 us; the launch traced here: 46.3 us
  starting transfers between devices  20.5 us (44%)
  Pallas kernels  13.1 us (28%)
  waiting for transfers between devices  11.6 us (25%)
  between operations  0.84 us (2%)
    ppermute x14, starting transfers between devices, exchanged(): return lax.ppermute(part, 'corr', [(i, i ^ s) for i in range(corridors)])  14.9 us
    pallas_call x7, Pallas kernels, kernel_call(): pl.pallas_call(body, out_shape=out_shape, in_specs=[SMEM] * len(scalars)...  10.9 us
    ppermute x14, waiting for transfers between devices, exchanged(): return lax.ppermute(part, 'corr', [(i, i ^ s) for i in range(corridors)])  9.09 us
    ppermute x1, starting transfers between devices, per_device_dense(): lax.ppermute(early[0], 'tm', [(i, (i - 1) % groups) for i in range(groups)])  2.86 us
    ppermute x1, starting transfers between devices, per_device_dense(): lax.ppermute(flows, 'tm', [(i, (i + 1) % groups) for i in range(groups)])  2.68 us
    ppermute x1, waiting for transfers between devices, per_device_dense(): lax.ppermute(early[0], 'tm', [(i, (i - 1) % groups) for i in range(groups)])  2.56 us
    pallas_call x1, Pallas kernels, per_device_dense(): pl.pallas_call(functools.partial(prepare_kernel, cap, order, links, CHUNK...  2.2 us
  transfers between devices with their start and end apart: 16, of which 5 were waited for; matrix products, arithmetic and copies ran while one was open for 0% of the time, Pallas kernels for 18%

profile of v10, /device:TPU:1, one launch (start us, length us, event | category | flops | bytes accessed | tf_op | source)
XLA Modules:
  0.0 46.3 jit_solution(4505990214034441624)
XLA Ops:
  0.6 0.0 copy-start.1
  0.6 2.7 %collective-permute-start = (bf16[2,24,1024]{2,1,0:T(8,128)(2,1)}, bf16[2,24,1024]{2,1,0:T(8,128)(2,1)S(1)}, u32[]{:S(2)}, u32[]{:S(2)}) collective-permute-start(bf16[2,24,1024]{2,1,0:T(8,128)(2,1)} %flows.5), channel_id=1, source_target_pairs={{0,1},{1,2},{2,3},{3,0},{4,5},{5,6},{6,7},{7,4},{8,9},{9,10},{10,1... | collective-permute-start | bytes 294920 | tf_op jit(solution)/shard_map/ppermute | solution.py:473
  3.3 2.2 %shard_map.131 = (s32[128]{0:T(128)S(1)}, bf16[64,128,128]{2,1,0:T(8,128)(2,1)S(1)}) custom-call(s32[1]{0:T(128)} %bitcast.1.me, s32[64]{0:T(128)} %rest_0_.1, s32[64]{0:T(128)} %rest_1_.1, s32[64]{0:T(128)} %rest_2_.1, s32[64]{0:T(128)} %rest_3_.1, bf16[64,128,128]{2,1,0:T(8,128)(2,1)} %rest_4_.1), custom_call_target="tpu_custom_call" | custom-call | tf_op jit(solution)/shard_map/pallas_call | solution.py:475
  5.5 0.0 collective-permute-done.before
  5.5 0.0 copy-done.1
  5.6 0.0 copy-start
  5.6 0.0 copy-start.3
  5.6 0.0 copy-start.4
  5.6 0.0 copy-start.5
  5.6 0.0 copy-start.6
  5.6 2.4 %shard_map.132 = (f32[8,48,128]{2,1,0:T(8,128)S(1)}, f32[8,48,128]{2,1,0:T(8,128)S(1)}, f32[8,48,128]{2,1,0:T(8,128)S(1)}, f32[8,48,128]{2,1,0:T(8,128)S(1)}, f3...) custom-call(s32[1]{0:T(128)} %bitcast.group, s32[128]{0:T(128)S(1)} %get-tuple-element.23.ahead, ...), custom_call_target="tpu_custom_call" | custom-call | tf_op jit(solution)/shard_map/pallas_call | solution.py:426
  8.1 1.3 %collective-permute-start.1 = (f16[8,48,128]{2,1,0:T(8,128)(2,1)S(1)}, f16[8,48,128]{2,1,0:T(8,128)(2,1)S(1)}, u32[]{:S(2)}, u32[]{:S(2)}) collective-permute-start(f16[8,48,128]{2,1,0:T(8,128)(2,1)S(1)} %convert_element_type.42), channel_id=1, source_target_pairs={{0,4},{4,0},{8,12},{12,8},{16,20},{20,16},{24,28},{28,24},{1,5},{5... | collective-permute-start | bytes 294920 | tf_op jit(solution)/shard_map/ppermute | solution.py:489
  9.4 0.3 collective-permute-start.3
  9.8 1.2 %collective-permute-start.5 = (f16[8,48,128]{2,1,0:T(8,128)(2,1)S(1)}, f16[8,48,128]{2,1,0:T(8,128)(2,1)S(1)}, u32[]{:S(2)}, u32[]{:S(2)}) collective-permute-start(f16[8,48,128]{2,1,0:T(8,128)(2,1)S(1)} %convert_element_type.50), channel_id=1, source_target_pairs={{0,4},{4,0},{8,12},{12,8},{16,20},{20,16},{24,28},{28,24},{1,5},{5... | collective-permute-start | bytes 294920 | tf_op jit(solution)/shard_map/ppermute | solution.py:489
  11.0 0.3 collective-permute-start.7
  11.4 0.9 %collective-permute-done.1 = f16[8,48,128]{2,1,0:T(8,128)(2,1)S(1)} collective-permute-done((f16[8,48,128]{2,1,0:T(8,128)(2,1)S(1)}, f16[8,48,128]{2,1,0:T(8,128)(2,1)S(1)}, u32[]{:S(2)}, u32[]{:S(2)}) %collective-permute-start.1) | collective-permute-done | bytes 98336 | tf_op jit(solution)/shard_map/ppermute | solution.py:489
  12.2 0.0 copy-start.2
  12.3 2.8 %collective-permute-start.2 = (f16[8,48,128]{2,1,0:T(8,128)(2,1)S(1)}, f16[8,48,128]{2,1,0:T(8,128)(2,1)S(1)}, u32[]{:S(2)}, u32[]{:S(2)}) collective-permute-start(f16[8,48,128]{2,1,0:T(8,128)(2,1)S(1)} %add_convert_fusion.2), channel_id=1, source_target_pairs={{0,24},{4,28},{8,16},{12,20},{16,8},{20,12},{24,0},{28,4},{1,25},{... | collective-permute-start | bytes 294920 | tf_op jit(solution)/shard_map/ppermute | solution.py:489
  15.0 0.0 collective-permute-done.3
  15.1 1.5 %collective-permute-start.4 = (f16[8,48,128]{2,1,0:T(8,128)(2,1)S(1)}, f16[8,48,128]{2,1,0:T(8,128)(2,1)S(1)}, u32[]{:S(2)}, u32[]{:S(2)}) collective-permute-start(f16[8,48,128]{2,1,0:T(8,128)(2,1)S(1)} %add_convert_fusion.1), channel_id=1, source_target_pairs={{0,16},{4,20},{8,24},{12,28},{16,0},{20,4},{24,8},{28,12},{1,17},{... | collective-permute-start | bytes 294920 | tf_op jit(solution)/shard_map/ppermute | solution.py:489
  16.6 0.0 collective-permute-done.5
  16.7 1.4 %collective-permute-start.6 = (f16[8,48,128]{2,1,0:T(8,128)(2,1)S(1)}, f16[8,48,128]{2,1,0:T(8,128)(2,1)S(1)}, u32[]{:S(2)}, u32[]{:S(2)}) collective-permute-start(f16[8,48,128]{2,1,0:T(8,128)(2,1)S(1)} %add_convert_fusion), channel_id=1, source_target_pairs={{0,8},{4,12},{8,0},{12,4},{16,24},{20,28},{24,16},{28,20},{1,9},{5... | collective-permute-start | bytes 294920 | tf_op jit(solution)/shard_map/ppermute | solution.py:489
  18.0 0.0 copy-done
  18.0 0.0 copy-done.3
  18.0 0.0 copy-done.4
  18.0 0.0 copy-done.5
  18.0 0.0 copy-done.6
  18.1 3.0 %shard_map.130 = (f32[8,48,128]{2,1,0:T(8,128)S(1)}, s32[87]{0:T(128)S(1)}) custom-call(s32[1]{0:T(128)} %bitcast.group, s32[1]{0:T(128)} %bitcast.1.me, s32[64]{0:T(128)S(1)} %copy-done.6, s32[64]{0:T(128)S(1)} %copy-done.3, s32[64]{0:T(128)S(1)} %copy-done.4, s32[64]{0:T(128)S(1)} %copy-done.5, bf16[2,24,1024]{2,1,0:T(8,128)(2,1)S(1)} %copy-done.1, ...), custom_call_target="tpu_custom_call" | custom-call | tf_op jit(solution)/shard_map/pallas_call | solution.py:426
  21.0 0.0 collective-permute-done.7
  21.1 0.0 collective-permute-done.2
  21.1 2.4 %collective-permute-done.4 = f16[8,48,128]{2,1,0:T(8,128)(2,1)S(1)} collective-permute-done((f16[8,48,128]{2,1,0:T(8,128)(2,1)S(1)}, f16[8,48,128]{2,1,0:T(8,128)(2,1)S(1)}, u32[]{:S(2)}, u32[]{:S(2)}) %collective-permute-start.4) | collective-permute-done | bytes 98336 | tf_op jit(solution)/shard_map/ppermute | solution.py:489
  23.5 0.0 collective-permute-done.6
  23.5 0.1 convert_add_fusion.totals
  23.6 0.0 copy-done.2
  23.6 0.7 %shard_map.133 = (f32[2,24,1024]{2,1,0:T(8,128)}, bf16[8,48,128]{2,1,0:T(8,128)(2,1)S(1)}) custom-call(f32[8,48,128]{2,1,0:T(8,128)S(1)} %convert_add_fusion.totals, f32[2,24,1024]{2,1,0:T(8,128)S(1)} %copy-done.2), custom_call_target="tpu_custom_call" | custom-call | tf_op jit(solution)/shard_map/pallas_call | solution.py:426
  24.3 0.1 collective-permute-start.8
  24.4 2.5 %collective-permute-start.11 = (bf16[8,48,128]{2,1,0:T(8,128)(2,1)S(1)}, bf16[8,48,128]{2,1,0:T(8,128)(2,1)S(1)}, u32[]{:S(2)}, u32[]{:S(2)}) collective-permute-start(bf16[8,48,128]{2,1,0:T(8,128)(2,1)S(1)} %get-tuple-element.34.signal), channel_id=1, source_target_pairs={{0,24},{4,28},{8,16},{12,20},{16,8},{20,12},{24,0},{28,4},{1,25},{... | collective-permute-start | bytes 294920 | tf_op jit(solution)/shard_map/ppermute | solution.py:489
  26.9 0.3 collective-permute-start.10
  27.2 0.8 %collective-permute-start.9 = (bf16[8,48,128]{2,1,0:T(8,128)(2,1)S(1)}, bf16[8,48,128]{2,1,0:T(8,128)(2,1)S(1)}, u32[]{:S(2)}, u32[]{:S(2)}) collective-permute-start(bf16[8,48,128]{2,1,0:T(8,128)(2,1)S(1)} %get-tuple-element.34.signal), channel_id=1, source_target_pairs={{0,4},{4,0},{8,12},{12,8},{16,20},{20,16},{24,28},{28,24},{1,5},{5... | collective-permute-start | bytes 294920 | tf_op jit(solution)/shard_map/ppermute | solution.py:489
  28.0 1.5 %shard_map.134.start = f32[640,128]{1,0:T(8,128)S(1)} custom-call(s32[64]{0:T(128)S(1)} %copy-done.3, s32[64]{0:T(128)S(1)} %copy-done.4, s32[64]{0:T(128)S(1)} %copy-done.5, bf16[8,48,128]{2,1,0:T(8,128)(2,1)S(1)} %get-tuple-element.34.signal, bf16[64,128,128]{2,1,0:T(8,128)(2,1)S(1)} %copy-done), custom_call_target="tpu_custom_call" | custom-call | tf_op jit(solution)/shard_map/pallas_call | solution.py:426
  29.6 0.0 collective-permute-done.8.rest_1_
  29.6 0.7 %collective-permute-start.13 = (bf16[8,48,128]{2,1,0:T(8,128)(2,1)S(1)}, bf16[8,48,128]{2,1,0:T(8,128)(2,1)S(1)}, u32[]{:S(2)}, u32[]{:S(2)}) collective-permute-start(bf16[8,48,128]{2,1,0:T(8,128)(2,1)S(1)} %collective-permute-done.8.rest_1_), channel_id=1, source_target_pairs={{0,4},{4,0},{8,12},{12,8},{16,20},{20,16},{24,28},{28,24},{1,5},{5... | collective-permute-start | bytes 294920 | tf_op jit(solution)/shard_map/ppermute | solution.py:489
  30.3 0.0 collective-permute-done.11.rest_3_
  30.3 0.8 %collective-permute-start.12 = (bf16[8,48,128]{2,1,0:T(8,128)(2,1)S(1)}, bf16[8,48,128]{2,1,0:T(8,128)(2,1)S(1)}, u32[]{:S(2)}, u32[]{:S(2)}) collective-permute-start(bf16[8,48,128]{2,1,0:T(8,128)(2,1)S(1)} %collective-permute-done.11.rest_3_), channel_id=1, source_target_pairs={{0,4},{4,0},{8,12},{12,8},{16,20},{20,16},{24,28},{28,24},{1,5},{5... | collective-permute-start | bytes 294920 | tf_op jit(solution)/shard_map/ppermute | solution.py:489
  31.1 3.9 %collective-permute-done.10.rest_2_ = bf16[8,48,128]{2,1,0:T(8,128)(2,1)S(1)} collective-permute-done((bf16[8,48,128]{2,1,0:T(8,128)(2,1)S(1)}, bf16[8,48,128]{2,1,0:T(8,128)(2,1)S(1)}, u32[]{:S(2)}, u32[]{:S(2)}) %collective-permute-start.10) | collective-permute-done | bytes 98336 | tf_op jit(solution)/shard_map/ppermute | solution.py:489
  35.1 0.8 %collective-permute-start.14 = (bf16[8,48,128]{2,1,0:T(8,128)(2,1)S(1)}, bf16[8,48,128]{2,1,0:T(8,128)(2,1)S(1)}, u32[]{:S(2)}, u32[]{:S(2)}) collective-permute-start(bf16[8,48,128]{2,1,0:T(8,128)(2,1)S(1)} %collective-permute-done.10.rest_2_), channel_id=1, source_target_pairs={{0,4},{4,0},{8,12},{12,8},{16,20},{20,16},{24,28},{28,24},{1,5},{5... | collective-permute-start | bytes 294920 | tf_op jit(solution)/shard_map/ppermute | solution.py:489
  35.9 0.0 collective-permute-done.9.rest_0_
  35.9 1.4 %shard_map.135.start = f32[640,128]{1,0:T(8,128)S(1)} custom-call(s32[87]{0:T(128)S(1)} %get-tuple-element.33.table, s32[128]{0:T(128)S(1)} %get-tuple-element.23.ahead, bf16[64,128,128]{2,1,0:T(8,128)(2,1)S(1)} %get-tuple-element.24.mats, f32[640,128]{1,0:T(8,128)S(1)} %shard_map.134.start, bf16[8,48,128]{2,1,0:T(8,128)(2,1)S(1)} %collective-permute-done.9.rest_0_, ...), custom_call_target="tpu_custom_call" | custom-call | flops 500000000 | bytes 1500000 | tf_op jit(solution)/shard_map/pallas_call | solution.py:426
  37.3 0.0 collective-permute-done.13.rest_1_
  37.3 0.0 collective-permute-done.12.rest_0_
  37.3 1.8 %collective-permute-done.14.rest_2_ = bf16[8,48,128]{2,1,0:T(8,128)(2,1)S(1)} collective-permute-done((bf16[8,48,128]{2,1,0:T(8,128)(2,1)S(1)}, bf16[8,48,128]{2,1,0:T(8,128)(2,1)S(1)}, u32[]{:S(2)}, u32[]{:S(2)}) %collective-permute-start.14) | collective-permute-done | bytes 98336 | tf_op jit(solution)/shard_map/ppermute | solution.py:489
  39.1 1.0 %shard_map.136 = (f32[640,128]{1,0:T(8,128)S(1)}, f32[16,16,128]{2,1,0:T(8,128)S(1)}) custom-call(s32[87]{0:T(128)S(1)} %get-tuple-element.33.table, s32[128]{0:T(128)S(1)} %get-tuple-element.23.ahead, bf16[64,128,128]{2,1,0:T(8,128)(2,1)S(1)} %get-tuple-element.24.mats, f32[640,128]{1,0:T(8,128)S(1)} %shard_map.135.start, ...), custom_call_target="tpu_custom_call" | custom-call | tf_op jit(solution)/shard_map/pallas_call | solution.py:426
  40.1 2.9 %collective-permute-start.15 = (f32[16,16,128]{2,1,0:T(8,128)S(1)}, f32[16,16,128]{2,1,0:T(8,128)S(1)}, u32[]{:S(2)}, u32[]{:S(2)}) collective-permute-start(f32[16,16,128]{2,1,0:T(8,128)S(1)} %get-tuple-element.38), channel_id=1, source_target_pairs={{0,3},{1,0},{2,1},{3,2},{4,7},{5,4},{6,5},{7,6},{8,11},{9,8},{10,9... | collective-permute-start | bytes 393224 | tf_op jit(solution)/shard_map/ppermute | solution.py:544
  43.0 2.6 %collective-permute-done.15.spill = f32[16,16,128]{2,1,0:T(8,128)S(1)} collective-permute-done((f32[16,16,128]{2,1,0:T(8,128)S(1)}, f32[16,16,128]{2,1,0:T(8,128)S(1)}, u32[]{:S(2)}, u32[]{:S(2)}) %collective-permute-start.15) | collective-permute-done | bytes 131104 | tf_op jit(solution)/shard_map/ppermute | solution.py:544
  45.5 0.8 %shard_map.137 = (f32[2,24,1024]{2,1,0:T(8,128)}, f32[2,24,1024]{2,1,0:T(8,128)}) custom-call(s32[1]{0:T(128)} %bitcast.group, f32[640,128]{1,0:T(8,128)S(1)} %get-tuple-element.37.total, f32[16,16,128]{2,1,0:T(8,128)S(1)} %collective-permute-done.15.spill, bf16[2,24,1024]{2,1,0:T(8,128)(2,1)S(1)} %copy-done.1), custom_call_target="tpu_custom_call" | custom-call | tf_op jit(solution)/shard_map/pallas_call | solution.py:426
  (7 shorter events, 0.2 us)
Async XLA Ops:
  0.6 4.9 %copy-start.1 = (bf16[2,24,1024]{2,1,0:T(8,128)(2,1)S(1)}, bf16[2,24,1024]{2,1,0:T(8,128)(2,1)}, u32[]{:S(2)}) copy-start(bf16[2,24,1024]{2,1,0:T(8,128)(2,1)} %flows.5) | copy-start | bytes 294916
  0.6 4.9 %collective-permute-start = (bf16[2,24,1024]{2,1,0:T(8,128)(2,1)}, bf16[2,24,1024]{2,1,0:T(8,128)(2,1)S(1)}, u32[]{:S(2)}, u32[]{:S(2)}) collective-permute-start(bf16[2,24,1024]{2,1,0:T(8,128)(2,1)} %flows.5), channel_id=1, source_target_pairs={{0,1},{1,2},{2,3},{3,0},{4,5},{5,6},{6,7},{7,4},{8,9},{9,10},{10,1... | collective-permute-start | bytes 294920 | tf_op jit(solution)/shard_map/ppermute | solution.py:473
  5.6 12.5 %copy-start = (bf16[64,128,128]{2,1,0:T(8,128)(2,1)S(1)}, bf16[64,128,128]{2,1,0:T(8,128)(2,1)}, u32[]{:S(2)}) copy-start(bf16[64,128,128]{2,1,0:T(8,128)(2,1)} %mats.3) | copy-start | bytes 6291460
  5.6 12.5 %copy-start.3 = (s32[64]{0:T(128)S(1)}, s32[64]{0:T(128)}, u32[]{:S(2)}) copy-start(s32[64]{0:T(128)} %path.3) | copy-start | bytes 772
  5.6 12.5 %copy-start.4 = (s32[64]{0:T(128)S(1)}, s32[64]{0:T(128)}, u32[]{:S(2)}) copy-start(s32[64]{0:T(128)} %link.3) | copy-start | bytes 772
  5.6 12.5 %copy-start.5 = (s32[64]{0:T(128)S(1)}, s32[64]{0:T(128)}, u32[]{:S(2)}) copy-start(s32[64]{0:T(128)} %lag.3) | copy-start | bytes 772
  5.6 12.4 %copy-start.6 = (s32[64]{0:T(128)S(1)}, s32[64]{0:T(128)}, u32[]{:S(2)}) copy-start(s32[64]{0:T(128)} %rest_3_.1) | copy-start | bytes 772
  8.1 4.2 %collective-permute-start.1 = (f16[8,48,128]{2,1,0:T(8,128)(2,1)S(1)}, f16[8,48,128]{2,1,0:T(8,128)(2,1)S(1)}, u32[]{:S(2)}, u32[]{:S(2)}) collective-permute-start(f16[8,48,128]{2,1,0:T(8,128)(2,1)S(1)} %convert_element_type.42), channel_id=1, source_target_pairs={{0,4},{4,0},{8,12},{12,8},{16,20},{20,16},{24,28},{28,24},{1,5},{5... | collective-permute-start | bytes 294920 | tf_op jit(solution)/shard_map/ppermute | solution.py:489
  9.4 5.7 %collective-permute-start.3 = (f16[8,48,128]{2,1,0:T(8,128)(2,1)S(1)}, f16[8,48,128]{2,1,0:T(8,128)(2,1)S(1)}, u32[]{:S(2)}, u32[]{:S(2)}) collective-permute-start(f16[8,48,128]{2,1,0:T(8,128)(2,1)S(1)} %convert_element_type.46), channel_id=1, source_target_pairs={{0,4},{4,0},{8,12},{12,8},{16,20},{20,16},{24,28},{28,24},{1,5},{5... | collective-permute-start | bytes 294920 | tf_op jit(solution)/shard_map/ppermute | solution.py:489
  9.8 6.9 %collective-permute-start.5 = (f16[8,48,128]{2,1,0:T(8,128)(2,1)S(1)}, f16[8,48,128]{2,1,0:T(8,128)(2,1)S(1)}, u32[]{:S(2)}, u32[]{:S(2)}) collective-permute-start(f16[8,48,128]{2,1,0:T(8,128)(2,1)S(1)} %convert_element_type.50), channel_id=1, source_target_pairs={{0,4},{4,0},{8,12},{12,8},{16,20},{20,16},{24,28},{28,24},{1,5},{5... | collective-permute-start | bytes 294920 | tf_op jit(solution)/shard_map/ppermute | solution.py:489
  11.0 10.0 %collective-permute-start.7 = (f16[8,48,128]{2,1,0:T(8,128)(2,1)S(1)}, f16[8,48,128]{2,1,0:T(8,128)(2,1)S(1)}, u32[]{:S(2)}, u32[]{:S(2)}) collective-permute-start(f16[8,48,128]{2,1,0:T(8,128)(2,1)S(1)} %convert_element_type.54), channel_id=1, source_target_pairs={{0,4},{4,0},{8,12},{12,8},{16,20},{20,16},{24,28},{28,24},{1,5},{5... | collective-permute-start | bytes 294920 | tf_op jit(solution)/shard_map/ppermute | solution.py:489
  12.2 11.3 %copy-start.2 = (f32[2,24,1024]{2,1,0:T(8,128)S(1)}, f32[2,24,1024]{2,1,0:T(8,128)}, u32[]{:S(2)}) copy-start(f32[2,24,1024]{2,1,0:T(8,128)} %counts.1) | copy-start | bytes 589828
  12.3 8.8 %collective-permute-start.2 = (f16[8,48,128]{2,1,0:T(8,128)(2,1)S(1)}, f16[8,48,128]{2,1,0:T(8,128)(2,1)S(1)}, u32[]{:S(2)}, u32[]{:S(2)}) collective-permute-start(f16[8,48,128]{2,1,0:T(8,128)(2,1)S(1)} %add_convert_fusion.2), channel_id=1, source_target_pairs={{0,24},{4,28},{8,16},{12,20},{16,8},{20,12},{24,0},{28,4},{1,25},{... | collective-permute-start | bytes 294920 | tf_op jit(solution)/shard_map/ppermute | solution.py:489
  15.1 8.4 %collective-permute-start.4 = (f16[8,48,128]{2,1,0:T(8,128)(2,1)S(1)}, f16[8,48,128]{2,1,0:T(8,128)(2,1)S(1)}, u32[]{:S(2)}, u32[]{:S(2)}) collective-permute-start(f16[8,48,128]{2,1,0:T(8,128)(2,1)S(1)} %add_convert_fusion.1), channel_id=1, source_target_pairs={{0,16},{4,20},{8,24},{12,28},{16,0},{20,4},{24,8},{28,12},{1,17},{... | collective-permute-start | bytes 294920 | tf_op jit(solution)/shard_map/ppermute | solution.py:489
  16.7 6.8 %collective-permute-start.6 = (f16[8,48,128]{2,1,0:T(8,128)(2,1)S(1)}, f16[8,48,128]{2,1,0:T(8,128)(2,1)S(1)}, u32[]{:S(2)}, u32[]{:S(2)}) collective-permute-start(f16[8,48,128]{2,1,0:T(8,128)(2,1)S(1)} %add_convert_fusion), channel_id=1, source_target_pairs={{0,8},{4,12},{8,0},{12,4},{16,24},{20,28},{24,16},{28,20},{1,9},{5... | collective-permute-start | bytes 294920 | tf_op jit(solution)/shard_map/ppermute | solution.py:489
  24.3 5.3 %collective-permute-start.8 = (bf16[8,48,128]{2,1,0:T(8,128)(2,1)S(1)}, bf16[8,48,128]{2,1,0:T(8,128)(2,1)S(1)}, u32[]{:S(2)}, u32[]{:S(2)}) collective-permute-start(bf16[8,48,128]{2,1,0:T(8,128)(2,1)S(1)} %get-tuple-element.34.signal), channel_id=1, source_target_pairs={{0,8},{4,12},{8,0},{12,4},{16,24},{20,28},{24,16},{28,20},{1,9},{5... | collective-permute-start | bytes 294920 | tf_op jit(solution)/shard_map/ppermute | solution.py:489
  24.4 5.9 %collective-permute-start.11 = (bf16[8,48,128]{2,1,0:T(8,128)(2,1)S(1)}, bf16[8,48,128]{2,1,0:T(8,128)(2,1)S(1)}, u32[]{:S(2)}, u32[]{:S(2)}) collective-permute-start(bf16[8,48,128]{2,1,0:T(8,128)(2,1)S(1)} %get-tuple-element.34.signal), channel_id=1, source_target_pairs={{0,24},{4,28},{8,16},{12,20},{16,8},{20,12},{24,0},{28,4},{1,25},{... | collective-permute-start | bytes 294920 | tf_op jit(solution)/shard_map/ppermute | solution.py:489
  26.9 8.1 %collective-permute-start.10 = (bf16[8,48,128]{2,1,0:T(8,128)(2,1)S(1)}, bf16[8,48,128]{2,1,0:T(8,128)(2,1)S(1)}, u32[]{:S(2)}, u32[]{:S(2)}) collective-permute-start(bf16[8,48,128]{2,1,0:T(8,128)(2,1)S(1)} %get-tuple-element.34.signal), channel_id=1, source_target_pairs={{0,16},{4,20},{8,24},{12,28},{16,0},{20,4},{24,8},{28,12},{1,17},{... | collective-permute-start | bytes 294920 | tf_op jit(solution)/shard_map/ppermute | solution.py:489
  27.2 8.6 %collective-permute-start.9 = (bf16[8,48,128]{2,1,0:T(8,128)(2,1)S(1)}, bf16[8,48,128]{2,1,0:T(8,128)(2,1)S(1)}, u32[]{:S(2)}, u32[]{:S(2)}) collective-permute-start(bf16[8,48,128]{2,1,0:T(8,128)(2,1)S(1)} %get-tuple-element.34.signal), channel_id=1, source_target_pairs={{0,4},{4,0},{8,12},{12,8},{16,20},{20,16},{24,28},{28,24},{1,5},{5... | collective-permute-start | bytes 294920 | tf_op jit(solution)/shard_map/ppermute | solution.py:489
  29.6 7.7 %collective-permute-start.13 = (bf16[8,48,128]{2,1,0:T(8,128)(2,1)S(1)}, bf16[8,48,128]{2,1,0:T(8,128)(2,1)S(1)}, u32[]{:S(2)}, u32[]{:S(2)}) collective-permute-start(bf16[8,48,128]{2,1,0:T(8,128)(2,1)S(1)} %collective-permute-done.8.rest_1_), channel_id=1, source_target_pairs={{0,4},{4,0},{8,12},{12,8},{16,20},{20,16},{24,28},{28,24},{1,5},{5... | collective-permute-start | bytes 294920 | tf_op jit(solution)/shard_map/ppermute | solution.py:489
  30.3 7.0 %collective-permute-start.12 = (bf16[8,48,128]{2,1,0:T(8,128)(2,1)S(1)}, bf16[8,48,128]{2,1,0:T(8,128)(2,1)S(1)}, u32[]{:S(2)}, u32[]{:S(2)}) collective-permute-start(bf16[8,48,128]{2,1,0:T(8,128)(2,1)S(1)} %collective-permute-done.11.rest_3_), channel_id=1, source_target_pairs={{0,4},{4,0},{8,12},{12,8},{16,20},{20,16},{24,28},{28,24},{1,5},{5... | collective-permute-start | bytes 294920 | tf_op jit(solution)/shard_map/ppermute | solution.py:489
  35.1 4.0 %collective-permute-start.14 = (bf16[8,48,128]{2,1,0:T(8,128)(2,1)S(1)}, bf16[8,48,128]{2,1,0:T(8,128)(2,1)S(1)}, u32[]{:S(2)}, u32[]{:S(2)}) collective-permute-start(bf16[8,48,128]{2,1,0:T(8,128)(2,1)S(1)} %collective-permute-done.10.rest_2_), channel_id=1, source_target_pairs={{0,4},{4,0},{8,12},{12,8},{16,20},{20,16},{24,28},{28,24},{1,5},{5... | collective-permute-start | bytes 294920 | tf_op jit(solution)/shard_map/ppermute | solution.py:489
  40.1 5.4 %collective-permute-start.15 = (f32[16,16,128]{2,1,0:T(8,128)S(1)}, f32[16,16,128]{2,1,0:T(8,128)S(1)}, u32[]{:S(2)}, u32[]{:S(2)}) collective-permute-start(f32[16,16,128]{2,1,0:T(8,128)S(1)} %get-tuple-element.38), channel_id=1, source_target_pairs={{0,3},{1,0},{2,1},{3,2},{4,7},{5,4},{6,5},{7,6},{8,11},{9,8},{10,9... | collective-permute-start | bytes 393224 | tf_op jit(solution)/shard_map/ppermute | solution.py:544

commit v11 on v10

--- a/solution.py
+++ b/solution.py
@@ -281,7 +281,7 @@
     return mat, base, block
 
 
-def forward_remote_kernel(days, cuts, links, group, ahead, flows, before, mats, *rest):
+def forward_remote_kernel(days, links, group, ahead, flows, before, mats, *rest):
     outs, (wide, acc) = rest[:-2], rest[-2:]
     minutes, width = flows.shape[1], mats.shape[2]
     blocks = mats.shape[0]
@@ -299,8 +299,8 @@
         days,
         minutes,
     )
-    for first, end, out in zip(cuts, cuts[1:], outs):
-        out[...] = acc[first * links : end * links]
+    for p, out in enumerate(outs):
+        out[...] = acc[p * links : (p + 1) * links]
 
 
 def local_views(path, link, lag, mats, unroll, row_step):
@@ -323,23 +323,27 @@
     fill_table(cap, order, me, slot, table)
 
 
-def signal_kernel(days, totals, counts, residual, signal):
-    blocks, _, width = totals.shape
+def residual_of(days, totals, counts, b, d):
+    width, minutes = totals.shape[2], counts.shape[1]
+    seen = counts[d, :, b * width : (b + 1) * width]
+    weight = seen + 1.0
+    return (totals[b, d * minutes : (d + 1) * minutes, :] - seen) / weight, weight
+
+
+def signal_kernel(days, totals, counts, signal):
     minutes = counts.shape[1]
-    for b in range(blocks):
-        cols = slice(b * width, (b + 1) * width)
-        total = totals[b]
+    for b in range(totals.shape[0]):
         for d in range(days):
-            rows = slice(d * minutes, (d + 1) * minutes)
-            seen = counts[d, :, cols]
-            weight = seen + 1.0
-            res = (total[rows] - seen) / weight
-            residual[d, :, cols] = res
-            signal[b, rows, :] = (res / weight).astype(signal.dtype)
-
-
-def backward_local_kernel(days, path, link, lag, signal, mats, out):
-    minutes = signal.shape[1] // days
+            res, weight = residual_of(days, totals, counts, b, d)
+            signal[b, d * minutes : (d + 1) * minutes, :] = (res / weight).astype(signal.dtype)
+
+
+def backward_local_kernel(days, path, link, lag, signal, mats, totals, counts, out, residual):
+    minutes, width = signal.shape[1] // days, totals.shape[2]
+    for b in range(totals.shape[0]):
+        for d in range(days):
+            res, _ = residual_of(days, totals, counts, b, d)
+            residual[d, :, b * width : (b + 1) * width] = res
     out[...] = jnp.zeros_like(out)
     unroll = step_of(mats.shape[0])
     mat, base, block = local_views(path, link, lag, mats, unroll, days * (HALO + minutes))
@@ -489,12 +493,11 @@
         return lax.ppermute(part, "corr", [(i, i ^ s) for i in range(corridors)])
 
     f32 = jnp.float32
-    cuts = range(len(order) + 1)
     outgoing = kernel_call(
-        functools.partial(forward_remote_kernel, days, cuts, links),
+        functools.partial(forward_remote_kernel, days, links),
         (group, ahead),
         (flows, before, remote_mats),
-        [shape(((end - first) * links, *piece[1:]), f32) for first, end in zip(cuts, cuts[1:])],
+        [shape(piece, f32) for _ in order],
         [wide, pltpu.VMEM((len(order) * links, *piece[1:]), f32)],
     )
     count = len(through)
@@ -514,21 +517,21 @@
         outs=[VMEM, SMEM],
     )
     totals = functools.reduce(jnp.add, [p.astype(f32) for p in received], own)
-    link_residual, signal = kernel_call(
+    (signal,) = kernel_call(
         functools.partial(signal_kernel, days),
         (),
         (totals, counts),
-        [shape(counts.shape, f32), shape(piece, jnp.bfloat16)],
+        [shape(piece, jnp.bfloat16)],
     )
     arrived = {s: exchanged(signal, s) for s in (*through, 1)}
     rows = [shape((paths * days * span, width), f32)]
-    (total,) = kernel_call(
+    total, link_residual = kernel_call(
         functools.partial(backward_local_kernel, days),
         local_index,
-        (signal, local_blocks),
-        rows,
-    )
-    arrived[2], total = lax.optimization_barrier((arrived[2], total))
+        (signal, local_blocks, totals, counts),
+        [*rows, shape(counts.shape, f32)],
+    )
+    arrived[through[-1]], total = lax.optimization_barrier((arrived[through[-1]], total))
     for s in through:
         arrived[s ^ 1] = exchanged(arrived[s], 1)
     edge = shape((paths * days, HALO, width), f32)

time: 46.5 us -> 47.2 us (1.015)
  starting transfers between devices: 20.5 us -> 21.5 us
    ppermute x14, waiting for transfers between devices: 9.09 us -> 7.41 us  [exchanged(): return lax.ppermute(part, 'corr', [(i, i ^ s) for i in range(corridors)])]
    ppermute x1, waiting for transfers between devices: 2.56 us -> 3.94 us  [per_device_dense(): lax.ppermute(early[0], 'tm', [(i, (i - 1) % groups) for i in range(groups)])]
    ppermute x14, starting transfers between devices: 14.9 us -> 15.9 us  [exchanged(): return lax.ppermute(part, 'corr', [(i, i ^ s) for i in range(corridors)])]
  transfers between devices with their start and end apart: 16 -> 16, of which waited for: 5 -> 5; matrix products, arithmetic and copies ran while one was open for 0% -> 0% of each run, Pallas kernels for 18% -> 19%
where the time goes in v11:
time: 47.2 us; the launch traced here: 47 us
  starting transfers between devices  21.5 us (46%)
  Pallas kernels  13.1 us (28%)
  waiting for transfers between devices  11.4 us (24%)
  between operations  0.84 us (2%)
    ppermute x14, starting transfers between devices, exchanged(): return lax.ppermute(part, 'corr', [(i, i ^ s) for i in range(corridors)])  15.9 us
    pallas_call x7, Pallas kernels, kernel_call(): pl.pallas_call(body, out_shape=out_shape, in_specs=[SMEM] * len(scalars)...  10.9 us
    ppermute x14, waiting for transfers between devices, exchanged(): return lax.ppermute(part, 'corr', [(i, i ^ s) for i in range(corridors)])  7.41 us
    ppermute x1, waiting for transfers between devices, per_device_dense(): lax.ppermute(early[0], 'tm', [(i, (i - 1) % groups) for i in range(groups)])  3.94 us
    ppermute x1, starting transfers between devices, per_device_dense(): lax.ppermute(early[0], 'tm', [(i, (i - 1) % groups) for i in range(groups)])  2.89 us
    ppermute x1, starting transfers between devices, per_device_dense(): lax.ppermute(flows, 'tm', [(i, (i + 1) % groups) for i in range(groups)])  2.68 us
    pallas_call x1, Pallas kernels, per_device_dense(): pl.pallas_call(functools.partial(prepare_kernel, cap, order, links, CHUNK...  2.2 us
  transfers between devices with their start and end apart: 16, of which 5 were waited for; matrix products, arithmetic and copies ran while one was open for 0% of the time, Pallas kernels for 19%

profile of v11, /device:TPU:1, one launch (start us, length us, event | category | flops | bytes accessed | tf_op | source)
XLA Modules:
  0.0 47.0 jit_solution(4182153191468453904)
XLA Ops:
  0.6 0.0 copy-start.1
  0.6 2.7 %collective-permute-start = (bf16[2,24,1024]{2,1,0:T(8,128)(2,1)}, bf16[2,24,1024]{2,1,0:T(8,128)(2,1)S(1)}, u32[]{:S(2)}, u32[]{:S(2)}) collective-permute-start(bf16[2,24,1024]{2,1,0:T(8,128)(2,1)} %flows.5), channel_id=1, source_target_pairs={{0,1},{1,2},{2,3},{3,0},{4,5},{5,6},{6,7},{7,4},{8,9},{9,10},{10,1... | collective-permute-start | bytes 294920 | tf_op jit(solution)/shard_map/ppermute | solution.py:477
  3.3 2.2 %shard_map.131 = (s32[128]{0:T(128)S(1)}, bf16[64,128,128]{2,1,0:T(8,128)(2,1)S(1)}) custom-call(s32[1]{0:T(128)} %bitcast.1.me, s32[64]{0:T(128)} %rest_0_.1, s32[64]{0:T(128)} %rest_1_.1, s32[64]{0:T(128)} %rest_2_.1, s32[64]{0:T(128)} %rest_3_.1, bf16[64,128,128]{2,1,0:T(8,128)(2,1)} %rest_4_.1), custom_call_target="tpu_custom_call" | custom-call | tf_op jit(solution)/shard_map/pallas_call | solution.py:479
  5.5 0.0 collective-permute-done.before
  5.5 0.0 copy-done.1
  5.6 0.0 copy-start
  5.6 0.0 copy-start.3
  5.6 0.0 copy-start.4
  5.6 0.0 copy-start.5
  5.6 0.0 copy-start.6
  5.6 2.4 %shard_map.132 = (f32[8,48,128]{2,1,0:T(8,128)S(1)}, f32[8,48,128]{2,1,0:T(8,128)S(1)}, f32[8,48,128]{2,1,0:T(8,128)S(1)}, f32[8,48,128]{2,1,0:T(8,128)S(1)}, f3...) custom-call(s32[1]{0:T(128)} %bitcast.group, s32[128]{0:T(128)S(1)} %get-tuple-element.23.ahead, ...), custom_call_target="tpu_custom_call" | custom-call | tf_op jit(solution)/shard_map/pallas_call | solution.py:430
  8.1 1.3 %collective-permute-start.1 = (f16[8,48,128]{2,1,0:T(8,128)(2,1)S(1)}, f16[8,48,128]{2,1,0:T(8,128)(2,1)S(1)}, u32[]{:S(2)}, u32[]{:S(2)}) collective-permute-start(f16[8,48,128]{2,1,0:T(8,128)(2,1)S(1)} %convert_element_type.42), channel_id=1, source_target_pairs={{0,4},{4,0},{8,12},{12,8},{16,20},{20,16},{24,28},{28,24},{1,5},{5... | collective-permute-start | bytes 294920 | tf_op jit(solution)/shard_map/ppermute | solution.py:493
  9.4 0.3 collective-permute-start.3
  9.7 1.3 %collective-permute-start.5 = (f16[8,48,128]{2,1,0:T(8,128)(2,1)S(1)}, f16[8,48,128]{2,1,0:T(8,128)(2,1)S(1)}, u32[]{:S(2)}, u32[]{:S(2)}) collective-permute-start(f16[8,48,128]{2,1,0:T(8,128)(2,1)S(1)} %convert_element_type.50), channel_id=1, source_target_pairs={{0,4},{4,0},{8,12},{12,8},{16,20},{20,16},{24,28},{28,24},{1,5},{5... | collective-permute-start | bytes 294920 | tf_op jit(solution)/shard_map/ppermute | solution.py:493
  11.0 0.3 collective-permute-start.7
  11.4 0.9 %collective-permute-done.1 = f16[8,48,128]{2,1,0:T(8,128)(2,1)S(1)} collective-permute-done((f16[8,48,128]{2,1,0:T(8,128)(2,1)S(1)}, f16[8,48,128]{2,1,0:T(8,128)(2,1)S(1)}, u32[]{:S(2)}, u32[]{:S(2)}) %collective-permute-start.1) | collective-permute-done | bytes 98336 | tf_op jit(solution)/shard_map/ppermute | solution.py:493
  12.2 0.0 copy-start.2
  12.3 2.8 %collective-permute-start.2 = (f16[8,48,128]{2,1,0:T(8,128)(2,1)S(1)}, f16[8,48,128]{2,1,0:T(8,128)(2,1)S(1)}, u32[]{:S(2)}, u32[]{:S(2)}) collective-permute-start(f16[8,48,128]{2,1,0:T(8,128)(2,1)S(1)} %add_convert_fusion.2), channel_id=1, source_target_pairs={{0,24},{4,28},{8,16},{12,20},{16,8},{20,12},{24,0},{28,4},{1,25},{... | collective-permute-start | bytes 294920 | tf_op jit(solution)/shard_map/ppermute | solution.py:493
  15.1 0.0 collective-permute-done.3
  15.1 1.5 %collective-permute-start.4 = (f16[8,48,128]{2,1,0:T(8,128)(2,1)S(1)}, f16[8,48,128]{2,1,0:T(8,128)(2,1)S(1)}, u32[]{:S(2)}, u32[]{:S(2)}) collective-permute-start(f16[8,48,128]{2,1,0:T(8,128)(2,1)S(1)} %add_convert_fusion.1), channel_id=1, source_target_pairs={{0,16},{4,20},{8,24},{12,28},{16,0},{20,4},{24,8},{28,12},{1,17},{... | collective-permute-start | bytes 294920 | tf_op jit(solution)/shard_map/ppermute | solution.py:493
  16.6 0.0 collective-permute-done.5
  16.7 1.4 %collective-permute-start.6 = (f16[8,48,128]{2,1,0:T(8,128)(2,1)S(1)}, f16[8,48,128]{2,1,0:T(8,128)(2,1)S(1)}, u32[]{:S(2)}, u32[]{:S(2)}) collective-permute-start(f16[8,48,128]{2,1,0:T(8,128)(2,1)S(1)} %add_convert_fusion), channel_id=1, source_target_pairs={{0,8},{4,12},{8,0},{12,4},{16,24},{20,28},{24,16},{28,20},{1,9},{5... | collective-permute-start | bytes 294920 | tf_op jit(solution)/shard_map/ppermute | solution.py:493
  18.0 0.0 copy-done
  18.0 0.0 copy-done.3
  18.0 0.0 copy-done.4
  18.0 0.0 copy-done.5
  18.0 0.0 copy-done.6
  18.0 3.0 %shard_map.130 = (f32[8,48,128]{2,1,0:T(8,128)S(1)}, s32[87]{0:T(128)S(1)}) custom-call(s32[1]{0:T(128)} %bitcast.group, s32[1]{0:T(128)} %bitcast.1.me, s32[64]{0:T(128)S(1)} %copy-done.3, s32[64]{0:T(128)S(1)} %copy-done.4, s32[64]{0:T(128)S(1)} %copy-done.5, s32[64]{0:T(128)S(1)} %copy-done.6, bf16[2,24,1024]{2,1,0:T(8,128)(2,1)S(1)} %copy-done.1, ...), custom_call_target="tpu_custom_call" | custom-call | tf_op jit(solution)/shard_map/pallas_call | solution.py:430
  21.0 0.0 collective-permute-done.7
  21.0 0.0 collective-permute-done.2
  21.1 2.5 %collective-permute-done.4 = f16[8,48,128]{2,1,0:T(8,128)(2,1)S(1)} collective-permute-done((f16[8,48,128]{2,1,0:T(8,128)(2,1)S(1)}, f16[8,48,128]{2,1,0:T(8,128)(2,1)S(1)}, u32[]{:S(2)}, u32[]{:S(2)}) %collective-permute-start.4) | collective-permute-done | bytes 98336 | tf_op jit(solution)/shard_map/ppermute | solution.py:493
  23.5 0.0 collective-permute-done.6
  23.5 0.1 convert_add_fusion.totals
  23.6 0.0 copy-done.2
  23.7 2.7 %collective-permute-start.8 = (bf16[8,48,128]{2,1,0:T(8,128)(2,1)S(1)}, bf16[8,48,128]{2,1,0:T(8,128)(2,1)S(1)}, u32[]{:S(2)}, u32[]{:S(2)}) collective-permute-start(bf16[8,48,128]{2,1,0:T(8,128)(2,1)S(1)} %shard_map.133.signal), channel_id=1, source_target_pairs={{0,24},{4,28},{8,16},{12,20},{16,8},{20,12},{24,0},{28,4},{1,25},{... | collective-permute-start | bytes 294920 | tf_op jit(solution)/shard_map/ppermute | solution.py:493
  26.3 0.0 collective-permute-start.10
  26.3 1.0 %collective-permute-start.11 = (bf16[8,48,128]{2,1,0:T(8,128)(2,1)S(1)}, bf16[8,48,128]{2,1,0:T(8,128)(2,1)S(1)}, u32[]{:S(2)}, u32[]{:S(2)}) collective-permute-start(bf16[8,48,128]{2,1,0:T(8,128)(2,1)S(1)} %shard_map.133.signal), channel_id=1, source_target_pairs={{0,16},{4,20},{8,24},{12,28},{16,0},{20,4},{24,8},{28,12},{1,17},{... | collective-permute-start | bytes 294920 | tf_op jit(solution)/shard_map/ppermute | solution.py:493
  27.3 1.1 %collective-permute-start.9 = (bf16[8,48,128]{2,1,0:T(8,128)(2,1)S(1)}, bf16[8,48,128]{2,1,0:T(8,128)(2,1)S(1)}, u32[]{:S(2)}, u32[]{:S(2)}) collective-permute-start(bf16[8,48,128]{2,1,0:T(8,128)(2,1)S(1)} %shard_map.133.signal), channel_id=1, source_target_pairs={{0,4},{4,0},{8,12},{12,8},{16,20},{20,16},{24,28},{28,24},{1,5},{5... | collective-permute-start | bytes 294920 | tf_op jit(solution)/shard_map/ppermute | solution.py:493
  28.3 2.2 %shard_map.134 = (f32[640,128]{1,0:T(8,128)S(1)}, f32[2,24,1024]{2,1,0:T(8,128)}) custom-call(s32[64]{0:T(128)S(1)} %copy-done.4, s32[64]{0:T(128)S(1)} %copy-done.5, s32[64]{0:T(128)S(1)} %copy-done.6, bf16[8,48,128]{2,1,0:T(8,128)(2,1)S(1)} %shard_map.133.signal, bf16[64,128,128]{2,1,0:T(8,128)(2,1)S(1)} %copy-done, ...), custom_call_target="tpu_custom_call" | custom-call | tf_op jit(solution)/shard_map/pallas_call | solution.py:430
  30.6 0.0 collective-permute-done.8.rest_3_
  30.6 0.4 collective-permute-start.12
  31.0 0.0 collective-permute-done.10.rest_1_
  31.0 1.1 %collective-permute-start.13 = (bf16[8,48,128]{2,1,0:T(8,128)(2,1)S(1)}, bf16[8,48,128]{2,1,0:T(8,128)(2,1)S(1)}, u32[]{:S(2)}, u32[]{:S(2)}) collective-permute-start(bf16[8,48,128]{2,1,0:T(8,128)(2,1)S(1)} %collective-permute-done.10.rest_1_), channel_id=1, source_target_pairs={{0,4},{4,0},{8,12},{12,8},{16,20},{20,16},{24,28},{28,24},{1,5},{5... | collective-permute-start | bytes 294920 | tf_op jit(solution)/shard_map/ppermute | solution.py:493
  32.1 1.9 %collective-permute-done.11.rest_2_ = bf16[8,48,128]{2,1,0:T(8,128)(2,1)S(1)} collective-permute-done((bf16[8,48,128]{2,1,0:T(8,128)(2,1)S(1)}, bf16[8,48,128]{2,1,0:T(8,128)(2,1)S(1)}, u32[]{:S(2)}, u32[]{:S(2)}) %collective-permute-start.11) | collective-permute-done | bytes 98336 | tf_op jit(solution)/shard_map/ppermute | solution.py:493
  33.9 0.9 %collective-permute-start.14 = (bf16[8,48,128]{2,1,0:T(8,128)(2,1)S(1)}, bf16[8,48,128]{2,1,0:T(8,128)(2,1)S(1)}, u32[]{:S(2)}, u32[]{:S(2)}) collective-permute-start(bf16[8,48,128]{2,1,0:T(8,128)(2,1)S(1)} %collective-permute-done.11.rest_2_), channel_id=1, source_target_pairs={{0,4},{4,0},{8,12},{12,8},{16,20},{20,16},{24,28},{28,24},{1,5},{5... | collective-permute-start | bytes 294920 | tf_op jit(solution)/shard_map/ppermute | solution.py:493
  34.8 0.0 collective-permute-done.9.rest_0_
  34.8 1.4 %shard_map.135.start = f32[640,128]{1,0:T(8,128)S(1)} custom-call(s32[87]{0:T(128)S(1)} %get-tuple-element.33.table, s32[128]{0:T(128)S(1)} %get-tuple-element.23.ahead, bf16[64,128,128]{2,1,0:T(8,128)(2,1)S(1)} %get-tuple-element.24.mats, f32[640,128]{1,0:T(8,128)S(1)} %get-tuple-element.35.start, bf16[8,48,128]{2,1,0:T(8,128)(2,1)S(1)} %collective-permute-done.9.rest_0_, ...), custom_call_target="tpu_custom_call" | custom-call | flops 500000000 | bytes 1500000 | tf_op jit(solution)/shard_map/pallas_call | solution.py:430
  36.2 0.0 collective-permute-done.12.rest_0_
  36.2 0.0 collective-permute-done.13.rest_1_
  36.2 2.2 %collective-permute-done.14.rest_2_ = bf16[8,48,128]{2,1,0:T(8,128)(2,1)S(1)} collective-permute-done((bf16[8,48,128]{2,1,0:T(8,128)(2,1)S(1)}, bf16[8,48,128]{2,1,0:T(8,128)(2,1)S(1)}, u32[]{:S(2)}, u32[]{:S(2)}) %collective-permute-start.14) | collective-permute-done | bytes 98336 | tf_op jit(solution)/shard_map/ppermute | solution.py:493
  38.4 1.0 %shard_map.136 = (f32[640,128]{1,0:T(8,128)S(1)}, f32[16,16,128]{2,1,0:T(8,128)S(1)}) custom-call(s32[87]{0:T(128)S(1)} %get-tuple-element.33.table, s32[128]{0:T(128)S(1)} %get-tuple-element.23.ahead, bf16[64,128,128]{2,1,0:T(8,128)(2,1)S(1)} %get-tuple-element.24.mats, f32[640,128]{1,0:T(8,128)S(1)} %shard_map.135.start, ...), custom_call_target="tpu_custom_call" | custom-call | tf_op jit(solution)/shard_map/pallas_call | solution.py:430
  39.4 2.9 %collective-permute-start.15 = (f32[16,16,128]{2,1,0:T(8,128)S(1)}, f32[16,16,128]{2,1,0:T(8,128)S(1)}, u32[]{:S(2)}, u32[]{:S(2)}) collective-permute-start(f32[16,16,128]{2,1,0:T(8,128)S(1)} %get-tuple-element.38), channel_id=1, source_target_pairs={{0,3},{1,0},{2,1},{3,2},{4,7},{5,4},{6,5},{7,6},{8,11},{9,8},{10,9... | collective-permute-start | bytes 393224 | tf_op jit(solution)/shard_map/ppermute | solution.py:547
  42.3 3.9 %collective-permute-done.15.spill = f32[16,16,128]{2,1,0:T(8,128)S(1)} collective-permute-done((f32[16,16,128]{2,1,0:T(8,128)S(1)}, f32[16,16,128]{2,1,0:T(8,128)S(1)}, u32[]{:S(2)}, u32[]{:S(2)}) %collective-permute-start.15) | collective-permute-done | bytes 131104 | tf_op jit(solution)/shard_map/ppermute | solution.py:547
  46.3 0.8 %shard_map.137 = (f32[2,24,1024]{2,1,0:T(8,128)}, f32[2,24,1024]{2,1,0:T(8,128)}) custom-call(s32[1]{0:T(128)} %bitcast.group, f32[640,128]{1,0:T(8,128)S(1)} %get-tuple-element.37.total, f32[16,16,128]{2,1,0:T(8,128)S(1)} %collective-permute-done.15.spill, bf16[2,24,1024]{2,1,0:T(8,128)(2,1)S(1)} %copy-done.1), custom_call_target="tpu_custom_call" | custom-call | tf_op jit(solution)/shard_map/pallas_call | solution.py:430
  (8 shorter events, 0.2 us)
Async XLA Ops:
  0.6 4.9 %copy-start.1 = (bf16[2,24,1024]{2,1,0:T(8,128)(2,1)S(1)}, bf16[2,24,1024]{2,1,0:T(8,128)(2,1)}, u32[]{:S(2)}) copy-start(bf16[2,24,1024]{2,1,0:T(8,128)(2,1)} %flows.5) | copy-start | bytes 294916
  0.6 4.9 %collective-permute-start = (bf16[2,24,1024]{2,1,0:T(8,128)(2,1)}, bf16[2,24,1024]{2,1,0:T(8,128)(2,1)S(1)}, u32[]{:S(2)}, u32[]{:S(2)}) collective-permute-start(bf16[2,24,1024]{2,1,0:T(8,128)(2,1)} %flows.5), channel_id=1, source_target_pairs={{0,1},{1,2},{2,3},{3,0},{4,5},{5,6},{6,7},{7,4},{8,9},{9,10},{10,1... | collective-permute-start | bytes 294920 | tf_op jit(solution)/shard_map/ppermute | solution.py:477
  5.6 12.5 %copy-start = (bf16[64,128,128]{2,1,0:T(8,128)(2,1)S(1)}, bf16[64,128,128]{2,1,0:T(8,128)(2,1)}, u32[]{:S(2)}) copy-start(bf16[64,128,128]{2,1,0:T(8,128)(2,1)} %mats.3) | copy-start | bytes 6291460
  5.6 12.5 %copy-start.3 = (s32[64]{0:T(128)S(1)}, s32[64]{0:T(128)}, u32[]{:S(2)}) copy-start(s32[64]{0:T(128)} %rest_3_.1) | copy-start | bytes 772
  5.6 12.5 %copy-start.4 = (s32[64]{0:T(128)S(1)}, s32[64]{0:T(128)}, u32[]{:S(2)}) copy-start(s32[64]{0:T(128)} %path.3) | copy-start | bytes 772
  5.6 12.4 %copy-start.5 = (s32[64]{0:T(128)S(1)}, s32[64]{0:T(128)}, u32[]{:S(2)}) copy-start(s32[64]{0:T(128)} %link.3) | copy-start | bytes 772
  5.6 12.4 %copy-start.6 = (s32[64]{0:T(128)S(1)}, s32[64]{0:T(128)}, u32[]{:S(2)}) copy-start(s32[64]{0:T(128)} %lag.3) | copy-start | bytes 772
  8.1 4.1 %collective-permute-start.1 = (f16[8,48,128]{2,1,0:T(8,128)(2,1)S(1)}, f16[8,48,128]{2,1,0:T(8,128)(2,1)S(1)}, u32[]{:S(2)}, u32[]{:S(2)}) collective-permute-start(f16[8,48,128]{2,1,0:T(8,128)(2,1)S(1)} %convert_element_type.42), channel_id=1, source_target_pairs={{0,4},{4,0},{8,12},{12,8},{16,20},{20,16},{24,28},{28,24},{1,5},{5... | collective-permute-start | bytes 294920 | tf_op jit(solution)/shard_map/ppermute | solution.py:493
  9.4 5.7 %collective-permute-start.3 = (f16[8,48,128]{2,1,0:T(8,128)(2,1)S(1)}, f16[8,48,128]{2,1,0:T(8,128)(2,1)S(1)}, u32[]{:S(2)}, u32[]{:S(2)}) collective-permute-start(f16[8,48,128]{2,1,0:T(8,128)(2,1)S(1)} %convert_element_type.46), channel_id=1, source_target_pairs={{0,4},{4,0},{8,12},{12,8},{16,20},{20,16},{24,28},{28,24},{1,5},{5... | collective-permute-start | bytes 294920 | tf_op jit(solution)/shard_map/ppermute | solution.py:493
  9.7 6.9 %collective-permute-start.5 = (f16[8,48,128]{2,1,0:T(8,128)(2,1)S(1)}, f16[8,48,128]{2,1,0:T(8,128)(2,1)S(1)}, u32[]{:S(2)}, u32[]{:S(2)}) collective-permute-start(f16[8,48,128]{2,1,0:T(8,128)(2,1)S(1)} %convert_element_type.50), channel_id=1, source_target_pairs={{0,4},{4,0},{8,12},{12,8},{16,20},{20,16},{24,28},{28,24},{1,5},{5... | collective-permute-start | bytes 294920 | tf_op jit(solution)/shard_map/ppermute | solution.py:493
  11.0 10.0 %collective-permute-start.7 = (f16[8,48,128]{2,1,0:T(8,128)(2,1)S(1)}, f16[8,48,128]{2,1,0:T(8,128)(2,1)S(1)}, u32[]{:S(2)}, u32[]{:S(2)}) collective-permute-start(f16[8,48,128]{2,1,0:T(8,128)(2,1)S(1)} %convert_element_type.54), channel_id=1, source_target_pairs={{0,4},{4,0},{8,12},{12,8},{16,20},{20,16},{24,28},{28,24},{1,5},{5... | collective-permute-start | bytes 294920 | tf_op jit(solution)/shard_map/ppermute | solution.py:493
  12.2 11.4 %copy-start.2 = (f32[2,24,1024]{2,1,0:T(8,128)S(1)}, f32[2,24,1024]{2,1,0:T(8,128)}, u32[]{:S(2)}) copy-start(f32[2,24,1024]{2,1,0:T(8,128)} %counts.3) | copy-start | bytes 589828
  12.3 8.8 %collective-permute-start.2 = (f16[8,48,128]{2,1,0:T(8,128)(2,1)S(1)}, f16[8,48,128]{2,1,0:T(8,128)(2,1)S(1)}, u32[]{:S(2)}, u32[]{:S(2)}) collective-permute-start(f16[8,48,128]{2,1,0:T(8,128)(2,1)S(1)} %add_convert_fusion.2), channel_id=1, source_target_pairs={{0,24},{4,28},{8,16},{12,20},{16,8},{20,12},{24,0},{28,4},{1,25},{... | collective-permute-start | bytes 294920 | tf_op jit(solution)/shard_map/ppermute | solution.py:493
  15.1 8.4 %collective-permute-start.4 = (f16[8,48,128]{2,1,0:T(8,128)(2,1)S(1)}, f16[8,48,128]{2,1,0:T(8,128)(2,1)S(1)}, u32[]{:S(2)}, u32[]{:S(2)}) collective-permute-start(f16[8,48,128]{2,1,0:T(8,128)(2,1)S(1)} %add_convert_fusion.1), channel_id=1, source_target_pairs={{0,16},{4,20},{8,24},{12,28},{16,0},{20,4},{24,8},{28,12},{1,17},{... | collective-permute-start | bytes 294920 | tf_op jit(solution)/shard_map/ppermute | solution.py:493
  16.7 6.9 %collective-permute-start.6 = (f16[8,48,128]{2,1,0:T(8,128)(2,1)S(1)}, f16[8,48,128]{2,1,0:T(8,128)(2,1)S(1)}, u32[]{:S(2)}, u32[]{:S(2)}) collective-permute-start(f16[8,48,128]{2,1,0:T(8,128)(2,1)S(1)} %add_convert_fusion), channel_id=1, source_target_pairs={{0,8},{4,12},{8,0},{12,4},{16,24},{20,28},{24,16},{28,20},{1,9},{5... | collective-permute-start | bytes 294920 | tf_op jit(solution)/shard_map/ppermute | solution.py:493
  23.7 6.9 %collective-permute-start.8 = (bf16[8,48,128]{2,1,0:T(8,128)(2,1)S(1)}, bf16[8,48,128]{2,1,0:T(8,128)(2,1)S(1)}, u32[]{:S(2)}, u32[]{:S(2)}) collective-permute-start(bf16[8,48,128]{2,1,0:T(8,128)(2,1)S(1)} %shard_map.133.signal), channel_id=1, source_target_pairs={{0,24},{4,28},{8,16},{12,20},{16,8},{20,12},{24,0},{28,4},{1,25},{... | collective-permute-start | bytes 294920 | tf_op jit(solution)/shard_map/ppermute | solution.py:493
  26.3 4.7 %collective-permute-start.10 = (bf16[8,48,128]{2,1,0:T(8,128)(2,1)S(1)}, bf16[8,48,128]{2,1,0:T(8,128)(2,1)S(1)}, u32[]{:S(2)}, u32[]{:S(2)}) collective-permute-start(bf16[8,48,128]{2,1,0:T(8,128)(2,1)S(1)} %shard_map.133.signal), channel_id=1, source_target_pairs={{0,8},{4,12},{8,0},{12,4},{16,24},{20,28},{24,16},{28,20},{1,9},{5... | collective-permute-start | bytes 294920 | tf_op jit(solution)/shard_map/ppermute | solution.py:493
  26.3 7.6 %collective-permute-start.11 = (bf16[8,48,128]{2,1,0:T(8,128)(2,1)S(1)}, bf16[8,48,128]{2,1,0:T(8,128)(2,1)S(1)}, u32[]{:S(2)}, u32[]{:S(2)}) collective-permute-start(bf16[8,48,128]{2,1,0:T(8,128)(2,1)S(1)} %shard_map.133.signal), channel_id=1, source_target_pairs={{0,16},{4,20},{8,24},{12,28},{16,0},{20,4},{24,8},{28,12},{1,17},{... | collective-permute-start | bytes 294920 | tf_op jit(solution)/shard_map/ppermute | solution.py:493
  27.3 7.5 %collective-permute-start.9 = (bf16[8,48,128]{2,1,0:T(8,128)(2,1)S(1)}, bf16[8,48,128]{2,1,0:T(8,128)(2,1)S(1)}, u32[]{:S(2)}, u32[]{:S(2)}) collective-permute-start(bf16[8,48,128]{2,1,0:T(8,128)(2,1)S(1)} %shard_map.133.signal), channel_id=1, source_target_pairs={{0,4},{4,0},{8,12},{12,8},{16,20},{20,16},{24,28},{28,24},{1,5},{5... | collective-permute-start | bytes 294920 | tf_op jit(solution)/shard_map/ppermute | solution.py:493
  30.6 5.6 %collective-permute-start.12 = (bf16[8,48,128]{2,1,0:T(8,128)(2,1)S(1)}, bf16[8,48,128]{2,1,0:T(8,128)(2,1)S(1)}, u32[]{:S(2)}, u32[]{:S(2)}) collective-permute-start(bf16[8,48,128]{2,1,0:T(8,128)(2,1)S(1)} %collective-permute-done.8.rest_3_), channel_id=1, source_target_pairs={{0,4},{4,0},{8,12},{12,8},{16,20},{20,16},{24,28},{28,24},{1,5},{5... | collective-permute-start | bytes 294920 | tf_op jit(solution)/shard_map/ppermute | solution.py:493
  31.0 5.2 %collective-permute-start.13 = (bf16[8,48,128]{2,1,0:T(8,128)(2,1)S(1)}, bf16[8,48,128]{2,1,0:T(8,128)(2,1)S(1)}, u32[]{:S(2)}, u32[]{:S(2)}) collective-permute-start(bf16[8,48,128]{2,1,0:T(8,128)(2,1)S(1)} %collective-permute-done.10.rest_1_), channel_id=1, source_target_pairs={{0,4},{4,0},{8,12},{12,8},{16,20},{20,16},{24,28},{28,24},{1,5},{5... | collective-permute-start | bytes 294920 | tf_op jit(solution)/shard_map/ppermute | solution.py:493
  33.9 4.5 %collective-permute-start.14 = (bf16[8,48,128]{2,1,0:T(8,128)(2,1)S(1)}, bf16[8,48,128]{2,1,0:T(8,128)(2,1)S(1)}, u32[]{:S(2)}, u32[]{:S(2)}) collective-permute-start(bf16[8,48,128]{2,1,0:T(8,128)(2,1)S(1)} %collective-permute-done.11.rest_2_), channel_id=1, source_target_pairs={{0,4},{4,0},{8,12},{12,8},{16,20},{20,16},{24,28},{28,24},{1,5},{5... | collective-permute-start | bytes 294920 | tf_op jit(solution)/shard_map/ppermute | solution.py:493
  39.4 6.8 %collective-permute-start.15 = (f32[16,16,128]{2,1,0:T(8,128)S(1)}, f32[16,16,128]{2,1,0:T(8,128)S(1)}, u32[]{:S(2)}, u32[]{:S(2)}) collective-permute-start(f32[16,16,128]{2,1,0:T(8,128)S(1)} %get-tuple-element.38), channel_id=1, source_target_pairs={{0,3},{1,0},{2,1},{3,2},{4,7},{5,4},{6,5},{7,6},{8,11},{9,8},{10,9... | collective-permute-start | bytes 393224 | tf_op jit(solution)/shard_map/ppermute | solution.py:547

commit v12 on v11

--- a/solution.py
+++ b/solution.py
@@ -338,12 +338,16 @@
             signal[b, d * minutes : (d + 1) * minutes, :] = (res / weight).astype(signal.dtype)
 
 
-def backward_local_kernel(days, path, link, lag, signal, mats, totals, counts, out, residual):
-    minutes, width = signal.shape[1] // days, totals.shape[2]
+def residual_kernel(days, totals, counts, residual):
+    width = totals.shape[2]
     for b in range(totals.shape[0]):
         for d in range(days):
             res, _ = residual_of(days, totals, counts, b, d)
             residual[d, :, b * width : (b + 1) * width] = res
+
+
+def backward_local_kernel(days, path, link, lag, signal, mats, out):
+    minutes = signal.shape[1] // days
     out[...] = jnp.zeros_like(out)
     unroll = step_of(mats.shape[0])
     mat, base, block = local_views(path, link, lag, mats, unroll, days * (HALO + minutes))
@@ -459,12 +463,8 @@
     remotes = remote_lag.shape[0]
     cap = (remotes + corridors - 2) // (corridors - 1)
     span = HALO + minutes
-    through = list(range(corridors - 2, 0, -2))
-    final = through[len(through) // 2]
-    rest = [s for s in through if s != final]
-    order = [s ^ 1 for s in (*rest, final)] + [1] + through
-    through = through[::-1]
-    order[-len(through):] = through
+    through = list(range(2, corridors, 2))
+    order = [s ^ 1 for s in reversed(through)] + [1] + through
     me = lax.axis_index("corr").astype(jnp.int32).reshape(1)
     group = lax.axis_index("tm").astype(jnp.int32).reshape(1)
     groups = lax.axis_size("tm")
@@ -523,28 +523,39 @@
         (totals, counts),
         [shape(piece, jnp.bfloat16)],
     )
-    arrived = {s: exchanged(signal, s) for s in (*through, 1)}
+    arrived = {s: exchanged(signal, s) for s in through}
     rows = [shape((paths * days * span, width), f32)]
-    total, link_residual = kernel_call(
+    (total,) = kernel_call(
         functools.partial(backward_local_kernel, days),
         local_index,
-        (signal, local_blocks, totals, counts),
-        [*rows, shape(counts.shape, f32)],
+        (signal, local_blocks),
+        rows,
     )
     arrived[through[-1]], total = lax.optimization_barrier((arrived[through[-1]], total))
-    for s in through:
+    for s in through[1:]:
         arrived[s ^ 1] = exchanged(arrived[s], 1)
+    passed = exchanged(jnp.concatenate([arrived[through[0]], signal], axis=0), 1)
     edge = shape((paths * days, HALO, width), f32)
-    for first, end, made in ((count, len(order), rows), (0, count, [*rows, edge])):
+    for first, end, parts, made in (
+        (count + 1, len(order), [arrived[s] for s in through], rows),
+        (0, count + 1, [*(arrived[s] for s in order[: count - 1]), passed], [*rows, edge]),
+    ):
         total, *early = kernel_call(
             functools.partial(backward_remote_kernel, days, cap, first, end, links),
             (table, ahead),
-            (remote_mats, total, *(arrived[s] for s in order[first:end])),
+            (remote_mats, total, *parts),
             made,
             [pltpu.VMEM(slots_shape, jnp.bfloat16)],
             cost=weight(BACKWARD_COST) if first else None,
         )
     spill = lax.ppermute(early[0], "tm", [(i, (i - 1) % groups) for i in range(groups)])
+    totals, total = lax.optimization_barrier((totals, total))
+    (link_residual,) = kernel_call(
+        functools.partial(residual_kernel, days),
+        (),
+        (totals, counts),
+        [shape(counts.shape, f32)],
+    )
     gradient, new_flows = kernel_call(
         functools.partial(finish_kernel, days, groups),
         (group,),

time: 47.2 us -> 46.2 us (0.979)
  starting transfers between devices: 21.5 us -> 18.8 us
  waiting for transfers between devices: 11.4 us -> 12.9 us
    ppermute x14 -> x13, waiting for transfers between devices: 7.41 us -> 11.2 us  [exchanged(): return lax.ppermute(part, 'corr', [(i, i ^ s) for i in range(corridors)])]
    ppermute x1, waiting for transfers between devices: 3.94 us -> 1.72 us  [per_device_dense(): lax.ppermute(early[0], 'tm', [(i, (i - 1) % groups) for i in range(groups)])]
    ppermute x14 -> x13, starting transfers between devices: 15.9 us -> 14 us  [exchanged(): return lax.ppermute(part, 'corr', [(i, i ^ s) for i in range(corridors)])]
    ppermute x1, starting transfers between devices: 2.89 us -> 2.15 us  [per_device_dense(): lax.ppermute(early[0], 'tm', [(i, (i - 1) % groups) for i in range(groups)])]
    pallas_call x7 -> x8, Pallas kernels: 10.9 us -> 10.9 us  [kernel_call(): pl.pallas_call(body, out_shape=out_shape, in_specs=[SMEM] * len(scalars)...]
  transfers between devices with their start and end apart: 16 -> 15, of which waited for: 5 -> 6; matrix products, arithmetic and copies ran while one was open for 0% -> 0% of each run, Pallas kernels for 19% -> 18%
where the time goes in v12:
time: 46.2 us; the launch traced here: 46 us
  starting transfers between devices  18.8 us (41%)
  Pallas kernels  13.1 us (28%)
  waiting for transfers between devices  12.9 us (28%)
  between operations  0.84 us (2%)
    ppermute x13, starting transfers between devices, exchanged(): return lax.ppermute(part, 'corr', [(i, i ^ s) for i in range(corridors)])  14 us
    ppermute x13, waiting for transfers between devices, exchanged(): return lax.ppermute(part, 'corr', [(i, i ^ s) for i in range(corridors)])  11.2 us
    pallas_call x8, Pallas kernels, kernel_call(): pl.pallas_call(body, out_shape=out_shape, in_specs=[SMEM] * len(scalars)...  10.9 us
    ppermute x1, starting transfers between devices, per_device_dense(): lax.ppermute(flows, 'tm', [(i, (i + 1) % groups) for i in range(groups)])  2.68 us
    pallas_call x1, Pallas kernels, per_device_dense(): pl.pallas_call(functools.partial(prepare_kernel, cap, order, links, CHUNK...  2.2 us
    ppermute x1, starting transfers between devices, per_device_dense(): lax.ppermute(early[0], 'tm', [(i, (i - 1) % groups) for i in range(groups)])  2.15 us
    ppermute x1, waiting for transfers between devices, per_device_dense(): lax.ppermute(early[0], 'tm', [(i, (i - 1) % groups) for i in range(groups)])  1.72 us
  transfers between devices with their start and end apart: 15, of which 6 were waited for; matrix products, arithmetic and copies ran while one was open for 0% of the time, Pallas kernels for 18%

profile of v12, /device:TPU:1, one launch (start us, length us, event | category | flops | bytes accessed | tf_op | source)
XLA Modules:
  0.0 46.0 jit_solution(5534875193629675554)
XLA Ops:
  0.6 0.0 copy-start.1
  0.6 2.7 %collective-permute-start = (bf16[2,24,1024]{2,1,0:T(8,128)(2,1)}, bf16[2,24,1024]{2,1,0:T(8,128)(2,1)S(1)}, u32[]{:S(2)}, u32[]{:S(2)}) collective-permute-start(bf16[2,24,1024]{2,1,0:T(8,128)(2,1)} %flows.5), channel_id=1, source_target_pairs={{0,1},{1,2},{2,3},{3,0},{4,5},{5,6},{6,7},{7,4},{8,9},{9,10},{10,1... | collective-permute-start | bytes 294920 | tf_op jit(solution)/shard_map/ppermute | solution.py:477
  3.3 2.2 %shard_map.131 = (s32[128]{0:T(128)S(1)}, bf16[64,128,128]{2,1,0:T(8,128)(2,1)S(1)}) custom-call(s32[1]{0:T(128)} %bitcast.1.me, s32[64]{0:T(128)} %rest_0_.1, s32[64]{0:T(128)} %rest_1_.1, s32[64]{0:T(128)} %rest_2_.1, s32[64]{0:T(128)} %rest_3_.1, bf16[64,128,128]{2,1,0:T(8,128)(2,1)} %rest_4_.1), custom_call_target="tpu_custom_call" | custom-call | tf_op jit(solution)/shard_map/pallas_call | solution.py:479
  5.5 0.0 collective-permute-done.before
  5.5 0.0 copy-done.1
  5.6 0.0 copy-start
  5.6 0.0 copy-start.3
  5.6 0.0 copy-start.4
  5.6 0.0 copy-start.5
  5.6 0.0 copy-start.6
  5.6 2.4 %shard_map.132 = (f32[8,48,128]{2,1,0:T(8,128)S(1)}, f32[8,48,128]{2,1,0:T(8,128)S(1)}, f32[8,48,128]{2,1,0:T(8,128)S(1)}, f32[8,48,128]{2,1,0:T(8,128)S(1)}, f3...) custom-call(s32[1]{0:T(128)} %bitcast.group, s32[128]{0:T(128)S(1)} %get-tuple-element.23.ahead, ...), custom_call_target="tpu_custom_call" | custom-call | tf_op jit(solution)/shard_map/pallas_call | solution.py:434
  8.1 1.3 %collective-permute-start.1 = (f16[8,48,128]{2,1,0:T(8,128)(2,1)S(1)}, f16[8,48,128]{2,1,0:T(8,128)(2,1)S(1)}, u32[]{:S(2)}, u32[]{:S(2)}) collective-permute-start(f16[8,48,128]{2,1,0:T(8,128)(2,1)S(1)} %convert_element_type.42), channel_id=1, source_target_pairs={{0,4},{4,0},{8,12},{12,8},{16,20},{20,16},{24,28},{28,24},{1,5},{5... | collective-permute-start | bytes 294920 | tf_op jit(solution)/shard_map/ppermute | solution.py:493
  9.4 0.3 collective-permute-start.3
  9.8 1.2 %collective-permute-start.5 = (f16[8,48,128]{2,1,0:T(8,128)(2,1)S(1)}, f16[8,48,128]{2,1,0:T(8,128)(2,1)S(1)}, u32[]{:S(2)}, u32[]{:S(2)}) collective-permute-start(f16[8,48,128]{2,1,0:T(8,128)(2,1)S(1)} %convert_element_type.50), channel_id=1, source_target_pairs={{0,4},{4,0},{8,12},{12,8},{16,20},{20,16},{24,28},{28,24},{1,5},{5... | collective-permute-start | bytes 294920 | tf_op jit(solution)/shard_map/ppermute | solution.py:493
  11.0 0.3 collective-permute-start.7
  11.4 0.9 %collective-permute-done.1 = f16[8,48,128]{2,1,0:T(8,128)(2,1)S(1)} collective-permute-done((f16[8,48,128]{2,1,0:T(8,128)(2,1)S(1)}, f16[8,48,128]{2,1,0:T(8,128)(2,1)S(1)}, u32[]{:S(2)}, u32[]{:S(2)}) %collective-permute-start.1) | collective-permute-done | bytes 98336 | tf_op jit(solution)/shard_map/ppermute | solution.py:493
  12.2 0.0 copy-start.2
  12.3 2.8 %collective-permute-start.2 = (f16[8,48,128]{2,1,0:T(8,128)(2,1)S(1)}, f16[8,48,128]{2,1,0:T(8,128)(2,1)S(1)}, u32[]{:S(2)}, u32[]{:S(2)}) collective-permute-start(f16[8,48,128]{2,1,0:T(8,128)(2,1)S(1)} %add_convert_fusion.2), channel_id=1, source_target_pairs={{0,24},{4,28},{8,16},{12,20},{16,8},{20,12},{24,0},{28,4},{1,25},{... | collective-permute-start | bytes 294920 | tf_op jit(solution)/shard_map/ppermute | solution.py:493
  15.0 0.0 collective-permute-done.3
  15.1 1.6 %collective-permute-start.4 = (f16[8,48,128]{2,1,0:T(8,128)(2,1)S(1)}, f16[8,48,128]{2,1,0:T(8,128)(2,1)S(1)}, u32[]{:S(2)}, u32[]{:S(2)}) collective-permute-start(f16[8,48,128]{2,1,0:T(8,128)(2,1)S(1)} %add_convert_fusion.1), channel_id=1, source_target_pairs={{0,16},{4,20},{8,24},{12,28},{16,0},{20,4},{24,8},{28,12},{1,17},{... | collective-permute-start | bytes 294920 | tf_op jit(solution)/shard_map/ppermute | solution.py:493
  16.6 0.0 collective-permute-done.5
  16.7 1.4 %collective-permute-start.6 = (f16[8,48,128]{2,1,0:T(8,128)(2,1)S(1)}, f16[8,48,128]{2,1,0:T(8,128)(2,1)S(1)}, u32[]{:S(2)}, u32[]{:S(2)}) collective-permute-start(f16[8,48,128]{2,1,0:T(8,128)(2,1)S(1)} %add_convert_fusion), channel_id=1, source_target_pairs={{0,8},{4,12},{8,0},{12,4},{16,24},{20,28},{24,16},{28,20},{1,9},{5... | collective-permute-start | bytes 294920 | tf_op jit(solution)/shard_map/ppermute | solution.py:493
  18.1 0.0 copy-done
  18.1 0.0 copy-done.3
  18.1 0.0 copy-done.4
  18.1 0.0 copy-done.5
  18.1 0.0 copy-done.6
  18.1 3.0 %shard_map.130 = (f32[8,48,128]{2,1,0:T(8,128)S(1)}, s32[87]{0:T(128)S(1)}) custom-call(s32[1]{0:T(128)} %bitcast.group, s32[1]{0:T(128)} %bitcast.1.me, s32[64]{0:T(128)S(1)} %copy-done.6, s32[64]{0:T(128)S(1)} %copy-done.3, s32[64]{0:T(128)S(1)} %copy-done.4, s32[64]{0:T(128)S(1)} %copy-done.5, bf16[2,24,1024]{2,1,0:T(8,128)(2,1)S(1)} %copy-done.1, ...), custom_call_target="tpu_custom_call" | custom-call | tf_op jit(solution)/shard_map/pallas_call | solution.py:434
  21.1 0.0 collective-permute-done.7
  21.1 0.0 collective-permute-done.2
  21.1 2.4 %collective-permute-done.4 = f16[8,48,128]{2,1,0:T(8,128)(2,1)S(1)} collective-permute-done((f16[8,48,128]{2,1,0:T(8,128)(2,1)S(1)}, f16[8,48,128]{2,1,0:T(8,128)(2,1)S(1)}, u32[]{:S(2)}, u32[]{:S(2)}) %collective-permute-start.4) | collective-permute-done | bytes 98336 | tf_op jit(solution)/shard_map/ppermute | solution.py:493
  23.5 0.0 collective-permute-done.6
  23.5 0.1 convert_add_fusion.totals
  23.6 0.0 copy-done.2
  23.7 0.1 collective-permute-start.9
  23.8 2.6 %collective-permute-start.8 = (bf16[8,48,128]{2,1,0:T(8,128)(2,1)S(1)}, bf16[8,48,128]{2,1,0:T(8,128)(2,1)S(1)}, u32[]{:S(2)}, u32[]{:S(2)}) collective-permute-start(bf16[8,48,128]{2,1,0:T(8,128)(2,1)S(1)} %shard_map.133.signal), channel_id=1, source_target_pairs={{0,24},{4,28},{8,16},{12,20},{16,8},{20,12},{24,0},{28,4},{1,25},{... | collective-permute-start | bytes 294920 | tf_op jit(solution)/shard_map/ppermute | solution.py:493
  26.4 0.2 collective-permute-start.10
  26.6 0.6 %collective-permute-done.9.rest_0_ = bf16[8,48,128]{2,1,0:T(8,128)(2,1)S(1)} collective-permute-done((bf16[8,48,128]{2,1,0:T(8,128)(2,1)S(1)}, bf16[8,48,128]{2,1,0:T(8,128)(2,1)S(1)}, u32[]{:S(2)}, u32[]{:S(2)}) %collective-permute-start.9) | collective-permute-done | bytes 98336 | tf_op jit(solution)/shard_map/ppermute | solution.py:493
  27.2 1.1 %collective-permute-start.13 = (bf16[16,48,128]{2,1,0:T(8,128)(2,1)S(1)}, bf16[16,48,128]{2,1,0:T(8,128)(2,1)S(1)}, u32[]{:S(2)}, u32[]{:S(2)}) collective-permute-start(bf16[16,48,128]{2,1,0:T(8,128)(2,1)S(1)} %pad_maximum_fusion), channel_id=1, source_target_pairs={{0,4},{4,0},{8,12},{12,8},{16,20},{20,16},{24,28},{28,24},{1,5},{5... | collective-permute-start | bytes 589832 | tf_op jit(solution)/shard_map/ppermute | solution.py:493
  28.4 1.5 %shard_map.134.start = f32[640,128]{1,0:T(8,128)S(1)} custom-call(s32[64]{0:T(128)S(1)} %copy-done.3, s32[64]{0:T(128)S(1)} %copy-done.4, s32[64]{0:T(128)S(1)} %copy-done.5, bf16[8,48,128]{2,1,0:T(8,128)(2,1)S(1)} %shard_map.133.signal, bf16[64,128,128]{2,1,0:T(8,128)(2,1)S(1)} %copy-done), custom_call_target="tpu_custom_call" | custom-call | tf_op jit(solution)/shard_map/pallas_call | solution.py:434
  29.9 0.0 collective-permute-done.8.rest_2_
  29.9 0.5 %collective-permute-start.11 = (bf16[8,48,128]{2,1,0:T(8,128)(2,1)S(1)}, bf16[8,48,128]{2,1,0:T(8,128)(2,1)S(1)}, u32[]{:S(2)}, u32[]{:S(2)}) collective-permute-start(bf16[8,48,128]{2,1,0:T(8,128)(2,1)S(1)} %collective-permute-done.8.rest_2_), channel_id=1, source_target_pairs={{0,4},{4,0},{8,12},{12,8},{16,20},{20,16},{24,28},{28,24},{1,5},{5... | collective-permute-start | bytes 294920 | tf_op jit(solution)/shard_map/ppermute | solution.py:493
  30.4 4.3 %collective-permute-done.10.rest_1_ = bf16[8,48,128]{2,1,0:T(8,128)(2,1)S(1)} collective-permute-done((bf16[8,48,128]{2,1,0:T(8,128)(2,1)S(1)}, bf16[8,48,128]{2,1,0:T(8,128)(2,1)S(1)}, u32[]{:S(2)}, u32[]{:S(2)}) %collective-permute-start.10) | collective-permute-done | bytes 98336 | tf_op jit(solution)/shard_map/ppermute | solution.py:493
  34.7 0.6 %collective-permute-start.12 = (bf16[8,48,128]{2,1,0:T(8,128)(2,1)S(1)}, bf16[8,48,128]{2,1,0:T(8,128)(2,1)S(1)}, u32[]{:S(2)}, u32[]{:S(2)}) collective-permute-start(bf16[8,48,128]{2,1,0:T(8,128)(2,1)S(1)} %collective-permute-done.10.rest_1_), channel_id=1, source_target_pairs={{0,4},{4,0},{8,12},{12,8},{16,20},{20,16},{24,28},{28,24},{1,5},{5... | collective-permute-start | bytes 294920 | tf_op jit(solution)/shard_map/ppermute | solution.py:493
  35.3 1.0 %shard_map.135.start = f32[640,128]{1,0:T(8,128)S(1)} custom-call(s32[87]{0:T(128)S(1)} %get-tuple-element.32.table, s32[128]{0:T(128)S(1)} %get-tuple-element.23.ahead, bf16[64,128,128]{2,1,0:T(8,128)(2,1)S(1)} %get-tuple-element.24.mats, f32[640,128]{1,0:T(8,128)S(1)} %shard_map.134.start, bf16[8,48,128]{2,1,0:T(8,128)(2,1)S(1)} %collective-permute-done.9.rest_0_, ...), custom_call_target="tpu_custom_call" | custom-call | flops 500000000 | bytes 1500000 | tf_op jit(solution)/shard_map/pallas_call | solution.py:434
  36.3 0.0 collective-permute-done.11.rest_0_
  36.3 3.0 %collective-permute-done.12.rest_1_ = bf16[8,48,128]{2,1,0:T(8,128)(2,1)S(1)} collective-permute-done((bf16[8,48,128]{2,1,0:T(8,128)(2,1)S(1)}, bf16[8,48,128]{2,1,0:T(8,128)(2,1)S(1)}, u32[]{:S(2)}, u32[]{:S(2)}) %collective-permute-start.12) | collective-permute-done | bytes 98336 | tf_op jit(solution)/shard_map/ppermute | solution.py:493
  39.3 0.0 collective-permute-done.13.rest_2_
  39.3 1.4 %shard_map.136 = (f32[640,128]{1,0:T(8,128)S(1)}, f32[16,16,128]{2,1,0:T(8,128)S(1)}) custom-call(s32[87]{0:T(128)S(1)} %get-tuple-element.32.table, s32[128]{0:T(128)S(1)} %get-tuple-element.23.ahead, bf16[64,128,128]{2,1,0:T(8,128)(2,1)S(1)} %get-tuple-element.24.mats, f32[640,128]{1,0:T(8,128)S(1)} %shard_map.135.start, ...), custom_call_target="tpu_custom_call" | custom-call | tf_op jit(solution)/shard_map/pallas_call | solution.py:434
  40.7 2.2 %collective-permute-start.14 = (f32[16,16,128]{2,1,0:T(8,128)S(1)}, f32[16,16,128]{2,1,0:T(8,128)S(1)}, u32[]{:S(2)}, u32[]{:S(2)}) collective-permute-start(f32[16,16,128]{2,1,0:T(8,128)S(1)} %get-tuple-element.38), channel_id=1, source_target_pairs={{0,3},{1,0},{2,1},{3,2},{4,7},{5,4},{6,5},{7,6},{8,11},{9,8},{10,9... | collective-permute-start | bytes 393224 | tf_op jit(solution)/shard_map/ppermute | solution.py:551
  42.8 0.7 %shard_map.137 = f32[2,24,1024]{2,1,0:T(8,128)} custom-call(f32[8,48,128]{2,1,0:T(8,128)S(1)} %convert_add_fusion.totals, f32[2,24,1024]{2,1,0:T(8,128)S(1)} %copy-done.2), custom_call_target="tpu_custom_call" | custom-call | tf_op jit(solution)/shard_map/pallas_call | solution.py:434
  43.5 1.7 %collective-permute-done.14.spill = f32[16,16,128]{2,1,0:T(8,128)S(1)} collective-permute-done((f32[16,16,128]{2,1,0:T(8,128)S(1)}, f32[16,16,128]{2,1,0:T(8,128)S(1)}, u32[]{:S(2)}, u32[]{:S(2)}) %collective-permute-start.14) | collective-permute-done | bytes 131104 | tf_op jit(solution)/shard_map/ppermute | solution.py:551
  45.2 0.8 %shard_map.138 = (f32[2,24,1024]{2,1,0:T(8,128)}, f32[2,24,1024]{2,1,0:T(8,128)}) custom-call(s32[1]{0:T(128)} %bitcast.group, f32[640,128]{1,0:T(8,128)S(1)} %get-tuple-element.37.total, f32[16,16,128]{2,1,0:T(8,128)S(1)} %collective-permute-done.14.spill, bf16[2,24,1024]{2,1,0:T(8,128)(2,1)S(1)} %copy-done.1), custom_call_target="tpu_custom_call" | custom-call | tf_op jit(solution)/shard_map/pallas_call | solution.py:434
  (9 shorter events, 0.2 us)
Async XLA Ops:
  0.6 4.9 %copy-start.1 = (bf16[2,24,1024]{2,1,0:T(8,128)(2,1)S(1)}, bf16[2,24,1024]{2,1,0:T(8,128)(2,1)}, u32[]{:S(2)}) copy-start(bf16[2,24,1024]{2,1,0:T(8,128)(2,1)} %flows.5) | copy-start | bytes 294916
  0.6 4.9 %collective-permute-start = (bf16[2,24,1024]{2,1,0:T(8,128)(2,1)}, bf16[2,24,1024]{2,1,0:T(8,128)(2,1)S(1)}, u32[]{:S(2)}, u32[]{:S(2)}) collective-permute-start(bf16[2,24,1024]{2,1,0:T(8,128)(2,1)} %flows.5), channel_id=1, source_target_pairs={{0,1},{1,2},{2,3},{3,0},{4,5},{5,6},{6,7},{7,4},{8,9},{9,10},{10,1... | collective-permute-start | bytes 294920 | tf_op jit(solution)/shard_map/ppermute | solution.py:477
  5.6 12.5 %copy-start = (bf16[64,128,128]{2,1,0:T(8,128)(2,1)S(1)}, bf16[64,128,128]{2,1,0:T(8,128)(2,1)}, u32[]{:S(2)}) copy-start(bf16[64,128,128]{2,1,0:T(8,128)(2,1)} %mats.3) | copy-start | bytes 6291460
  5.6 12.5 %copy-start.3 = (s32[64]{0:T(128)S(1)}, s32[64]{0:T(128)}, u32[]{:S(2)}) copy-start(s32[64]{0:T(128)} %path.3) | copy-start | bytes 772
  5.6 12.5 %copy-start.4 = (s32[64]{0:T(128)S(1)}, s32[64]{0:T(128)}, u32[]{:S(2)}) copy-start(s32[64]{0:T(128)} %link.3) | copy-start | bytes 772
  5.6 12.5 %copy-start.5 = (s32[64]{0:T(128)S(1)}, s32[64]{0:T(128)}, u32[]{:S(2)}) copy-start(s32[64]{0:T(128)} %lag.3) | copy-start | bytes 772
  5.6 12.5 %copy-start.6 = (s32[64]{0:T(128)S(1)}, s32[64]{0:T(128)}, u32[]{:S(2)}) copy-start(s32[64]{0:T(128)} %rest_3_.1) | copy-start | bytes 772
  8.1 4.2 %collective-permute-start.1 = (f16[8,48,128]{2,1,0:T(8,128)(2,1)S(1)}, f16[8,48,128]{2,1,0:T(8,128)(2,1)S(1)}, u32[]{:S(2)}, u32[]{:S(2)}) collective-permute-start(f16[8,48,128]{2,1,0:T(8,128)(2,1)S(1)} %convert_element_type.42), channel_id=1, source_target_pairs={{0,4},{4,0},{8,12},{12,8},{16,20},{20,16},{24,28},{28,24},{1,5},{5... | collective-permute-start | bytes 294920 | tf_op jit(solution)/shard_map/ppermute | solution.py:493
  9.4 5.7 %collective-permute-start.3 = (f16[8,48,128]{2,1,0:T(8,128)(2,1)S(1)}, f16[8,48,128]{2,1,0:T(8,128)(2,1)S(1)}, u32[]{:S(2)}, u32[]{:S(2)}) collective-permute-start(f16[8,48,128]{2,1,0:T(8,128)(2,1)S(1)} %convert_element_type.46), channel_id=1, source_target_pairs={{0,4},{4,0},{8,12},{12,8},{16,20},{20,16},{24,28},{28,24},{1,5},{5... | collective-permute-start | bytes 294920 | tf_op jit(solution)/shard_map/ppermute | solution.py:493
  9.8 6.9 %collective-permute-start.5 = (f16[8,48,128]{2,1,0:T(8,128)(2,1)S(1)}, f16[8,48,128]{2,1,0:T(8,128)(2,1)S(1)}, u32[]{:S(2)}, u32[]{:S(2)}) collective-permute-start(f16[8,48,128]{2,1,0:T(8,128)(2,1)S(1)} %convert_element_type.50), channel_id=1, source_target_pairs={{0,4},{4,0},{8,12},{12,8},{16,20},{20,16},{24,28},{28,24},{1,5},{5... | collective-permute-start | bytes 294920 | tf_op jit(solution)/shard_map/ppermute | solution.py:493
  11.0 10.1 %collective-permute-start.7 = (f16[8,48,128]{2,1,0:T(8,128)(2,1)S(1)}, f16[8,48,128]{2,1,0:T(8,128)(2,1)S(1)}, u32[]{:S(2)}, u32[]{:S(2)}) collective-permute-start(f16[8,48,128]{2,1,0:T(8,128)(2,1)S(1)} %convert_element_type.54), channel_id=1, source_target_pairs={{0,4},{4,0},{8,12},{12,8},{16,20},{20,16},{24,28},{28,24},{1,5},{5... | collective-permute-start | bytes 294920 | tf_op jit(solution)/shard_map/ppermute | solution.py:493
  12.2 11.4 %copy-start.2 = (f32[2,24,1024]{2,1,0:T(8,128)S(1)}, f32[2,24,1024]{2,1,0:T(8,128)}, u32[]{:S(2)}) copy-start(f32[2,24,1024]{2,1,0:T(8,128)} %counts.3) | copy-start | bytes 589828
  12.3 8.8 %collective-permute-start.2 = (f16[8,48,128]{2,1,0:T(8,128)(2,1)S(1)}, f16[8,48,128]{2,1,0:T(8,128)(2,1)S(1)}, u32[]{:S(2)}, u32[]{:S(2)}) collective-permute-start(f16[8,48,128]{2,1,0:T(8,128)(2,1)S(1)} %add_convert_fusion.2), channel_id=1, source_target_pairs={{0,24},{4,28},{8,16},{12,20},{16,8},{20,12},{24,0},{28,4},{1,25},{... | collective-permute-start | bytes 294920 | tf_op jit(solution)/shard_map/ppermute | solution.py:493
  15.1 8.4 %collective-permute-start.4 = (f16[8,48,128]{2,1,0:T(8,128)(2,1)S(1)}, f16[8,48,128]{2,1,0:T(8,128)(2,1)S(1)}, u32[]{:S(2)}, u32[]{:S(2)}) collective-permute-start(f16[8,48,128]{2,1,0:T(8,128)(2,1)S(1)} %add_convert_fusion.1), channel_id=1, source_target_pairs={{0,16},{4,20},{8,24},{12,28},{16,0},{20,4},{24,8},{28,12},{1,17},{... | collective-permute-start | bytes 294920 | tf_op jit(solution)/shard_map/ppermute | solution.py:493
  16.7 6.8 %collective-permute-start.6 = (f16[8,48,128]{2,1,0:T(8,128)(2,1)S(1)}, f16[8,48,128]{2,1,0:T(8,128)(2,1)S(1)}, u32[]{:S(2)}, u32[]{:S(2)}) collective-permute-start(f16[8,48,128]{2,1,0:T(8,128)(2,1)S(1)} %add_convert_fusion), channel_id=1, source_target_pairs={{0,8},{4,12},{8,0},{12,4},{16,24},{20,28},{24,16},{28,20},{1,9},{5... | collective-permute-start | bytes 294920 | tf_op jit(solution)/shard_map/ppermute | solution.py:493
  23.7 3.5 %collective-permute-start.9 = (bf16[8,48,128]{2,1,0:T(8,128)(2,1)S(1)}, bf16[8,48,128]{2,1,0:T(8,128)(2,1)S(1)}, u32[]{:S(2)}, u32[]{:S(2)}) collective-permute-start(bf16[8,48,128]{2,1,0:T(8,128)(2,1)S(1)} %shard_map.133.signal), channel_id=1, source_target_pairs={{0,8},{4,12},{8,0},{12,4},{16,24},{20,28},{24,16},{28,20},{1,9},{5... | collective-permute-start | bytes 294920 | tf_op jit(solution)/shard_map/ppermute | solution.py:493
  23.8 6.1 %collective-permute-start.8 = (bf16[8,48,128]{2,1,0:T(8,128)(2,1)S(1)}, bf16[8,48,128]{2,1,0:T(8,128)(2,1)S(1)}, u32[]{:S(2)}, u32[]{:S(2)}) collective-permute-start(bf16[8,48,128]{2,1,0:T(8,128)(2,1)S(1)} %shard_map.133.signal), channel_id=1, source_target_pairs={{0,24},{4,28},{8,16},{12,20},{16,8},{20,12},{24,0},{28,4},{1,25},{... | collective-permute-start | bytes 294920 | tf_op jit(solution)/shard_map/ppermute | solution.py:493
  26.4 8.3 %collective-permute-start.10 = (bf16[8,48,128]{2,1,0:T(8,128)(2,1)S(1)}, bf16[8,48,128]{2,1,0:T(8,128)(2,1)S(1)}, u32[]{:S(2)}, u32[]{:S(2)}) collective-permute-start(bf16[8,48,128]{2,1,0:T(8,128)(2,1)S(1)} %shard_map.133.signal), channel_id=1, source_target_pairs={{0,16},{4,20},{8,24},{12,28},{16,0},{20,4},{24,8},{28,12},{1,17},{... | collective-permute-start | bytes 294920 | tf_op jit(solution)/shard_map/ppermute | solution.py:493
  27.2 12.0 %collective-permute-start.13 = (bf16[16,48,128]{2,1,0:T(8,128)(2,1)S(1)}, bf16[16,48,128]{2,1,0:T(8,128)(2,1)S(1)}, u32[]{:S(2)}, u32[]{:S(2)}) collective-permute-start(bf16[16,48,128]{2,1,0:T(8,128)(2,1)S(1)} %pad_maximum_fusion), channel_id=1, source_target_pairs={{0,4},{4,0},{8,12},{12,8},{16,20},{20,16},{24,28},{28,24},{1,5},{5... | collective-permute-start | bytes 589832 | tf_op jit(solution)/shard_map/ppermute | solution.py:493
  29.9 6.4 %collective-permute-start.11 = (bf16[8,48,128]{2,1,0:T(8,128)(2,1)S(1)}, bf16[8,48,128]{2,1,0:T(8,128)(2,1)S(1)}, u32[]{:S(2)}, u32[]{:S(2)}) collective-permute-start(bf16[8,48,128]{2,1,0:T(8,128)(2,1)S(1)} %collective-permute-done.8.rest_2_), channel_id=1, source_target_pairs={{0,4},{4,0},{8,12},{12,8},{16,20},{20,16},{24,28},{28,24},{1,5},{5... | collective-permute-start | bytes 294920 | tf_op jit(solution)/shard_map/ppermute | solution.py:493
  34.7 4.5 %collective-permute-start.12 = (bf16[8,48,128]{2,1,0:T(8,128)(2,1)S(1)}, bf16[8,48,128]{2,1,0:T(8,128)(2,1)S(1)}, u32[]{:S(2)}, u32[]{:S(2)}) collective-permute-start(bf16[8,48,128]{2,1,0:T(8,128)(2,1)S(1)} %collective-permute-done.10.rest_1_), channel_id=1, source_target_pairs={{0,4},{4,0},{8,12},{12,8},{16,20},{20,16},{24,28},{28,24},{1,5},{5... | collective-permute-start | bytes 294920 | tf_op jit(solution)/shard_map/ppermute | solution.py:493
  40.7 4.6 %collective-permute-start.14 = (f32[16,16,128]{2,1,0:T(8,128)S(1)}, f32[16,16,128]{2,1,0:T(8,128)S(1)}, u32[]{:S(2)}, u32[]{:S(2)}) collective-permute-start(f32[16,16,128]{2,1,0:T(8,128)S(1)} %get-tuple-element.38), channel_id=1, source_target_pairs={{0,3},{1,0},{2,1},{3,2},{4,7},{5,4},{6,5},{7,6},{8,11},{9,8},{10,9... | collective-permute-start | bytes 393224 | tf_op jit(solution)/shard_map/ppermute | solution.py:551

commit v13 on v12

--- a/solution.py
+++ b/solution.py
@@ -373,8 +373,12 @@
     minutes = signals[0].shape[1] // days
     place = first * links
     for part in signals:
-        everyone[place : place + part.shape[0]] = part[...]
-        place += part.shape[0]
+        everyone[place : place + links] = part[...]
+        place += links
+    if first == 0:
+        half = links // 2
+        everyone[place - links : place - half] = signals[-1][links - half :]
+        everyone[place - half : place] = signals[-1][: links - half]
     blank = everyone.shape[0] - 1
     everyone[blank] = jnp.zeros(everyone.shape[1:], everyone.dtype)
     out[...] = start[...]
@@ -523,7 +527,11 @@
         (totals, counts),
         [shape(piece, jnp.bfloat16)],
     )
-    arrived = {s: exchanged(signal, s) for s in through}
+    arrived = {s: exchanged(signal, s) for s in (*through, 1)}
+    half = links // 2
+    first = arrived[through[0]]
+    turned = jnp.concatenate([first[half:], first[:half]], axis=0)
+    passed = exchanged(turned, 1)
     rows = [shape((paths * days * span, width), f32)]
     (total,) = kernel_call(
         functools.partial(backward_local_kernel, days),
@@ -531,14 +539,12 @@
         (signal, local_blocks),
         rows,
     )
-    arrived[through[-1]], total = lax.optimization_barrier((arrived[through[-1]], total))
     for s in through[1:]:
         arrived[s ^ 1] = exchanged(arrived[s], 1)
-    passed = exchanged(jnp.concatenate([arrived[through[0]], signal], axis=0), 1)
     edge = shape((paths * days, HALO, width), f32)
     for first, end, parts, made in (
-        (count + 1, len(order), [arrived[s] for s in through], rows),
-        (0, count + 1, [*(arrived[s] for s in order[: count - 1]), passed], [*rows, edge]),
+        (count, len(order), [arrived[s] for s in (1, *through)], rows),
+        (0, count, [*(arrived[s] for s in order[: count - 1]), passed], [*rows, edge]),
     ):
         total, *early = kernel_call(
             functools.partial(backward_remote_kernel, days, cap, first, end, links),

time: 46.2 us -> 47.8 us (1.035)
  starting transfers between devices: 18.8 us -> 22.1 us
  waiting for transfers between devices: 12.9 us -> 11.3 us
    ppermute x13 -> x14, waiting for transfers between devices: 11.2 us -> 7.82 us  [exchanged(): return lax.ppermute(part, 'corr', [(i, i ^ s) for i in range(corridors)])]
    ppermute x1, starting transfers between devices: 2.15 us -> 3.93 us  [per_device_dense(): lax.ppermute(early[0], 'tm', [(i, (i - 1) % groups) for i in range(groups)])]
    ppermute x1, waiting for transfers between devices: 1.72 us -> 3.45 us  [per_device_dense(): lax.ppermute(early[0], 'tm', [(i, (i - 1) % groups) for i in range(groups)])]
    ppermute x13 -> x14, starting transfers between devices: 14 us -> 15.5 us  [exchanged(): return lax.ppermute(part, 'corr', [(i, i ^ s) for i in range(corridors)])]
  transfers between devices with their start and end apart: 15 -> 16, of which waited for: 6 -> 5; matrix products, arithmetic and copies ran while one was open for 0% -> 0% of each run, Pallas kernels for 18% -> 19%
where the time goes in v13:
time: 47.8 us; the launch traced here: 47.7 us
  starting transfers between devices  22.1 us (46%)
  Pallas kernels  13.1 us (27%)
  waiting for transfers between devices  11.3 us (24%)
  between operations  0.86 us (2%)
    ppermute x14, starting transfers between devices, exchanged(): return lax.ppermute(part, 'corr', [(i, i ^ s) for i in range(corridors)])  15.5 us
    pallas_call x8, Pallas kernels, kernel_call(): pl.pallas_call(body, out_shape=out_shape, in_specs=[SMEM] * len(scalars)...  10.9 us
    ppermute x14, waiting for transfers between devices, exchanged(): return lax.ppermute(part, 'corr', [(i, i ^ s) for i in range(corridors)])  7.82 us
    ppermute x1, starting transfers between devices, per_device_dense(): lax.ppermute(early[0], 'tm', [(i, (i - 1) % groups) for i in range(groups)])  3.93 us
    ppermute x1, waiting for transfers between devices, per_device_dense(): lax.ppermute(early[0], 'tm', [(i, (i - 1) % groups) for i in range(groups)])  3.45 us
    ppermute x1, starting transfers between devices, per_device_dense(): lax.ppermute(flows, 'tm', [(i, (i + 1) % groups) for i in range(groups)])  2.68 us
    pallas_call x1, Pallas kernels, per_device_dense(): pl.pallas_call(functools.partial(prepare_kernel, cap, order, links, CHUNK...  2.2 us
  transfers between devices with their start and end apart: 16, of which 5 were waited for; matrix products, arithmetic and copies ran while one was open for 0% of the time, Pallas kernels for 19%

profile of v13, /device:TPU:1, one launch (start us, length us, event | category | flops | bytes accessed | tf_op | source)
XLA Modules:
  0.0 47.7 jit_solution(12330022693267010752)
XLA Ops:
  0.6 0.0 copy-start.1
  0.6 2.7 %collective-permute-start = (bf16[2,24,1024]{2,1,0:T(8,128)(2,1)}, bf16[2,24,1024]{2,1,0:T(8,128)(2,1)S(1)}, u32[]{:S(2)}, u32[]{:S(2)}) collective-permute-start(bf16[2,24,1024]{2,1,0:T(8,128)(2,1)} %flows.5), channel_id=1, source_target_pairs={{0,1},{1,2},{2,3},{3,0},{4,5},{5,6},{6,7},{7,4},{8,9},{9,10},{10,1... | collective-permute-start | bytes 294920 | tf_op jit(solution)/shard_map/ppermute | solution.py:481
  3.3 2.2 %shard_map.131 = (s32[128]{0:T(128)S(1)}, bf16[64,128,128]{2,1,0:T(8,128)(2,1)S(1)}) custom-call(s32[1]{0:T(128)} %bitcast.1.me, s32[64]{0:T(128)} %rest_0_.1, s32[64]{0:T(128)} %rest_1_.1, s32[64]{0:T(128)} %rest_2_.1, s32[64]{0:T(128)} %rest_3_.1, bf16[64,128,128]{2,1,0:T(8,128)(2,1)} %rest_4_.1), custom_call_target="tpu_custom_call" | custom-call | tf_op jit(solution)/shard_map/pallas_call | solution.py:483
  5.5 0.0 collective-permute-done.before
  5.5 0.0 copy-done.1
  5.6 0.0 copy-start
  5.6 0.0 copy-start.3
  5.6 0.0 copy-start.4
  5.6 0.0 copy-start.5
  5.6 0.0 copy-start.6
  5.6 2.4 %shard_map.132 = (f32[8,48,128]{2,1,0:T(8,128)S(1)}, f32[8,48,128]{2,1,0:T(8,128)S(1)}, f32[8,48,128]{2,1,0:T(8,128)S(1)}, f32[8,48,128]{2,1,0:T(8,128)S(1)}, f3...) custom-call(s32[1]{0:T(128)} %bitcast.group, s32[128]{0:T(128)S(1)} %get-tuple-element.21.ahead, ...), custom_call_target="tpu_custom_call" | custom-call | tf_op jit(solution)/shard_map/pallas_call | solution.py:438
  8.1 1.3 %collective-permute-start.1 = (f16[8,48,128]{2,1,0:T(8,128)(2,1)S(1)}, f16[8,48,128]{2,1,0:T(8,128)(2,1)S(1)}, u32[]{:S(2)}, u32[]{:S(2)}) collective-permute-start(f16[8,48,128]{2,1,0:T(8,128)(2,1)S(1)} %convert_element_type.42), channel_id=1, source_target_pairs={{0,4},{4,0},{8,12},{12,8},{16,20},{20,16},{24,28},{28,24},{1,5},{5... | collective-permute-start | bytes 294920 | tf_op jit(solution)/shard_map/ppermute | solution.py:497
  9.4 0.3 collective-permute-start.3
  9.7 1.3 %collective-permute-start.5 = (f16[8,48,128]{2,1,0:T(8,128)(2,1)S(1)}, f16[8,48,128]{2,1,0:T(8,128)(2,1)S(1)}, u32[]{:S(2)}, u32[]{:S(2)}) collective-permute-start(f16[8,48,128]{2,1,0:T(8,128)(2,1)S(1)} %convert_element_type.50), channel_id=1, source_target_pairs={{0,4},{4,0},{8,12},{12,8},{16,20},{20,16},{24,28},{28,24},{1,5},{5... | collective-permute-start | bytes 294920 | tf_op jit(solution)/shard_map/ppermute | solution.py:497
  11.0 0.3 collective-permute-start.7
  11.4 0.9 %collective-permute-done.1 = f16[8,48,128]{2,1,0:T(8,128)(2,1)S(1)} collective-permute-done((f16[8,48,128]{2,1,0:T(8,128)(2,1)S(1)}, f16[8,48,128]{2,1,0:T(8,128)(2,1)S(1)}, u32[]{:S(2)}, u32[]{:S(2)}) %collective-permute-start.1) | collective-permute-done | bytes 98336 | tf_op jit(solution)/shard_map/ppermute | solution.py:497
  12.2 0.0 copy-start.2
  12.3 2.8 %collective-permute-start.2 = (f16[8,48,128]{2,1,0:T(8,128)(2,1)S(1)}, f16[8,48,128]{2,1,0:T(8,128)(2,1)S(1)}, u32[]{:S(2)}, u32[]{:S(2)}) collective-permute-start(f16[8,48,128]{2,1,0:T(8,128)(2,1)S(1)} %add_convert_fusion.2), channel_id=1, source_target_pairs={{0,24},{4,28},{8,16},{12,20},{16,8},{20,12},{24,0},{28,4},{1,25},{... | collective-permute-start | bytes 294920 | tf_op jit(solution)/shard_map/ppermute | solution.py:497
  15.1 0.0 collective-permute-done.3
  15.1 1.5 %collective-permute-start.4 = (f16[8,48,128]{2,1,0:T(8,128)(2,1)S(1)}, f16[8,48,128]{2,1,0:T(8,128)(2,1)S(1)}, u32[]{:S(2)}, u32[]{:S(2)}) collective-permute-start(f16[8,48,128]{2,1,0:T(8,128)(2,1)S(1)} %add_convert_fusion.1), channel_id=1, source_target_pairs={{0,16},{4,20},{8,24},{12,28},{16,0},{20,4},{24,8},{28,12},{1,17},{... | collective-permute-start | bytes 294920 | tf_op jit(solution)/shard_map/ppermute | solution.py:497
  16.6 0.0 collective-permute-done.5
  16.7 1.4 %collective-permute-start.6 = (f16[8,48,128]{2,1,0:T(8,128)(2,1)S(1)}, f16[8,48,128]{2,1,0:T(8,128)(2,1)S(1)}, u32[]{:S(2)}, u32[]{:S(2)}) collective-permute-start(f16[8,48,128]{2,1,0:T(8,128)(2,1)S(1)} %add_convert_fusion), channel_id=1, source_target_pairs={{0,8},{4,12},{8,0},{12,4},{16,24},{20,28},{24,16},{28,20},{1,9},{5... | collective-permute-start | bytes 294920 | tf_op jit(solution)/shard_map/ppermute | solution.py:497
  18.0 0.0 copy-done
  18.0 0.0 copy-done.3
  18.0 0.0 copy-done.4
  18.0 0.0 copy-done.5
  18.0 0.0 copy-done.6
  18.1 3.0 %shard_map.130 = (f32[8,48,128]{2,1,0:T(8,128)S(1)}, s32[87]{0:T(128)S(1)}) custom-call(s32[1]{0:T(128)} %bitcast.group, s32[1]{0:T(128)} %bitcast.1.me, s32[64]{0:T(128)S(1)} %copy-done.6, s32[64]{0:T(128)S(1)} %copy-done.3, s32[64]{0:T(128)S(1)} %copy-done.4, s32[64]{0:T(128)S(1)} %copy-done.5, bf16[2,24,1024]{2,1,0:T(8,128)(2,1)S(1)} %copy-done.1, ...), custom_call_target="tpu_custom_call" | custom-call | tf_op jit(solution)/shard_map/pallas_call | solution.py:438
  21.0 0.0 collective-permute-done.7
  21.1 0.0 collective-permute-done.2
  21.1 2.4 %collective-permute-done.4 = f16[8,48,128]{2,1,0:T(8,128)(2,1)S(1)} collective-permute-done((f16[8,48,128]{2,1,0:T(8,128)(2,1)S(1)}, f16[8,48,128]{2,1,0:T(8,128)(2,1)S(1)}, u32[]{:S(2)}, u32[]{:S(2)}) %collective-permute-start.4) | collective-permute-done | bytes 98336 | tf_op jit(solution)/shard_map/ppermute | solution.py:497
  23.5 0.0 collective-permute-done.6
  23.5 0.1 convert_add_fusion.totals
  23.6 0.0 copy-done.2
  23.7 0.1 collective-permute-start.9
  23.8 2.8 %collective-permute-start.10 = (bf16[8,48,128]{2,1,0:T(8,128)(2,1)S(1)}, bf16[8,48,128]{2,1,0:T(8,128)(2,1)S(1)}, u32[]{:S(2)}, u32[]{:S(2)}) collective-permute-start(bf16[8,48,128]{2,1,0:T(8,128)(2,1)S(1)} %shard_map.133.signal), channel_id=1, source_target_pairs={{0,16},{4,20},{8,24},{12,28},{16,0},{20,4},{24,8},{28,12},{1,17},{... | collective-permute-start | bytes 294920 | tf_op jit(solution)/shard_map/ppermute | solution.py:497
  26.6 0.7 %collective-permute-start.11 = (bf16[8,48,128]{2,1,0:T(8,128)(2,1)S(1)}, bf16[8,48,128]{2,1,0:T(8,128)(2,1)S(1)}, u32[]{:S(2)}, u32[]{:S(2)}) collective-permute-start(bf16[8,48,128]{2,1,0:T(8,128)(2,1)S(1)} %shard_map.133.signal), channel_id=1, source_target_pairs={{0,24},{4,28},{8,16},{12,20},{16,8},{20,12},{24,0},{28,4},{1,25},{... | collective-permute-start | bytes 294920 | tf_op jit(solution)/shard_map/ppermute | solution.py:497
  27.3 1.1 %collective-permute-start.8 = (bf16[8,48,128]{2,1,0:T(8,128)(2,1)S(1)}, bf16[8,48,128]{2,1,0:T(8,128)(2,1)S(1)}, u32[]{:S(2)}, u32[]{:S(2)}) collective-permute-start(bf16[8,48,128]{2,1,0:T(8,128)(2,1)S(1)} %shard_map.133.signal), channel_id=1, source_target_pairs={{0,4},{4,0},{8,12},{12,8},{16,20},{20,16},{24,28},{28,24},{1,5},{5... | collective-permute-start | bytes 294920 | tf_op jit(solution)/shard_map/ppermute | solution.py:497
  28.3 0.0 collective-permute-done.9.rest_1_
  28.4 0.5 collective-permute-start.14
  28.8 4.0 %collective-permute-done.11.rest_3_ = bf16[8,48,128]{2,1,0:T(8,128)(2,1)S(1)} collective-permute-done((bf16[8,48,128]{2,1,0:T(8,128)(2,1)S(1)}, bf16[8,48,128]{2,1,0:T(8,128)(2,1)S(1)}, u32[]{:S(2)}, u32[]{:S(2)}) %collective-permute-start.11) | collective-permute-done | bytes 98336 | tf_op jit(solution)/shard_map/ppermute | solution.py:497
  32.8 0.2 collective-permute-start.12
  33.1 0.0 collective-permute-done.10.rest_2_
  33.1 1.2 %collective-permute-start.13 = (bf16[8,48,128]{2,1,0:T(8,128)(2,1)S(1)}, bf16[8,48,128]{2,1,0:T(8,128)(2,1)S(1)}, u32[]{:S(2)}, u32[]{:S(2)}) collective-permute-start(bf16[8,48,128]{2,1,0:T(8,128)(2,1)S(1)} %collective-permute-done.10.rest_2_), channel_id=1, source_target_pairs={{0,4},{4,0},{8,12},{12,8},{16,20},{20,16},{24,28},{28,24},{1,5},{5... | collective-permute-start | bytes 294920 | tf_op jit(solution)/shard_map/ppermute | solution.py:497
  34.3 1.5 %shard_map.134.start = f32[640,128]{1,0:T(8,128)S(1)} custom-call(s32[64]{0:T(128)S(1)} %copy-done.3, s32[64]{0:T(128)S(1)} %copy-done.4, s32[64]{0:T(128)S(1)} %copy-done.5, bf16[8,48,128]{2,1,0:T(8,128)(2,1)S(1)} %shard_map.133.signal, bf16[64,128,128]{2,1,0:T(8,128)(2,1)S(1)} %copy-done), custom_call_target="tpu_custom_call" | custom-call | tf_op jit(solution)/shard_map/pallas_call | solution.py:438
  35.8 0.0 collective-permute-done.8.rest_0_
  35.9 1.4 %shard_map.135.start = f32[640,128]{1,0:T(8,128)S(1)} custom-call(s32[87]{0:T(128)S(1)} %get-tuple-element.30.table, s32[128]{0:T(128)S(1)} %get-tuple-element.21.ahead, bf16[64,128,128]{2,1,0:T(8,128)(2,1)S(1)} %get-tuple-element.22.mats, f32[640,128]{1,0:T(8,128)S(1)} %shard_map.134.start, bf16[8,48,128]{2,1,0:T(8,128)(2,1)S(1)} %collective-permute-done.8.rest_0_, ...), custom_call_target="tpu_custom_call" | custom-call | flops 500000000 | bytes 1500000 | tf_op jit(solution)/shard_map/pallas_call | solution.py:438
  37.3 0.0 collective-permute-done.14.rest_2_
  37.3 0.0 collective-permute-done.12.rest_0_
  37.3 0.5 %collective-permute-done.13.rest_1_ = bf16[8,48,128]{2,1,0:T(8,128)(2,1)S(1)} collective-permute-done((bf16[8,48,128]{2,1,0:T(8,128)(2,1)S(1)}, bf16[8,48,128]{2,1,0:T(8,128)(2,1)S(1)}, u32[]{:S(2)}, u32[]{:S(2)}) %collective-permute-start.13) | collective-permute-done | bytes 98336 | tf_op jit(solution)/shard_map/ppermute | solution.py:497
  37.8 1.0 %shard_map.136 = (f32[640,128]{1,0:T(8,128)S(1)}, f32[16,16,128]{2,1,0:T(8,128)S(1)}) custom-call(s32[87]{0:T(128)S(1)} %get-tuple-element.30.table, s32[128]{0:T(128)S(1)} %get-tuple-element.21.ahead, bf16[64,128,128]{2,1,0:T(8,128)(2,1)S(1)} %get-tuple-element.22.mats, f32[640,128]{1,0:T(8,128)S(1)} %shard_map.135.start, ...), custom_call_target="tpu_custom_call" | custom-call | tf_op jit(solution)/shard_map/pallas_call | solution.py:438
  38.8 3.9 %collective-permute-start.15 = (f32[16,16,128]{2,1,0:T(8,128)S(1)}, f32[16,16,128]{2,1,0:T(8,128)S(1)}, u32[]{:S(2)}, u32[]{:S(2)}) collective-permute-start(f32[16,16,128]{2,1,0:T(8,128)S(1)} %get-tuple-element.34), channel_id=1, source_target_pairs={{0,3},{1,0},{2,1},{3,2},{4,7},{5,4},{6,5},{7,6},{8,11},{9,8},{10,9... | collective-permute-start | bytes 393224 | tf_op jit(solution)/shard_map/ppermute | solution.py:557
  42.7 0.7 %shard_map.137 = f32[2,24,1024]{2,1,0:T(8,128)} custom-call(f32[8,48,128]{2,1,0:T(8,128)S(1)} %convert_add_fusion.totals, f32[2,24,1024]{2,1,0:T(8,128)S(1)} %copy-done.2), custom_call_target="tpu_custom_call" | custom-call | tf_op jit(solution)/shard_map/pallas_call | solution.py:438
  43.5 3.5 %collective-permute-done.15.spill = f32[16,16,128]{2,1,0:T(8,128)S(1)} collective-permute-done((f32[16,16,128]{2,1,0:T(8,128)S(1)}, f32[16,16,128]{2,1,0:T(8,128)S(1)}, u32[]{:S(2)}, u32[]{:S(2)}) %collective-permute-start.15) | collective-permute-done | bytes 131104 | tf_op jit(solution)/shard_map/ppermute | solution.py:557
  46.9 0.8 %shard_map.138 = (f32[2,24,1024]{2,1,0:T(8,128)}, f32[2,24,1024]{2,1,0:T(8,128)}) custom-call(s32[1]{0:T(128)} %bitcast.group, f32[640,128]{1,0:T(8,128)S(1)} %get-tuple-element.33.total, f32[16,16,128]{2,1,0:T(8,128)S(1)} %collective-permute-done.15.spill, bf16[2,24,1024]{2,1,0:T(8,128)(2,1)S(1)} %copy-done.1), custom_call_target="tpu_custom_call" | custom-call | tf_op jit(solution)/shard_map/pallas_call | solution.py:438
  (10 shorter events, 0.2 us)
Async XLA Ops:
  0.6 4.9 %copy-start.1 = (bf16[2,24,1024]{2,1,0:T(8,128)(2,1)S(1)}, bf16[2,24,1024]{2,1,0:T(8,128)(2,1)}, u32[]{:S(2)}) copy-start(bf16[2,24,1024]{2,1,0:T(8,128)(2,1)} %flows.5) | copy-start | bytes 294916
  0.6 4.9 %collective-permute-start = (bf16[2,24,1024]{2,1,0:T(8,128)(2,1)}, bf16[2,24,1024]{2,1,0:T(8,128)(2,1)S(1)}, u32[]{:S(2)}, u32[]{:S(2)}) collective-permute-start(bf16[2,24,1024]{2,1,0:T(8,128)(2,1)} %flows.5), channel_id=1, source_target_pairs={{0,1},{1,2},{2,3},{3,0},{4,5},{5,6},{6,7},{7,4},{8,9},{9,10},{10,1... | collective-permute-start | bytes 294920 | tf_op jit(solution)/shard_map/ppermute | solution.py:481
  5.6 12.5 %copy-start = (bf16[64,128,128]{2,1,0:T(8,128)(2,1)S(1)}, bf16[64,128,128]{2,1,0:T(8,128)(2,1)}, u32[]{:S(2)}) copy-start(bf16[64,128,128]{2,1,0:T(8,128)(2,1)} %mats.3) | copy-start | bytes 6291460
  5.6 12.5 %copy-start.3 = (s32[64]{0:T(128)S(1)}, s32[64]{0:T(128)}, u32[]{:S(2)}) copy-start(s32[64]{0:T(128)} %path.3) | copy-start | bytes 772
  5.6 12.5 %copy-start.4 = (s32[64]{0:T(128)S(1)}, s32[64]{0:T(128)}, u32[]{:S(2)}) copy-start(s32[64]{0:T(128)} %link.3) | copy-start | bytes 772
  5.6 12.5 %copy-start.5 = (s32[64]{0:T(128)S(1)}, s32[64]{0:T(128)}, u32[]{:S(2)}) copy-start(s32[64]{0:T(128)} %lag.3) | copy-start | bytes 772
  5.6 12.4 %copy-start.6 = (s32[64]{0:T(128)S(1)}, s32[64]{0:T(128)}, u32[]{:S(2)}) copy-start(s32[64]{0:T(128)} %rest_3_.1) | copy-start | bytes 772
  8.1 4.2 %collective-permute-start.1 = (f16[8,48,128]{2,1,0:T(8,128)(2,1)S(1)}, f16[8,48,128]{2,1,0:T(8,128)(2,1)S(1)}, u32[]{:S(2)}, u32[]{:S(2)}) collective-permute-start(f16[8,48,128]{2,1,0:T(8,128)(2,1)S(1)} %convert_element_type.42), channel_id=1, source_target_pairs={{0,4},{4,0},{8,12},{12,8},{16,20},{20,16},{24,28},{28,24},{1,5},{5... | collective-permute-start | bytes 294920 | tf_op jit(solution)/shard_map/ppermute | solution.py:497
  9.4 5.7 %collective-permute-start.3 = (f16[8,48,128]{2,1,0:T(8,128)(2,1)S(1)}, f16[8,48,128]{2,1,0:T(8,128)(2,1)S(1)}, u32[]{:S(2)}, u32[]{:S(2)}) collective-permute-start(f16[8,48,128]{2,1,0:T(8,128)(2,1)S(1)} %convert_element_type.46), channel_id=1, source_target_pairs={{0,4},{4,0},{8,12},{12,8},{16,20},{20,16},{24,28},{28,24},{1,5},{5... | collective-permute-start | bytes 294920 | tf_op jit(solution)/shard_map/ppermute | solution.py:497
  9.7 6.9 %collective-permute-start.5 = (f16[8,48,128]{2,1,0:T(8,128)(2,1)S(1)}, f16[8,48,128]{2,1,0:T(8,128)(2,1)S(1)}, u32[]{:S(2)}, u32[]{:S(2)}) collective-permute-start(f16[8,48,128]{2,1,0:T(8,128)(2,1)S(1)} %convert_element_type.50), channel_id=1, source_target_pairs={{0,4},{4,0},{8,12},{12,8},{16,20},{20,16},{24,28},{28,24},{1,5},{5... | collective-permute-start | bytes 294920 | tf_op jit(solution)/shard_map/ppermute | solution.py:497
  11.0 10.0 %collective-permute-start.7 = (f16[8,48,128]{2,1,0:T(8,128)(2,1)S(1)}, f16[8,48,128]{2,1,0:T(8,128)(2,1)S(1)}, u32[]{:S(2)}, u32[]{:S(2)}) collective-permute-start(f16[8,48,128]{2,1,0:T(8,128)(2,1)S(1)} %convert_element_type.54), channel_id=1, source_target_pairs={{0,4},{4,0},{8,12},{12,8},{16,20},{20,16},{24,28},{28,24},{1,5},{5... | collective-permute-start | bytes 294920 | tf_op jit(solution)/shard_map/ppermute | solution.py:497
  12.2 11.4 %copy-start.2 = (f32[2,24,1024]{2,1,0:T(8,128)S(1)}, f32[2,24,1024]{2,1,0:T(8,128)}, u32[]{:S(2)}) copy-start(f32[2,24,1024]{2,1,0:T(8,128)} %counts.3) | copy-start | bytes 589828
  12.3 8.8 %collective-permute-start.2 = (f16[8,48,128]{2,1,0:T(8,128)(2,1)S(1)}, f16[8,48,128]{2,1,0:T(8,128)(2,1)S(1)}, u32[]{:S(2)}, u32[]{:S(2)}) collective-permute-start(f16[8,48,128]{2,1,0:T(8,128)(2,1)S(1)} %add_convert_fusion.2), channel_id=1, source_target_pairs={{0,24},{4,28},{8,16},{12,20},{16,8},{20,12},{24,0},{28,4},{1,25},{... | collective-permute-start | bytes 294920 | tf_op jit(solution)/shard_map/ppermute | solution.py:497
  15.1 8.4 %collective-permute-start.4 = (f16[8,48,128]{2,1,0:T(8,128)(2,1)S(1)}, f16[8,48,128]{2,1,0:T(8,128)(2,1)S(1)}, u32[]{:S(2)}, u32[]{:S(2)}) collective-permute-start(f16[8,48,128]{2,1,0:T(8,128)(2,1)S(1)} %add_convert_fusion.1), channel_id=1, source_target_pairs={{0,16},{4,20},{8,24},{12,28},{16,0},{20,4},{24,8},{28,12},{1,17},{... | collective-permute-start | bytes 294920 | tf_op jit(solution)/shard_map/ppermute | solution.py:497
  16.7 6.9 %collective-permute-start.6 = (f16[8,48,128]{2,1,0:T(8,128)(2,1)S(1)}, f16[8,48,128]{2,1,0:T(8,128)(2,1)S(1)}, u32[]{:S(2)}, u32[]{:S(2)}) collective-permute-start(f16[8,48,128]{2,1,0:T(8,128)(2,1)S(1)} %add_convert_fusion), channel_id=1, source_target_pairs={{0,8},{4,12},{8,0},{12,4},{16,24},{20,28},{24,16},{28,20},{1,9},{5... | collective-permute-start | bytes 294920 | tf_op jit(solution)/shard_map/ppermute | solution.py:497
  23.7 4.7 %collective-permute-start.9 = (bf16[8,48,128]{2,1,0:T(8,128)(2,1)S(1)}, bf16[8,48,128]{2,1,0:T(8,128)(2,1)S(1)}, u32[]{:S(2)}, u32[]{:S(2)}) collective-permute-start(bf16[8,48,128]{2,1,0:T(8,128)(2,1)S(1)} %shard_map.133.signal), channel_id=1, source_target_pairs={{0,8},{4,12},{8,0},{12,4},{16,24},{20,28},{24,16},{28,20},{1,9},{5... | collective-permute-start | bytes 294920 | tf_op jit(solution)/shard_map/ppermute | solution.py:497
  23.8 9.3 %collective-permute-start.10 = (bf16[8,48,128]{2,1,0:T(8,128)(2,1)S(1)}, bf16[8,48,128]{2,1,0:T(8,128)(2,1)S(1)}, u32[]{:S(2)}, u32[]{:S(2)}) collective-permute-start(bf16[8,48,128]{2,1,0:T(8,128)(2,1)S(1)} %shard_map.133.signal), channel_id=1, source_target_pairs={{0,16},{4,20},{8,24},{12,28},{16,0},{20,4},{24,8},{28,12},{1,17},{... | collective-permute-start | bytes 294920 | tf_op jit(solution)/shard_map/ppermute | solution.py:497
  26.6 6.2 %collective-permute-start.11 = (bf16[8,48,128]{2,1,0:T(8,128)(2,1)S(1)}, bf16[8,48,128]{2,1,0:T(8,128)(2,1)S(1)}, u32[]{:S(2)}, u32[]{:S(2)}) collective-permute-start(bf16[8,48,128]{2,1,0:T(8,128)(2,1)S(1)} %shard_map.133.signal), channel_id=1, source_target_pairs={{0,24},{4,28},{8,16},{12,20},{16,8},{20,12},{24,0},{28,4},{1,25},{... | collective-permute-start | bytes 294920 | tf_op jit(solution)/shard_map/ppermute | solution.py:497
  27.3 8.6 %collective-permute-start.8 = (bf16[8,48,128]{2,1,0:T(8,128)(2,1)S(1)}, bf16[8,48,128]{2,1,0:T(8,128)(2,1)S(1)}, u32[]{:S(2)}, u32[]{:S(2)}) collective-permute-start(bf16[8,48,128]{2,1,0:T(8,128)(2,1)S(1)} %shard_map.133.signal), channel_id=1, source_target_pairs={{0,4},{4,0},{8,12},{12,8},{16,20},{20,16},{24,28},{28,24},{1,5},{5... | collective-permute-start | bytes 294920 | tf_op jit(solution)/shard_map/ppermute | solution.py:497
  28.4 8.9 %collective-permute-start.14 = (bf16[8,48,128]{2,1,0:T(8,128)(2,1)S(1)}, bf16[8,48,128]{2,1,0:T(8,128)(2,1)S(1)}, u32[]{:S(2)}, u32[]{:S(2)}) collective-permute-start(bf16[8,48,128]{2,1,0:T(8,128)(2,1)S(1)} %pad_maximum_fusion), channel_id=1, source_target_pairs={{0,4},{4,0},{8,12},{12,8},{16,20},{20,16},{24,28},{28,24},{1,5},{5... | collective-permute-start | bytes 294920 | tf_op jit(solution)/shard_map/ppermute | solution.py:497
  32.8 4.4 %collective-permute-start.12 = (bf16[8,48,128]{2,1,0:T(8,128)(2,1)S(1)}, bf16[8,48,128]{2,1,0:T(8,128)(2,1)S(1)}, u32[]{:S(2)}, u32[]{:S(2)}) collective-permute-start(bf16[8,48,128]{2,1,0:T(8,128)(2,1)S(1)} %collective-permute-done.11.rest_3_), channel_id=1, source_target_pairs={{0,4},{4,0},{8,12},{12,8},{16,20},{20,16},{24,28},{28,24},{1,5},{5... | collective-permute-start | bytes 294920 | tf_op jit(solution)/shard_map/ppermute | solution.py:497
  33.1 4.7 %collective-permute-start.13 = (bf16[8,48,128]{2,1,0:T(8,128)(2,1)S(1)}, bf16[8,48,128]{2,1,0:T(8,128)(2,1)S(1)}, u32[]{:S(2)}, u32[]{:S(2)}) collective-permute-start(bf16[8,48,128]{2,1,0:T(8,128)(2,1)S(1)} %collective-permute-done.10.rest_2_), channel_id=1, source_target_pairs={{0,4},{4,0},{8,12},{12,8},{16,20},{20,16},{24,28},{28,24},{1,5},{5... | collective-permute-start | bytes 294920 | tf_op jit(solution)/shard_map/ppermute | solution.py:497
  38.8 8.1 %collective-permute-start.15 = (f32[16,16,128]{2,1,0:T(8,128)S(1)}, f32[16,16,128]{2,1,0:T(8,128)S(1)}, u32[]{:S(2)}, u32[]{:S(2)}) collective-permute-start(f32[16,16,128]{2,1,0:T(8,128)S(1)} %get-tuple-element.34), channel_id=1, source_target_pairs={{0,3},{1,0},{2,1},{3,2},{4,7},{5,4},{6,5},{7,6},{8,11},{9,8},{10,9... | collective-permute-start | bytes 393224 | tf_op jit(solution)/shard_map/ppermute | solution.py:557

commit v14 on v11

--- a/solution.py
+++ b/solution.py
@@ -338,12 +338,16 @@
             signal[b, d * minutes : (d + 1) * minutes, :] = (res / weight).astype(signal.dtype)
 
 
-def backward_local_kernel(days, path, link, lag, signal, mats, totals, counts, out, residual):
-    minutes, width = signal.shape[1] // days, totals.shape[2]
+def residual_kernel(days, totals, counts, residual):
+    width = totals.shape[2]
     for b in range(totals.shape[0]):
         for d in range(days):
             res, _ = residual_of(days, totals, counts, b, d)
             residual[d, :, b * width : (b + 1) * width] = res
+
+
+def backward_local_kernel(days, path, link, lag, signal, mats, out):
+    minutes = signal.shape[1] // days
     out[...] = jnp.zeros_like(out)
     unroll = step_of(mats.shape[0])
     mat, base, block = local_views(path, link, lag, mats, unroll, days * (HALO + minutes))
@@ -525,11 +529,11 @@
     )
     arrived = {s: exchanged(signal, s) for s in (*through, 1)}
     rows = [shape((paths * days * span, width), f32)]
-    total, link_residual = kernel_call(
+    (total,) = kernel_call(
         functools.partial(backward_local_kernel, days),
         local_index,
-        (signal, local_blocks, totals, counts),
-        [*rows, shape(counts.shape, f32)],
+        (signal, local_blocks),
+        rows,
     )
     arrived[through[-1]], total = lax.optimization_barrier((arrived[through[-1]], total))
     for s in through:
@@ -545,6 +549,13 @@
             cost=weight(BACKWARD_COST) if first else None,
         )
     spill = lax.ppermute(early[0], "tm", [(i, (i - 1) % groups) for i in range(groups)])
+    totals, total = lax.optimization_barrier((totals, total))
+    (link_residual,) = kernel_call(
+        functools.partial(residual_kernel, days),
+        (),
+        (totals, counts),
+        [shape(counts.shape, f32)],
+    )
     gradient, new_flows = kernel_call(
         functools.partial(finish_kernel, days, groups),
         (group,),

time: 47.2 us -> 47 us (level)
    ppermute x1, waiting for transfers between devices: 3.94 us -> 3.22 us  [per_device_dense(): lax.ppermute(early[0], 'tm', [(i, (i - 1) % groups) for i in range(groups)])]
    ppermute x14, waiting for transfers between devices: 7.41 us -> 7.9 us  [exchanged(): return lax.ppermute(part, 'corr', [(i, i ^ s) for i in range(corridors)])]
    pallas_call x7 -> x8, Pallas kernels: 10.9 us -> 10.9 us  [kernel_call(): pl.pallas_call(body, out_shape=out_shape, in_specs=[SMEM] * len(scalars)...]
  transfers between devices with their start and end apart: 16 -> 16, of which waited for: 5 -> 6; matrix products, arithmetic and copies ran while one was open for 0% -> 0% of each run, Pallas kernels for 19% -> 19%
where the time goes in v14:
time: 47 us; the launch traced here: 46.8 us
  starting transfers between devices  21.5 us (46%)
  Pallas kernels  13.1 us (28%)
  waiting for transfers between devices  11.1 us (24%)
  between operations  0.85 us (2%)
    ppermute x14, starting transfers between devices, exchanged(): return lax.ppermute(part, 'corr', [(i, i ^ s) for i in range(corridors)])  16.3 us
    pallas_call x8, Pallas kernels, kernel_call(): pl.pallas_call(body, out_shape=out_shape, in_specs=[SMEM] * len(scalars)...  10.9 us
    ppermute x14, waiting for transfers between devices, exchanged(): return lax.ppermute(part, 'corr', [(i, i ^ s) for i in range(corridors)])  7.9 us
    ppermute x1, waiting for transfers between devices, per_device_dense(): lax.ppermute(early[0], 'tm', [(i, (i - 1) % groups) for i in range(groups)])  3.22 us
    ppermute x1, starting transfers between devices, per_device_dense(): lax.ppermute(flows, 'tm', [(i, (i + 1) % groups) for i in range(groups)])  2.68 us
    ppermute x1, starting transfers between devices, per_device_dense(): lax.ppermute(early[0], 'tm', [(i, (i - 1) % groups) for i in range(groups)])  2.51 us
    pallas_call x1, Pallas kernels, per_device_dense(): pl.pallas_call(functools.partial(prepare_kernel, cap, order, links, CHUNK...  2.2 us
  transfers between devices with their start and end apart: 16, of which 6 were waited for; matrix products, arithmetic and copies ran while one was open for 0% of the time, Pallas kernels for 19%

profile of v14, /device:TPU:1, one launch (start us, length us, event | category | flops | bytes accessed | tf_op | source)
XLA Modules:
  0.0 46.8 jit_solution(16708326291763486175)
XLA Ops:
  0.6 0.0 copy-start.1
  0.6 2.7 %collective-permute-start = (bf16[2,24,1024]{2,1,0:T(8,128)(2,1)}, bf16[2,24,1024]{2,1,0:T(8,128)(2,1)S(1)}, u32[]{:S(2)}, u32[]{:S(2)}) collective-permute-start(bf16[2,24,1024]{2,1,0:T(8,128)(2,1)} %flows.5), channel_id=1, source_target_pairs={{0,1},{1,2},{2,3},{3,0},{4,5},{5,6},{6,7},{7,4},{8,9},{9,10},{10,1... | collective-permute-start | bytes 294920 | tf_op jit(solution)/shard_map/ppermute | solution.py:481
  3.3 2.2 %shard_map.131 = (s32[128]{0:T(128)S(1)}, bf16[64,128,128]{2,1,0:T(8,128)(2,1)S(1)}) custom-call(s32[1]{0:T(128)} %bitcast.1.me, s32[64]{0:T(128)} %rest_0_.1, s32[64]{0:T(128)} %rest_1_.1, s32[64]{0:T(128)} %rest_2_.1, s32[64]{0:T(128)} %rest_3_.1, bf16[64,128,128]{2,1,0:T(8,128)(2,1)} %rest_4_.1), custom_call_target="tpu_custom_call" | custom-call | tf_op jit(solution)/shard_map/pallas_call | solution.py:483
  5.5 0.0 collective-permute-done.before
  5.5 0.0 copy-done.1
  5.6 0.0 copy-start
  5.6 0.0 copy-start.3
  5.6 0.0 copy-start.4
  5.6 0.0 copy-start.5
  5.6 0.0 copy-start.6
  5.6 2.4 %shard_map.132 = (f32[8,48,128]{2,1,0:T(8,128)S(1)}, f32[8,48,128]{2,1,0:T(8,128)S(1)}, f32[8,48,128]{2,1,0:T(8,128)S(1)}, f32[8,48,128]{2,1,0:T(8,128)S(1)}, f3...) custom-call(s32[1]{0:T(128)} %bitcast.group, s32[128]{0:T(128)S(1)} %get-tuple-element.23.ahead, ...), custom_call_target="tpu_custom_call" | custom-call | tf_op jit(solution)/shard_map/pallas_call | solution.py:434
  8.1 1.3 %collective-permute-start.1 = (f16[8,48,128]{2,1,0:T(8,128)(2,1)S(1)}, f16[8,48,128]{2,1,0:T(8,128)(2,1)S(1)}, u32[]{:S(2)}, u32[]{:S(2)}) collective-permute-start(f16[8,48,128]{2,1,0:T(8,128)(2,1)S(1)} %convert_element_type.42), channel_id=1, source_target_pairs={{0,4},{4,0},{8,12},{12,8},{16,20},{20,16},{24,28},{28,24},{1,5},{5... | collective-permute-start | bytes 294920 | tf_op jit(solution)/shard_map/ppermute | solution.py:497
  9.4 0.3 collective-permute-start.3
  9.7 1.3 %collective-permute-start.5 = (f16[8,48,128]{2,1,0:T(8,128)(2,1)S(1)}, f16[8,48,128]{2,1,0:T(8,128)(2,1)S(1)}, u32[]{:S(2)}, u32[]{:S(2)}) collective-permute-start(f16[8,48,128]{2,1,0:T(8,128)(2,1)S(1)} %convert_element_type.50), channel_id=1, source_target_pairs={{0,4},{4,0},{8,12},{12,8},{16,20},{20,16},{24,28},{28,24},{1,5},{5... | collective-permute-start | bytes 294920 | tf_op jit(solution)/shard_map/ppermute | solution.py:497
  11.0 0.3 collective-permute-start.7
  11.4 0.9 %collective-permute-done.1 = f16[8,48,128]{2,1,0:T(8,128)(2,1)S(1)} collective-permute-done((f16[8,48,128]{2,1,0:T(8,128)(2,1)S(1)}, f16[8,48,128]{2,1,0:T(8,128)(2,1)S(1)}, u32[]{:S(2)}, u32[]{:S(2)}) %collective-permute-start.1) | collective-permute-done | bytes 98336 | tf_op jit(solution)/shard_map/ppermute | solution.py:497
  12.2 0.0 copy-start.2
  12.3 2.8 %collective-permute-start.2 = (f16[8,48,128]{2,1,0:T(8,128)(2,1)S(1)}, f16[8,48,128]{2,1,0:T(8,128)(2,1)S(1)}, u32[]{:S(2)}, u32[]{:S(2)}) collective-permute-start(f16[8,48,128]{2,1,0:T(8,128)(2,1)S(1)} %add_convert_fusion.2), channel_id=1, source_target_pairs={{0,24},{4,28},{8,16},{12,20},{16,8},{20,12},{24,0},{28,4},{1,25},{... | collective-permute-start | bytes 294920 | tf_op jit(solution)/shard_map/ppermute | solution.py:497
  15.0 0.0 collective-permute-done.3
  15.1 1.6 %collective-permute-start.4 = (f16[8,48,128]{2,1,0:T(8,128)(2,1)S(1)}, f16[8,48,128]{2,1,0:T(8,128)(2,1)S(1)}, u32[]{:S(2)}, u32[]{:S(2)}) collective-permute-start(f16[8,48,128]{2,1,0:T(8,128)(2,1)S(1)} %add_convert_fusion.1), channel_id=1, source_target_pairs={{0,16},{4,20},{8,24},{12,28},{16,0},{20,4},{24,8},{28,12},{1,17},{... | collective-permute-start | bytes 294920 | tf_op jit(solution)/shard_map/ppermute | solution.py:497
  16.6 0.0 collective-permute-done.5
  16.7 1.3 %collective-permute-start.6 = (f16[8,48,128]{2,1,0:T(8,128)(2,1)S(1)}, f16[8,48,128]{2,1,0:T(8,128)(2,1)S(1)}, u32[]{:S(2)}, u32[]{:S(2)}) collective-permute-start(f16[8,48,128]{2,1,0:T(8,128)(2,1)S(1)} %add_convert_fusion), channel_id=1, source_target_pairs={{0,8},{4,12},{8,0},{12,4},{16,24},{20,28},{24,16},{28,20},{1,9},{5... | collective-permute-start | bytes 294920 | tf_op jit(solution)/shard_map/ppermute | solution.py:497
  18.0 0.0 copy-done
  18.0 0.0 copy-done.3
  18.0 0.0 copy-done.4
  18.0 0.0 copy-done.5
  18.0 0.0 copy-done.6
  18.0 3.0 %shard_map.130 = (f32[8,48,128]{2,1,0:T(8,128)S(1)}, s32[87]{0:T(128)S(1)}) custom-call(s32[1]{0:T(128)} %bitcast.group, s32[1]{0:T(128)} %bitcast.1.me, s32[64]{0:T(128)S(1)} %copy-done.6, s32[64]{0:T(128)S(1)} %copy-done.3, s32[64]{0:T(128)S(1)} %copy-done.4, s32[64]{0:T(128)S(1)} %copy-done.5, bf16[2,24,1024]{2,1,0:T(8,128)(2,1)S(1)} %copy-done.1, ...), custom_call_target="tpu_custom_call" | custom-call | tf_op jit(solution)/shard_map/pallas_call | solution.py:434
  21.0 0.0 collective-permute-done.7
  21.0 0.0 collective-permute-done.2
  21.1 2.4 %collective-permute-done.4 = f16[8,48,128]{2,1,0:T(8,128)(2,1)S(1)} collective-permute-done((f16[8,48,128]{2,1,0:T(8,128)(2,1)S(1)}, f16[8,48,128]{2,1,0:T(8,128)(2,1)S(1)}, u32[]{:S(2)}, u32[]{:S(2)}) %collective-permute-start.4) | collective-permute-done | bytes 98336 | tf_op jit(solution)/shard_map/ppermute | solution.py:497
  23.5 0.0 collective-permute-done.6
  23.5 0.1 convert_add_fusion.totals
  23.6 0.0 copy-done.2
  23.6 2.7 %collective-permute-start.8 = (bf16[8,48,128]{2,1,0:T(8,128)(2,1)S(1)}, bf16[8,48,128]{2,1,0:T(8,128)(2,1)S(1)}, u32[]{:S(2)}, u32[]{:S(2)}) collective-permute-start(bf16[8,48,128]{2,1,0:T(8,128)(2,1)S(1)} %shard_map.133.signal), channel_id=1, source_target_pairs={{0,24},{4,28},{8,16},{12,20},{16,8},{20,12},{24,0},{28,4},{1,25},{... | collective-permute-start | bytes 294920 | tf_op jit(solution)/shard_map/ppermute | solution.py:497
  26.3 0.0 collective-permute-start.10
  26.3 0.9 %collective-permute-start.11 = (bf16[8,48,128]{2,1,0:T(8,128)(2,1)S(1)}, bf16[8,48,128]{2,1,0:T(8,128)(2,1)S(1)}, u32[]{:S(2)}, u32[]{:S(2)}) collective-permute-start(bf16[8,48,128]{2,1,0:T(8,128)(2,1)S(1)} %shard_map.133.signal), channel_id=1, source_target_pairs={{0,16},{4,20},{8,24},{12,28},{16,0},{20,4},{24,8},{28,12},{1,17},{... | collective-permute-start | bytes 294920 | tf_op jit(solution)/shard_map/ppermute | solution.py:497
  27.3 1.1 %collective-permute-start.9 = (bf16[8,48,128]{2,1,0:T(8,128)(2,1)S(1)}, bf16[8,48,128]{2,1,0:T(8,128)(2,1)S(1)}, u32[]{:S(2)}, u32[]{:S(2)}) collective-permute-start(bf16[8,48,128]{2,1,0:T(8,128)(2,1)S(1)} %shard_map.133.signal), channel_id=1, source_target_pairs={{0,4},{4,0},{8,12},{12,8},{16,20},{20,16},{24,28},{28,24},{1,5},{5... | collective-permute-start | bytes 294920 | tf_op jit(solution)/shard_map/ppermute | solution.py:497
  28.3 1.5 %shard_map.134.start = f32[640,128]{1,0:T(8,128)S(1)} custom-call(s32[64]{0:T(128)S(1)} %copy-done.3, s32[64]{0:T(128)S(1)} %copy-done.4, s32[64]{0:T(128)S(1)} %copy-done.5, bf16[8,48,128]{2,1,0:T(8,128)(2,1)S(1)} %shard_map.133.signal, bf16[64,128,128]{2,1,0:T(8,128)(2,1)S(1)} %copy-done), custom_call_target="tpu_custom_call" | custom-call | tf_op jit(solution)/shard_map/pallas_call | solution.py:434
  29.9 0.0 collective-permute-done.8.rest_3_
  29.9 0.5 collective-permute-start.12
  30.4 0.4 collective-permute-done.10.rest_1_
  30.7 1.3 %collective-permute-start.13 = (bf16[8,48,128]{2,1,0:T(8,128)(2,1)S(1)}, bf16[8,48,128]{2,1,0:T(8,128)(2,1)S(1)}, u32[]{:S(2)}, u32[]{:S(2)}) collective-permute-start(bf16[8,48,128]{2,1,0:T(8,128)(2,1)S(1)} %collective-permute-done.10.rest_1_), channel_id=1, source_target_pairs={{0,4},{4,0},{8,12},{12,8},{16,20},{20,16},{24,28},{28,24},{1,5},{5... | collective-permute-start | bytes 294920 | tf_op jit(solution)/shard_map/ppermute | solution.py:497
  32.0 1.8 %collective-permute-done.11.rest_2_ = bf16[8,48,128]{2,1,0:T(8,128)(2,1)S(1)} collective-permute-done((bf16[8,48,128]{2,1,0:T(8,128)(2,1)S(1)}, bf16[8,48,128]{2,1,0:T(8,128)(2,1)S(1)}, u32[]{:S(2)}, u32[]{:S(2)}) %collective-permute-start.11) | collective-permute-done | bytes 98336 | tf_op jit(solution)/shard_map/ppermute | solution.py:497
  33.9 0.9 %collective-permute-start.14 = (bf16[8,48,128]{2,1,0:T(8,128)(2,1)S(1)}, bf16[8,48,128]{2,1,0:T(8,128)(2,1)S(1)}, u32[]{:S(2)}, u32[]{:S(2)}) collective-permute-start(bf16[8,48,128]{2,1,0:T(8,128)(2,1)S(1)} %collective-permute-done.11.rest_2_), channel_id=1, source_target_pairs={{0,4},{4,0},{8,12},{12,8},{16,20},{20,16},{24,28},{28,24},{1,5},{5... | collective-permute-start | bytes 294920 | tf_op jit(solution)/shard_map/ppermute | solution.py:497
  34.8 0.0 collective-permute-done.9.rest_0_
  34.8 1.4 %shard_map.135.start = f32[640,128]{1,0:T(8,128)S(1)} custom-call(s32[87]{0:T(128)S(1)} %get-tuple-element.32.table, s32[128]{0:T(128)S(1)} %get-tuple-element.23.ahead, bf16[64,128,128]{2,1,0:T(8,128)(2,1)S(1)} %get-tuple-element.24.mats, f32[640,128]{1,0:T(8,128)S(1)} %shard_map.134.start, bf16[8,48,128]{2,1,0:T(8,128)(2,1)S(1)} %collective-permute-done.9.rest_0_, ...), custom_call_target="tpu_custom_call" | custom-call | flops 500000000 | bytes 1500000 | tf_op jit(solution)/shard_map/pallas_call | solution.py:434
  36.2 0.0 collective-permute-done.12.rest_0_
  36.2 0.0 collective-permute-done.13.rest_1_
  36.2 2.4 %collective-permute-done.14.rest_2_ = bf16[8,48,128]{2,1,0:T(8,128)(2,1)S(1)} collective-permute-done((bf16[8,48,128]{2,1,0:T(8,128)(2,1)S(1)}, bf16[8,48,128]{2,1,0:T(8,128)(2,1)S(1)}, u32[]{:S(2)}, u32[]{:S(2)}) %collective-permute-start.14) | collective-permute-done | bytes 98336 | tf_op jit(solution)/shard_map/ppermute | solution.py:497
  38.6 1.0 %shard_map.136 = (f32[640,128]{1,0:T(8,128)S(1)}, f32[16,16,128]{2,1,0:T(8,128)S(1)}) custom-call(s32[87]{0:T(128)S(1)} %get-tuple-element.32.table, s32[128]{0:T(128)S(1)} %get-tuple-element.23.ahead, bf16[64,128,128]{2,1,0:T(8,128)(2,1)S(1)} %get-tuple-element.24.mats, f32[640,128]{1,0:T(8,128)S(1)} %shard_map.135.start, ...), custom_call_target="tpu_custom_call" | custom-call | tf_op jit(solution)/shard_map/pallas_call | solution.py:434
  39.6 2.5 %collective-permute-start.15 = (f32[16,16,128]{2,1,0:T(8,128)S(1)}, f32[16,16,128]{2,1,0:T(8,128)S(1)}, u32[]{:S(2)}, u32[]{:S(2)}) collective-permute-start(f32[16,16,128]{2,1,0:T(8,128)S(1)} %get-tuple-element.38), channel_id=1, source_target_pairs={{0,3},{1,0},{2,1},{3,2},{4,7},{5,4},{6,5},{7,6},{8,11},{9,8},{10,9... | collective-permute-start | bytes 393224 | tf_op jit(solution)/shard_map/ppermute | solution.py:551
  42.1 0.7 %shard_map.137 = f32[2,24,1024]{2,1,0:T(8,128)} custom-call(f32[8,48,128]{2,1,0:T(8,128)S(1)} %convert_add_fusion.totals, f32[2,24,1024]{2,1,0:T(8,128)S(1)} %copy-done.2), custom_call_target="tpu_custom_call" | custom-call | tf_op jit(solution)/shard_map/pallas_call | solution.py:434
  42.8 3.2 %collective-permute-done.15.spill = f32[16,16,128]{2,1,0:T(8,128)S(1)} collective-permute-done((f32[16,16,128]{2,1,0:T(8,128)S(1)}, f32[16,16,128]{2,1,0:T(8,128)S(1)}, u32[]{:S(2)}, u32[]{:S(2)}) %collective-permute-start.15) | collective-permute-done | bytes 131104 | tf_op jit(solution)/shard_map/ppermute | solution.py:551
  46.1 0.8 %shard_map.138 = (f32[2,24,1024]{2,1,0:T(8,128)}, f32[2,24,1024]{2,1,0:T(8,128)}) custom-call(s32[1]{0:T(128)} %bitcast.group, f32[640,128]{1,0:T(8,128)S(1)} %get-tuple-element.37.total, f32[16,16,128]{2,1,0:T(8,128)S(1)} %collective-permute-done.15.spill, bf16[2,24,1024]{2,1,0:T(8,128)(2,1)S(1)} %copy-done.1), custom_call_target="tpu_custom_call" | custom-call | tf_op jit(solution)/shard_map/pallas_call | solution.py:434
  (8 shorter events, 0.2 us)
Async XLA Ops:
  0.6 4.9 %copy-start.1 = (bf16[2,24,1024]{2,1,0:T(8,128)(2,1)S(1)}, bf16[2,24,1024]{2,1,0:T(8,128)(2,1)}, u32[]{:S(2)}) copy-start(bf16[2,24,1024]{2,1,0:T(8,128)(2,1)} %flows.5) | copy-start | bytes 294916
  0.6 4.9 %collective-permute-start = (bf16[2,24,1024]{2,1,0:T(8,128)(2,1)}, bf16[2,24,1024]{2,1,0:T(8,128)(2,1)S(1)}, u32[]{:S(2)}, u32[]{:S(2)}) collective-permute-start(bf16[2,24,1024]{2,1,0:T(8,128)(2,1)} %flows.5), channel_id=1, source_target_pairs={{0,1},{1,2},{2,3},{3,0},{4,5},{5,6},{6,7},{7,4},{8,9},{9,10},{10,1... | collective-permute-start | bytes 294920 | tf_op jit(solution)/shard_map/ppermute | solution.py:481
  5.6 12.5 %copy-start = (bf16[64,128,128]{2,1,0:T(8,128)(2,1)S(1)}, bf16[64,128,128]{2,1,0:T(8,128)(2,1)}, u32[]{:S(2)}) copy-start(bf16[64,128,128]{2,1,0:T(8,128)(2,1)} %mats.3) | copy-start | bytes 6291460
  5.6 12.5 %copy-start.3 = (s32[64]{0:T(128)S(1)}, s32[64]{0:T(128)}, u32[]{:S(2)}) copy-start(s32[64]{0:T(128)} %path.3) | copy-start | bytes 772
  5.6 12.5 %copy-start.4 = (s32[64]{0:T(128)S(1)}, s32[64]{0:T(128)}, u32[]{:S(2)}) copy-start(s32[64]{0:T(128)} %link.3) | copy-start | bytes 772
  5.6 12.4 %copy-start.5 = (s32[64]{0:T(128)S(1)}, s32[64]{0:T(128)}, u32[]{:S(2)}) copy-start(s32[64]{0:T(128)} %lag.3) | copy-start | bytes 772
  5.6 12.4 %copy-start.6 = (s32[64]{0:T(128)S(1)}, s32[64]{0:T(128)}, u32[]{:S(2)}) copy-start(s32[64]{0:T(128)} %rest_3_.1) | copy-start | bytes 772
  8.1 4.2 %collective-permute-start.1 = (f16[8,48,128]{2,1,0:T(8,128)(2,1)S(1)}, f16[8,48,128]{2,1,0:T(8,128)(2,1)S(1)}, u32[]{:S(2)}, u32[]{:S(2)}) collective-permute-start(f16[8,48,128]{2,1,0:T(8,128)(2,1)S(1)} %convert_element_type.42), channel_id=1, source_target_pairs={{0,4},{4,0},{8,12},{12,8},{16,20},{20,16},{24,28},{28,24},{1,5},{5... | collective-permute-start | bytes 294920 | tf_op jit(solution)/shard_map/ppermute | solution.py:497
  9.4 5.7 %collective-permute-start.3 = (f16[8,48,128]{2,1,0:T(8,128)(2,1)S(1)}, f16[8,48,128]{2,1,0:T(8,128)(2,1)S(1)}, u32[]{:S(2)}, u32[]{:S(2)}) collective-permute-start(f16[8,48,128]{2,1,0:T(8,128)(2,1)S(1)} %convert_element_type.46), channel_id=1, source_target_pairs={{0,4},{4,0},{8,12},{12,8},{16,20},{20,16},{24,28},{28,24},{1,5},{5... | collective-permute-start | bytes 294920 | tf_op jit(solution)/shard_map/ppermute | solution.py:497
  9.7 6.9 %collective-permute-start.5 = (f16[8,48,128]{2,1,0:T(8,128)(2,1)S(1)}, f16[8,48,128]{2,1,0:T(8,128)(2,1)S(1)}, u32[]{:S(2)}, u32[]{:S(2)}) collective-permute-start(f16[8,48,128]{2,1,0:T(8,128)(2,1)S(1)} %convert_element_type.50), channel_id=1, source_target_pairs={{0,4},{4,0},{8,12},{12,8},{16,20},{20,16},{24,28},{28,24},{1,5},{5... | collective-permute-start | bytes 294920 | tf_op jit(solution)/shard_map/ppermute | solution.py:497
  11.0 10.0 %collective-permute-start.7 = (f16[8,48,128]{2,1,0:T(8,128)(2,1)S(1)}, f16[8,48,128]{2,1,0:T(8,128)(2,1)S(1)}, u32[]{:S(2)}, u32[]{:S(2)}) collective-permute-start(f16[8,48,128]{2,1,0:T(8,128)(2,1)S(1)} %convert_element_type.54), channel_id=1, source_target_pairs={{0,4},{4,0},{8,12},{12,8},{16,20},{20,16},{24,28},{28,24},{1,5},{5... | collective-permute-start | bytes 294920 | tf_op jit(solution)/shard_map/ppermute | solution.py:497
  12.2 11.3 %copy-start.2 = (f32[2,24,1024]{2,1,0:T(8,128)S(1)}, f32[2,24,1024]{2,1,0:T(8,128)}, u32[]{:S(2)}) copy-start(f32[2,24,1024]{2,1,0:T(8,128)} %counts.3) | copy-start | bytes 589828
  12.3 8.8 %collective-permute-start.2 = (f16[8,48,128]{2,1,0:T(8,128)(2,1)S(1)}, f16[8,48,128]{2,1,0:T(8,128)(2,1)S(1)}, u32[]{:S(2)}, u32[]{:S(2)}) collective-permute-start(f16[8,48,128]{2,1,0:T(8,128)(2,1)S(1)} %add_convert_fusion.2), channel_id=1, source_target_pairs={{0,24},{4,28},{8,16},{12,20},{16,8},{20,12},{24,0},{28,4},{1,25},{... | collective-permute-start | bytes 294920 | tf_op jit(solution)/shard_map/ppermute | solution.py:497
  15.1 8.4 %collective-permute-start.4 = (f16[8,48,128]{2,1,0:T(8,128)(2,1)S(1)}, f16[8,48,128]{2,1,0:T(8,128)(2,1)S(1)}, u32[]{:S(2)}, u32[]{:S(2)}) collective-permute-start(f16[8,48,128]{2,1,0:T(8,128)(2,1)S(1)} %add_convert_fusion.1), channel_id=1, source_target_pairs={{0,16},{4,20},{8,24},{12,28},{16,0},{20,4},{24,8},{28,12},{1,17},{... | collective-permute-start | bytes 294920 | tf_op jit(solution)/shard_map/ppermute | solution.py:497
  16.7 6.8 %collective-permute-start.6 = (f16[8,48,128]{2,1,0:T(8,128)(2,1)S(1)}, f16[8,48,128]{2,1,0:T(8,128)(2,1)S(1)}, u32[]{:S(2)}, u32[]{:S(2)}) collective-permute-start(f16[8,48,128]{2,1,0:T(8,128)(2,1)S(1)} %add_convert_fusion), channel_id=1, source_target_pairs={{0,8},{4,12},{8,0},{12,4},{16,24},{20,28},{24,16},{28,20},{1,9},{5... | collective-permute-start | bytes 294920 | tf_op jit(solution)/shard_map/ppermute | solution.py:497
  23.6 6.2 %collective-permute-start.8 = (bf16[8,48,128]{2,1,0:T(8,128)(2,1)S(1)}, bf16[8,48,128]{2,1,0:T(8,128)(2,1)S(1)}, u32[]{:S(2)}, u32[]{:S(2)}) collective-permute-start(bf16[8,48,128]{2,1,0:T(8,128)(2,1)S(1)} %shard_map.133.signal), channel_id=1, source_target_pairs={{0,24},{4,28},{8,16},{12,20},{16,8},{20,12},{24,0},{28,4},{1,25},{... | collective-permute-start | bytes 294920 | tf_op jit(solution)/shard_map/ppermute | solution.py:497
  26.3 4.4 %collective-permute-start.10 = (bf16[8,48,128]{2,1,0:T(8,128)(2,1)S(1)}, bf16[8,48,128]{2,1,0:T(8,128)(2,1)S(1)}, u32[]{:S(2)}, u32[]{:S(2)}) collective-permute-start(bf16[8,48,128]{2,1,0:T(8,128)(2,1)S(1)} %shard_map.133.signal), channel_id=1, source_target_pairs={{0,8},{4,12},{8,0},{12,4},{16,24},{20,28},{24,16},{28,20},{1,9},{5... | collective-permute-start | bytes 294920 | tf_op jit(solution)/shard_map/ppermute | solution.py:497
  26.3 7.5 %collective-permute-start.11 = (bf16[8,48,128]{2,1,0:T(8,128)(2,1)S(1)}, bf16[8,48,128]{2,1,0:T(8,128)(2,1)S(1)}, u32[]{:S(2)}, u32[]{:S(2)}) collective-permute-start(bf16[8,48,128]{2,1,0:T(8,128)(2,1)S(1)} %shard_map.133.signal), channel_id=1, source_target_pairs={{0,16},{4,20},{8,24},{12,28},{16,0},{20,4},{24,8},{28,12},{1,17},{... | collective-permute-start | bytes 294920 | tf_op jit(solution)/shard_map/ppermute | solution.py:497
  27.3 7.5 %collective-permute-start.9 = (bf16[8,48,128]{2,1,0:T(8,128)(2,1)S(1)}, bf16[8,48,128]{2,1,0:T(8,128)(2,1)S(1)}, u32[]{:S(2)}, u32[]{:S(2)}) collective-permute-start(bf16[8,48,128]{2,1,0:T(8,128)(2,1)S(1)} %shard_map.133.signal), channel_id=1, source_target_pairs={{0,4},{4,0},{8,12},{12,8},{16,20},{20,16},{24,28},{28,24},{1,5},{5... | collective-permute-start | bytes 294920 | tf_op jit(solution)/shard_map/ppermute | solution.py:497
  29.9 6.3 %collective-permute-start.12 = (bf16[8,48,128]{2,1,0:T(8,128)(2,1)S(1)}, bf16[8,48,128]{2,1,0:T(8,128)(2,1)S(1)}, u32[]{:S(2)}, u32[]{:S(2)}) collective-permute-start(bf16[8,48,128]{2,1,0:T(8,128)(2,1)S(1)} %collective-permute-done.8.rest_3_), channel_id=1, source_target_pairs={{0,4},{4,0},{8,12},{12,8},{16,20},{20,16},{24,28},{28,24},{1,5},{5... | collective-permute-start | bytes 294920 | tf_op jit(solution)/shard_map/ppermute | solution.py:497
  30.7 5.5 %collective-permute-start.13 = (bf16[8,48,128]{2,1,0:T(8,128)(2,1)S(1)}, bf16[8,48,128]{2,1,0:T(8,128)(2,1)S(1)}, u32[]{:S(2)}, u32[]{:S(2)}) collective-permute-start(bf16[8,48,128]{2,1,0:T(8,128)(2,1)S(1)} %collective-permute-done.10.rest_1_), channel_id=1, source_target_pairs={{0,4},{4,0},{8,12},{12,8},{16,20},{20,16},{24,28},{28,24},{1,5},{5... | collective-permute-start | bytes 294920 | tf_op jit(solution)/shard_map/ppermute | solution.py:497
  33.9 4.7 %collective-permute-start.14 = (bf16[8,48,128]{2,1,0:T(8,128)(2,1)S(1)}, bf16[8,48,128]{2,1,0:T(8,128)(2,1)S(1)}, u32[]{:S(2)}, u32[]{:S(2)}) collective-permute-start(bf16[8,48,128]{2,1,0:T(8,128)(2,1)S(1)} %collective-permute-done.11.rest_2_), channel_id=1, source_target_pairs={{0,4},{4,0},{8,12},{12,8},{16,20},{20,16},{24,28},{28,24},{1,5},{5... | collective-permute-start | bytes 294920 | tf_op jit(solution)/shard_map/ppermute | solution.py:497
  39.6 6.4 %collective-permute-start.15 = (f32[16,16,128]{2,1,0:T(8,128)S(1)}, f32[16,16,128]{2,1,0:T(8,128)S(1)}, u32[]{:S(2)}, u32[]{:S(2)}) collective-permute-start(f32[16,16,128]{2,1,0:T(8,128)S(1)} %get-tuple-element.38), channel_id=1, source_target_pairs={{0,3},{1,0},{2,1},{3,2},{4,7},{5,4},{6,5},{7,6},{8,11},{9,8},{10,9... | collective-permute-start | bytes 393224 | tf_op jit(solution)/shard_map/ppermute | solution.py:551

commit v15 on v14

--- a/solution.py
+++ b/solution.py
@@ -505,8 +505,14 @@
         [wide, pltpu.VMEM((len(order) * links, *piece[1:]), f32)],
     )
     count = len(through)
-    crossed = [exchanged(part.astype(WIRE), 1) for part in outgoing[:count]]
-    near = exchanged(outgoing[count].astype(WIRE), 1)
+    waves = [part.astype(WIRE) for part in outgoing[: count + 1]]
+    lead = exchanged(waves[0], 1)
+    held = [i for i in range(1, count + 1) if order[i] != final ^ 1]
+    lead, *late = lax.optimization_barrier((lead, *(waves[i] for i in held)))
+    for i, wave in zip(held, late):
+        waves[i] = wave
+    crossed = [lead, *(exchanged(wave, 1) for wave in waves[1:count])]
+    near = exchanged(waves[count], 1)
     received = []
     for s, kept in reversed(list(zip(through, outgoing[count + 1 :]))):
         met = crossed[order.index(s ^ 1)].astype(f32)

time: 47 us -> 46.9 us (level)
  starting transfers between devices: 21.5 us -> 19.1 us
  waiting for transfers between devices: 11.1 us -> 13.3 us
    ppermute x14, starting transfers between devices: 16.3 us -> 11.9 us  [exchanged(): return lax.ppermute(part, 'corr', [(i, i ^ s) for i in range(corridors)])]
    ppermute x14, waiting for transfers between devices: 7.9 us -> 11 us  [exchanged(): return lax.ppermute(part, 'corr', [(i, i ^ s) for i in range(corridors)])]
    ppermute x1, starting transfers between devices: 2.51 us -> 4.55 us  [per_device_dense(): lax.ppermute(early[0], 'tm', [(i, (i - 1) % groups) for i in range(groups)])]
    ppermute x1, waiting for transfers between devices: 3.22 us -> 2.29 us  [per_device_dense(): lax.ppermute(early[0], 'tm', [(i, (i - 1) % groups) for i in range(groups)])]
  transfers between devices with their start and end apart: 16 -> 16, of which waited for: 6 -> 8; matrix products, arithmetic and copies ran while one was open for 0% -> 0% of each run, Pallas kernels for 19% -> 19%
where the time goes in v15:
time: 46.9 us; the launch traced here: 46.8 us
  starting transfers between devices  19.1 us (41%)
  waiting for transfers between devices  13.3 us (28%)
  Pallas kernels  13.1 us (28%)
  between operations  0.89 us (2%)
    ppermute x14, starting transfers between devices, exchanged(): return lax.ppermute(part, 'corr', [(i, i ^ s) for i in range(corridors)])  11.9 us
    ppermute x14, waiting for transfers between devices, exchanged(): return lax.ppermute(part, 'corr', [(i, i ^ s) for i in range(corridors)])  11 us
    pallas_call x8, Pallas kernels, kernel_call(): pl.pallas_call(body, out_shape=out_shape, in_specs=[SMEM] * len(scalars)...  10.9 us
    ppermute x1, starting transfers between devices, per_device_dense(): lax.ppermute(early[0], 'tm', [(i, (i - 1) % groups) for i in range(groups)])  4.55 us
    ppermute x1, starting transfers between devices, per_device_dense(): lax.ppermute(flows, 'tm', [(i, (i + 1) % groups) for i in range(groups)])  2.68 us
    ppermute x1, waiting for transfers between devices, per_device_dense(): lax.ppermute(early[0], 'tm', [(i, (i - 1) % groups) for i in range(groups)])  2.29 us
    pallas_call x1, Pallas kernels, per_device_dense(): pl.pallas_call(functools.partial(prepare_kernel, cap, order, links, CHUNK...  2.2 us
  transfers between devices with their start and end apart: 16, of which 8 were waited for; matrix products, arithmetic and copies ran while one was open for 0% of the time, Pallas kernels for 19%

profile of v15, /device:TPU:1, one launch (start us, length us, event | category | flops | bytes accessed | tf_op | source)
XLA Modules:
  0.0 46.8 jit_solution(2593425869877240041)
XLA Ops:
  0.6 0.0 copy-start.1
  0.6 2.7 %collective-permute-start = (bf16[2,24,1024]{2,1,0:T(8,128)(2,1)}, bf16[2,24,1024]{2,1,0:T(8,128)(2,1)S(1)}, u32[]{:S(2)}, u32[]{:S(2)}) collective-permute-start(bf16[2,24,1024]{2,1,0:T(8,128)(2,1)} %flows.5), channel_id=1, source_target_pairs={{0,1},{1,2},{2,3},{3,0},{4,5},{5,6},{6,7},{7,4},{8,9},{9,10},{10,1... | collective-permute-start | bytes 294920 | tf_op jit(solution)/shard_map/ppermute | solution.py:481
  3.3 2.2 %shard_map.131 = (s32[128]{0:T(128)S(1)}, bf16[64,128,128]{2,1,0:T(8,128)(2,1)S(1)}) custom-call(s32[1]{0:T(128)} %bitcast.1.me, s32[64]{0:T(128)} %rest_0_.1, s32[64]{0:T(128)} %rest_1_.1, s32[64]{0:T(128)} %rest_2_.1, s32[64]{0:T(128)} %rest_3_.1, bf16[64,128,128]{2,1,0:T(8,128)(2,1)} %rest_4_.1), custom_call_target="tpu_custom_call" | custom-call | tf_op jit(solution)/shard_map/pallas_call | solution.py:483
  5.5 0.0 collective-permute-done.before
  5.5 0.0 copy-done.1
  5.6 0.0 copy-start
  5.6 0.0 copy-start.3
  5.6 0.0 copy-start.4
  5.6 0.0 copy-start.5
  5.6 0.0 copy-start.6
  5.6 2.4 %shard_map.132 = (f32[8,48,128]{2,1,0:T(8,128)S(1)}, f32[8,48,128]{2,1,0:T(8,128)S(1)}, f32[8,48,128]{2,1,0:T(8,128)S(1)}, f32[8,48,128]{2,1,0:T(8,128)S(1)}, f3...) custom-call(s32[1]{0:T(128)} %bitcast.group, s32[128]{0:T(128)S(1)} %get-tuple-element.26.ahead, ...), custom_call_target="tpu_custom_call" | custom-call | tf_op jit(solution)/shard_map/pallas_call | solution.py:434
  8.1 1.3 %collective-permute-start.1 = (f16[8,48,128]{2,1,0:T(8,128)(2,1)S(1)}, f16[8,48,128]{2,1,0:T(8,128)(2,1)S(1)}, u32[]{:S(2)}, u32[]{:S(2)}) collective-permute-start(f16[8,48,128]{2,1,0:T(8,128)(2,1)S(1)} %convert_element_type.42), channel_id=1, source_target_pairs={{0,4},{4,0},{8,12},{12,8},{16,20},{20,16},{24,28},{28,24},{1,5},{5... | collective-permute-start | bytes 294920 | tf_op jit(solution)/shard_map/ppermute | solution.py:497
  9.4 0.3 collective-permute-start.3
  9.8 2.5 %collective-permute-done.1 = f16[8,48,128]{2,1,0:T(8,128)(2,1)S(1)} collective-permute-done((f16[8,48,128]{2,1,0:T(8,128)(2,1)S(1)}, f16[8,48,128]{2,1,0:T(8,128)(2,1)S(1)}, u32[]{:S(2)}, u32[]{:S(2)}) %collective-permute-start.1) | collective-permute-done | bytes 98336 | tf_op jit(solution)/shard_map/ppermute | solution.py:497
  12.2 0.0 copy-start.2
  12.3 2.8 %collective-permute-start.2 = (f16[8,48,128]{2,1,0:T(8,128)(2,1)S(1)}, f16[8,48,128]{2,1,0:T(8,128)(2,1)S(1)}, u32[]{:S(2)}, u32[]{:S(2)}) collective-permute-start(f16[8,48,128]{2,1,0:T(8,128)(2,1)S(1)} %add_convert_fusion.2), channel_id=1, source_target_pairs={{0,24},{4,28},{8,16},{12,20},{16,8},{20,12},{24,0},{28,4},{1,25},{... | collective-permute-start | bytes 294920 | tf_op jit(solution)/shard_map/ppermute | solution.py:497
  15.0 1.2 %collective-permute-start.5 = (f16[8,48,128]{2,1,0:T(8,128)(2,1)S(1)}, f16[8,48,128]{2,1,0:T(8,128)(2,1)S(1)}, u32[]{:S(2)}, u32[]{:S(2)}) collective-permute-start(f16[8,48,128]{2,1,0:T(8,128)(2,1)S(1)} %convert_element_type.43), channel_id=1, source_target_pairs={{0,4},{4,0},{8,12},{12,8},{16,20},{20,16},{24,28},{28,24},{1,5},{5... | collective-permute-start | bytes 294920 | tf_op jit(solution)/shard_map/ppermute | solution.py:497
  16.3 0.2 collective-permute-start.7
  16.5 0.0 collective-permute-done.3
  16.6 0.2 collective-permute-start.4
  16.7 1.8 %collective-permute-done.5 = f16[8,48,128]{2,1,0:T(8,128)(2,1)S(1)} collective-permute-done((f16[8,48,128]{2,1,0:T(8,128)(2,1)S(1)}, f16[8,48,128]{2,1,0:T(8,128)(2,1)S(1)}, u32[]{:S(2)}, u32[]{:S(2)}) %collective-permute-start.5) | collective-permute-done | bytes 98336 | tf_op jit(solution)/shard_map/ppermute | solution.py:497
  18.5 0.1 collective-permute-start.6
  18.6 0.0 copy-done
  18.6 0.0 copy-done.3
  18.6 0.0 copy-done.4
  18.7 0.0 copy-done.5
  18.7 0.0 copy-done.6
  18.7 3.0 %shard_map.130 = (f32[8,48,128]{2,1,0:T(8,128)S(1)}, s32[87]{0:T(128)S(1)}) custom-call(s32[1]{0:T(128)} %bitcast.group, s32[1]{0:T(128)} %bitcast.1.me, s32[64]{0:T(128)S(1)} %copy-done.6, s32[64]{0:T(128)S(1)} %copy-done.3, s32[64]{0:T(128)S(1)} %copy-done.4, s32[64]{0:T(128)S(1)} %copy-done.5, bf16[2,24,1024]{2,1,0:T(8,128)(2,1)S(1)} %copy-done.1, ...), custom_call_target="tpu_custom_call" | custom-call | tf_op jit(solution)/shard_map/pallas_call | solution.py:434
  21.7 0.0 collective-permute-done.2
  21.7 0.0 collective-permute-done.7
  21.7 1.2 %collective-permute-done.4 = f16[8,48,128]{2,1,0:T(8,128)(2,1)S(1)} collective-permute-done((f16[8,48,128]{2,1,0:T(8,128)(2,1)S(1)}, f16[8,48,128]{2,1,0:T(8,128)(2,1)S(1)}, u32[]{:S(2)}, u32[]{:S(2)}) %collective-permute-start.4) | collective-permute-done | bytes 98336 | tf_op jit(solution)/shard_map/ppermute | solution.py:497
  22.9 0.6 %collective-permute-done.6 = f16[8,48,128]{2,1,0:T(8,128)(2,1)S(1)} collective-permute-done((f16[8,48,128]{2,1,0:T(8,128)(2,1)S(1)}, f16[8,48,128]{2,1,0:T(8,128)(2,1)S(1)}, u32[]{:S(2)}, u32[]{:S(2)}) %collective-permute-start.6) | collective-permute-done | bytes 98336 | tf_op jit(solution)/shard_map/ppermute | solution.py:497
  23.5 0.1 convert_add_fusion.totals
  23.6 0.0 copy-done.2
  23.7 3.1 %collective-permute-start.8 = (bf16[8,48,128]{2,1,0:T(8,128)(2,1)S(1)}, bf16[8,48,128]{2,1,0:T(8,128)(2,1)S(1)}, u32[]{:S(2)}, u32[]{:S(2)}) collective-permute-start(bf16[8,48,128]{2,1,0:T(8,128)(2,1)S(1)} %shard_map.133.signal), channel_id=1, source_target_pairs={{0,24},{4,28},{8,16},{12,20},{16,8},{20,12},{24,0},{28,4},{1,25},{... | collective-permute-start | bytes 294920 | tf_op jit(solution)/shard_map/ppermute | solution.py:497
  26.8 0.0 collective-permute-start.10
  26.8 0.5 %collective-permute-start.11 = (bf16[8,48,128]{2,1,0:T(8,128)(2,1)S(1)}, bf16[8,48,128]{2,1,0:T(8,128)(2,1)S(1)}, u32[]{:S(2)}, u32[]{:S(2)}) collective-permute-start(bf16[8,48,128]{2,1,0:T(8,128)(2,1)S(1)} %shard_map.133.signal), channel_id=1, source_target_pairs={{0,16},{4,20},{8,24},{12,28},{16,0},{20,4},{24,8},{28,12},{1,17},{... | collective-permute-start | bytes 294920 | tf_op jit(solution)/shard_map/ppermute | solution.py:497
  27.3 1.1 %collective-permute-start.9 = (bf16[8,48,128]{2,1,0:T(8,128)(2,1)S(1)}, bf16[8,48,128]{2,1,0:T(8,128)(2,1)S(1)}, u32[]{:S(2)}, u32[]{:S(2)}) collective-permute-start(bf16[8,48,128]{2,1,0:T(8,128)(2,1)S(1)} %shard_map.133.signal), channel_id=1, source_target_pairs={{0,4},{4,0},{8,12},{12,8},{16,20},{20,16},{24,28},{28,24},{1,5},{5... | collective-permute-start | bytes 294920 | tf_op jit(solution)/shard_map/ppermute | solution.py:497
  28.4 1.6 %shard_map.134.start = f32[640,128]{1,0:T(8,128)S(1)} custom-call(s32[64]{0:T(128)S(1)} %copy-done.3, s32[64]{0:T(128)S(1)} %copy-done.4, s32[64]{0:T(128)S(1)} %copy-done.5, bf16[8,48,128]{2,1,0:T(8,128)(2,1)S(1)} %shard_map.133.signal, bf16[64,128,128]{2,1,0:T(8,128)(2,1)S(1)} %copy-done), custom_call_target="tpu_custom_call" | custom-call | tf_op jit(solution)/shard_map/pallas_call | solution.py:434
  29.9 0.0 collective-permute-done.8.rest_3_
  29.9 0.4 collective-permute-start.12
  30.4 0.6 %collective-permute-done.10.rest_1_ = bf16[8,48,128]{2,1,0:T(8,128)(2,1)S(1)} collective-permute-done((bf16[8,48,128]{2,1,0:T(8,128)(2,1)S(1)}, bf16[8,48,128]{2,1,0:T(8,128)(2,1)S(1)}, u32[]{:S(2)}, u32[]{:S(2)}) %collective-permute-start.10) | collective-permute-done | bytes 98336 | tf_op jit(solution)/shard_map/ppermute | solution.py:497
  30.9 0.7 %collective-permute-start.13 = (bf16[8,48,128]{2,1,0:T(8,128)(2,1)S(1)}, bf16[8,48,128]{2,1,0:T(8,128)(2,1)S(1)}, u32[]{:S(2)}, u32[]{:S(2)}) collective-permute-start(bf16[8,48,128]{2,1,0:T(8,128)(2,1)S(1)} %collective-permute-done.10.rest_1_), channel_id=1, source_target_pairs={{0,4},{4,0},{8,12},{12,8},{16,20},{20,16},{24,28},{28,24},{1,5},{5... | collective-permute-start | bytes 294920 | tf_op jit(solution)/shard_map/ppermute | solution.py:497
  31.6 2.3 %collective-permute-done.11.rest_2_ = bf16[8,48,128]{2,1,0:T(8,128)(2,1)S(1)} collective-permute-done((bf16[8,48,128]{2,1,0:T(8,128)(2,1)S(1)}, bf16[8,48,128]{2,1,0:T(8,128)(2,1)S(1)}, u32[]{:S(2)}, u32[]{:S(2)}) %collective-permute-start.11) | collective-permute-done | bytes 98336 | tf_op jit(solution)/shard_map/ppermute | solution.py:497
  33.9 0.0 collective-permute-start.14
  34.0 0.0 collective-permute-done.9.rest_0_
  34.0 1.4 %shard_map.135.start = f32[640,128]{1,0:T(8,128)S(1)} custom-call(s32[87]{0:T(128)S(1)} %get-tuple-element.38.table, s32[128]{0:T(128)S(1)} %get-tuple-element.26.ahead, bf16[64,128,128]{2,1,0:T(8,128)(2,1)S(1)} %get-tuple-element.27.mats, f32[640,128]{1,0:T(8,128)S(1)} %shard_map.134.start, bf16[8,48,128]{2,1,0:T(8,128)(2,1)S(1)} %collective-permute-done.9.rest_0_, ...), custom_call_target="tpu_custom_call" | custom-call | flops 500000000 | bytes 1500000 | tf_op jit(solution)/shard_map/pallas_call | solution.py:434
  35.4 0.0 collective-permute-done.12.rest_0_
  35.4 0.0 collective-permute-done.13.rest_1_
  35.4 2.0 %collective-permute-done.14.rest_2_ = bf16[8,48,128]{2,1,0:T(8,128)(2,1)S(1)} collective-permute-done((bf16[8,48,128]{2,1,0:T(8,128)(2,1)S(1)}, bf16[8,48,128]{2,1,0:T(8,128)(2,1)S(1)}, u32[]{:S(2)}, u32[]{:S(2)}) %collective-permute-start.14) | collective-permute-done | bytes 98336 | tf_op jit(solution)/shard_map/ppermute | solution.py:497
  37.4 1.0 %shard_map.136 = (f32[640,128]{1,0:T(8,128)S(1)}, f32[16,16,128]{2,1,0:T(8,128)S(1)}) custom-call(s32[87]{0:T(128)S(1)} %get-tuple-element.38.table, s32[128]{0:T(128)S(1)} %get-tuple-element.26.ahead, bf16[64,128,128]{2,1,0:T(8,128)(2,1)S(1)} %get-tuple-element.27.mats, f32[640,128]{1,0:T(8,128)S(1)} %shard_map.135.start, ...), custom_call_target="tpu_custom_call" | custom-call | tf_op jit(solution)/shard_map/pallas_call | solution.py:434
  38.4 4.5 %collective-permute-start.15 = (f32[16,16,128]{2,1,0:T(8,128)S(1)}, f32[16,16,128]{2,1,0:T(8,128)S(1)}, u32[]{:S(2)}, u32[]{:S(2)}) collective-permute-start(f32[16,16,128]{2,1,0:T(8,128)S(1)} %get-tuple-element.44), channel_id=1, source_target_pairs={{0,3},{1,0},{2,1},{3,2},{4,7},{5,4},{6,5},{7,6},{8,11},{9,8},{10,9... | collective-permute-start | bytes 393224 | tf_op jit(solution)/shard_map/ppermute | solution.py:557
  43.0 0.7 %shard_map.137 = f32[2,24,1024]{2,1,0:T(8,128)} custom-call(f32[8,48,128]{2,1,0:T(8,128)S(1)} %convert_add_fusion.totals, f32[2,24,1024]{2,1,0:T(8,128)S(1)} %copy-done.2), custom_call_target="tpu_custom_call" | custom-call | tf_op jit(solution)/shard_map/pallas_call | solution.py:434
  43.7 2.3 %collective-permute-done.15.spill = f32[16,16,128]{2,1,0:T(8,128)S(1)} collective-permute-done((f32[16,16,128]{2,1,0:T(8,128)S(1)}, f32[16,16,128]{2,1,0:T(8,128)S(1)}, u32[]{:S(2)}, u32[]{:S(2)}) %collective-permute-start.15) | collective-permute-done | bytes 131104 | tf_op jit(solution)/shard_map/ppermute | solution.py:557
  46.0 0.8 %shard_map.138 = (f32[2,24,1024]{2,1,0:T(8,128)}, f32[2,24,1024]{2,1,0:T(8,128)}) custom-call(s32[1]{0:T(128)} %bitcast.group, f32[640,128]{1,0:T(8,128)S(1)} %get-tuple-element.43.total, f32[16,16,128]{2,1,0:T(8,128)S(1)} %collective-permute-done.15.spill, bf16[2,24,1024]{2,1,0:T(8,128)(2,1)S(1)} %copy-done.1), custom_call_target="tpu_custom_call" | custom-call | tf_op jit(solution)/shard_map/pallas_call | solution.py:434
  (8 shorter events, 0.2 us)
Async XLA Ops:
  0.6 4.9 %copy-start.1 = (bf16[2,24,1024]{2,1,0:T(8,128)(2,1)S(1)}, bf16[2,24,1024]{2,1,0:T(8,128)(2,1)}, u32[]{:S(2)}) copy-start(bf16[2,24,1024]{2,1,0:T(8,128)(2,1)} %flows.5) | copy-start | bytes 294916
  0.6 4.9 %collective-permute-start = (bf16[2,24,1024]{2,1,0:T(8,128)(2,1)}, bf16[2,24,1024]{2,1,0:T(8,128)(2,1)S(1)}, u32[]{:S(2)}, u32[]{:S(2)}) collective-permute-start(bf16[2,24,1024]{2,1,0:T(8,128)(2,1)} %flows.5), channel_id=1, source_target_pairs={{0,1},{1,2},{2,3},{3,0},{4,5},{5,6},{6,7},{7,4},{8,9},{9,10},{10,1... | collective-permute-start | bytes 294920 | tf_op jit(solution)/shard_map/ppermute | solution.py:481
  5.6 13.1 %copy-start = (bf16[64,128,128]{2,1,0:T(8,128)(2,1)S(1)}, bf16[64,128,128]{2,1,0:T(8,128)(2,1)}, u32[]{:S(2)}) copy-start(bf16[64,128,128]{2,1,0:T(8,128)(2,1)} %mats.3) | copy-start | bytes 6291460
  5.6 13.1 %copy-start.3 = (s32[64]{0:T(128)S(1)}, s32[64]{0:T(128)}, u32[]{:S(2)}) copy-start(s32[64]{0:T(128)} %path.3) | copy-start | bytes 772
  5.6 13.1 %copy-start.4 = (s32[64]{0:T(128)S(1)}, s32[64]{0:T(128)}, u32[]{:S(2)}) copy-start(s32[64]{0:T(128)} %link.3) | copy-start | bytes 772
  5.6 13.1 %copy-start.5 = (s32[64]{0:T(128)S(1)}, s32[64]{0:T(128)}, u32[]{:S(2)}) copy-start(s32[64]{0:T(128)} %lag.3) | copy-start | bytes 772
  5.6 13.1 %copy-start.6 = (s32[64]{0:T(128)S(1)}, s32[64]{0:T(128)}, u32[]{:S(2)}) copy-start(s32[64]{0:T(128)} %rest_3_.1) | copy-start | bytes 772
  8.1 4.1 %collective-permute-start.1 = (f16[8,48,128]{2,1,0:T(8,128)(2,1)S(1)}, f16[8,48,128]{2,1,0:T(8,128)(2,1)S(1)}, u32[]{:S(2)}, u32[]{:S(2)}) collective-permute-start(f16[8,48,128]{2,1,0:T(8,128)(2,1)S(1)} %convert_element_type.42), channel_id=1, source_target_pairs={{0,4},{4,0},{8,12},{12,8},{16,20},{20,16},{24,28},{28,24},{1,5},{5... | collective-permute-start | bytes 294920 | tf_op jit(solution)/shard_map/ppermute | solution.py:497
  9.4 7.1 %collective-permute-start.3 = (f16[8,48,128]{2,1,0:T(8,128)(2,1)S(1)}, f16[8,48,128]{2,1,0:T(8,128)(2,1)S(1)}, u32[]{:S(2)}, u32[]{:S(2)}) collective-permute-start(f16[8,48,128]{2,1,0:T(8,128)(2,1)S(1)} %convert_element_type.48), channel_id=1, source_target_pairs={{0,4},{4,0},{8,12},{12,8},{16,20},{20,16},{24,28},{28,24},{1,5},{5... | collective-permute-start | bytes 294920 | tf_op jit(solution)/shard_map/ppermute | solution.py:497
  12.2 11.4 %copy-start.2 = (f32[2,24,1024]{2,1,0:T(8,128)S(1)}, f32[2,24,1024]{2,1,0:T(8,128)}, u32[]{:S(2)}) copy-start(f32[2,24,1024]{2,1,0:T(8,128)} %counts.3) | copy-start | bytes 589828
  12.3 9.4 %collective-permute-start.2 = (f16[8,48,128]{2,1,0:T(8,128)(2,1)S(1)}, f16[8,48,128]{2,1,0:T(8,128)(2,1)S(1)}, u32[]{:S(2)}, u32[]{:S(2)}) collective-permute-start(f16[8,48,128]{2,1,0:T(8,128)(2,1)S(1)} %add_convert_fusion.2), channel_id=1, source_target_pairs={{0,24},{4,28},{8,16},{12,20},{16,8},{20,12},{24,0},{28,4},{1,25},{... | collective-permute-start | bytes 294920 | tf_op jit(solution)/shard_map/ppermute | solution.py:497
  15.0 3.5 %collective-permute-start.5 = (f16[8,48,128]{2,1,0:T(8,128)(2,1)S(1)}, f16[8,48,128]{2,1,0:T(8,128)(2,1)S(1)}, u32[]{:S(2)}, u32[]{:S(2)}) collective-permute-start(f16[8,48,128]{2,1,0:T(8,128)(2,1)S(1)} %convert_element_type.43), channel_id=1, source_target_pairs={{0,4},{4,0},{8,12},{12,8},{16,20},{20,16},{24,28},{28,24},{1,5},{5... | collective-permute-start | bytes 294920 | tf_op jit(solution)/shard_map/ppermute | solution.py:497
  16.3 5.4 %collective-permute-start.7 = (f16[8,48,128]{2,1,0:T(8,128)(2,1)S(1)}, f16[8,48,128]{2,1,0:T(8,128)(2,1)S(1)}, u32[]{:S(2)}, u32[]{:S(2)}) collective-permute-start(f16[8,48,128]{2,1,0:T(8,128)(2,1)S(1)} %convert_element_type.44), channel_id=1, source_target_pairs={{0,4},{4,0},{8,12},{12,8},{16,20},{20,16},{24,28},{28,24},{1,5},{5... | collective-permute-start | bytes 294920 | tf_op jit(solution)/shard_map/ppermute | solution.py:497
  16.6 6.4 %collective-permute-start.4 = (f16[8,48,128]{2,1,0:T(8,128)(2,1)S(1)}, f16[8,48,128]{2,1,0:T(8,128)(2,1)S(1)}, u32[]{:S(2)}, u32[]{:S(2)}) collective-permute-start(f16[8,48,128]{2,1,0:T(8,128)(2,1)S(1)} %add_convert_fusion.1), channel_id=1, source_target_pairs={{0,16},{4,20},{8,24},{12,28},{16,0},{20,4},{24,8},{28,12},{1,17},{... | collective-permute-start | bytes 294920 | tf_op jit(solution)/shard_map/ppermute | solution.py:497
  18.5 5.0 %collective-permute-start.6 = (f16[8,48,128]{2,1,0:T(8,128)(2,1)S(1)}, f16[8,48,128]{2,1,0:T(8,128)(2,1)S(1)}, u32[]{:S(2)}, u32[]{:S(2)}) collective-permute-start(f16[8,48,128]{2,1,0:T(8,128)(2,1)S(1)} %add_convert_fusion), channel_id=1, source_target_pairs={{0,8},{4,12},{8,0},{12,4},{16,24},{20,28},{24,16},{28,20},{1,9},{5... | collective-permute-start | bytes 294920 | tf_op jit(solution)/shard_map/ppermute | solution.py:497
  23.7 6.3 %collective-permute-start.8 = (bf16[8,48,128]{2,1,0:T(8,128)(2,1)S(1)}, bf16[8,48,128]{2,1,0:T(8,128)(2,1)S(1)}, u32[]{:S(2)}, u32[]{:S(2)}) collective-permute-start(bf16[8,48,128]{2,1,0:T(8,128)(2,1)S(1)} %shard_map.133.signal), channel_id=1, source_target_pairs={{0,24},{4,28},{8,16},{12,20},{16,8},{20,12},{24,0},{28,4},{1,25},{... | collective-permute-start | bytes 294920 | tf_op jit(solution)/shard_map/ppermute | solution.py:497
  26.8 4.1 %collective-permute-start.10 = (bf16[8,48,128]{2,1,0:T(8,128)(2,1)S(1)}, bf16[8,48,128]{2,1,0:T(8,128)(2,1)S(1)}, u32[]{:S(2)}, u32[]{:S(2)}) collective-permute-start(bf16[8,48,128]{2,1,0:T(8,128)(2,1)S(1)} %shard_map.133.signal), channel_id=1, source_target_pairs={{0,8},{4,12},{8,0},{12,4},{16,24},{20,28},{24,16},{28,20},{1,9},{5... | collective-permute-start | bytes 294920 | tf_op jit(solution)/shard_map/ppermute | solution.py:497
  26.8 7.1 %collective-permute-start.11 = (bf16[8,48,128]{2,1,0:T(8,128)(2,1)S(1)}, bf16[8,48,128]{2,1,0:T(8,128)(2,1)S(1)}, u32[]{:S(2)}, u32[]{:S(2)}) collective-permute-start(bf16[8,48,128]{2,1,0:T(8,128)(2,1)S(1)} %shard_map.133.signal), channel_id=1, source_target_pairs={{0,16},{4,20},{8,24},{12,28},{16,0},{20,4},{24,8},{28,12},{1,17},{... | collective-permute-start | bytes 294920 | tf_op jit(solution)/shard_map/ppermute | solution.py:497
  27.3 6.7 %collective-permute-start.9 = (bf16[8,48,128]{2,1,0:T(8,128)(2,1)S(1)}, bf16[8,48,128]{2,1,0:T(8,128)(2,1)S(1)}, u32[]{:S(2)}, u32[]{:S(2)}) collective-permute-start(bf16[8,48,128]{2,1,0:T(8,128)(2,1)S(1)} %shard_map.133.signal), channel_id=1, source_target_pairs={{0,4},{4,0},{8,12},{12,8},{16,20},{20,16},{24,28},{28,24},{1,5},{5... | collective-permute-start | bytes 294920 | tf_op jit(solution)/shard_map/ppermute | solution.py:497
  29.9 5.4 %collective-permute-start.12 = (bf16[8,48,128]{2,1,0:T(8,128)(2,1)S(1)}, bf16[8,48,128]{2,1,0:T(8,128)(2,1)S(1)}, u32[]{:S(2)}, u32[]{:S(2)}) collective-permute-start(bf16[8,48,128]{2,1,0:T(8,128)(2,1)S(1)} %collective-permute-done.8.rest_3_), channel_id=1, source_target_pairs={{0,4},{4,0},{8,12},{12,8},{16,20},{20,16},{24,28},{28,24},{1,5},{5... | collective-permute-start | bytes 294920 | tf_op jit(solution)/shard_map/ppermute | solution.py:497
  30.9 4.4 %collective-permute-start.13 = (bf16[8,48,128]{2,1,0:T(8,128)(2,1)S(1)}, bf16[8,48,128]{2,1,0:T(8,128)(2,1)S(1)}, u32[]{:S(2)}, u32[]{:S(2)}) collective-permute-start(bf16[8,48,128]{2,1,0:T(8,128)(2,1)S(1)} %collective-permute-done.10.rest_1_), channel_id=1, source_target_pairs={{0,4},{4,0},{8,12},{12,8},{16,20},{20,16},{24,28},{28,24},{1,5},{5... | collective-permute-start | bytes 294920 | tf_op jit(solution)/shard_map/ppermute | solution.py:497
  33.9 3.5 %collective-permute-start.14 = (bf16[8,48,128]{2,1,0:T(8,128)(2,1)S(1)}, bf16[8,48,128]{2,1,0:T(8,128)(2,1)S(1)}, u32[]{:S(2)}, u32[]{:S(2)}) collective-permute-start(bf16[8,48,128]{2,1,0:T(8,128)(2,1)S(1)} %collective-permute-done.11.rest_2_), channel_id=1, source_target_pairs={{0,4},{4,0},{8,12},{12,8},{16,20},{20,16},{24,28},{28,24},{1,5},{5... | collective-permute-start | bytes 294920 | tf_op jit(solution)/shard_map/ppermute | solution.py:497
  38.4 7.6 %collective-permute-start.15 = (f32[16,16,128]{2,1,0:T(8,128)S(1)}, f32[16,16,128]{2,1,0:T(8,128)S(1)}, u32[]{:S(2)}, u32[]{:S(2)}) collective-permute-start(f32[16,16,128]{2,1,0:T(8,128)S(1)} %get-tuple-element.44), channel_id=1, source_target_pairs={{0,3},{1,0},{2,1},{3,2},{4,7},{5,4},{6,5},{7,6},{8,11},{9,8},{10,9... | collective-permute-start | bytes 393224 | tf_op jit(solution)/shard_map/ppermute | solution.py:557

commit v16 on v12

--- a/solution.py
+++ b/solution.py
@@ -548,7 +548,8 @@
             [pltpu.VMEM(slots_shape, jnp.bfloat16)],
             cost=weight(BACKWARD_COST) if first else None,
         )
-    spill = lax.ppermute(early[0], "tm", [(i, (i - 1) % groups) for i in range(groups)])
+    route = [(i, (i - 1) % groups) for i in range(groups)]
+    spill = lax.ppermute(early[0].astype(WIRE), "tm", route).astype(f32)
     totals, total = lax.optimization_barrier((totals, total))
     (link_residual,) = kernel_call(
         functools.partial(residual_kernel, days),

time: 46.2 us -> 45.7 us (0.989)
  waiting for transfers between devices: 12.9 us -> 12.2 us
    ppermute x1, waiting for transfers between devices: 1.72 us -> 1.02 us  [per_device_dense(): spill = lax.ppermute(early[0].astype(WIRE), 'tm', route).astype(f32)]
  transfers between devices with their start and end apart: 15 -> 15, of which waited for: 6 -> 6; matrix products, arithmetic and copies ran while one was open for 0% -> 0% of each run, Pallas kernels for 18% -> 19%
where the time goes in v16:
time: 45.7 us; the launch traced here: 45.4 us
  starting transfers between devices  18.8 us (41%)
  Pallas kernels  13.1 us (29%)
  waiting for transfers between devices  12.2 us (27%)
  between operations  0.86 us (2%)
    ppermute x13, starting transfers between devices, exchanged(): return lax.ppermute(part, 'corr', [(i, i ^ s) for i in range(corridors)])  14 us
    ppermute x13, waiting for transfers between devices, exchanged(): return lax.ppermute(part, 'corr', [(i, i ^ s) for i in range(corridors)])  11.2 us
    pallas_call x8, Pallas kernels, kernel_call(): pl.pallas_call(body, out_shape=out_shape, in_specs=[SMEM] * len(scalars)...  10.9 us
    ppermute x1, starting transfers between devices, per_device_dense(): lax.ppermute(flows, 'tm', [(i, (i + 1) % groups) for i in range(groups)])  2.68 us
    pallas_call x1, Pallas kernels, per_device_dense(): pl.pallas_call(functools.partial(prepare_kernel, cap, order, links, CHUNK...  2.2 us
    ppermute x1, starting transfers between devices, per_device_dense(): spill = lax.ppermute(early[0].astype(WIRE), 'tm', route).astype(f32)  2.14 us
    ppermute x1, waiting for transfers between devices, per_device_dense(): spill = lax.ppermute(early[0].astype(WIRE), 'tm', route).astype(f32)  1.02 us
  transfers between devices with their start and end apart: 15, of which 6 were waited for; matrix products, arithmetic and copies ran while one was open for 0% of the time, Pallas kernels for 19%

profile of v16, /device:TPU:1, one launch (start us, length us, event | category | flops | bytes accessed | tf_op | source)
XLA Modules:
  0.0 45.4 jit_solution(9043629421713016401)
XLA Ops:
  0.6 0.0 copy-start.1
  0.6 2.7 %collective-permute-start = (bf16[2,24,1024]{2,1,0:T(8,128)(2,1)}, bf16[2,24,1024]{2,1,0:T(8,128)(2,1)S(1)}, u32[]{:S(2)}, u32[]{:S(2)}) collective-permute-start(bf16[2,24,1024]{2,1,0:T(8,128)(2,1)} %flows.5), channel_id=1, source_target_pairs={{0,1},{1,2},{2,3},{3,0},{4,5},{5,6},{6,7},{7,4},{8,9},{9,10},{10,1... | collective-permute-start | bytes 294920 | tf_op jit(solution)/shard_map/ppermute | solution.py:477
  3.3 2.2 %shard_map.131 = (s32[128]{0:T(128)S(1)}, bf16[64,128,128]{2,1,0:T(8,128)(2,1)S(1)}) custom-call(s32[1]{0:T(128)} %bitcast.1.me, s32[64]{0:T(128)} %rest_0_.1, s32[64]{0:T(128)} %rest_1_.1, s32[64]{0:T(128)} %rest_2_.1, s32[64]{0:T(128)} %rest_3_.1, bf16[64,128,128]{2,1,0:T(8,128)(2,1)} %rest_4_.1), custom_call_target="tpu_custom_call" | custom-call | tf_op jit(solution)/shard_map/pallas_call | solution.py:479
  5.5 0.0 collective-permute-done.before
  5.5 0.0 copy-done.1
  5.6 0.0 copy-start
  5.6 0.0 copy-start.3
  5.6 0.0 copy-start.4
  5.6 0.0 copy-start.5
  5.6 0.0 copy-start.6
  5.6 2.4 %shard_map.132 = (f32[8,48,128]{2,1,0:T(8,128)S(1)}, f32[8,48,128]{2,1,0:T(8,128)S(1)}, f32[8,48,128]{2,1,0:T(8,128)S(1)}, f32[8,48,128]{2,1,0:T(8,128)S(1)}, f3...) custom-call(s32[1]{0:T(128)} %bitcast.group, s32[128]{0:T(128)S(1)} %get-tuple-element.23.ahead, ...), custom_call_target="tpu_custom_call" | custom-call | tf_op jit(solution)/shard_map/pallas_call | solution.py:434
  8.1 1.3 %collective-permute-start.1 = (f16[8,48,128]{2,1,0:T(8,128)(2,1)S(1)}, f16[8,48,128]{2,1,0:T(8,128)(2,1)S(1)}, u32[]{:S(2)}, u32[]{:S(2)}) collective-permute-start(f16[8,48,128]{2,1,0:T(8,128)(2,1)S(1)} %convert_element_type.48), channel_id=1, source_target_pairs={{0,4},{4,0},{8,12},{12,8},{16,20},{20,16},{24,28},{28,24},{1,5},{5... | collective-permute-start | bytes 294920 | tf_op jit(solution)/shard_map/ppermute | solution.py:493
  9.4 0.3 collective-permute-start.3
  9.7 1.3 %collective-permute-start.5 = (f16[8,48,128]{2,1,0:T(8,128)(2,1)S(1)}, f16[8,48,128]{2,1,0:T(8,128)(2,1)S(1)}, u32[]{:S(2)}, u32[]{:S(2)}) collective-permute-start(f16[8,48,128]{2,1,0:T(8,128)(2,1)S(1)} %convert_element_type.56), channel_id=1, source_target_pairs={{0,4},{4,0},{8,12},{12,8},{16,20},{20,16},{24,28},{28,24},{1,5},{5... | collective-permute-start | bytes 294920 | tf_op jit(solution)/shard_map/ppermute | solution.py:493
  11.0 0.3 collective-permute-start.7
  11.4 0.9 %collective-permute-done.1 = f16[8,48,128]{2,1,0:T(8,128)(2,1)S(1)} collective-permute-done((f16[8,48,128]{2,1,0:T(8,128)(2,1)S(1)}, f16[8,48,128]{2,1,0:T(8,128)(2,1)S(1)}, u32[]{:S(2)}, u32[]{:S(2)}) %collective-permute-start.1) | collective-permute-done | bytes 98336 | tf_op jit(solution)/shard_map/ppermute | solution.py:493
  12.2 0.0 copy-start.2
  12.3 2.8 %collective-permute-start.2 = (f16[8,48,128]{2,1,0:T(8,128)(2,1)S(1)}, f16[8,48,128]{2,1,0:T(8,128)(2,1)S(1)}, u32[]{:S(2)}, u32[]{:S(2)}) collective-permute-start(f16[8,48,128]{2,1,0:T(8,128)(2,1)S(1)} %add_convert_fusion.2), channel_id=1, source_target_pairs={{0,24},{4,28},{8,16},{12,20},{16,8},{20,12},{24,0},{28,4},{1,25},{... | collective-permute-start | bytes 294920 | tf_op jit(solution)/shard_map/ppermute | solution.py:493
  15.1 0.0 collective-permute-done.3
  15.1 1.5 %collective-permute-start.4 = (f16[8,48,128]{2,1,0:T(8,128)(2,1)S(1)}, f16[8,48,128]{2,1,0:T(8,128)(2,1)S(1)}, u32[]{:S(2)}, u32[]{:S(2)}) collective-permute-start(f16[8,48,128]{2,1,0:T(8,128)(2,1)S(1)} %add_convert_fusion.1), channel_id=1, source_target_pairs={{0,16},{4,20},{8,24},{12,28},{16,0},{20,4},{24,8},{28,12},{1,17},{... | collective-permute-start | bytes 294920 | tf_op jit(solution)/shard_map/ppermute | solution.py:493
  16.6 0.0 collective-permute-done.5
  16.7 1.4 %collective-permute-start.6 = (f16[8,48,128]{2,1,0:T(8,128)(2,1)S(1)}, f16[8,48,128]{2,1,0:T(8,128)(2,1)S(1)}, u32[]{:S(2)}, u32[]{:S(2)}) collective-permute-start(f16[8,48,128]{2,1,0:T(8,128)(2,1)S(1)} %add_convert_fusion), channel_id=1, source_target_pairs={{0,8},{4,12},{8,0},{12,4},{16,24},{20,28},{24,16},{28,20},{1,9},{5... | collective-permute-start | bytes 294920 | tf_op jit(solution)/shard_map/ppermute | solution.py:493
  18.0 0.0 copy-done
  18.0 0.0 copy-done.3
  18.0 0.0 copy-done.4
  18.0 0.0 copy-done.5
  18.1 0.0 copy-done.6
  18.1 3.0 %shard_map.130 = (f32[8,48,128]{2,1,0:T(8,128)S(1)}, s32[87]{0:T(128)S(1)}) custom-call(s32[1]{0:T(128)} %bitcast.group, s32[1]{0:T(128)} %bitcast.1.me, s32[64]{0:T(128)S(1)} %copy-done.6, s32[64]{0:T(128)S(1)} %copy-done.3, s32[64]{0:T(128)S(1)} %copy-done.4, s32[64]{0:T(128)S(1)} %copy-done.5, bf16[2,24,1024]{2,1,0:T(8,128)(2,1)S(1)} %copy-done.1, ...), custom_call_target="tpu_custom_call" | custom-call | tf_op jit(solution)/shard_map/pallas_call | solution.py:434
  21.1 0.0 collective-permute-done.7
  21.1 0.0 collective-permute-done.2
  21.1 2.5 %collective-permute-done.4 = f16[8,48,128]{2,1,0:T(8,128)(2,1)S(1)} collective-permute-done((f16[8,48,128]{2,1,0:T(8,128)(2,1)S(1)}, f16[8,48,128]{2,1,0:T(8,128)(2,1)S(1)}, u32[]{:S(2)}, u32[]{:S(2)}) %collective-permute-start.4) | collective-permute-done | bytes 98336 | tf_op jit(solution)/shard_map/ppermute | solution.py:493
  23.5 0.0 collective-permute-done.6
  23.5 0.1 convert_add_fusion.totals
  23.6 0.0 copy-done.2
  23.7 0.1 collective-permute-start.9
  23.8 2.6 %collective-permute-start.8 = (bf16[8,48,128]{2,1,0:T(8,128)(2,1)S(1)}, bf16[8,48,128]{2,1,0:T(8,128)(2,1)S(1)}, u32[]{:S(2)}, u32[]{:S(2)}) collective-permute-start(bf16[8,48,128]{2,1,0:T(8,128)(2,1)S(1)} %shard_map.133.signal), channel_id=1, source_target_pairs={{0,24},{4,28},{8,16},{12,20},{16,8},{20,12},{24,0},{28,4},{1,25},{... | collective-permute-start | bytes 294920 | tf_op jit(solution)/shard_map/ppermute | solution.py:493
  26.4 0.2 collective-permute-start.10
  26.6 0.6 %collective-permute-done.9.rest_0_ = bf16[8,48,128]{2,1,0:T(8,128)(2,1)S(1)} collective-permute-done((bf16[8,48,128]{2,1,0:T(8,128)(2,1)S(1)}, bf16[8,48,128]{2,1,0:T(8,128)(2,1)S(1)}, u32[]{:S(2)}, u32[]{:S(2)}) %collective-permute-start.9) | collective-permute-done | bytes 98336 | tf_op jit(solution)/shard_map/ppermute | solution.py:493
  27.2 1.1 %collective-permute-start.13 = (bf16[16,48,128]{2,1,0:T(8,128)(2,1)S(1)}, bf16[16,48,128]{2,1,0:T(8,128)(2,1)S(1)}, u32[]{:S(2)}, u32[]{:S(2)}) collective-permute-start(bf16[16,48,128]{2,1,0:T(8,128)(2,1)S(1)} %pad_maximum_fusion), channel_id=1, source_target_pairs={{0,4},{4,0},{8,12},{12,8},{16,20},{20,16},{24,28},{28,24},{1,5},{5... | collective-permute-start | bytes 589832 | tf_op jit(solution)/shard_map/ppermute | solution.py:493
  28.3 1.5 %shard_map.134.start = f32[640,128]{1,0:T(8,128)S(1)} custom-call(s32[64]{0:T(128)S(1)} %copy-done.3, s32[64]{0:T(128)S(1)} %copy-done.4, s32[64]{0:T(128)S(1)} %copy-done.5, bf16[8,48,128]{2,1,0:T(8,128)(2,1)S(1)} %shard_map.133.signal, bf16[64,128,128]{2,1,0:T(8,128)(2,1)S(1)} %copy-done), custom_call_target="tpu_custom_call" | custom-call | tf_op jit(solution)/shard_map/pallas_call | solution.py:434
  29.9 0.0 collective-permute-done.8.rest_2_
  29.9 0.5 %collective-permute-start.11 = (bf16[8,48,128]{2,1,0:T(8,128)(2,1)S(1)}, bf16[8,48,128]{2,1,0:T(8,128)(2,1)S(1)}, u32[]{:S(2)}, u32[]{:S(2)}) collective-permute-start(bf16[8,48,128]{2,1,0:T(8,128)(2,1)S(1)} %collective-permute-done.8.rest_2_), channel_id=1, source_target_pairs={{0,4},{4,0},{8,12},{12,8},{16,20},{20,16},{24,28},{28,24},{1,5},{5... | collective-permute-start | bytes 294920 | tf_op jit(solution)/shard_map/ppermute | solution.py:493
  30.4 4.3 %collective-permute-done.10.rest_1_ = bf16[8,48,128]{2,1,0:T(8,128)(2,1)S(1)} collective-permute-done((bf16[8,48,128]{2,1,0:T(8,128)(2,1)S(1)}, bf16[8,48,128]{2,1,0:T(8,128)(2,1)S(1)}, u32[]{:S(2)}, u32[]{:S(2)}) %collective-permute-start.10) | collective-permute-done | bytes 98336 | tf_op jit(solution)/shard_map/ppermute | solution.py:493
  34.7 0.5 %collective-permute-start.12 = (bf16[8,48,128]{2,1,0:T(8,128)(2,1)S(1)}, bf16[8,48,128]{2,1,0:T(8,128)(2,1)S(1)}, u32[]{:S(2)}, u32[]{:S(2)}) collective-permute-start(bf16[8,48,128]{2,1,0:T(8,128)(2,1)S(1)} %collective-permute-done.10.rest_1_), channel_id=1, source_target_pairs={{0,4},{4,0},{8,12},{12,8},{16,20},{20,16},{24,28},{28,24},{1,5},{5... | collective-permute-start | bytes 294920 | tf_op jit(solution)/shard_map/ppermute | solution.py:493
  35.3 1.0 %shard_map.135.start = f32[640,128]{1,0:T(8,128)S(1)} custom-call(s32[87]{0:T(128)S(1)} %get-tuple-element.32.table, s32[128]{0:T(128)S(1)} %get-tuple-element.23.ahead, bf16[64,128,128]{2,1,0:T(8,128)(2,1)S(1)} %get-tuple-element.24.mats, f32[640,128]{1,0:T(8,128)S(1)} %shard_map.134.start, bf16[8,48,128]{2,1,0:T(8,128)(2,1)S(1)} %collective-permute-done.9.rest_0_, ...), custom_call_target="tpu_custom_call" | custom-call | flops 500000000 | bytes 1500000 | tf_op jit(solution)/shard_map/pallas_call | solution.py:434
  36.3 0.0 collective-permute-done.11.rest_0_
  36.3 3.0 %collective-permute-done.12.rest_1_ = bf16[8,48,128]{2,1,0:T(8,128)(2,1)S(1)} collective-permute-done((bf16[8,48,128]{2,1,0:T(8,128)(2,1)S(1)}, bf16[8,48,128]{2,1,0:T(8,128)(2,1)S(1)}, u32[]{:S(2)}, u32[]{:S(2)}) %collective-permute-start.12) | collective-permute-done | bytes 98336 | tf_op jit(solution)/shard_map/ppermute | solution.py:493
  39.3 0.0 collective-permute-done.13.rest_2_
  39.3 1.4 %shard_map.136 = (f32[640,128]{1,0:T(8,128)S(1)}, f32[16,16,128]{2,1,0:T(8,128)S(1)}) custom-call(s32[87]{0:T(128)S(1)} %get-tuple-element.32.table, s32[128]{0:T(128)S(1)} %get-tuple-element.23.ahead, bf16[64,128,128]{2,1,0:T(8,128)(2,1)S(1)} %get-tuple-element.24.mats, f32[640,128]{1,0:T(8,128)S(1)} %shard_map.135.start, ...), custom_call_target="tpu_custom_call" | custom-call | tf_op jit(solution)/shard_map/pallas_call | solution.py:434
  40.7 2.1 %collective-permute-start.14 = (f16[16,16,128]{2,1,0:T(8,128)(2,1)S(1)}, f16[16,16,128]{2,1,0:T(8,128)(2,1)S(1)}, u32[]{:S(2)}, u32[]{:S(2)}) collective-permute-start(f16[16,16,128]{2,1,0:T(8,128)(2,1)S(1)} %convert_element_type.62), channel_id=1, source_target_pairs={{0,3},{1,0},{2,1},{3,2},{4,7},{5,4},{6,5},{7,6},{8,11},{9,8},{10,9... | collective-permute-start | bytes 196616 | tf_op jit(solution)/shard_map/ppermute | solution.py:552
  42.8 0.7 %shard_map.137 = f32[2,24,1024]{2,1,0:T(8,128)} custom-call(f32[8,48,128]{2,1,0:T(8,128)S(1)} %convert_add_fusion.totals, f32[2,24,1024]{2,1,0:T(8,128)S(1)} %copy-done.2), custom_call_target="tpu_custom_call" | custom-call | tf_op jit(solution)/shard_map/pallas_call | solution.py:434
  43.5 1.0 %collective-permute-done.14 = f16[16,16,128]{2,1,0:T(8,128)(2,1)S(1)} collective-permute-done((f16[16,16,128]{2,1,0:T(8,128)(2,1)S(1)}, f16[16,16,128]{2,1,0:T(8,128)(2,1)S(1)}, u32[]{:S(2)}, u32[]{:S(2)}) %collective-permute-start.14) | collective-permute-done | bytes 65568 | tf_op jit(solution)/shard_map/ppermute | solution.py:552
  44.6 0.8 %shard_map.138 = (f32[2,24,1024]{2,1,0:T(8,128)}, f32[2,24,1024]{2,1,0:T(8,128)}) custom-call(s32[1]{0:T(128)} %bitcast.group, f32[640,128]{1,0:T(8,128)S(1)} %get-tuple-element.37.total, f32[16,16,128]{2,1,0:T(8,128)S(1)} %convert_element_type.63.spill, bf16[2,24,1024]{2,1,0:T(8,128)(2,1)S(1)} %copy-done.1), custom_call_target="tpu_custom_call" | custom-call | tf_op jit(solution)/shard_map/pallas_call | solution.py:434
  (11 shorter events, 0.3 us)
Async XLA Ops:
  0.6 4.9 %copy-start.1 = (bf16[2,24,1024]{2,1,0:T(8,128)(2,1)S(1)}, bf16[2,24,1024]{2,1,0:T(8,128)(2,1)}, u32[]{:S(2)}) copy-start(bf16[2,24,1024]{2,1,0:T(8,128)(2,1)} %flows.5) | copy-start | bytes 294916
  0.6 4.9 %collective-permute-start = (bf16[2,24,1024]{2,1,0:T(8,128)(2,1)}, bf16[2,24,1024]{2,1,0:T(8,128)(2,1)S(1)}, u32[]{:S(2)}, u32[]{:S(2)}) collective-permute-start(bf16[2,24,1024]{2,1,0:T(8,128)(2,1)} %flows.5), channel_id=1, source_target_pairs={{0,1},{1,2},{2,3},{3,0},{4,5},{5,6},{6,7},{7,4},{8,9},{9,10},{10,1... | collective-permute-start | bytes 294920 | tf_op jit(solution)/shard_map/ppermute | solution.py:477
  5.6 12.5 %copy-start = (bf16[64,128,128]{2,1,0:T(8,128)(2,1)S(1)}, bf16[64,128,128]{2,1,0:T(8,128)(2,1)}, u32[]{:S(2)}) copy-start(bf16[64,128,128]{2,1,0:T(8,128)(2,1)} %mats.3) | copy-start | bytes 6291460
  5.6 12.5 %copy-start.3 = (s32[64]{0:T(128)S(1)}, s32[64]{0:T(128)}, u32[]{:S(2)}) copy-start(s32[64]{0:T(128)} %path.3) | copy-start | bytes 772
  5.6 12.5 %copy-start.4 = (s32[64]{0:T(128)S(1)}, s32[64]{0:T(128)}, u32[]{:S(2)}) copy-start(s32[64]{0:T(128)} %link.3) | copy-start | bytes 772
  5.6 12.5 %copy-start.5 = (s32[64]{0:T(128)S(1)}, s32[64]{0:T(128)}, u32[]{:S(2)}) copy-start(s32[64]{0:T(128)} %lag.3) | copy-start | bytes 772
  5.6 12.5 %copy-start.6 = (s32[64]{0:T(128)S(1)}, s32[64]{0:T(128)}, u32[]{:S(2)}) copy-start(s32[64]{0:T(128)} %rest_3_.1) | copy-start | bytes 772
  8.1 4.2 %collective-permute-start.1 = (f16[8,48,128]{2,1,0:T(8,128)(2,1)S(1)}, f16[8,48,128]{2,1,0:T(8,128)(2,1)S(1)}, u32[]{:S(2)}, u32[]{:S(2)}) collective-permute-start(f16[8,48,128]{2,1,0:T(8,128)(2,1)S(1)} %convert_element_type.48), channel_id=1, source_target_pairs={{0,4},{4,0},{8,12},{12,8},{16,20},{20,16},{24,28},{28,24},{1,5},{5... | collective-permute-start | bytes 294920 | tf_op jit(solution)/shard_map/ppermute | solution.py:493
  9.4 5.7 %collective-permute-start.3 = (f16[8,48,128]{2,1,0:T(8,128)(2,1)S(1)}, f16[8,48,128]{2,1,0:T(8,128)(2,1)S(1)}, u32[]{:S(2)}, u32[]{:S(2)}) collective-permute-start(f16[8,48,128]{2,1,0:T(8,128)(2,1)S(1)} %convert_element_type.52), channel_id=1, source_target_pairs={{0,4},{4,0},{8,12},{12,8},{16,20},{20,16},{24,28},{28,24},{1,5},{5... | collective-permute-start | bytes 294920 | tf_op jit(solution)/shard_map/ppermute | solution.py:493
  9.7 6.9 %collective-permute-start.5 = (f16[8,48,128]{2,1,0:T(8,128)(2,1)S(1)}, f16[8,48,128]{2,1,0:T(8,128)(2,1)S(1)}, u32[]{:S(2)}, u32[]{:S(2)}) collective-permute-start(f16[8,48,128]{2,1,0:T(8,128)(2,1)S(1)} %convert_element_type.56), channel_id=1, source_target_pairs={{0,4},{4,0},{8,12},{12,8},{16,20},{20,16},{24,28},{28,24},{1,5},{5... | collective-permute-start | bytes 294920 | tf_op jit(solution)/shard_map/ppermute | solution.py:493
  11.0 10.0 %collective-permute-start.7 = (f16[8,48,128]{2,1,0:T(8,128)(2,1)S(1)}, f16[8,48,128]{2,1,0:T(8,128)(2,1)S(1)}, u32[]{:S(2)}, u32[]{:S(2)}) collective-permute-start(f16[8,48,128]{2,1,0:T(8,128)(2,1)S(1)} %convert_element_type.60), channel_id=1, source_target_pairs={{0,4},{4,0},{8,12},{12,8},{16,20},{20,16},{24,28},{28,24},{1,5},{5... | collective-permute-start | bytes 294920 | tf_op jit(solution)/shard_map/ppermute | solution.py:493
  12.2 11.4 %copy-start.2 = (f32[2,24,1024]{2,1,0:T(8,128)S(1)}, f32[2,24,1024]{2,1,0:T(8,128)}, u32[]{:S(2)}) copy-start(f32[2,24,1024]{2,1,0:T(8,128)} %counts.3) | copy-start | bytes 589828
  12.3 8.8 %collective-permute-start.2 = (f16[8,48,128]{2,1,0:T(8,128)(2,1)S(1)}, f16[8,48,128]{2,1,0:T(8,128)(2,1)S(1)}, u32[]{:S(2)}, u32[]{:S(2)}) collective-permute-start(f16[8,48,128]{2,1,0:T(8,128)(2,1)S(1)} %add_convert_fusion.2), channel_id=1, source_target_pairs={{0,24},{4,28},{8,16},{12,20},{16,8},{20,12},{24,0},{28,4},{1,25},{... | collective-permute-start | bytes 294920 | tf_op jit(solution)/shard_map/ppermute | solution.py:493
  15.1 8.4 %collective-permute-start.4 = (f16[8,48,128]{2,1,0:T(8,128)(2,1)S(1)}, f16[8,48,128]{2,1,0:T(8,128)(2,1)S(1)}, u32[]{:S(2)}, u32[]{:S(2)}) collective-permute-start(f16[8,48,128]{2,1,0:T(8,128)(2,1)S(1)} %add_convert_fusion.1), channel_id=1, source_target_pairs={{0,16},{4,20},{8,24},{12,28},{16,0},{20,4},{24,8},{28,12},{1,17},{... | collective-permute-start | bytes 294920 | tf_op jit(solution)/shard_map/ppermute | solution.py:493
  16.7 6.9 %collective-permute-start.6 = (f16[8,48,128]{2,1,0:T(8,128)(2,1)S(1)}, f16[8,48,128]{2,1,0:T(8,128)(2,1)S(1)}, u32[]{:S(2)}, u32[]{:S(2)}) collective-permute-start(f16[8,48,128]{2,1,0:T(8,128)(2,1)S(1)} %add_convert_fusion), channel_id=1, source_target_pairs={{0,8},{4,12},{8,0},{12,4},{16,24},{20,28},{24,16},{28,20},{1,9},{5... | collective-permute-start | bytes 294920 | tf_op jit(solution)/shard_map/ppermute | solution.py:493
  23.7 3.5 %collective-permute-start.9 = (bf16[8,48,128]{2,1,0:T(8,128)(2,1)S(1)}, bf16[8,48,128]{2,1,0:T(8,128)(2,1)S(1)}, u32[]{:S(2)}, u32[]{:S(2)}) collective-permute-start(bf16[8,48,128]{2,1,0:T(8,128)(2,1)S(1)} %shard_map.133.signal), channel_id=1, source_target_pairs={{0,8},{4,12},{8,0},{12,4},{16,24},{20,28},{24,16},{28,20},{1,9},{5... | collective-permute-start | bytes 294920 | tf_op jit(solution)/shard_map/ppermute | solution.py:493
  23.8 6.1 %collective-permute-start.8 = (bf16[8,48,128]{2,1,0:T(8,128)(2,1)S(1)}, bf16[8,48,128]{2,1,0:T(8,128)(2,1)S(1)}, u32[]{:S(2)}, u32[]{:S(2)}) collective-permute-start(bf16[8,48,128]{2,1,0:T(8,128)(2,1)S(1)} %shard_map.133.signal), channel_id=1, source_target_pairs={{0,24},{4,28},{8,16},{12,20},{16,8},{20,12},{24,0},{28,4},{1,25},{... | collective-permute-start | bytes 294920 | tf_op jit(solution)/shard_map/ppermute | solution.py:493
  26.4 8.3 %collective-permute-start.10 = (bf16[8,48,128]{2,1,0:T(8,128)(2,1)S(1)}, bf16[8,48,128]{2,1,0:T(8,128)(2,1)S(1)}, u32[]{:S(2)}, u32[]{:S(2)}) collective-permute-start(bf16[8,48,128]{2,1,0:T(8,128)(2,1)S(1)} %shard_map.133.signal), channel_id=1, source_target_pairs={{0,16},{4,20},{8,24},{12,28},{16,0},{20,4},{24,8},{28,12},{1,17},{... | collective-permute-start | bytes 294920 | tf_op jit(solution)/shard_map/ppermute | solution.py:493
  27.2 12.0 %collective-permute-start.13 = (bf16[16,48,128]{2,1,0:T(8,128)(2,1)S(1)}, bf16[16,48,128]{2,1,0:T(8,128)(2,1)S(1)}, u32[]{:S(2)}, u32[]{:S(2)}) collective-permute-start(bf16[16,48,128]{2,1,0:T(8,128)(2,1)S(1)} %pad_maximum_fusion), channel_id=1, source_target_pairs={{0,4},{4,0},{8,12},{12,8},{16,20},{20,16},{24,28},{28,24},{1,5},{5... | collective-permute-start | bytes 589832 | tf_op jit(solution)/shard_map/ppermute | solution.py:493
  29.9 6.4 %collective-permute-start.11 = (bf16[8,48,128]{2,1,0:T(8,128)(2,1)S(1)}, bf16[8,48,128]{2,1,0:T(8,128)(2,1)S(1)}, u32[]{:S(2)}, u32[]{:S(2)}) collective-permute-start(bf16[8,48,128]{2,1,0:T(8,128)(2,1)S(1)} %collective-permute-done.8.rest_2_), channel_id=1, source_target_pairs={{0,4},{4,0},{8,12},{12,8},{16,20},{20,16},{24,28},{28,24},{1,5},{5... | collective-permute-start | bytes 294920 | tf_op jit(solution)/shard_map/ppermute | solution.py:493
  34.7 4.6 %collective-permute-start.12 = (bf16[8,48,128]{2,1,0:T(8,128)(2,1)S(1)}, bf16[8,48,128]{2,1,0:T(8,128)(2,1)S(1)}, u32[]{:S(2)}, u32[]{:S(2)}) collective-permute-start(bf16[8,48,128]{2,1,0:T(8,128)(2,1)S(1)} %collective-permute-done.10.rest_1_), channel_id=1, source_target_pairs={{0,4},{4,0},{8,12},{12,8},{16,20},{20,16},{24,28},{28,24},{1,5},{5... | collective-permute-start | bytes 294920 | tf_op jit(solution)/shard_map/ppermute | solution.py:493
  40.7 3.9 %collective-permute-start.14 = (f16[16,16,128]{2,1,0:T(8,128)(2,1)S(1)}, f16[16,16,128]{2,1,0:T(8,128)(2,1)S(1)}, u32[]{:S(2)}, u32[]{:S(2)}) collective-permute-start(f16[16,16,128]{2,1,0:T(8,128)(2,1)S(1)} %convert_element_type.62), channel_id=1, source_target_pairs={{0,3},{1,0},{2,1},{3,2},{4,7},{5,4},{6,5},{7,6},{8,11},{9,8},{10,9... | collective-permute-start | bytes 196616 | tf_op jit(solution)/shard_map/ppermute | solution.py:552

commit v17 on v16

--- a/solution.py
+++ b/solution.py
@@ -160,7 +160,7 @@
 
 HALO = 16
 WIRE = jnp.float16
-UNROLL = 32
+UNROLL = 64
 CHUNKS = 8
 
 

time: 45.7 us -> 45.3 us (level)
  Pallas kernels: 13.1 us -> 12.4 us
    pallas_call x8, Pallas kernels: 10.9 us -> 10.2 us  [kernel_call(): pl.pallas_call(body, out_shape=out_shape, in_specs=[SMEM] * len(scalars)...]
  transfers between devices with their start and end apart: 15 -> 15, of which waited for: 6 -> 6; matrix products, arithmetic and copies ran while one was open for 0% -> 0% of each run, Pallas kernels for 19% -> 18%
where the time goes in v17:
time: 45.3 us; the launch traced here: 45 us
  starting transfers between devices  18.8 us (42%)
  waiting for transfers between devices  12.6 us (28%)
  Pallas kernels  12.4 us (27%)
  between operations  0.85 us (2%)
    ppermute x13, starting transfers between devices, exchanged(): return lax.ppermute(part, 'corr', [(i, i ^ s) for i in range(corridors)])  14.1 us
    ppermute x13, waiting for transfers between devices, exchanged(): return lax.ppermute(part, 'corr', [(i, i ^ s) for i in range(corridors)])  11.6 us
    pallas_call x8, Pallas kernels, kernel_call(): pl.pallas_call(body, out_shape=out_shape, in_specs=[SMEM] * len(scalars)...  10.2 us
    ppermute x1, starting transfers between devices, per_device_dense(): lax.ppermute(flows, 'tm', [(i, (i + 1) % groups) for i in range(groups)])  2.68 us
    pallas_call x1, Pallas kernels, per_device_dense(): pl.pallas_call(functools.partial(prepare_kernel, cap, order, links, CHUNK...  2.2 us
    ppermute x1, starting transfers between devices, per_device_dense(): spill = lax.ppermute(early[0].astype(WIRE), 'tm', route).astype(f32)  2.03 us
    ppermute x1, waiting for transfers between devices, per_device_dense(): spill = lax.ppermute(early[0].astype(WIRE), 'tm', route).astype(f32)  1.04 us
  transfers between devices with their start and end apart: 15, of which 6 were waited for; matrix products, arithmetic and copies ran while one was open for 0% of the time, Pallas kernels for 18%

profile of v17, /device:TPU:1, one launch (start us, length us, event | category | flops | bytes accessed | tf_op | source)
XLA Modules:
  0.0 45.0 jit_solution(10024493492025248131)
XLA Ops:
  0.6 0.0 copy-start.1
  0.6 2.7 %collective-permute-start = (bf16[2,24,1024]{2,1,0:T(8,128)(2,1)}, bf16[2,24,1024]{2,1,0:T(8,128)(2,1)S(1)}, u32[]{:S(2)}, u32[]{:S(2)}) collective-permute-start(bf16[2,24,1024]{2,1,0:T(8,128)(2,1)} %flows.5), channel_id=1, source_target_pairs={{0,1},{1,2},{2,3},{3,0},{4,5},{5,6},{6,7},{7,4},{8,9},{9,10},{10,1... | collective-permute-start | bytes 294920 | tf_op jit(solution)/shard_map/ppermute | solution.py:477
  3.3 2.2 %shard_map.131 = (s32[128]{0:T(128)S(1)}, bf16[64,128,128]{2,1,0:T(8,128)(2,1)S(1)}) custom-call(s32[1]{0:T(128)} %bitcast.1.me, s32[64]{0:T(128)} %rest_0_.1, s32[64]{0:T(128)} %rest_1_.1, s32[64]{0:T(128)} %rest_2_.1, s32[64]{0:T(128)} %rest_3_.1, bf16[64,128,128]{2,1,0:T(8,128)(2,1)} %rest_4_.1), custom_call_target="tpu_custom_call" | custom-call | tf_op jit(solution)/shard_map/pallas_call | solution.py:479
  5.5 0.0 collective-permute-done.before
  5.5 0.0 copy-done.1
  5.6 0.0 copy-start
  5.6 0.0 copy-start.3
  5.6 0.0 copy-start.4
  5.6 0.0 copy-start.5
  5.6 0.0 copy-start.6
  5.6 2.3 %shard_map.132 = (f32[8,48,128]{2,1,0:T(8,128)S(1)}, f32[8,48,128]{2,1,0:T(8,128)S(1)}, f32[8,48,128]{2,1,0:T(8,128)S(1)}, f32[8,48,128]{2,1,0:T(8,128)S(1)}, f3...) custom-call(s32[1]{0:T(128)} %bitcast.group, s32[128]{0:T(128)S(1)} %get-tuple-element.23.ahead, ...), custom_call_target="tpu_custom_call" | custom-call | tf_op jit(solution)/shard_map/pallas_call | solution.py:434
  7.9 1.3 %collective-permute-start.1 = (f16[8,48,128]{2,1,0:T(8,128)(2,1)S(1)}, f16[8,48,128]{2,1,0:T(8,128)(2,1)S(1)}, u32[]{:S(2)}, u32[]{:S(2)}) collective-permute-start(f16[8,48,128]{2,1,0:T(8,128)(2,1)S(1)} %convert_element_type.48), channel_id=1, source_target_pairs={{0,4},{4,0},{8,12},{12,8},{16,20},{20,16},{24,28},{28,24},{1,5},{5... | collective-permute-start | bytes 294920 | tf_op jit(solution)/shard_map/ppermute | solution.py:493
  9.2 0.4 collective-permute-start.3
  9.6 1.2 %collective-permute-start.5 = (f16[8,48,128]{2,1,0:T(8,128)(2,1)S(1)}, f16[8,48,128]{2,1,0:T(8,128)(2,1)S(1)}, u32[]{:S(2)}, u32[]{:S(2)}) collective-permute-start(f16[8,48,128]{2,1,0:T(8,128)(2,1)S(1)} %convert_element_type.56), channel_id=1, source_target_pairs={{0,4},{4,0},{8,12},{12,8},{16,20},{20,16},{24,28},{28,24},{1,5},{5... | collective-permute-start | bytes 294920 | tf_op jit(solution)/shard_map/ppermute | solution.py:493
  10.9 0.4 collective-permute-start.7
  11.2 0.9 %collective-permute-done.1 = f16[8,48,128]{2,1,0:T(8,128)(2,1)S(1)} collective-permute-done((f16[8,48,128]{2,1,0:T(8,128)(2,1)S(1)}, f16[8,48,128]{2,1,0:T(8,128)(2,1)S(1)}, u32[]{:S(2)}, u32[]{:S(2)}) %collective-permute-start.1) | collective-permute-done | bytes 98336 | tf_op jit(solution)/shard_map/ppermute | solution.py:493
  12.1 0.0 copy-start.2
  12.2 2.8 %collective-permute-start.2 = (f16[8,48,128]{2,1,0:T(8,128)(2,1)S(1)}, f16[8,48,128]{2,1,0:T(8,128)(2,1)S(1)}, u32[]{:S(2)}, u32[]{:S(2)}) collective-permute-start(f16[8,48,128]{2,1,0:T(8,128)(2,1)S(1)} %add_convert_fusion.2), channel_id=1, source_target_pairs={{0,24},{4,28},{8,16},{12,20},{16,8},{20,12},{24,0},{28,4},{1,25},{... | collective-permute-start | bytes 294920 | tf_op jit(solution)/shard_map/ppermute | solution.py:493
  14.9 0.0 collective-permute-done.3
  15.0 1.5 %collective-permute-start.4 = (f16[8,48,128]{2,1,0:T(8,128)(2,1)S(1)}, f16[8,48,128]{2,1,0:T(8,128)(2,1)S(1)}, u32[]{:S(2)}, u32[]{:S(2)}) collective-permute-start(f16[8,48,128]{2,1,0:T(8,128)(2,1)S(1)} %add_convert_fusion.1), channel_id=1, source_target_pairs={{0,16},{4,20},{8,24},{12,28},{16,0},{20,4},{24,8},{28,12},{1,17},{... | collective-permute-start | bytes 294920 | tf_op jit(solution)/shard_map/ppermute | solution.py:493
  16.5 0.0 collective-permute-done.5
  16.5 1.4 %collective-permute-start.6 = (f16[8,48,128]{2,1,0:T(8,128)(2,1)S(1)}, f16[8,48,128]{2,1,0:T(8,128)(2,1)S(1)}, u32[]{:S(2)}, u32[]{:S(2)}) collective-permute-start(f16[8,48,128]{2,1,0:T(8,128)(2,1)S(1)} %add_convert_fusion), channel_id=1, source_target_pairs={{0,8},{4,12},{8,0},{12,4},{16,24},{20,28},{24,16},{28,20},{1,9},{5... | collective-permute-start | bytes 294920 | tf_op jit(solution)/shard_map/ppermute | solution.py:493
  17.9 0.0 copy-done
  17.9 0.0 copy-done.3
  17.9 0.0 copy-done.4
  17.9 0.0 copy-done.5
  17.9 0.0 copy-done.6
  17.9 2.8 %shard_map.130 = (f32[8,48,128]{2,1,0:T(8,128)S(1)}, s32[87]{0:T(128)S(1)}) custom-call(s32[1]{0:T(128)} %bitcast.group, s32[1]{0:T(128)} %bitcast.1.me, s32[64]{0:T(128)S(1)} %copy-done.6, s32[64]{0:T(128)S(1)} %copy-done.3, s32[64]{0:T(128)S(1)} %copy-done.4, s32[64]{0:T(128)S(1)} %copy-done.5, bf16[2,24,1024]{2,1,0:T(8,128)(2,1)S(1)} %copy-done.1, ...), custom_call_target="tpu_custom_call" | custom-call | tf_op jit(solution)/shard_map/pallas_call | solution.py:434
  20.8 0.0 collective-permute-done.7
  20.8 0.0 collective-permute-done.2
  20.8 2.6 %collective-permute-done.4 = f16[8,48,128]{2,1,0:T(8,128)(2,1)S(1)} collective-permute-done((f16[8,48,128]{2,1,0:T(8,128)(2,1)S(1)}, f16[8,48,128]{2,1,0:T(8,128)(2,1)S(1)}, u32[]{:S(2)}, u32[]{:S(2)}) %collective-permute-start.4) | collective-permute-done | bytes 98336 | tf_op jit(solution)/shard_map/ppermute | solution.py:493
  23.4 0.0 collective-permute-done.6
  23.4 0.1 convert_add_fusion.totals
  23.5 0.0 copy-done.2
  23.5 0.1 collective-permute-start.9
  23.7 2.6 %collective-permute-start.8 = (bf16[8,48,128]{2,1,0:T(8,128)(2,1)S(1)}, bf16[8,48,128]{2,1,0:T(8,128)(2,1)S(1)}, u32[]{:S(2)}, u32[]{:S(2)}) collective-permute-start(bf16[8,48,128]{2,1,0:T(8,128)(2,1)S(1)} %shard_map.133.signal), channel_id=1, source_target_pairs={{0,24},{4,28},{8,16},{12,20},{16,8},{20,12},{24,0},{28,4},{1,25},{... | collective-permute-start | bytes 294920 | tf_op jit(solution)/shard_map/ppermute | solution.py:493
  26.3 0.2 collective-permute-start.10
  26.5 0.6 %collective-permute-done.9.rest_0_ = bf16[8,48,128]{2,1,0:T(8,128)(2,1)S(1)} collective-permute-done((bf16[8,48,128]{2,1,0:T(8,128)(2,1)S(1)}, bf16[8,48,128]{2,1,0:T(8,128)(2,1)S(1)}, u32[]{:S(2)}, u32[]{:S(2)}) %collective-permute-start.9) | collective-permute-done | bytes 98336 | tf_op jit(solution)/shard_map/ppermute | solution.py:493
  27.1 1.1 %collective-permute-start.13 = (bf16[16,48,128]{2,1,0:T(8,128)(2,1)S(1)}, bf16[16,48,128]{2,1,0:T(8,128)(2,1)S(1)}, u32[]{:S(2)}, u32[]{:S(2)}) collective-permute-start(bf16[16,48,128]{2,1,0:T(8,128)(2,1)S(1)} %pad_maximum_fusion), channel_id=1, source_target_pairs={{0,4},{4,0},{8,12},{12,8},{16,20},{20,16},{24,28},{28,24},{1,5},{5... | collective-permute-start | bytes 589832 | tf_op jit(solution)/shard_map/ppermute | solution.py:493
  28.2 1.3 %shard_map.134.start = f32[640,128]{1,0:T(8,128)S(1)} custom-call(s32[64]{0:T(128)S(1)} %copy-done.3, s32[64]{0:T(128)S(1)} %copy-done.4, s32[64]{0:T(128)S(1)} %copy-done.5, bf16[8,48,128]{2,1,0:T(8,128)(2,1)S(1)} %shard_map.133.signal, bf16[64,128,128]{2,1,0:T(8,128)(2,1)S(1)} %copy-done), custom_call_target="tpu_custom_call" | custom-call | tf_op jit(solution)/shard_map/pallas_call | solution.py:434
  29.6 0.0 collective-permute-done.8.rest_2_
  29.6 0.6 %collective-permute-start.11 = (bf16[8,48,128]{2,1,0:T(8,128)(2,1)S(1)}, bf16[8,48,128]{2,1,0:T(8,128)(2,1)S(1)}, u32[]{:S(2)}, u32[]{:S(2)}) collective-permute-start(bf16[8,48,128]{2,1,0:T(8,128)(2,1)S(1)} %collective-permute-done.8.rest_2_), channel_id=1, source_target_pairs={{0,4},{4,0},{8,12},{12,8},{16,20},{20,16},{24,28},{28,24},{1,5},{5... | collective-permute-start | bytes 294920 | tf_op jit(solution)/shard_map/ppermute | solution.py:493
  30.1 4.4 %collective-permute-done.10.rest_1_ = bf16[8,48,128]{2,1,0:T(8,128)(2,1)S(1)} collective-permute-done((bf16[8,48,128]{2,1,0:T(8,128)(2,1)S(1)}, bf16[8,48,128]{2,1,0:T(8,128)(2,1)S(1)}, u32[]{:S(2)}, u32[]{:S(2)}) %collective-permute-start.10) | collective-permute-done | bytes 98336 | tf_op jit(solution)/shard_map/ppermute | solution.py:493
  34.6 0.6 %collective-permute-start.12 = (bf16[8,48,128]{2,1,0:T(8,128)(2,1)S(1)}, bf16[8,48,128]{2,1,0:T(8,128)(2,1)S(1)}, u32[]{:S(2)}, u32[]{:S(2)}) collective-permute-start(bf16[8,48,128]{2,1,0:T(8,128)(2,1)S(1)} %collective-permute-done.10.rest_1_), channel_id=1, source_target_pairs={{0,4},{4,0},{8,12},{12,8},{16,20},{20,16},{24,28},{28,24},{1,5},{5... | collective-permute-start | bytes 294920 | tf_op jit(solution)/shard_map/ppermute | solution.py:493
  35.1 1.0 %shard_map.135.start = f32[640,128]{1,0:T(8,128)S(1)} custom-call(s32[87]{0:T(128)S(1)} %get-tuple-element.32.table, s32[128]{0:T(128)S(1)} %get-tuple-element.23.ahead, bf16[64,128,128]{2,1,0:T(8,128)(2,1)S(1)} %get-tuple-element.24.mats, f32[640,128]{1,0:T(8,128)S(1)} %shard_map.134.start, bf16[8,48,128]{2,1,0:T(8,128)(2,1)S(1)} %collective-permute-done.9.rest_0_, ...), custom_call_target="tpu_custom_call" | custom-call | flops 500000000 | bytes 1500000 | tf_op jit(solution)/shard_map/pallas_call | solution.py:434
  36.1 0.0 collective-permute-done.11.rest_0_
  36.2 3.1 %collective-permute-done.12.rest_1_ = bf16[8,48,128]{2,1,0:T(8,128)(2,1)S(1)} collective-permute-done((bf16[8,48,128]{2,1,0:T(8,128)(2,1)S(1)}, bf16[8,48,128]{2,1,0:T(8,128)(2,1)S(1)}, u32[]{:S(2)}, u32[]{:S(2)}) %collective-permute-start.12) | collective-permute-done | bytes 98336 | tf_op jit(solution)/shard_map/ppermute | solution.py:493
  39.2 0.0 collective-permute-done.13.rest_2_
  39.2 1.1 %shard_map.136 = (f32[640,128]{1,0:T(8,128)S(1)}, f32[16,16,128]{2,1,0:T(8,128)S(1)}) custom-call(s32[87]{0:T(128)S(1)} %get-tuple-element.32.table, s32[128]{0:T(128)S(1)} %get-tuple-element.23.ahead, bf16[64,128,128]{2,1,0:T(8,128)(2,1)S(1)} %get-tuple-element.24.mats, f32[640,128]{1,0:T(8,128)S(1)} %shard_map.135.start, ...), custom_call_target="tpu_custom_call" | custom-call | tf_op jit(solution)/shard_map/pallas_call | solution.py:434
  40.4 2.0 %collective-permute-start.14 = (f16[16,16,128]{2,1,0:T(8,128)(2,1)S(1)}, f16[16,16,128]{2,1,0:T(8,128)(2,1)S(1)}, u32[]{:S(2)}, u32[]{:S(2)}) collective-permute-start(f16[16,16,128]{2,1,0:T(8,128)(2,1)S(1)} %convert_element_type.62), channel_id=1, source_target_pairs={{0,3},{1,0},{2,1},{3,2},{4,7},{5,4},{6,5},{7,6},{8,11},{9,8},{10,9... | collective-permute-start | bytes 196616 | tf_op jit(solution)/shard_map/ppermute | solution.py:552
  42.4 0.7 %shard_map.137 = f32[2,24,1024]{2,1,0:T(8,128)} custom-call(f32[8,48,128]{2,1,0:T(8,128)S(1)} %convert_add_fusion.totals, f32[2,24,1024]{2,1,0:T(8,128)S(1)} %copy-done.2), custom_call_target="tpu_custom_call" | custom-call | tf_op jit(solution)/shard_map/pallas_call | solution.py:434
  43.1 1.0 %collective-permute-done.14 = f16[16,16,128]{2,1,0:T(8,128)(2,1)S(1)} collective-permute-done((f16[16,16,128]{2,1,0:T(8,128)(2,1)S(1)}, f16[16,16,128]{2,1,0:T(8,128)(2,1)S(1)}, u32[]{:S(2)}, u32[]{:S(2)}) %collective-permute-start.14) | collective-permute-done | bytes 65568 | tf_op jit(solution)/shard_map/ppermute | solution.py:552
  44.2 0.8 %shard_map.138 = (f32[2,24,1024]{2,1,0:T(8,128)}, f32[2,24,1024]{2,1,0:T(8,128)}) custom-call(s32[1]{0:T(128)} %bitcast.group, f32[640,128]{1,0:T(8,128)S(1)} %get-tuple-element.37.total, f32[16,16,128]{2,1,0:T(8,128)S(1)} %convert_element_type.63.spill, bf16[2,24,1024]{2,1,0:T(8,128)(2,1)S(1)} %copy-done.1), custom_call_target="tpu_custom_call" | custom-call | tf_op jit(solution)/shard_map/pallas_call | solution.py:434
  (11 shorter events, 0.3 us)
Async XLA Ops:
  0.6 4.9 %copy-start.1 = (bf16[2,24,1024]{2,1,0:T(8,128)(2,1)S(1)}, bf16[2,24,1024]{2,1,0:T(8,128)(2,1)}, u32[]{:S(2)}) copy-start(bf16[2,24,1024]{2,1,0:T(8,128)(2,1)} %flows.5) | copy-start | bytes 294916
  0.6 4.9 %collective-permute-start = (bf16[2,24,1024]{2,1,0:T(8,128)(2,1)}, bf16[2,24,1024]{2,1,0:T(8,128)(2,1)S(1)}, u32[]{:S(2)}, u32[]{:S(2)}) collective-permute-start(bf16[2,24,1024]{2,1,0:T(8,128)(2,1)} %flows.5), channel_id=1, source_target_pairs={{0,1},{1,2},{2,3},{3,0},{4,5},{5,6},{6,7},{7,4},{8,9},{9,10},{10,1... | collective-permute-start | bytes 294920 | tf_op jit(solution)/shard_map/ppermute | solution.py:477
  5.6 12.4 %copy-start = (bf16[64,128,128]{2,1,0:T(8,128)(2,1)S(1)}, bf16[64,128,128]{2,1,0:T(8,128)(2,1)}, u32[]{:S(2)}) copy-start(bf16[64,128,128]{2,1,0:T(8,128)(2,1)} %mats.3) | copy-start | bytes 6291460
  5.6 12.3 %copy-start.3 = (s32[64]{0:T(128)S(1)}, s32[64]{0:T(128)}, u32[]{:S(2)}) copy-start(s32[64]{0:T(128)} %path.3) | copy-start | bytes 772
  5.6 12.3 %copy-start.4 = (s32[64]{0:T(128)S(1)}, s32[64]{0:T(128)}, u32[]{:S(2)}) copy-start(s32[64]{0:T(128)} %link.3) | copy-start | bytes 772
  5.6 12.3 %copy-start.5 = (s32[64]{0:T(128)S(1)}, s32[64]{0:T(128)}, u32[]{:S(2)}) copy-start(s32[64]{0:T(128)} %lag.3) | copy-start | bytes 772
  5.6 12.3 %copy-start.6 = (s32[64]{0:T(128)S(1)}, s32[64]{0:T(128)}, u32[]{:S(2)}) copy-start(s32[64]{0:T(128)} %rest_3_.1) | copy-start | bytes 772
  7.9 4.2 %collective-permute-start.1 = (f16[8,48,128]{2,1,0:T(8,128)(2,1)S(1)}, f16[8,48,128]{2,1,0:T(8,128)(2,1)S(1)}, u32[]{:S(2)}, u32[]{:S(2)}) collective-permute-start(f16[8,48,128]{2,1,0:T(8,128)(2,1)S(1)} %convert_element_type.48), channel_id=1, source_target_pairs={{0,4},{4,0},{8,12},{12,8},{16,20},{20,16},{24,28},{28,24},{1,5},{5... | collective-permute-start | bytes 294920 | tf_op jit(solution)/shard_map/ppermute | solution.py:493
  9.2 5.7 %collective-permute-start.3 = (f16[8,48,128]{2,1,0:T(8,128)(2,1)S(1)}, f16[8,48,128]{2,1,0:T(8,128)(2,1)S(1)}, u32[]{:S(2)}, u32[]{:S(2)}) collective-permute-start(f16[8,48,128]{2,1,0:T(8,128)(2,1)S(1)} %convert_element_type.52), channel_id=1, source_target_pairs={{0,4},{4,0},{8,12},{12,8},{16,20},{20,16},{24,28},{28,24},{1,5},{5... | collective-permute-start | bytes 294920 | tf_op jit(solution)/shard_map/ppermute | solution.py:493
  9.6 6.9 %collective-permute-start.5 = (f16[8,48,128]{2,1,0:T(8,128)(2,1)S(1)}, f16[8,48,128]{2,1,0:T(8,128)(2,1)S(1)}, u32[]{:S(2)}, u32[]{:S(2)}) collective-permute-start(f16[8,48,128]{2,1,0:T(8,128)(2,1)S(1)} %convert_element_type.56), channel_id=1, source_target_pairs={{0,4},{4,0},{8,12},{12,8},{16,20},{20,16},{24,28},{28,24},{1,5},{5... | collective-permute-start | bytes 294920 | tf_op jit(solution)/shard_map/ppermute | solution.py:493
  10.9 9.9 %collective-permute-start.7 = (f16[8,48,128]{2,1,0:T(8,128)(2,1)S(1)}, f16[8,48,128]{2,1,0:T(8,128)(2,1)S(1)}, u32[]{:S(2)}, u32[]{:S(2)}) collective-permute-start(f16[8,48,128]{2,1,0:T(8,128)(2,1)S(1)} %convert_element_type.60), channel_id=1, source_target_pairs={{0,4},{4,0},{8,12},{12,8},{16,20},{20,16},{24,28},{28,24},{1,5},{5... | collective-permute-start | bytes 294920 | tf_op jit(solution)/shard_map/ppermute | solution.py:493
  12.1 11.4 %copy-start.2 = (f32[2,24,1024]{2,1,0:T(8,128)S(1)}, f32[2,24,1024]{2,1,0:T(8,128)}, u32[]{:S(2)}) copy-start(f32[2,24,1024]{2,1,0:T(8,128)} %counts.3) | copy-start | bytes 589828
  12.2 8.6 %collective-permute-start.2 = (f16[8,48,128]{2,1,0:T(8,128)(2,1)S(1)}, f16[8,48,128]{2,1,0:T(8,128)(2,1)S(1)}, u32[]{:S(2)}, u32[]{:S(2)}) collective-permute-start(f16[8,48,128]{2,1,0:T(8,128)(2,1)S(1)} %add_convert_fusion.2), channel_id=1, source_target_pairs={{0,24},{4,28},{8,16},{12,20},{16,8},{20,12},{24,0},{28,4},{1,25},{... | collective-permute-start | bytes 294920 | tf_op jit(solution)/shard_map/ppermute | solution.py:493
  15.0 8.4 %collective-permute-start.4 = (f16[8,48,128]{2,1,0:T(8,128)(2,1)S(1)}, f16[8,48,128]{2,1,0:T(8,128)(2,1)S(1)}, u32[]{:S(2)}, u32[]{:S(2)}) collective-permute-start(f16[8,48,128]{2,1,0:T(8,128)(2,1)S(1)} %add_convert_fusion.1), channel_id=1, source_target_pairs={{0,16},{4,20},{8,24},{12,28},{16,0},{20,4},{24,8},{28,12},{1,17},{... | collective-permute-start | bytes 294920 | tf_op jit(solution)/shard_map/ppermute | solution.py:493
  16.5 6.9 %collective-permute-start.6 = (f16[8,48,128]{2,1,0:T(8,128)(2,1)S(1)}, f16[8,48,128]{2,1,0:T(8,128)(2,1)S(1)}, u32[]{:S(2)}, u32[]{:S(2)}) collective-permute-start(f16[8,48,128]{2,1,0:T(8,128)(2,1)S(1)} %add_convert_fusion), channel_id=1, source_target_pairs={{0,8},{4,12},{8,0},{12,4},{16,24},{20,28},{24,16},{28,20},{1,9},{5... | collective-permute-start | bytes 294920 | tf_op jit(solution)/shard_map/ppermute | solution.py:493
  23.5 3.5 %collective-permute-start.9 = (bf16[8,48,128]{2,1,0:T(8,128)(2,1)S(1)}, bf16[8,48,128]{2,1,0:T(8,128)(2,1)S(1)}, u32[]{:S(2)}, u32[]{:S(2)}) collective-permute-start(bf16[8,48,128]{2,1,0:T(8,128)(2,1)S(1)} %shard_map.133.signal), channel_id=1, source_target_pairs={{0,8},{4,12},{8,0},{12,4},{16,24},{20,28},{24,16},{28,20},{1,9},{5... | collective-permute-start | bytes 294920 | tf_op jit(solution)/shard_map/ppermute | solution.py:493
  23.7 5.9 %collective-permute-start.8 = (bf16[8,48,128]{2,1,0:T(8,128)(2,1)S(1)}, bf16[8,48,128]{2,1,0:T(8,128)(2,1)S(1)}, u32[]{:S(2)}, u32[]{:S(2)}) collective-permute-start(bf16[8,48,128]{2,1,0:T(8,128)(2,1)S(1)} %shard_map.133.signal), channel_id=1, source_target_pairs={{0,24},{4,28},{8,16},{12,20},{16,8},{20,12},{24,0},{28,4},{1,25},{... | collective-permute-start | bytes 294920 | tf_op jit(solution)/shard_map/ppermute | solution.py:493
  26.3 8.3 %collective-permute-start.10 = (bf16[8,48,128]{2,1,0:T(8,128)(2,1)S(1)}, bf16[8,48,128]{2,1,0:T(8,128)(2,1)S(1)}, u32[]{:S(2)}, u32[]{:S(2)}) collective-permute-start(bf16[8,48,128]{2,1,0:T(8,128)(2,1)S(1)} %shard_map.133.signal), channel_id=1, source_target_pairs={{0,16},{4,20},{8,24},{12,28},{16,0},{20,4},{24,8},{28,12},{1,17},{... | collective-permute-start | bytes 294920 | tf_op jit(solution)/shard_map/ppermute | solution.py:493
  27.1 12.1 %collective-permute-start.13 = (bf16[16,48,128]{2,1,0:T(8,128)(2,1)S(1)}, bf16[16,48,128]{2,1,0:T(8,128)(2,1)S(1)}, u32[]{:S(2)}, u32[]{:S(2)}) collective-permute-start(bf16[16,48,128]{2,1,0:T(8,128)(2,1)S(1)} %pad_maximum_fusion), channel_id=1, source_target_pairs={{0,4},{4,0},{8,12},{12,8},{16,20},{20,16},{24,28},{28,24},{1,5},{5... | collective-permute-start | bytes 589832 | tf_op jit(solution)/shard_map/ppermute | solution.py:493
  29.6 6.6 %collective-permute-start.11 = (bf16[8,48,128]{2,1,0:T(8,128)(2,1)S(1)}, bf16[8,48,128]{2,1,0:T(8,128)(2,1)S(1)}, u32[]{:S(2)}, u32[]{:S(2)}) collective-permute-start(bf16[8,48,128]{2,1,0:T(8,128)(2,1)S(1)} %collective-permute-done.8.rest_2_), channel_id=1, source_target_pairs={{0,4},{4,0},{8,12},{12,8},{16,20},{20,16},{24,28},{28,24},{1,5},{5... | collective-permute-start | bytes 294920 | tf_op jit(solution)/shard_map/ppermute | solution.py:493
  34.6 4.7 %collective-permute-start.12 = (bf16[8,48,128]{2,1,0:T(8,128)(2,1)S(1)}, bf16[8,48,128]{2,1,0:T(8,128)(2,1)S(1)}, u32[]{:S(2)}, u32[]{:S(2)}) collective-permute-start(bf16[8,48,128]{2,1,0:T(8,128)(2,1)S(1)} %collective-permute-done.10.rest_1_), channel_id=1, source_target_pairs={{0,4},{4,0},{8,12},{12,8},{16,20},{20,16},{24,28},{28,24},{1,5},{5... | collective-permute-start | bytes 294920 | tf_op jit(solution)/shard_map/ppermute | solution.py:493
  40.4 3.8 %collective-permute-start.14 = (f16[16,16,128]{2,1,0:T(8,128)(2,1)S(1)}, f16[16,16,128]{2,1,0:T(8,128)(2,1)S(1)}, u32[]{:S(2)}, u32[]{:S(2)}) collective-permute-start(f16[16,16,128]{2,1,0:T(8,128)(2,1)S(1)} %convert_element_type.62), channel_id=1, source_target_pairs={{0,3},{1,0},{2,1},{3,2},{4,7},{5,4},{6,5},{7,6},{8,11},{9,8},{10,9... | collective-permute-start | bytes 196616 | tf_op jit(solution)/shard_map/ppermute | solution.py:552

commit v18 on v17

--- a/solution.py
+++ b/solution.py
@@ -531,7 +531,8 @@
         (signal, local_blocks),
         rows,
     )
-    arrived[through[-1]], total = lax.optimization_barrier((arrived[through[-1]], total))
+    middle = through[len(through) // 2]
+    arrived[middle], total = lax.optimization_barrier((arrived[middle], total))
     for s in through[1:]:
         arrived[s ^ 1] = exchanged(arrived[s], 1)
     passed = exchanged(jnp.concatenate([arrived[through[0]], signal], axis=0), 1)

time: 45.3 us -> 45.9 us (1.013)
  starting transfers between devices: 18.8 us -> 20.9 us
  waiting for transfers between devices: 12.6 us -> 11.3 us
    ppermute x13, waiting for transfers between devices: 11.6 us -> 8.62 us  [exchanged(): return lax.ppermute(part, 'corr', [(i, i ^ s) for i in range(corridors)])]
    ppermute x1, starting transfers between devices: 2.03 us -> 3.87 us  [per_device_dense(): spill = lax.ppermute(early[0].astype(WIRE), 'tm', route).astype(f32)]
    ppermute x1, waiting for transfers between devices: 1.04 us -> 2.67 us  [per_device_dense(): spill = lax.ppermute(early[0].astype(WIRE), 'tm', route).astype(f32)]
  transfers between devices with their start and end apart: 15 -> 15, of which waited for: 6 -> 5; matrix products, arithmetic and copies ran while one was open for 0% -> 0% of each run, Pallas kernels for 18% -> 18%
where the time goes in v18:
time: 45.9 us; the launch traced here: 45.8 us
  starting transfers between devices  20.9 us (46%)
  Pallas kernels  12.4 us (27%)
  waiting for transfers between devices  11.3 us (25%)
  between operations  0.85 us (2%)
    ppermute x13, starting transfers between devices, exchanged(): return lax.ppermute(part, 'corr', [(i, i ^ s) for i in range(corridors)])  14.4 us
    pallas_call x8, Pallas kernels, kernel_call(): pl.pallas_call(body, out_shape=out_shape, in_specs=[SMEM] * len(scalars)...  10.2 us
    ppermute x13, waiting for transfers between devices, exchanged(): return lax.ppermute(part, 'corr', [(i, i ^ s) for i in range(corridors)])  8.62 us
    ppermute x1, starting transfers between devices, per_device_dense(): spill = lax.ppermute(early[0].astype(WIRE), 'tm', route).astype(f32)  3.87 us
    ppermute x1, starting transfers between devices, per_device_dense(): lax.ppermute(flows, 'tm', [(i, (i + 1) % groups) for i in range(groups)])  2.68 us
    ppermute x1, waiting for transfers between devices, per_device_dense(): spill = lax.ppermute(early[0].astype(WIRE), 'tm', route).astype(f32)  2.67 us
    pallas_call x1, Pallas kernels, per_device_dense(): pl.pallas_call(functools.partial(prepare_kernel, cap, order, links, CHUNK...  2.2 us
  transfers between devices with their start and end apart: 15, of which 5 were waited for; matrix products, arithmetic and copies ran while one was open for 0% of the time, Pallas kernels for 18%

profile of v18, /device:TPU:1, one launch (start us, length us, event | category | flops | bytes accessed | tf_op | source)
XLA Modules:
  0.0 45.8 jit_solution(10963301854087664814)
XLA Ops:
  0.6 0.0 copy-start.1
  0.6 2.7 %collective-permute-start = (bf16[2,24,1024]{2,1,0:T(8,128)(2,1)}, bf16[2,24,1024]{2,1,0:T(8,128)(2,1)S(1)}, u32[]{:S(2)}, u32[]{:S(2)}) collective-permute-start(bf16[2,24,1024]{2,1,0:T(8,128)(2,1)} %flows.5), channel_id=1, source_target_pairs={{0,1},{1,2},{2,3},{3,0},{4,5},{5,6},{6,7},{7,4},{8,9},{9,10},{10,1... | collective-permute-start | bytes 294920 | tf_op jit(solution)/shard_map/ppermute | solution.py:477
  3.3 2.2 %shard_map.131 = (s32[128]{0:T(128)S(1)}, bf16[64,128,128]{2,1,0:T(8,128)(2,1)S(1)}) custom-call(s32[1]{0:T(128)} %bitcast.1.me, s32[64]{0:T(128)} %rest_0_.1, s32[64]{0:T(128)} %rest_1_.1, s32[64]{0:T(128)} %rest_2_.1, s32[64]{0:T(128)} %rest_3_.1, bf16[64,128,128]{2,1,0:T(8,128)(2,1)} %rest_4_.1), custom_call_target="tpu_custom_call" | custom-call | tf_op jit(solution)/shard_map/pallas_call | solution.py:479
  5.5 0.0 collective-permute-done.before
  5.5 0.0 copy-done.1
  5.6 0.0 copy-start
  5.6 0.0 copy-start.3
  5.6 0.0 copy-start.4
  5.6 0.0 copy-start.5
  5.6 0.0 copy-start.6
  5.6 2.3 %shard_map.132 = (f32[8,48,128]{2,1,0:T(8,128)S(1)}, f32[8,48,128]{2,1,0:T(8,128)S(1)}, f32[8,48,128]{2,1,0:T(8,128)S(1)}, f32[8,48,128]{2,1,0:T(8,128)S(1)}, f3...) custom-call(s32[1]{0:T(128)} %bitcast.group, s32[128]{0:T(128)S(1)} %get-tuple-element.23.ahead, ...), custom_call_target="tpu_custom_call" | custom-call | tf_op jit(solution)/shard_map/pallas_call | solution.py:434
  7.9 1.3 %collective-permute-start.1 = (f16[8,48,128]{2,1,0:T(8,128)(2,1)S(1)}, f16[8,48,128]{2,1,0:T(8,128)(2,1)S(1)}, u32[]{:S(2)}, u32[]{:S(2)}) collective-permute-start(f16[8,48,128]{2,1,0:T(8,128)(2,1)S(1)} %convert_element_type.48), channel_id=1, source_target_pairs={{0,4},{4,0},{8,12},{12,8},{16,20},{20,16},{24,28},{28,24},{1,5},{5... | collective-permute-start | bytes 294920 | tf_op jit(solution)/shard_map/ppermute | solution.py:493
  9.2 0.3 collective-permute-start.3
  9.6 1.2 %collective-permute-start.5 = (f16[8,48,128]{2,1,0:T(8,128)(2,1)S(1)}, f16[8,48,128]{2,1,0:T(8,128)(2,1)S(1)}, u32[]{:S(2)}, u32[]{:S(2)}) collective-permute-start(f16[8,48,128]{2,1,0:T(8,128)(2,1)S(1)} %convert_element_type.56), channel_id=1, source_target_pairs={{0,4},{4,0},{8,12},{12,8},{16,20},{20,16},{24,28},{28,24},{1,5},{5... | collective-permute-start | bytes 294920 | tf_op jit(solution)/shard_map/ppermute | solution.py:493
  10.9 0.3 collective-permute-start.7
  11.2 0.9 %collective-permute-done.1 = f16[8,48,128]{2,1,0:T(8,128)(2,1)S(1)} collective-permute-done((f16[8,48,128]{2,1,0:T(8,128)(2,1)S(1)}, f16[8,48,128]{2,1,0:T(8,128)(2,1)S(1)}, u32[]{:S(2)}, u32[]{:S(2)}) %collective-permute-start.1) | collective-permute-done | bytes 98336 | tf_op jit(solution)/shard_map/ppermute | solution.py:493
  12.1 0.0 copy-start.2
  12.1 2.8 %collective-permute-start.2 = (f16[8,48,128]{2,1,0:T(8,128)(2,1)S(1)}, f16[8,48,128]{2,1,0:T(8,128)(2,1)S(1)}, u32[]{:S(2)}, u32[]{:S(2)}) collective-permute-start(f16[8,48,128]{2,1,0:T(8,128)(2,1)S(1)} %add_convert_fusion.2), channel_id=1, source_target_pairs={{0,24},{4,28},{8,16},{12,20},{16,8},{20,12},{24,0},{28,4},{1,25},{... | collective-permute-start | bytes 294920 | tf_op jit(solution)/shard_map/ppermute | solution.py:493
  14.9 0.0 collective-permute-done.3
  15.0 1.5 %collective-permute-start.4 = (f16[8,48,128]{2,1,0:T(8,128)(2,1)S(1)}, f16[8,48,128]{2,1,0:T(8,128)(2,1)S(1)}, u32[]{:S(2)}, u32[]{:S(2)}) collective-permute-start(f16[8,48,128]{2,1,0:T(8,128)(2,1)S(1)} %add_convert_fusion.1), channel_id=1, source_target_pairs={{0,16},{4,20},{8,24},{12,28},{16,0},{20,4},{24,8},{28,12},{1,17},{... | collective-permute-start | bytes 294920 | tf_op jit(solution)/shard_map/ppermute | solution.py:493
  16.5 0.0 collective-permute-done.5
  16.5 1.4 %collective-permute-start.6 = (f16[8,48,128]{2,1,0:T(8,128)(2,1)S(1)}, f16[8,48,128]{2,1,0:T(8,128)(2,1)S(1)}, u32[]{:S(2)}, u32[]{:S(2)}) collective-permute-start(f16[8,48,128]{2,1,0:T(8,128)(2,1)S(1)} %add_convert_fusion), channel_id=1, source_target_pairs={{0,8},{4,12},{8,0},{12,4},{16,24},{20,28},{24,16},{28,20},{1,9},{5... | collective-permute-start | bytes 294920 | tf_op jit(solution)/shard_map/ppermute | solution.py:493
  17.9 0.0 copy-done
  17.9 0.0 copy-done.3
  17.9 0.0 copy-done.4
  17.9 0.0 copy-done.5
  17.9 0.0 copy-done.6
  17.9 2.9 %shard_map.130 = (f32[8,48,128]{2,1,0:T(8,128)S(1)}, s32[87]{0:T(128)S(1)}) custom-call(s32[1]{0:T(128)} %bitcast.group, s32[1]{0:T(128)} %bitcast.1.me, s32[64]{0:T(128)S(1)} %copy-done.6, s32[64]{0:T(128)S(1)} %copy-done.3, s32[64]{0:T(128)S(1)} %copy-done.4, s32[64]{0:T(128)S(1)} %copy-done.5, bf16[2,24,1024]{2,1,0:T(8,128)(2,1)S(1)} %copy-done.1, ...), custom_call_target="tpu_custom_call" | custom-call | tf_op jit(solution)/shard_map/pallas_call | solution.py:434
  20.8 0.0 collective-permute-done.7
  20.8 0.0 collective-permute-done.2
  20.8 2.6 %collective-permute-done.4 = f16[8,48,128]{2,1,0:T(8,128)(2,1)S(1)} collective-permute-done((f16[8,48,128]{2,1,0:T(8,128)(2,1)S(1)}, f16[8,48,128]{2,1,0:T(8,128)(2,1)S(1)}, u32[]{:S(2)}, u32[]{:S(2)}) %collective-permute-start.4) | collective-permute-done | bytes 98336 | tf_op jit(solution)/shard_map/ppermute | solution.py:493
  23.4 0.0 collective-permute-done.6
  23.4 0.1 convert_add_fusion.totals
  23.5 0.0 copy-done.2
  23.5 0.1 collective-permute-start.9
  23.7 2.8 %collective-permute-start.8 = (bf16[8,48,128]{2,1,0:T(8,128)(2,1)S(1)}, bf16[8,48,128]{2,1,0:T(8,128)(2,1)S(1)}, u32[]{:S(2)}, u32[]{:S(2)}) collective-permute-start(bf16[8,48,128]{2,1,0:T(8,128)(2,1)S(1)} %shard_map.133.signal), channel_id=1, source_target_pairs={{0,16},{4,20},{8,24},{12,28},{16,0},{20,4},{24,8},{28,12},{1,17},{... | collective-permute-start | bytes 294920 | tf_op jit(solution)/shard_map/ppermute | solution.py:493
  26.5 0.7 %collective-permute-start.10 = (bf16[8,48,128]{2,1,0:T(8,128)(2,1)S(1)}, bf16[8,48,128]{2,1,0:T(8,128)(2,1)S(1)}, u32[]{:S(2)}, u32[]{:S(2)}) collective-permute-start(bf16[8,48,128]{2,1,0:T(8,128)(2,1)S(1)} %shard_map.133.signal), channel_id=1, source_target_pairs={{0,24},{4,28},{8,16},{12,20},{16,8},{20,12},{24,0},{28,4},{1,25},{... | collective-permute-start | bytes 294920 | tf_op jit(solution)/shard_map/ppermute | solution.py:493
  27.2 0.0 collective-permute-done.9.rest_0_
  27.2 1.1 %collective-permute-start.13 = (bf16[16,48,128]{2,1,0:T(8,128)(2,1)S(1)}, bf16[16,48,128]{2,1,0:T(8,128)(2,1)S(1)}, u32[]{:S(2)}, u32[]{:S(2)}) collective-permute-start(bf16[16,48,128]{2,1,0:T(8,128)(2,1)S(1)} %pad_maximum_fusion), channel_id=1, source_target_pairs={{0,4},{4,0},{8,12},{12,8},{16,20},{20,16},{24,28},{28,24},{1,5},{5... | collective-permute-start | bytes 589832 | tf_op jit(solution)/shard_map/ppermute | solution.py:493
  28.3 1.3 %shard_map.134.start = f32[640,128]{1,0:T(8,128)S(1)} custom-call(s32[64]{0:T(128)S(1)} %copy-done.3, s32[64]{0:T(128)S(1)} %copy-done.4, s32[64]{0:T(128)S(1)} %copy-done.5, bf16[8,48,128]{2,1,0:T(8,128)(2,1)S(1)} %shard_map.133.signal, bf16[64,128,128]{2,1,0:T(8,128)(2,1)S(1)} %copy-done), custom_call_target="tpu_custom_call" | custom-call | tf_op jit(solution)/shard_map/pallas_call | solution.py:434
  29.6 0.0 collective-permute-done.8.rest_1_
  29.6 0.5 %collective-permute-start.12 = (bf16[8,48,128]{2,1,0:T(8,128)(2,1)S(1)}, bf16[8,48,128]{2,1,0:T(8,128)(2,1)S(1)}, u32[]{:S(2)}, u32[]{:S(2)}) collective-permute-start(bf16[8,48,128]{2,1,0:T(8,128)(2,1)S(1)} %collective-permute-done.8.rest_1_), channel_id=1, source_target_pairs={{0,4},{4,0},{8,12},{12,8},{16,20},{20,16},{24,28},{28,24},{1,5},{5... | collective-permute-start | bytes 294920 | tf_op jit(solution)/shard_map/ppermute | solution.py:493
  30.1 2.6 %collective-permute-done.10.rest_2_ = bf16[8,48,128]{2,1,0:T(8,128)(2,1)S(1)} collective-permute-done((bf16[8,48,128]{2,1,0:T(8,128)(2,1)S(1)}, bf16[8,48,128]{2,1,0:T(8,128)(2,1)S(1)}, u32[]{:S(2)}, u32[]{:S(2)}) %collective-permute-start.10) | collective-permute-done | bytes 98336 | tf_op jit(solution)/shard_map/ppermute | solution.py:493
  32.7 0.3 collective-permute-start.11
  32.9 1.0 %shard_map.135.start = f32[640,128]{1,0:T(8,128)S(1)} custom-call(s32[87]{0:T(128)S(1)} %get-tuple-element.32.table, s32[128]{0:T(128)S(1)} %get-tuple-element.23.ahead, bf16[64,128,128]{2,1,0:T(8,128)(2,1)S(1)} %get-tuple-element.24.mats, f32[640,128]{1,0:T(8,128)S(1)} %shard_map.134.start, bf16[8,48,128]{2,1,0:T(8,128)(2,1)S(1)} %collective-permute-done.9.rest_0_, ...), custom_call_target="tpu_custom_call" | custom-call | flops 500000000 | bytes 1500000 | tf_op jit(solution)/shard_map/pallas_call | solution.py:434
  34.0 0.0 collective-permute-done.12.rest_1_
  34.0 2.6 %collective-permute-done.11.rest_0_ = bf16[8,48,128]{2,1,0:T(8,128)(2,1)S(1)} collective-permute-done((bf16[8,48,128]{2,1,0:T(8,128)(2,1)S(1)}, bf16[8,48,128]{2,1,0:T(8,128)(2,1)S(1)}, u32[]{:S(2)}, u32[]{:S(2)}) %collective-permute-start.11) | collective-permute-done | bytes 98336 | tf_op jit(solution)/shard_map/ppermute | solution.py:493
  36.5 0.0 collective-permute-done.13.rest_2_
  36.5 1.1 %shard_map.136 = (f32[640,128]{1,0:T(8,128)S(1)}, f32[16,16,128]{2,1,0:T(8,128)S(1)}) custom-call(s32[87]{0:T(128)S(1)} %get-tuple-element.32.table, s32[128]{0:T(128)S(1)} %get-tuple-element.23.ahead, bf16[64,128,128]{2,1,0:T(8,128)(2,1)S(1)} %get-tuple-element.24.mats, f32[640,128]{1,0:T(8,128)S(1)} %shard_map.135.start, ...), custom_call_target="tpu_custom_call" | custom-call | tf_op jit(solution)/shard_map/pallas_call | solution.py:434
  37.7 3.9 %collective-permute-start.14 = (f16[16,16,128]{2,1,0:T(8,128)(2,1)S(1)}, f16[16,16,128]{2,1,0:T(8,128)(2,1)S(1)}, u32[]{:S(2)}, u32[]{:S(2)}) collective-permute-start(f16[16,16,128]{2,1,0:T(8,128)(2,1)S(1)} %convert_element_type.62), channel_id=1, source_target_pairs={{0,3},{1,0},{2,1},{3,2},{4,7},{5,4},{6,5},{7,6},{8,11},{9,8},{10,9... | collective-permute-start | bytes 196616 | tf_op jit(solution)/shard_map/ppermute | solution.py:553
  41.6 0.7 %shard_map.137 = f32[2,24,1024]{2,1,0:T(8,128)} custom-call(f32[8,48,128]{2,1,0:T(8,128)S(1)} %convert_add_fusion.totals, f32[2,24,1024]{2,1,0:T(8,128)S(1)} %copy-done.2), custom_call_target="tpu_custom_call" | custom-call | tf_op jit(solution)/shard_map/pallas_call | solution.py:434
  42.3 2.7 %collective-permute-done.14 = f16[16,16,128]{2,1,0:T(8,128)(2,1)S(1)} collective-permute-done((f16[16,16,128]{2,1,0:T(8,128)(2,1)S(1)}, f16[16,16,128]{2,1,0:T(8,128)(2,1)S(1)}, u32[]{:S(2)}, u32[]{:S(2)}) %collective-permute-start.14) | collective-permute-done | bytes 65568 | tf_op jit(solution)/shard_map/ppermute | solution.py:553
  45.0 0.8 %shard_map.138 = (f32[2,24,1024]{2,1,0:T(8,128)}, f32[2,24,1024]{2,1,0:T(8,128)}) custom-call(s32[1]{0:T(128)} %bitcast.group, f32[640,128]{1,0:T(8,128)S(1)} %get-tuple-element.37.total, f32[16,16,128]{2,1,0:T(8,128)S(1)} %convert_element_type.63.spill, bf16[2,24,1024]{2,1,0:T(8,128)(2,1)S(1)} %copy-done.1), custom_call_target="tpu_custom_call" | custom-call | tf_op jit(solution)/shard_map/pallas_call | solution.py:434
  (11 shorter events, 0.3 us)
Async XLA Ops:
  0.6 4.9 %copy-start.1 = (bf16[2,24,1024]{2,1,0:T(8,128)(2,1)S(1)}, bf16[2,24,1024]{2,1,0:T(8,128)(2,1)}, u32[]{:S(2)}) copy-start(bf16[2,24,1024]{2,1,0:T(8,128)(2,1)} %flows.5) | copy-start | bytes 294916
  0.6 4.9 %collective-permute-start = (bf16[2,24,1024]{2,1,0:T(8,128)(2,1)}, bf16[2,24,1024]{2,1,0:T(8,128)(2,1)S(1)}, u32[]{:S(2)}, u32[]{:S(2)}) collective-permute-start(bf16[2,24,1024]{2,1,0:T(8,128)(2,1)} %flows.5), channel_id=1, source_target_pairs={{0,1},{1,2},{2,3},{3,0},{4,5},{5,6},{6,7},{7,4},{8,9},{9,10},{10,1... | collective-permute-start | bytes 294920 | tf_op jit(solution)/shard_map/ppermute | solution.py:477
  5.6 12.4 %copy-start = (bf16[64,128,128]{2,1,0:T(8,128)(2,1)S(1)}, bf16[64,128,128]{2,1,0:T(8,128)(2,1)}, u32[]{:S(2)}) copy-start(bf16[64,128,128]{2,1,0:T(8,128)(2,1)} %mats.3) | copy-start | bytes 6291460
  5.6 12.3 %copy-start.3 = (s32[64]{0:T(128)S(1)}, s32[64]{0:T(128)}, u32[]{:S(2)}) copy-start(s32[64]{0:T(128)} %path.3) | copy-start | bytes 772
  5.6 12.3 %copy-start.4 = (s32[64]{0:T(128)S(1)}, s32[64]{0:T(128)}, u32[]{:S(2)}) copy-start(s32[64]{0:T(128)} %link.3) | copy-start | bytes 772
  5.6 12.3 %copy-start.5 = (s32[64]{0:T(128)S(1)}, s32[64]{0:T(128)}, u32[]{:S(2)}) copy-start(s32[64]{0:T(128)} %lag.3) | copy-start | bytes 772
  5.6 12.3 %copy-start.6 = (s32[64]{0:T(128)S(1)}, s32[64]{0:T(128)}, u32[]{:S(2)}) copy-start(s32[64]{0:T(128)} %rest_3_.1) | copy-start | bytes 772
  7.9 4.2 %collective-permute-start.1 = (f16[8,48,128]{2,1,0:T(8,128)(2,1)S(1)}, f16[8,48,128]{2,1,0:T(8,128)(2,1)S(1)}, u32[]{:S(2)}, u32[]{:S(2)}) collective-permute-start(f16[8,48,128]{2,1,0:T(8,128)(2,1)S(1)} %convert_element_type.48), channel_id=1, source_target_pairs={{0,4},{4,0},{8,12},{12,8},{16,20},{20,16},{24,28},{28,24},{1,5},{5... | collective-permute-start | bytes 294920 | tf_op jit(solution)/shard_map/ppermute | solution.py:493
  9.2 5.7 %collective-permute-start.3 = (f16[8,48,128]{2,1,0:T(8,128)(2,1)S(1)}, f16[8,48,128]{2,1,0:T(8,128)(2,1)S(1)}, u32[]{:S(2)}, u32[]{:S(2)}) collective-permute-start(f16[8,48,128]{2,1,0:T(8,128)(2,1)S(1)} %convert_element_type.52), channel_id=1, source_target_pairs={{0,4},{4,0},{8,12},{12,8},{16,20},{20,16},{24,28},{28,24},{1,5},{5... | collective-permute-start | bytes 294920 | tf_op jit(solution)/shard_map/ppermute | solution.py:493
  9.6 6.9 %collective-permute-start.5 = (f16[8,48,128]{2,1,0:T(8,128)(2,1)S(1)}, f16[8,48,128]{2,1,0:T(8,128)(2,1)S(1)}, u32[]{:S(2)}, u32[]{:S(2)}) collective-permute-start(f16[8,48,128]{2,1,0:T(8,128)(2,1)S(1)} %convert_element_type.56), channel_id=1, source_target_pairs={{0,4},{4,0},{8,12},{12,8},{16,20},{20,16},{24,28},{28,24},{1,5},{5... | collective-permute-start | bytes 294920 | tf_op jit(solution)/shard_map/ppermute | solution.py:493
  10.9 9.9 %collective-permute-start.7 = (f16[8,48,128]{2,1,0:T(8,128)(2,1)S(1)}, f16[8,48,128]{2,1,0:T(8,128)(2,1)S(1)}, u32[]{:S(2)}, u32[]{:S(2)}) collective-permute-start(f16[8,48,128]{2,1,0:T(8,128)(2,1)S(1)} %convert_element_type.60), channel_id=1, source_target_pairs={{0,4},{4,0},{8,12},{12,8},{16,20},{20,16},{24,28},{28,24},{1,5},{5... | collective-permute-start | bytes 294920 | tf_op jit(solution)/shard_map/ppermute | solution.py:493
  12.1 11.4 %copy-start.2 = (f32[2,24,1024]{2,1,0:T(8,128)S(1)}, f32[2,24,1024]{2,1,0:T(8,128)}, u32[]{:S(2)}) copy-start(f32[2,24,1024]{2,1,0:T(8,128)} %counts.3) | copy-start | bytes 589828
  12.1 8.7 %collective-permute-start.2 = (f16[8,48,128]{2,1,0:T(8,128)(2,1)S(1)}, f16[8,48,128]{2,1,0:T(8,128)(2,1)S(1)}, u32[]{:S(2)}, u32[]{:S(2)}) collective-permute-start(f16[8,48,128]{2,1,0:T(8,128)(2,1)S(1)} %add_convert_fusion.2), channel_id=1, source_target_pairs={{0,24},{4,28},{8,16},{12,20},{16,8},{20,12},{24,0},{28,4},{1,25},{... | collective-permute-start | bytes 294920 | tf_op jit(solution)/shard_map/ppermute | solution.py:493
  15.0 8.4 %collective-permute-start.4 = (f16[8,48,128]{2,1,0:T(8,128)(2,1)S(1)}, f16[8,48,128]{2,1,0:T(8,128)(2,1)S(1)}, u32[]{:S(2)}, u32[]{:S(2)}) collective-permute-start(f16[8,48,128]{2,1,0:T(8,128)(2,1)S(1)} %add_convert_fusion.1), channel_id=1, source_target_pairs={{0,16},{4,20},{8,24},{12,28},{16,0},{20,4},{24,8},{28,12},{1,17},{... | collective-permute-start | bytes 294920 | tf_op jit(solution)/shard_map/ppermute | solution.py:493
  16.5 6.9 %collective-permute-start.6 = (f16[8,48,128]{2,1,0:T(8,128)(2,1)S(1)}, f16[8,48,128]{2,1,0:T(8,128)(2,1)S(1)}, u32[]{:S(2)}, u32[]{:S(2)}) collective-permute-start(f16[8,48,128]{2,1,0:T(8,128)(2,1)S(1)} %add_convert_fusion), channel_id=1, source_target_pairs={{0,8},{4,12},{8,0},{12,4},{16,24},{20,28},{24,16},{28,20},{1,9},{5... | collective-permute-start | bytes 294920 | tf_op jit(solution)/shard_map/ppermute | solution.py:493
  23.5 3.6 %collective-permute-start.9 = (bf16[8,48,128]{2,1,0:T(8,128)(2,1)S(1)}, bf16[8,48,128]{2,1,0:T(8,128)(2,1)S(1)}, u32[]{:S(2)}, u32[]{:S(2)}) collective-permute-start(bf16[8,48,128]{2,1,0:T(8,128)(2,1)S(1)} %shard_map.133.signal), channel_id=1, source_target_pairs={{0,8},{4,12},{8,0},{12,4},{16,24},{20,28},{24,16},{28,20},{1,9},{5... | collective-permute-start | bytes 294920 | tf_op jit(solution)/shard_map/ppermute | solution.py:493
  23.7 6.0 %collective-permute-start.8 = (bf16[8,48,128]{2,1,0:T(8,128)(2,1)S(1)}, bf16[8,48,128]{2,1,0:T(8,128)(2,1)S(1)}, u32[]{:S(2)}, u32[]{:S(2)}) collective-permute-start(bf16[8,48,128]{2,1,0:T(8,128)(2,1)S(1)} %shard_map.133.signal), channel_id=1, source_target_pairs={{0,16},{4,20},{8,24},{12,28},{16,0},{20,4},{24,8},{28,12},{1,17},{... | collective-permute-start | bytes 294920 | tf_op jit(solution)/shard_map/ppermute | solution.py:493
  26.5 6.2 %collective-permute-start.10 = (bf16[8,48,128]{2,1,0:T(8,128)(2,1)S(1)}, bf16[8,48,128]{2,1,0:T(8,128)(2,1)S(1)}, u32[]{:S(2)}, u32[]{:S(2)}) collective-permute-start(bf16[8,48,128]{2,1,0:T(8,128)(2,1)S(1)} %shard_map.133.signal), channel_id=1, source_target_pairs={{0,24},{4,28},{8,16},{12,20},{16,8},{20,12},{24,0},{28,4},{1,25},{... | collective-permute-start | bytes 294920 | tf_op jit(solution)/shard_map/ppermute | solution.py:493
  27.2 9.4 %collective-permute-start.13 = (bf16[16,48,128]{2,1,0:T(8,128)(2,1)S(1)}, bf16[16,48,128]{2,1,0:T(8,128)(2,1)S(1)}, u32[]{:S(2)}, u32[]{:S(2)}) collective-permute-start(bf16[16,48,128]{2,1,0:T(8,128)(2,1)S(1)} %pad_maximum_fusion), channel_id=1, source_target_pairs={{0,4},{4,0},{8,12},{12,8},{16,20},{20,16},{24,28},{28,24},{1,5},{5... | collective-permute-start | bytes 589832 | tf_op jit(solution)/shard_map/ppermute | solution.py:493
  29.6 4.3 %collective-permute-start.12 = (bf16[8,48,128]{2,1,0:T(8,128)(2,1)S(1)}, bf16[8,48,128]{2,1,0:T(8,128)(2,1)S(1)}, u32[]{:S(2)}, u32[]{:S(2)}) collective-permute-start(bf16[8,48,128]{2,1,0:T(8,128)(2,1)S(1)} %collective-permute-done.8.rest_1_), channel_id=1, source_target_pairs={{0,4},{4,0},{8,12},{12,8},{16,20},{20,16},{24,28},{28,24},{1,5},{5... | collective-permute-start | bytes 294920 | tf_op jit(solution)/shard_map/ppermute | solution.py:493
  32.7 3.9 %collective-permute-start.11 = (bf16[8,48,128]{2,1,0:T(8,128)(2,1)S(1)}, bf16[8,48,128]{2,1,0:T(8,128)(2,1)S(1)}, u32[]{:S(2)}, u32[]{:S(2)}) collective-permute-start(bf16[8,48,128]{2,1,0:T(8,128)(2,1)S(1)} %collective-permute-done.10.rest_2_), channel_id=1, source_target_pairs={{0,4},{4,0},{8,12},{12,8},{16,20},{20,16},{24,28},{28,24},{1,5},{5... | collective-permute-start | bytes 294920 | tf_op jit(solution)/shard_map/ppermute | solution.py:493
  37.7 7.2 %collective-permute-start.14 = (f16[16,16,128]{2,1,0:T(8,128)(2,1)S(1)}, f16[16,16,128]{2,1,0:T(8,128)(2,1)S(1)}, u32[]{:S(2)}, u32[]{:S(2)}) collective-permute-start(f16[16,16,128]{2,1,0:T(8,128)(2,1)S(1)} %convert_element_type.62), channel_id=1, source_target_pairs={{0,3},{1,0},{2,1},{3,2},{4,7},{5,4},{6,5},{7,6},{8,11},{9,8},{10,9... | collective-permute-start | bytes 196616 | tf_op jit(solution)/shard_map/ppermute | solution.py:553

commit v19 on v17

--- a/solution.py
+++ b/solution.py
@@ -502,7 +502,8 @@
     )
     count = len(through)
     crossed = [exchanged(part.astype(WIRE), 1) for part in outgoing[:count]]
-    near = exchanged(outgoing[count].astype(WIRE), 1)
+    crossed[0], near = lax.optimization_barrier((crossed[0], outgoing[count].astype(WIRE)))
+    near = exchanged(near, 1)
     received = []
     for s, kept in reversed(list(zip(through, outgoing[count + 1 :]))):
         met = crossed[order.index(s ^ 1)].astype(f32)

time: 45.3 us -> 45.7 us (level)
  starting transfers between devices: 18.8 us -> 19.4 us
where the time goes in v19:
time: 45.7 us; the launch traced here: 45.4 us
  starting transfers between devices  19.4 us (42%)
  Pallas kernels  12.4 us (27%)
  waiting for transfers between devices  12.4 us (27%)
  between operations  0.85 us (2%)
    ppermute x13, starting transfers between devices, exchanged(): return lax.ppermute(part, 'corr', [(i, i ^ s) for i in range(corridors)])  14.3 us
    ppermute x13, waiting for transfers between devices, exchanged(): return lax.ppermute(part, 'corr', [(i, i ^ s) for i in range(corridors)])  11.4 us
    pallas_call x8, Pallas kernels, kernel_call(): pl.pallas_call(body, out_shape=out_shape, in_specs=[SMEM] * len(scalars)...  10.2 us
    ppermute x1, starting transfers between devices, per_device_dense(): lax.ppermute(flows, 'tm', [(i, (i + 1) % groups) for i in range(groups)])  2.68 us
    ppermute x1, starting transfers between devices, per_device_dense(): spill = lax.ppermute(early[0].astype(WIRE), 'tm', route).astype(f32)  2.45 us
    pallas_call x1, Pallas kernels, per_device_dense(): pl.pallas_call(functools.partial(prepare_kernel, cap, order, links, CHUNK...  2.2 us
    ppermute x1, waiting for transfers between devices, per_device_dense(): spill = lax.ppermute(early[0].astype(WIRE), 'tm', route).astype(f32)  1.03 us
  transfers between devices with their start and end apart: 15, of which 6 were waited for; matrix products, arithmetic and copies ran while one was open for 0% of the time, Pallas kernels for 18%

profile of v19, /device:TPU:1, one launch (start us, length us, event | category | flops | bytes accessed | tf_op | source)
XLA Modules:
  0.0 45.4 jit_solution(8127295009555592499)
XLA Ops:
  0.6 0.0 copy-start.1
  0.6 2.7 %collective-permute-start = (bf16[2,24,1024]{2,1,0:T(8,128)(2,1)}, bf16[2,24,1024]{2,1,0:T(8,128)(2,1)S(1)}, u32[]{:S(2)}, u32[]{:S(2)}) collective-permute-start(bf16[2,24,1024]{2,1,0:T(8,128)(2,1)} %flows.5), channel_id=1, source_target_pairs={{0,1},{1,2},{2,3},{3,0},{4,5},{5,6},{6,7},{7,4},{8,9},{9,10},{10,1... | collective-permute-start | bytes 294920 | tf_op jit(solution)/shard_map/ppermute | solution.py:477
  3.3 2.2 %shard_map.131 = (s32[128]{0:T(128)S(1)}, bf16[64,128,128]{2,1,0:T(8,128)(2,1)S(1)}) custom-call(s32[1]{0:T(128)} %bitcast.1.me, s32[64]{0:T(128)} %rest_0_.1, s32[64]{0:T(128)} %rest_1_.1, s32[64]{0:T(128)} %rest_2_.1, s32[64]{0:T(128)} %rest_3_.1, bf16[64,128,128]{2,1,0:T(8,128)(2,1)} %rest_4_.1), custom_call_target="tpu_custom_call" | custom-call | tf_op jit(solution)/shard_map/pallas_call | solution.py:479
  5.5 0.0 collective-permute-done.before
  5.5 0.0 copy-done.1
  5.6 0.0 copy-start
  5.6 0.0 copy-start.3
  5.6 0.0 copy-start.4
  5.6 0.0 copy-start.5
  5.6 0.0 copy-start.6
  5.6 2.3 %shard_map.132 = (f32[8,48,128]{2,1,0:T(8,128)S(1)}, f32[8,48,128]{2,1,0:T(8,128)S(1)}, f32[8,48,128]{2,1,0:T(8,128)S(1)}, f32[8,48,128]{2,1,0:T(8,128)S(1)}, f3...) custom-call(s32[1]{0:T(128)} %bitcast.group, s32[128]{0:T(128)S(1)} %get-tuple-element.25.ahead, ...), custom_call_target="tpu_custom_call" | custom-call | tf_op jit(solution)/shard_map/pallas_call | solution.py:434
  7.9 1.3 %collective-permute-start.1 = (f16[8,48,128]{2,1,0:T(8,128)(2,1)S(1)}, f16[8,48,128]{2,1,0:T(8,128)(2,1)S(1)}, u32[]{:S(2)}, u32[]{:S(2)}) collective-permute-start(f16[8,48,128]{2,1,0:T(8,128)(2,1)S(1)} %convert_element_type.48), channel_id=1, source_target_pairs={{0,4},{4,0},{8,12},{12,8},{16,20},{20,16},{24,28},{28,24},{1,5},{5... | collective-permute-start | bytes 294920 | tf_op jit(solution)/shard_map/ppermute | solution.py:493
  9.3 0.3 collective-permute-start.3
  9.6 1.3 %collective-permute-start.5 = (f16[8,48,128]{2,1,0:T(8,128)(2,1)S(1)}, f16[8,48,128]{2,1,0:T(8,128)(2,1)S(1)}, u32[]{:S(2)}, u32[]{:S(2)}) collective-permute-start(f16[8,48,128]{2,1,0:T(8,128)(2,1)S(1)} %convert_element_type.57), channel_id=1, source_target_pairs={{0,4},{4,0},{8,12},{12,8},{16,20},{20,16},{24,28},{28,24},{1,5},{5... | collective-permute-start | bytes 294920 | tf_op jit(solution)/shard_map/ppermute | solution.py:493
  10.9 1.2 %collective-permute-done.1 = f16[8,48,128]{2,1,0:T(8,128)(2,1)S(1)} collective-permute-done((f16[8,48,128]{2,1,0:T(8,128)(2,1)S(1)}, f16[8,48,128]{2,1,0:T(8,128)(2,1)S(1)}, u32[]{:S(2)}, u32[]{:S(2)}) %collective-permute-start.1) | collective-permute-done | bytes 98336 | tf_op jit(solution)/shard_map/ppermute | solution.py:493
  12.1 0.0 copy-start.2
  12.1 2.8 %collective-permute-start.2 = (f16[8,48,128]{2,1,0:T(8,128)(2,1)S(1)}, f16[8,48,128]{2,1,0:T(8,128)(2,1)S(1)}, u32[]{:S(2)}, u32[]{:S(2)}) collective-permute-start(f16[8,48,128]{2,1,0:T(8,128)(2,1)S(1)} %add_convert_fusion.2), channel_id=1, source_target_pairs={{0,24},{4,28},{8,16},{12,20},{16,8},{20,12},{24,0},{28,4},{1,25},{... | collective-permute-start | bytes 294920 | tf_op jit(solution)/shard_map/ppermute | solution.py:493
  14.9 1.2 %collective-permute-start.7 = (f16[8,48,128]{2,1,0:T(8,128)(2,1)S(1)}, f16[8,48,128]{2,1,0:T(8,128)(2,1)S(1)}, u32[]{:S(2)}, u32[]{:S(2)}) collective-permute-start(f16[8,48,128]{2,1,0:T(8,128)(2,1)S(1)} %convert_element_type.49), channel_id=1, source_target_pairs={{0,4},{4,0},{8,12},{12,8},{16,20},{20,16},{24,28},{28,24},{1,5},{5... | collective-permute-start | bytes 294920 | tf_op jit(solution)/shard_map/ppermute | solution.py:493
  16.1 0.0 collective-permute-done.3
  16.2 0.4 collective-permute-start.4
  16.5 0.0 collective-permute-done.5
  16.6 1.4 %collective-permute-start.6 = (f16[8,48,128]{2,1,0:T(8,128)(2,1)S(1)}, f16[8,48,128]{2,1,0:T(8,128)(2,1)S(1)}, u32[]{:S(2)}, u32[]{:S(2)}) collective-permute-start(f16[8,48,128]{2,1,0:T(8,128)(2,1)S(1)} %add_convert_fusion), channel_id=1, source_target_pairs={{0,8},{4,12},{8,0},{12,4},{16,24},{20,28},{24,16},{28,20},{1,9},{5... | collective-permute-start | bytes 294920 | tf_op jit(solution)/shard_map/ppermute | solution.py:493
  17.9 0.0 copy-done
  17.9 0.0 copy-done.3
  17.9 0.0 copy-done.4
  17.9 0.0 copy-done.5
  18.0 0.0 copy-done.6
  18.0 2.8 %shard_map.130 = (f32[8,48,128]{2,1,0:T(8,128)S(1)}, s32[87]{0:T(128)S(1)}) custom-call(s32[1]{0:T(128)} %bitcast.group, s32[1]{0:T(128)} %bitcast.1.me, s32[64]{0:T(128)S(1)} %copy-done.6, s32[64]{0:T(128)S(1)} %copy-done.3, s32[64]{0:T(128)S(1)} %copy-done.4, s32[64]{0:T(128)S(1)} %copy-done.5, bf16[2,24,1024]{2,1,0:T(8,128)(2,1)S(1)} %copy-done.1, ...), custom_call_target="tpu_custom_call" | custom-call | tf_op jit(solution)/shard_map/pallas_call | solution.py:434
  20.8 0.0 collective-permute-done.2
  20.8 0.0 collective-permute-done.7
  20.8 1.9 %collective-permute-done.4 = f16[8,48,128]{2,1,0:T(8,128)(2,1)S(1)} collective-permute-done((f16[8,48,128]{2,1,0:T(8,128)(2,1)S(1)}, f16[8,48,128]{2,1,0:T(8,128)(2,1)S(1)}, u32[]{:S(2)}, u32[]{:S(2)}) %collective-permute-start.4) | collective-permute-done | bytes 98336 | tf_op jit(solution)/shard_map/ppermute | solution.py:493
  22.8 0.0 collective-permute-done.6
  22.8 0.1 convert_add_fusion.totals
  22.9 0.0 copy-done.2
  22.9 0.9 %collective-permute-start.9 = (bf16[8,48,128]{2,1,0:T(8,128)(2,1)S(1)}, bf16[8,48,128]{2,1,0:T(8,128)(2,1)S(1)}, u32[]{:S(2)}, u32[]{:S(2)}) collective-permute-start(bf16[8,48,128]{2,1,0:T(8,128)(2,1)S(1)} %shard_map.133.signal), channel_id=1, source_target_pairs={{0,8},{4,12},{8,0},{12,4},{16,24},{20,28},{24,16},{28,20},{1,9},{5... | collective-permute-start | bytes 294920 | tf_op jit(solution)/shard_map/ppermute | solution.py:493
  23.8 2.9 %collective-permute-start.8 = (bf16[8,48,128]{2,1,0:T(8,128)(2,1)S(1)}, bf16[8,48,128]{2,1,0:T(8,128)(2,1)S(1)}, u32[]{:S(2)}, u32[]{:S(2)}) collective-permute-start(bf16[8,48,128]{2,1,0:T(8,128)(2,1)S(1)} %shard_map.133.signal), channel_id=1, source_target_pairs={{0,24},{4,28},{8,16},{12,20},{16,8},{20,12},{24,0},{28,4},{1,25},{... | collective-permute-start | bytes 294920 | tf_op jit(solution)/shard_map/ppermute | solution.py:493
  26.7 0.2 collective-permute-start.10
  26.9 0.0 collective-permute-done.9.rest_0_
  26.9 1.3 %collective-permute-start.13 = (bf16[16,48,128]{2,1,0:T(8,128)(2,1)S(1)}, bf16[16,48,128]{2,1,0:T(8,128)(2,1)S(1)}, u32[]{:S(2)}, u32[]{:S(2)}) collective-permute-start(bf16[16,48,128]{2,1,0:T(8,128)(2,1)S(1)} %pad_maximum_fusion), channel_id=1, source_target_pairs={{0,4},{4,0},{8,12},{12,8},{16,20},{20,16},{24,28},{28,24},{1,5},{5... | collective-permute-start | bytes 589832 | tf_op jit(solution)/shard_map/ppermute | solution.py:493
  28.2 1.3 %shard_map.134.start = f32[640,128]{1,0:T(8,128)S(1)} custom-call(s32[64]{0:T(128)S(1)} %copy-done.3, s32[64]{0:T(128)S(1)} %copy-done.4, s32[64]{0:T(128)S(1)} %copy-done.5, bf16[8,48,128]{2,1,0:T(8,128)(2,1)S(1)} %shard_map.133.signal, bf16[64,128,128]{2,1,0:T(8,128)(2,1)S(1)} %copy-done), custom_call_target="tpu_custom_call" | custom-call | tf_op jit(solution)/shard_map/pallas_call | solution.py:434
  29.6 0.3 collective-permute-done.8.rest_2_
  29.9 0.3 collective-permute-start.11
  30.2 4.9 %collective-permute-done.10.rest_1_ = bf16[8,48,128]{2,1,0:T(8,128)(2,1)S(1)} collective-permute-done((bf16[8,48,128]{2,1,0:T(8,128)(2,1)S(1)}, bf16[8,48,128]{2,1,0:T(8,128)(2,1)S(1)}, u32[]{:S(2)}, u32[]{:S(2)}) %collective-permute-start.10) | collective-permute-done | bytes 98336 | tf_op jit(solution)/shard_map/ppermute | solution.py:493
  35.1 0.1 collective-permute-start.12
  35.2 1.0 %shard_map.135.start = f32[640,128]{1,0:T(8,128)S(1)} custom-call(s32[87]{0:T(128)S(1)} %get-tuple-element.36.table, s32[128]{0:T(128)S(1)} %get-tuple-element.25.ahead, bf16[64,128,128]{2,1,0:T(8,128)(2,1)S(1)} %get-tuple-element.26.mats, f32[640,128]{1,0:T(8,128)S(1)} %shard_map.134.start, bf16[8,48,128]{2,1,0:T(8,128)(2,1)S(1)} %collective-permute-done.9.rest_0_, ...), custom_call_target="tpu_custom_call" | custom-call | flops 500000000 | bytes 1500000 | tf_op jit(solution)/shard_map/pallas_call | solution.py:434
  36.2 0.0 collective-permute-done.11.rest_0_
  36.2 3.0 %collective-permute-done.12.rest_1_ = bf16[8,48,128]{2,1,0:T(8,128)(2,1)S(1)} collective-permute-done((bf16[8,48,128]{2,1,0:T(8,128)(2,1)S(1)}, bf16[8,48,128]{2,1,0:T(8,128)(2,1)S(1)}, u32[]{:S(2)}, u32[]{:S(2)}) %collective-permute-start.12) | collective-permute-done | bytes 98336 | tf_op jit(solution)/shard_map/ppermute | solution.py:493
  39.2 0.0 collective-permute-done.13.rest_2_
  39.2 1.1 %shard_map.136 = (f32[640,128]{1,0:T(8,128)S(1)}, f32[16,16,128]{2,1,0:T(8,128)S(1)}) custom-call(s32[87]{0:T(128)S(1)} %get-tuple-element.36.table, s32[128]{0:T(128)S(1)} %get-tuple-element.25.ahead, bf16[64,128,128]{2,1,0:T(8,128)(2,1)S(1)} %get-tuple-element.26.mats, f32[640,128]{1,0:T(8,128)S(1)} %shard_map.135.start, ...), custom_call_target="tpu_custom_call" | custom-call | tf_op jit(solution)/shard_map/pallas_call | solution.py:434
  40.4 2.4 %collective-permute-start.14 = (f16[16,16,128]{2,1,0:T(8,128)(2,1)S(1)}, f16[16,16,128]{2,1,0:T(8,128)(2,1)S(1)}, u32[]{:S(2)}, u32[]{:S(2)}) collective-permute-start(f16[16,16,128]{2,1,0:T(8,128)(2,1)S(1)} %convert_element_type.62), channel_id=1, source_target_pairs={{0,3},{1,0},{2,1},{3,2},{4,7},{5,4},{6,5},{7,6},{8,11},{9,8},{10,9... | collective-permute-start | bytes 196616 | tf_op jit(solution)/shard_map/ppermute | solution.py:553
  42.9 0.7 %shard_map.137 = f32[2,24,1024]{2,1,0:T(8,128)} custom-call(f32[8,48,128]{2,1,0:T(8,128)S(1)} %convert_add_fusion.totals, f32[2,24,1024]{2,1,0:T(8,128)S(1)} %copy-done.2), custom_call_target="tpu_custom_call" | custom-call | tf_op jit(solution)/shard_map/pallas_call | solution.py:434
  43.6 1.0 %collective-permute-done.14 = f16[16,16,128]{2,1,0:T(8,128)(2,1)S(1)} collective-permute-done((f16[16,16,128]{2,1,0:T(8,128)(2,1)S(1)}, f16[16,16,128]{2,1,0:T(8,128)(2,1)S(1)}, u32[]{:S(2)}, u32[]{:S(2)}) %collective-permute-start.14) | collective-permute-done | bytes 65568 | tf_op jit(solution)/shard_map/ppermute | solution.py:553
  44.6 0.8 %shard_map.138 = (f32[2,24,1024]{2,1,0:T(8,128)}, f32[2,24,1024]{2,1,0:T(8,128)}) custom-call(s32[1]{0:T(128)} %bitcast.group, f32[640,128]{1,0:T(8,128)S(1)} %get-tuple-element.41.total, f32[16,16,128]{2,1,0:T(8,128)S(1)} %convert_element_type.63.spill, bf16[2,24,1024]{2,1,0:T(8,128)(2,1)S(1)} %copy-done.1), custom_call_target="tpu_custom_call" | custom-call | tf_op jit(solution)/shard_map/pallas_call | solution.py:434
  (11 shorter events, 0.3 us)
Async XLA Ops:
  0.6 4.9 %copy-start.1 = (bf16[2,24,1024]{2,1,0:T(8,128)(2,1)S(1)}, bf16[2,24,1024]{2,1,0:T(8,128)(2,1)}, u32[]{:S(2)}) copy-start(bf16[2,24,1024]{2,1,0:T(8,128)(2,1)} %flows.5) | copy-start | bytes 294916
  0.6 4.9 %collective-permute-start = (bf16[2,24,1024]{2,1,0:T(8,128)(2,1)}, bf16[2,24,1024]{2,1,0:T(8,128)(2,1)S(1)}, u32[]{:S(2)}, u32[]{:S(2)}) collective-permute-start(bf16[2,24,1024]{2,1,0:T(8,128)(2,1)} %flows.5), channel_id=1, source_target_pairs={{0,1},{1,2},{2,3},{3,0},{4,5},{5,6},{6,7},{7,4},{8,9},{9,10},{10,1... | collective-permute-start | bytes 294920 | tf_op jit(solution)/shard_map/ppermute | solution.py:477
  5.6 12.4 %copy-start = (bf16[64,128,128]{2,1,0:T(8,128)(2,1)S(1)}, bf16[64,128,128]{2,1,0:T(8,128)(2,1)}, u32[]{:S(2)}) copy-start(bf16[64,128,128]{2,1,0:T(8,128)(2,1)} %mats.3) | copy-start | bytes 6291460
  5.6 12.4 %copy-start.3 = (s32[64]{0:T(128)S(1)}, s32[64]{0:T(128)}, u32[]{:S(2)}) copy-start(s32[64]{0:T(128)} %path.3) | copy-start | bytes 772
  5.6 12.4 %copy-start.4 = (s32[64]{0:T(128)S(1)}, s32[64]{0:T(128)}, u32[]{:S(2)}) copy-start(s32[64]{0:T(128)} %link.3) | copy-start | bytes 772
  5.6 12.4 %copy-start.5 = (s32[64]{0:T(128)S(1)}, s32[64]{0:T(128)}, u32[]{:S(2)}) copy-start(s32[64]{0:T(128)} %lag.3) | copy-start | bytes 772
  5.6 12.4 %copy-start.6 = (s32[64]{0:T(128)S(1)}, s32[64]{0:T(128)}, u32[]{:S(2)}) copy-start(s32[64]{0:T(128)} %rest_3_.1) | copy-start | bytes 772
  7.9 4.2 %collective-permute-start.1 = (f16[8,48,128]{2,1,0:T(8,128)(2,1)S(1)}, f16[8,48,128]{2,1,0:T(8,128)(2,1)S(1)}, u32[]{:S(2)}, u32[]{:S(2)}) collective-permute-start(f16[8,48,128]{2,1,0:T(8,128)(2,1)S(1)} %convert_element_type.48), channel_id=1, source_target_pairs={{0,4},{4,0},{8,12},{12,8},{16,20},{20,16},{24,28},{28,24},{1,5},{5... | collective-permute-start | bytes 294920 | tf_op jit(solution)/shard_map/ppermute | solution.py:493
  9.3 6.9 %collective-permute-start.3 = (f16[8,48,128]{2,1,0:T(8,128)(2,1)S(1)}, f16[8,48,128]{2,1,0:T(8,128)(2,1)S(1)}, u32[]{:S(2)}, u32[]{:S(2)}) collective-permute-start(f16[8,48,128]{2,1,0:T(8,128)(2,1)S(1)} %convert_element_type.53), channel_id=1, source_target_pairs={{0,4},{4,0},{8,12},{12,8},{16,20},{20,16},{24,28},{28,24},{1,5},{5... | collective-permute-start | bytes 294920 | tf_op jit(solution)/shard_map/ppermute | solution.py:493
  9.6 6.9 %collective-permute-start.5 = (f16[8,48,128]{2,1,0:T(8,128)(2,1)S(1)}, f16[8,48,128]{2,1,0:T(8,128)(2,1)S(1)}, u32[]{:S(2)}, u32[]{:S(2)}) collective-permute-start(f16[8,48,128]{2,1,0:T(8,128)(2,1)S(1)} %convert_element_type.57), channel_id=1, source_target_pairs={{0,4},{4,0},{8,12},{12,8},{16,20},{20,16},{24,28},{28,24},{1,5},{5... | collective-permute-start | bytes 294920 | tf_op jit(solution)/shard_map/ppermute | solution.py:493
  12.1 10.8 %copy-start.2 = (f32[2,24,1024]{2,1,0:T(8,128)S(1)}, f32[2,24,1024]{2,1,0:T(8,128)}, u32[]{:S(2)}) copy-start(f32[2,24,1024]{2,1,0:T(8,128)} %counts.3) | copy-start | bytes 589828
  12.1 8.7 %collective-permute-start.2 = (f16[8,48,128]{2,1,0:T(8,128)(2,1)S(1)}, f16[8,48,128]{2,1,0:T(8,128)(2,1)S(1)}, u32[]{:S(2)}, u32[]{:S(2)}) collective-permute-start(f16[8,48,128]{2,1,0:T(8,128)(2,1)S(1)} %add_convert_fusion.2), channel_id=1, source_target_pairs={{0,24},{4,28},{8,16},{12,20},{16,8},{20,12},{24,0},{28,4},{1,25},{... | collective-permute-start | bytes 294920 | tf_op jit(solution)/shard_map/ppermute | solution.py:493
  14.9 5.9 %collective-permute-start.7 = (f16[8,48,128]{2,1,0:T(8,128)(2,1)S(1)}, f16[8,48,128]{2,1,0:T(8,128)(2,1)S(1)}, u32[]{:S(2)}, u32[]{:S(2)}) collective-permute-start(f16[8,48,128]{2,1,0:T(8,128)(2,1)S(1)} %convert_element_type.49), channel_id=1, source_target_pairs={{0,4},{4,0},{8,12},{12,8},{16,20},{20,16},{24,28},{28,24},{1,5},{5... | collective-permute-start | bytes 294920 | tf_op jit(solution)/shard_map/ppermute | solution.py:493
  16.2 6.6 %collective-permute-start.4 = (f16[8,48,128]{2,1,0:T(8,128)(2,1)S(1)}, f16[8,48,128]{2,1,0:T(8,128)(2,1)S(1)}, u32[]{:S(2)}, u32[]{:S(2)}) collective-permute-start(f16[8,48,128]{2,1,0:T(8,128)(2,1)S(1)} %add_convert_fusion.1), channel_id=1, source_target_pairs={{0,16},{4,20},{8,24},{12,28},{16,0},{20,4},{24,8},{28,12},{1,17},{... | collective-permute-start | bytes 294920 | tf_op jit(solution)/shard_map/ppermute | solution.py:493
  16.6 6.2 %collective-permute-start.6 = (f16[8,48,128]{2,1,0:T(8,128)(2,1)S(1)}, f16[8,48,128]{2,1,0:T(8,128)(2,1)S(1)}, u32[]{:S(2)}, u32[]{:S(2)}) collective-permute-start(f16[8,48,128]{2,1,0:T(8,128)(2,1)S(1)} %add_convert_fusion), channel_id=1, source_target_pairs={{0,8},{4,12},{8,0},{12,4},{16,24},{20,28},{24,16},{28,20},{1,9},{5... | collective-permute-start | bytes 294920 | tf_op jit(solution)/shard_map/ppermute | solution.py:493
  22.9 4.0 %collective-permute-start.9 = (bf16[8,48,128]{2,1,0:T(8,128)(2,1)S(1)}, bf16[8,48,128]{2,1,0:T(8,128)(2,1)S(1)}, u32[]{:S(2)}, u32[]{:S(2)}) collective-permute-start(bf16[8,48,128]{2,1,0:T(8,128)(2,1)S(1)} %shard_map.133.signal), channel_id=1, source_target_pairs={{0,8},{4,12},{8,0},{12,4},{16,24},{20,28},{24,16},{28,20},{1,9},{5... | collective-permute-start | bytes 294920 | tf_op jit(solution)/shard_map/ppermute | solution.py:493
  23.8 6.1 %collective-permute-start.8 = (bf16[8,48,128]{2,1,0:T(8,128)(2,1)S(1)}, bf16[8,48,128]{2,1,0:T(8,128)(2,1)S(1)}, u32[]{:S(2)}, u32[]{:S(2)}) collective-permute-start(bf16[8,48,128]{2,1,0:T(8,128)(2,1)S(1)} %shard_map.133.signal), channel_id=1, source_target_pairs={{0,24},{4,28},{8,16},{12,20},{16,8},{20,12},{24,0},{28,4},{1,25},{... | collective-permute-start | bytes 294920 | tf_op jit(solution)/shard_map/ppermute | solution.py:493
  26.7 8.4 %collective-permute-start.10 = (bf16[8,48,128]{2,1,0:T(8,128)(2,1)S(1)}, bf16[8,48,128]{2,1,0:T(8,128)(2,1)S(1)}, u32[]{:S(2)}, u32[]{:S(2)}) collective-permute-start(bf16[8,48,128]{2,1,0:T(8,128)(2,1)S(1)} %shard_map.133.signal), channel_id=1, source_target_pairs={{0,16},{4,20},{8,24},{12,28},{16,0},{20,4},{24,8},{28,12},{1,17},{... | collective-permute-start | bytes 294920 | tf_op jit(solution)/shard_map/ppermute | solution.py:493
  26.9 12.3 %collective-permute-start.13 = (bf16[16,48,128]{2,1,0:T(8,128)(2,1)S(1)}, bf16[16,48,128]{2,1,0:T(8,128)(2,1)S(1)}, u32[]{:S(2)}, u32[]{:S(2)}) collective-permute-start(bf16[16,48,128]{2,1,0:T(8,128)(2,1)S(1)} %pad_maximum_fusion), channel_id=1, source_target_pairs={{0,4},{4,0},{8,12},{12,8},{16,20},{20,16},{24,28},{28,24},{1,5},{5... | collective-permute-start | bytes 589832 | tf_op jit(solution)/shard_map/ppermute | solution.py:493
  29.9 6.3 %collective-permute-start.11 = (bf16[8,48,128]{2,1,0:T(8,128)(2,1)S(1)}, bf16[8,48,128]{2,1,0:T(8,128)(2,1)S(1)}, u32[]{:S(2)}, u32[]{:S(2)}) collective-permute-start(bf16[8,48,128]{2,1,0:T(8,128)(2,1)S(1)} %collective-permute-done.8.rest_2_), channel_id=1, source_target_pairs={{0,4},{4,0},{8,12},{12,8},{16,20},{20,16},{24,28},{28,24},{1,5},{5... | collective-permute-start | bytes 294920 | tf_op jit(solution)/shard_map/ppermute | solution.py:493
  35.1 4.2 %collective-permute-start.12 = (bf16[8,48,128]{2,1,0:T(8,128)(2,1)S(1)}, bf16[8,48,128]{2,1,0:T(8,128)(2,1)S(1)}, u32[]{:S(2)}, u32[]{:S(2)}) collective-permute-start(bf16[8,48,128]{2,1,0:T(8,128)(2,1)S(1)} %collective-permute-done.10.rest_1_), channel_id=1, source_target_pairs={{0,4},{4,0},{8,12},{12,8},{16,20},{20,16},{24,28},{28,24},{1,5},{5... | collective-permute-start | bytes 294920 | tf_op jit(solution)/shard_map/ppermute | solution.py:493
  40.4 4.2 %collective-permute-start.14 = (f16[16,16,128]{2,1,0:T(8,128)(2,1)S(1)}, f16[16,16,128]{2,1,0:T(8,128)(2,1)S(1)}, u32[]{:S(2)}, u32[]{:S(2)}) collective-permute-start(f16[16,16,128]{2,1,0:T(8,128)(2,1)S(1)} %convert_element_type.62), channel_id=1, source_target_pairs={{0,3},{1,0},{2,1},{3,2},{4,7},{5,4},{6,5},{7,6},{8,11},{9,8},{10,9... | collective-permute-start | bytes 196616 | tf_op jit(solution)/shard_map/ppermute | solution.py:553
